TPU v7x, 256 devices: a whole 4x4x8 slice. The times are simulated.
256 devices in a mesh: seq: 128 (over y, z, x_lo, core), slide: 2 (over x_hi).
Axes of the slice: x: 4 (x_hi: 2, x_lo: 2; x = x_hi * 2 + x_lo), y: 4, z: 8, core: 2. Of those that a mesh axis runs over, the one named last changes fastest.
Arguments:
- layer_input: bfloat16 [2, 32768, 768], P('slide', 'seq'), may hold values from -6 to 6
- cotangent: bfloat16 [2, 32768, 768], P('slide', 'seq'), may hold values from -6 to 6
- layer_norm_gain: float32 [768], replicated, may hold values from 0.25 to 1.75
- layer_norm_bias: float32 [768], replicated, may hold values from -3 to 3
- query_key_value_weight: bfloat16 [768, 2304], replicated, may hold values from -4 to 4
- output_weight: bfloat16 [768, 768], replicated, may hold values from -0.21875 to 0.21875
Outputs:
- layer_output: bfloat16 [2, 32768, 768], P('slide', 'seq')
- input_grad: bfloat16 [2, 32768, 768], P('slide', 'seq')
- grad_qkv: float32 [768, 2304], P('seq')
- grad_out: float32 [768, 768], P('seq')
- grad_gain: float32 [768], replicated
- grad_bias: float32 [768], replicated
All inputs are finite; a program needn't handle non-finite values.
Results may differ from a plain program's by a relative error of at most 0.011.
Values may be sent and summed in bfloat16 or wider, within the bound.
No kernel may reach another device: no remote copies, remote signals or barrier semaphores. Data moves between devices by JAX's collectives and lax.ppermute only.
A program may use at most 128 MiB of HBM per device.

v0:
```python
import jax
import jax.numpy as jnp
from jax import lax
from jax.sharding import Mesh
from jax.sharding import PartitionSpec as P

HEADS = 12
SEQ = ("seq_0", "seq_1", "seq_2", "seq_3")
SEQ_SLIDE = ("seq_0", "seq_1", "seq_2", "seq_3", "slide")


EPS = 1e-05


def from_behind(block, axis, distance):
    devices = range(lax.axis_size(axis))
    route = [(i - distance, i) for i in devices if i - distance in devices]
    return lax.ppermute(block, axis, route)


def one_axis_at_a_time(shard, axes):
    for axis in axes:
        shard = lax.psum(shard, axis)
    return shard


def cut_along(shard, dim, peers):
    before, after = (shard.shape[:dim], shard.shape[dim + 1 :])
    return jnp.moveaxis(shard.reshape(*before, peers, -1, *after), dim, 0)


def sent_and_summed(shard, axis, dim):
    peers = lax.axis_size(axis)
    pieces = lax.all_to_all(cut_along(shard, dim, peers), axis, 0, 0, tiled=True)
    return jnp.sum(pieces.astype(jnp.float32), axis=0)


def summed_rows(shard, axes, dim):
    far, near = axes
    own = sent_and_summed(cut_along(shard, dim, lax.axis_size(far)), near, dim + 1)
    return jnp.sum(
        lax.all_to_all(own.astype(jnp.bfloat16), far, 0, 0, tiled=True).astype(jnp.float32), axis=0
    )


def sent_to_all(shard, axis):
    copies = jnp.broadcast_to(shard, (lax.axis_size(axis), *shard.shape))
    return lax.all_to_all(copies, axis, split_axis=0, concat_axis=0, tiled=True)


def over_copies(shard, axis):
    return sent_to_all(shard, axis).astype(jnp.float32).sum(axis=0)


def apply_layer_norm(token_rows, scale_gain, shift_bias):
    values = token_rows.astype(jnp.float32)
    centered_rows = values - jnp.mean(values, axis=-1, keepdims=True)
    inverse_deviation = lax.rsqrt(
        jnp.mean(centered_rows * centered_rows, axis=-1, keepdims=True) + EPS
    )
    normalized_rows = centered_rows * inverse_deviation
    return (
        (normalized_rows * scale_gain + shift_bias).astype(jnp.bfloat16),
        normalized_rows,
        inverse_deviation,
    )


def attend(qkv_self, memory_key_value, memory_present):
    token_length = qkv_self.shape[0]
    feature_width = memory_key_value.shape[1] // 2
    head_dim = feature_width // HEADS
    query = qkv_self[:, :feature_width].reshape(token_length, HEADS, head_dim)
    keys = jnp.concatenate(
        [memory_key_value[:, :feature_width], qkv_self[:, feature_width : 2 * feature_width]], 0
    ).reshape(2 * token_length, HEADS, head_dim)
    values = jnp.concatenate(
        [memory_key_value[:, feature_width:], qkv_self[:, 2 * feature_width :]], 0
    ).reshape(2 * token_length, HEADS, head_dim)
    scores = jnp.einsum(
        "qhe,khe->hqk", query, keys, preferred_element_type=jnp.float32
    ) * head_dim ** (-0.5)
    row_ids = lax.broadcasted_iota(jnp.int32, (token_length, 2 * token_length), 0)
    col_ids = lax.broadcasted_iota(jnp.int32, (token_length, 2 * token_length), 1)
    allowed = jnp.where(col_ids < token_length, memory_present, col_ids - token_length <= row_ids)
    scores = jnp.where(allowed[None], scores, -1e30)
    top = jnp.max(scores, axis=-1, keepdims=True)
    weights = jnp.exp(scores - top)
    probs = weights / jnp.sum(weights, axis=-1, keepdims=True)
    probs_b = probs.astype(jnp.bfloat16)
    mixed = jnp.einsum("hqk,khe->qhe", probs_b, values, preferred_element_type=jnp.float32)
    mixed = mixed.reshape(token_length, feature_width).astype(jnp.bfloat16)
    return (mixed, probs, probs_b, query, keys, values)


def attend_back(d_mixed, probs, probs_b, query, keys, values):
    token_length, heads, head_dim = query.shape
    grad_heads = d_mixed.reshape(token_length, heads, head_dim)
    d_probs = jnp.einsum("qhe,khe->hqk", grad_heads, values, preferred_element_type=jnp.float32)
    d_scores = probs * (d_probs - jnp.sum(d_probs * probs, axis=-1, keepdims=True))
    d_scores_b = (d_scores * head_dim ** (-0.5)).astype(jnp.bfloat16)
    d_query = jnp.einsum("hqk,khe->qhe", d_scores_b, keys, preferred_element_type=jnp.float32)
    d_keys = jnp.einsum("hqk,qhe->khe", d_scores_b, query, preferred_element_type=jnp.float32)
    d_values = jnp.einsum("hqk,qhe->khe", probs_b, grad_heads, preferred_element_type=jnp.float32)
    return (
        d_query.reshape(token_length, -1).astype(jnp.bfloat16),
        d_keys.reshape(2 * token_length, -1).astype(jnp.bfloat16),
        d_values.reshape(2 * token_length, -1).astype(jnp.bfloat16),
    )


def block_forward(
    token_rows,
    gradient_list,
    current_query_key_value,
    memory_key_value,
    memory_present,
    current_normed,
    current_normalized,
    current_inverse_deviation,
    query_key_value_weight,
    output_weight,
    scale_gain,
):
    token_length = token_rows.shape[0]
    mixed, probs, probs_b, query, keys, values = attend(
        current_query_key_value, memory_key_value, memory_present
    )
    block_output = (
        token_rows.astype(jnp.float32)
        + jnp.dot(mixed, output_weight, preferred_element_type=jnp.float32)
    ).astype(jnp.bfloat16)
    d_mixed = jnp.dot(gradient_list, output_weight.T, preferred_element_type=jnp.float32).astype(
        jnp.bfloat16
    )
    grad_wout = jnp.dot(mixed.T, gradient_list, preferred_element_type=jnp.float32)
    d_query, d_keys, d_values = attend_back(d_mixed, probs, probs_b, query, keys, values)
    d_own = jnp.concatenate([d_query, d_keys[token_length:], d_values[token_length:]], 1)
    memory_gradient = jnp.concatenate([d_keys[:token_length], d_values[:token_length]], 1)
    grad_wqkv = jnp.dot(current_normed.T, d_own, preferred_element_type=jnp.float32)
    normed_gradient = jnp.dot(d_own, query_key_value_weight.T, preferred_element_type=jnp.float32)
    gain_gradient = jnp.sum(normed_gradient * current_normalized, axis=0)
    grad_b = jnp.sum(normed_gradient, axis=0)
    normalized_gradient = normed_gradient * scale_gain
    row_gradient = current_inverse_deviation * (
        normalized_gradient
        - jnp.mean(normalized_gradient, axis=-1, keepdims=True)
        - current_normalized
        * jnp.mean(normalized_gradient * current_normalized, axis=-1, keepdims=True)
    )
    input_gradient = (gradient_list.astype(jnp.float32) + row_gradient).astype(jnp.bfloat16)
    return (
        block_output,
        input_gradient,
        memory_gradient,
        (grad_wqkv, grad_wout, gain_gradient, grad_b),
    )


def memory_contributions(prior_normed, prior_normalized, memory_gradient, query_key_value_weight):
    feature_width = prior_normed.shape[1]
    key_value_gradient = jnp.dot(
        prior_normed.T, memory_gradient, preferred_element_type=jnp.float32
    )
    normed_gradient = jnp.dot(
        memory_gradient,
        query_key_value_weight[:, feature_width:].T,
        preferred_element_type=jnp.float32,
    )
    return (
        key_value_gradient,
        jnp.sum(normed_gradient * prior_normalized, axis=0),
        jnp.sum(normed_gradient, axis=0),
    )


def on_device(
    layer_input, cotangent, layer_norm_gain, layer_norm_bias, query_key_value_weight, output_weight
):
    token_rows = layer_input[0]
    gradient_list = cotangent[0]
    feature_width = token_rows.shape[1]
    normed_rows, normalized_rows, inverse_deviation = apply_layer_norm(
        token_rows, layer_norm_gain, layer_norm_bias
    )
    query_key_value = jnp.dot(
        normed_rows, query_key_value_weight, preferred_element_type=jnp.float32
    ).astype(jnp.bfloat16)
    has_first = lax.axis_index(SEQ) > 0
    previous_token_rows = from_behind(token_rows, SEQ, 1)
    previous_normed_rows, previous_normalized, ignored_value = apply_layer_norm(
        previous_token_rows, layer_norm_gain, layer_norm_bias
    )
    kv_before = jnp.dot(
        previous_normed_rows,
        query_key_value_weight[:, feature_width:],
        preferred_element_type=jnp.float32,
    ).astype(jnp.bfloat16)
    block_output, input_gradient, memory_gradient, term_list = block_forward(
        token_rows,
        gradient_list,
        query_key_value,
        kv_before,
        has_first,
        normed_rows,
        normalized_rows,
        inverse_deviation,
        query_key_value_weight,
        output_weight,
        layer_norm_gain,
    )
    acc_qkv = term_list[0]
    acc_out = term_list[1]
    acc_gain = term_list[2]
    acc_bias = term_list[3]
    key_value_gradient, memory_gain, memory_bias = memory_contributions(
        previous_normed_rows, previous_normalized, memory_gradient, query_key_value_weight
    )
    acc_gain = acc_gain + memory_gain
    acc_bias = acc_bias + memory_bias
    combined = jnp.concatenate(
        [acc_qkv[:, :feature_width], acc_qkv[:, feature_width:] + key_value_gradient, acc_out], 1
    )
    seq_count = lax.axis_size(SEQ)
    slide_count = lax.axis_size("slide")
    factor = 1.0 / float(seq_count * slide_count * token_rows.shape[0]) ** 0.5
    gain_sum, bias_sum = (
        one_axis_at_a_time(acc_gain, SEQ_SLIDE),
        one_axis_at_a_time(acc_bias, SEQ_SLIDE),
    )
    shard = summed_rows(combined.astype(jnp.bfloat16), (("seq_0", "seq_1", "seq_2"), "seq_3"), 0)
    shard = over_copies(shard.astype(jnp.bfloat16), "slide").astype(jnp.float32)
    shard = shard * factor
    layer_output = block_output[None]
    input_grad = input_gradient[None]
    return (
        layer_output,
        input_grad,
        shard[:, : 3 * feature_width],
        shard[:, 3 * feature_width :],
        gain_sum * factor,
        bias_sum * factor,
    )


def solution(mesh):
    torus = Mesh(
        mesh.devices.reshape(4, 8, 2, 2, mesh.shape["slide"]),
        ("seq_0", "seq_1", "seq_2", "seq_3", "slide"),
    )
    return jax.shard_map(
        on_device,
        mesh=torus,
        in_specs=(P("slide", SEQ, None), P("slide", SEQ, None), P(), P(), P(), P()),
        out_specs=(
            P("slide", SEQ, None),
            P("slide", SEQ, None),
            P(SEQ, None),
            P(SEQ, None),
            P(),
            P(),
        ),
        check_vma=False,
    )
```

profile of v0, /device:TPU:2, one launch (start us, length us, event | category | flops | bytes accessed | tf_op | source)
XLA Modules:
  0.0 255.8 jit_solution(15733544273675283821)
XLA Ops:
  5.1 3.4 %convolution_convert_fusion = bf16[256,2304]{1,0:T(8,128)(2,1)S(1)} fusion(bf16[768,2304]{1,0:T(8,128)(2,1)} %param.10, f32[256]{0:T(256)S(1)} %add_rsqrt_fusion, f32[256]{0:T(256)S(1)} %broadcast_multiply_fusion.5, f32[768]{0:T(1024)} %param.9, f32[768]{0:T(1024)} %param.8, bf16[1,256,768]{2,1,0:T(8,128)(2,1)} %param.6), kind=kOutput, calls=%fused_computation.11 | convolution fusion | flops 907739136 | bytes 5120000 | tf_op jit(solution)/shard_map/dot_general | solution.py:186
  13.5 2.5 convolution_convert_fusion.1
  21.0 6.8 %fusion.96 = (f32[12,256]{1,0:T(8,128)}, f32[12,256,512]{2,1,0:T(8,128)}) fusion(pred[256,512]{1,0:T(8,128)(4,1)} %fusion.70, bf16[256,12,64]{0,2,1:T(8,128)(2,1)} %bitcast.78, bf16[512,12,64]{0,2,1:T(8,128)(2,1)} %bitcast.76), kind=kOutput, calls=%fused_computation.108 | convolution fusion | flops 207618560 | bytes 7614464 | tf_op jit(solution)/shard_map/sub | solution.py:88
  27.8 4.1 %fusion.38 = bf16[12,64,256]{2,1,0:T(8,128)(2,1)S(1)} fusion(bf16[512,12,64]{0,2,1:T(8,128)(2,1)S(1)} %bitcast.62, f32[12,256,512]{2,1,0:T(8,128)} %get-tuple-element.32, f32[12,256]{1,0:T(8,128)} %get-tuple-element.31), kind=kOutput, calls=%fused_computation.36 | convolution fusion | flops 204668928 | bytes 7483392 | tf_op jit(solution)/shard_map/hqk,khe->qhe/dot_general | solution.py:91
  34.1 3.7 %fusion.97 = f32[12,256,512]{2,1,0:T(8,128)} fusion(bf16[256,12,64]{0,2,1:T(8,128)(2,1)S(1)} %bitcast.65, bf16[512,12,64]{0,2,1:T(8,128)(2,1)S(1)} %bitcast.63), kind=kOutput, calls=%fused_computation.109 | convolution fusion | flops 201326592 | bytes 7471104 | tf_op jit(solution)/shard_map/qhe,khe->hqk/dot_general | solution.py:99
  37.8 23.1 %fusion.34 = bf16[512,12,64]{0,2,1:T(8,128)(2,1)} fusion(bf16[256,12,64]{0,2,1:T(8,128)(2,1)} %bitcast.79, f32[12,256,512]{2,1,0:T(8,128)} %fusion.97, f32[12,256,512]{2,1,0:T(8,128)} %get-tuple-element.32, f32[12,256]{1,0:T(8,128)} %get-tuple-element.31), kind=kOutput, calls=%fused_computation.33 | convolution fusion | flops 212733440 | bytes 13774848 | tf_op jit(solution)/shard_map/hqk,qhe->khe/dot_general | solution.py:103
  60.9 25.5 %fusion.41 = bf16[12,64,256]{2,1,0:T(8,128)(2,1)} fusion(bf16[512,12,64]{0,2,1:T(8,128)(2,1)S(1)} %bitcast.77, f32[12,256,512]{2,1,0:T(8,128)} %fusion.97, f32[12,256,512]{2,1,0:T(8,128)} %get-tuple-element.32, f32[12,256]{1,0:T(8,128)S(1)} %copy-done.27), kind=kOutput, calls=%fused_computation.37 | convolution fusion | flops 212536832 | bytes 13774848 | tf_op jit(solution)/shard_map/hqk,khe->qhe/dot_general | solution.py:102
  94.6 2.5 fusion.4
  97.0 4.9 %concatenate.26 = bf16[64,2,6,1536]{3,2,1,0:T(8,128)(2,1)} reshape(bf16[768,1536]{1,0:T(8,128)(2,1)} %fusion.4) | data formatting | bytes 4718592 | tf_op jit(solution)/shard_map/concatenate | solution.py:221
  102.0 3.2 %concatenate.24 = bf16[64,2,6,768]{3,2,1,0:T(8,128)(2,1)} reshape(bf16[768,768]{1,0:T(8,128)(2,1)} %slice.95) | data formatting | bytes 2359296 | tf_op jit(solution)/shard_map/concatenate | solution.py:221
  105.2 3.9 %maximum_bitcast_fusion = bf16[2,64,6,3072]{3,2,0,1:T(8,128)(2,1)S(1)} fusion(bf16[64,2,6,768]{3,2,1,0:T(8,128)(2,1)S(1)} %copy.62, bf16[64,2,6,1536]{3,2,1,0:T(8,128)(2,1)} %concatenate.26, bf16[64,2,6,768]{3,2,1,0:T(8,128)(2,1)} %concatenate.24), kind=kLoop, calls=%fused_computation.2 | loop fusion | flops 14155776 | bytes 9437184 | tf_op jit(solution)/shard_map/transpose | solution.py:29
  109.1 2.6 %copy.63 = bf16[2,64,6,3072]{3,1,2,0:T(8,128)(2,1)S(1)} copy(bf16[2,64,6,3072]{3,2,0,1:T(8,128)(2,1)S(1)} %maximum_bitcast_fusion) | data formatting | bytes 9437184 | tf_op jit(solution)/shard_map/transpose | solution.py:29
  111.7 10.1 %all_to_all.15 = bf16[2,64,6,3072]{3,1,2,0:T(8,128)(2,1)} all-to-all(bf16[2,64,6,3072]{3,1,2,0:T(8,128)(2,1)S(1)} %copy.63), channel_id=1, replica_groups=mesh['seq_0'=4,'seq_1'=8,'seq_2'=2,'seq_3'=2,'slide'=2] {'seq_3'}, dimensions={0} | all-to-all | bytes 9437184 | tf_op jit(solution)/shard_map/all_to_all | solution.py:34
  121.8 5.5 %reduce_sum.149 = bf16[64,6,3072]{2,0,1:T(8,128)(2,1)} reduce(bf16[2,64,6,3072]{3,1,2,0:T(8,128)(2,1)} %all_to_all.15, bf16[]{:T(256)} %constant.51.clone.1), dimensions={0}, to_apply=%region_9.10 | reduce | flops 1179648 | bytes 7077890 | tf_op jit(solution)/shard_map/reduce_sum | solution.py:35
  127.3 4.6 %copy.64 = bf16[64,6,3072]{2,1,0:T(8,128)(2,1)} copy(bf16[64,6,3072]{2,0,1:T(8,128)(2,1)} %reduce_sum.149) | data formatting | bytes 4718592 | tf_op jit(solution)/shard_map/reduce_sum | solution.py:35
  132.0 12.5 %all-to-all-start.1 = ((bf16[64,6,3072]{2,1,0:T(8,128)(2,1)}), bf16[64,6,3072]{2,1,0:T(8,128)(2,1)}, u32[]{:S(2)}, u32[]{:S(2)}) async-start(bf16[64,6,3072]{2,1,0:T(8,128)(2,1)} %copy.64), calls=%async_computation.1 | async-start | bytes 6291456 | tf_op jit(solution)/shard_map/all_to_all | solution.py:42
  144.6 2.7 %fusion.91 = (f32[768]{0:T(1024)S(1)}, f32[768]{0:T(1024)S(1)}) fusion(f32[256]{0:T(256)} %copy-done.22, f32[256]{0:T(256)S(1)} %copy-done.21, bf16[256,768]{1,0:T(8,128)(2,1)S(1)} %collective-permute-done, bf16[768,2304]{1,0:T(8,128)(2,1)} %param.10, bf16[256,768]{0,1:T(8,128)(2,1)S(1)} %bitcast.73, bf16[256,768]{0,1:T(8,128)(2,1)S(1)} %bitcast.75), kind=kOutput, calls=%fused_computation.103 | convolution fusion | flops 606730752 | bytes 3547136 | tf_op jit(solution)/shard_map/dot_general | solution.py:165
  149.6 10.9 %all-reduce.1 = (f32[768]{0:T(1024)S(1)}, f32[768]{0:T(1024)S(1)}) all-reduce(f32[768]{0:T(1024)S(1)} %add.86, f32[768]{0:T(1024)S(1)} %add.87), channel_id=1, replica_groups=mesh['seq_0'=4,'seq_1'=8,'seq_2'=2,'seq_3'=2,'slide'=2] {'seq_0'}, use_global_device_ids=true, to_apply=%region_14.15 | all-reduce | flops 1536 | bytes 12288 | tf_op jit(solution)/shard_map/psum | solution.py:23
  160.5 63.8 %all-reduce = (f32[768]{0:T(1024)S(1)}, f32[768]{0:T(1024)S(1)}) all-reduce(f32[768]{0:T(1024)S(1)} %get-tuple-element.14, f32[768]{0:T(1024)S(1)} %get-tuple-element.15), channel_id=1, replica_groups=mesh['seq_0'=4,'seq_1'=8,'seq_2'=2,'seq_3'=2,'slide'=2] {'seq_1'}, use_global_device_ids=true, to_apply=%region_15.16 | all-reduce | flops 1536 | bytes 12288 | tf_op jit(solution)/shard_map/psum | solution.py:23
  224.2 5.0 %all-reduce.4 = (f32[768]{0:T(1024)S(1)}, f32[768]{0:T(1024)S(1)}) all-reduce(f32[768]{0:T(1024)S(1)} %get-tuple-element.12, f32[768]{0:T(1024)S(1)} %get-tuple-element.13), channel_id=1, replica_groups=mesh['seq_0'=4,'seq_1'=8,'seq_2'=2,'seq_3'=2,'slide'=2] {'seq_2'}, use_global_device_ids=true, to_apply=%region_16.17 | all-reduce | flops 1536 | bytes 12288 | tf_op jit(solution)/shard_map/psum | solution.py:23
  231.7 6.5 %all-reduce.2 = (f32[768]{0:T(1024)S(1)}, f32[768]{0:T(1024)S(1)}) all-reduce(f32[768]{0:T(1024)S(1)} %get-tuple-element.18, f32[768]{0:T(1024)S(1)} %get-tuple-element.19), channel_id=1, replica_groups=mesh['seq_0'=4,'seq_1'=8,'seq_2'=2,'seq_3'=2,'slide'=2] {'slide'}, use_global_device_ids=true, to_apply=%region_18.19 | all-reduce | flops 1536 | bytes 12288 | tf_op jit(solution)/shard_map/psum | solution.py:23
  241.9 2.5 reduce_sum.150
  245.0 3.7 %all-to-all-start.2 = ((bf16[2,6,3072]{2,1,0:T(8,128)(2,1)}), bf16[2,6,3072]{2,1,0:T(8,128)(2,1)S(1)}, u32[]{:S(2)}, u32[]{:S(2)}) async-start(bf16[2,6,3072]{2,1,0:T(8,128)(2,1)} %broadcast_in_dim.27), calls=%async_computation.2 | async-start | bytes 196608 | tf_op jit(solution)/shard_map/all_to_all | solution.py:48
  250.0 4.5 %all-to-all-done.2 = bf16[2,6,3072]{2,1,0:T(8,128)(2,1)S(1)} async-done(((bf16[2,6,3072]{2,1,0:T(8,128)(2,1)}), bf16[2,6,3072]{2,1,0:T(8,128)(2,1)S(1)}, u32[]{:S(2)}, u32[]{:S(2)}) %all-to-all-start.2) | async-done | bytes 73760 | tf_op jit(solution)/shard_map/all_to_all | solution.py:48
  (101 shorter events, 36.1 us)
Async XLA Ops:
  0.6 8.0 %copy-start = (bf16[768,768]{1,0:T(8,128)(2,1)S(1)}, bf16[768,768]{1,0:T(8,128)(2,1)}, u32[]{:S(2)}) copy-start(bf16[768,768]{1,0:T(8,128)(2,1)} %param.11) | copy-start | bytes 3538948
  0.6 11.5 %collective-permute-start = (bf16[256,768]{1,0:T(8,128)(2,1)}, bf16[256,768]{1,0:T(8,128)(2,1)S(1)}, u32[]{:S(2)}, u32[]{:S(2)}) collective-permute-start(bf16[256,768]{1,0:T(8,128)(2,1)} %bitcast.61), channel_id=1, source_target_pairs={{0,2},{2,4},{4,6},{6,8},{8,10},{10,12},{12,14},{14,16},{16,18},{18... | collective-permute-start | bytes 1179656 | tf_op jit(solution)/shard_map/ppermute | solution.py:18
  5.1 3.5 %copy-start.2 = (bf16[1,256,768]{2,1,0:T(8,128)(2,1)S(1)}, bf16[1,256,768]{2,1,0:T(8,128)(2,1)}, u32[]{:S(2)}) copy-start(bf16[1,256,768]{2,1,0:T(8,128)(2,1)} %param.7) | copy-start | bytes 1179652
  8.5 5.0 %copy-start.17 = (f32[768]{0:T(1024)S(1)}, f32[768]{0:T(1024)}, u32[]{:S(2)}) copy-start(f32[768]{0:T(1024)} %param.8) | copy-start | bytes 9220
  8.5 5.0 %copy-start.18 = (f32[768]{0:T(1024)S(1)}, f32[768]{0:T(1024)}, u32[]{:S(2)}) copy-start(f32[768]{0:T(1024)} %param.9) | copy-start | bytes 9220
  27.8 4.6 %copy-start.25 = (f32[12,256,512]{2,1,0:T(8,128)S(1)}, f32[12,256,512]{2,1,0:T(8,128)}, u32[]{:S(2)}) copy-start(f32[12,256,512]{2,1,0:T(8,128)} %get-tuple-element.32) | copy-start | bytes 18874372
  27.8 4.6 %copy-start.26 = (f32[12,256]{1,0:T(8,128)S(1)}, f32[12,256]{1,0:T(8,128)}, u32[]{:S(2)}) copy-start(f32[12,256]{1,0:T(8,128)} %get-tuple-element.31) | copy-start | bytes 36868
  31.9 58.8 %copy-start.4 = (bf16[12,64,256]{2,1,0:T(8,128)(2,1)}, bf16[12,64,256]{2,1,0:T(8,128)(2,1)S(1)}, u32[]{:S(2)}) copy-start(bf16[12,64,256]{2,1,0:T(8,128)(2,1)S(1)} %fusion.38) | copy-start | bytes 1179652
  37.8 23.1 %copy-start.14 = (bf16[512,768]{0,1:T(8,128)(2,1)S(1)}, bf16[512,768]{0,1:T(8,128)(2,1)}, u32[]{:S(2)}) copy-start(bf16[512,768]{0,1:T(8,128)(2,1)} %copy.59) | copy-start | bytes 2359300
  37.8 23.1 %copy-start.27 = (f32[12,256]{1,0:T(8,128)S(1)}, f32[12,256]{1,0:T(8,128)}, u32[]{:S(2)}) copy-start(f32[12,256]{1,0:T(8,128)} %get-tuple-element.31) | copy-start | bytes 36868
  88.5 3.5 %copy-start.1 = (bf16[1,256,768]{2,1,0:T(8,128)(2,1)S(1)}, bf16[1,256,768]{2,1,0:T(8,128)(2,1)}, u32[]{:S(2)}) copy-start(bf16[1,256,768]{2,1,0:T(8,128)(2,1)} %param.6) | copy-start | bytes 1179652
  92.0 2.5 copy-start.10
  92.0 2.5 copy-start.12
  132.0 12.5 %copy-start.11 = (bf16[256,12,64]{0,2,1:T(8,128)(2,1)S(1)}, bf16[256,12,64]{0,2,1:T(8,128)(2,1)}, u32[]{:S(2)}) copy-start(bf16[256,12,64]{0,2,1:T(8,128)(2,1)} %get-tuple-element.27) | copy-start | bytes 1179652
  132.0 12.5 %copy-start.13 = (bf16[256,12,64]{0,2,1:T(8,128)(2,1)S(1)}, bf16[256,12,64]{0,2,1:T(8,128)(2,1)}, u32[]{:S(2)}) copy-start(bf16[256,12,64]{0,2,1:T(8,128)(2,1)} %get-tuple-element.25) | copy-start | bytes 1179652
  132.0 12.5 %copy-start.21 = (f32[256]{0:T(256)S(1)}, f32[256]{0:T(256)}, u32[]{:S(2)}) copy-start(f32[256]{0:T(256)} %copy-done.19) | copy-start | bytes 3076
  132.0 109.9 %all-to-all-start.1 = ((bf16[64,6,3072]{2,1,0:T(8,128)(2,1)}), bf16[64,6,3072]{2,1,0:T(8,128)(2,1)}, u32[]{:S(2)}, u32[]{:S(2)}) async-start(bf16[64,6,3072]{2,1,0:T(8,128)(2,1)} %copy.64), calls=%async_computation.1 | async-start | bytes 6291456 | tf_op jit(solution)/shard_map/all_to_all | solution.py:42
  144.5 2.7 %copy-start.7 = (bf16[256,12,64]{0,2,1:T(8,128)(2,1)S(1)}, bf16[256,12,64]{0,2,1:T(8,128)(2,1)}, u32[]{:S(2)}) copy-start(bf16[256,12,64]{0,2,1:T(8,128)(2,1)} %get-tuple-element.28) | copy-start | bytes 1179652
  144.5 2.7 %copy-start.9 = (bf16[256,12,64]{0,2,1:T(8,128)(2,1)S(1)}, bf16[256,12,64]{0,2,1:T(8,128)(2,1)}, u32[]{:S(2)}) copy-start(bf16[256,12,64]{0,2,1:T(8,128)(2,1)} %get-tuple-element.26) | copy-start | bytes 1179652
  144.5 2.7 %copy-start.16 = (bf16[12,64,256]{2,1,0:T(8,128)(2,1)S(1)}, bf16[12,64,256]{2,1,0:T(8,128)(2,1)}, u32[]{:S(2)}) copy-start(bf16[12,64,256]{2,1,0:T(8,128)(2,1)} %fusion.41) | copy-start | bytes 1179652
  144.6 3.1 %copy-start.24 = (bf16[768,2304]{1,0:T(8,128)(2,1)S(1)}, bf16[768,2304]{1,0:T(8,128)(2,1)}, u32[]{:S(2)}) copy-start(bf16[768,2304]{1,0:T(8,128)(2,1)} %param.10) | copy-start | bytes 10616836
  147.6 93.2 %copy-start.3 = (bf16[1,256,768]{2,1,0:T(8,128)(2,1)S(1)}, bf16[1,256,768]{2,1,0:T(8,128)(2,1)}, u32[]{:S(2)}) copy-start(bf16[1,256,768]{2,1,0:T(8,128)(2,1)} %param.7) | copy-start | bytes 1179652
  149.6 99.2 %copy-start.5 = (bf16[12,64,256]{2,1,0:T(8,128)(2,1)S(1)}, bf16[12,64,256]{2,1,0:T(8,128)(2,1)}, u32[]{:S(2)}) copy-start(bf16[12,64,256]{2,1,0:T(8,128)(2,1)} %copy-done.4) | copy-start | bytes 1179652
  245.0 9.5 %all-to-all-start.2 = ((bf16[2,6,3072]{2,1,0:T(8,128)(2,1)}), bf16[2,6,3072]{2,1,0:T(8,128)(2,1)S(1)}, u32[]{:S(2)}, u32[]{:S(2)}) async-start(bf16[2,6,3072]{2,1,0:T(8,128)(2,1)} %broadcast_in_dim.27), calls=%async_computation.2 | async-start | bytes 196608 | tf_op jit(solution)/shard_map/all_to_all | solution.py:48
  (7 other events, 9.8 us)
where the time goes:
time: 257 us; the launch traced here: 256 us
  blocking collectives  98.7 us (38%)
  matrix products  81.4 us (32%)
  local copies, waits for them, and re-layouts  30.1 us (12%)
  other arithmetic  21.6 us (8%)
  starting transfers between devices  18.3 us (7%)
  waiting for transfers between devices  4.55 us (2%)
    psum x5, blocking collectives, one_axis_at_a_time(): shard = lax.psum(shard, axis)  88.7 us
    dot_general x1, matrix products, attend_back(): jnp.einsum('hqk,khe->qhe', d_scores_b, keys, preferred_element_type=jnp.f...  25.5 us
    dot_general x1, matrix products, attend_back(): jnp.einsum('hqk,qhe->khe', d_scores_b, query, preferred_element_type=jnp....  23.1 us
    all_to_all x1, starting transfers between devices, summed_rows(): lax.all_to_all(own.astype(jnp.bfloat16), far, 0, 0, tiled=True)  12.5 us
    all_to_all x1, blocking collectives, sent_and_summed(): lax.all_to_all(cut_along(shard, dim, peers), axis, 0, 0, tiled=True)  10.1 us
    concatenate x2, local copies, waits for them, and re-layouts, on_device(): jnp.concatenate([acc_qkv[:, :feature_width], acc_qkv[:, feature_width:] +...  8.11 us
    sub x1, matrix products, attend(): weights = jnp.exp(scores - top)  6.78 us
    reduce_sum x1, other arithmetic, sent_and_summed(): return jnp.sum(pieces.astype(jnp.float32), axis=0)  5.53 us
  transfers between devices with their start and end apart: 3, of which 1 were waited for; matrix products, arithmetic and copies ran while one was open for 7% of the time, Pallas kernels for 0%

commit v1 on v0

v1 whole, which is shorter than its diff:
```python
import functools

import jax
import jax.numpy as jnp
from jax import lax
from jax.experimental import pallas as pl
from jax.experimental.pallas import tpu as pltpu
from jax.sharding import Mesh
from jax.sharding import PartitionSpec as P

HEADS = 12
EPS = 1e-05
SEQ = ("y", "z", "xl", "c")
PLANE = ("y", "xl", "xh")
COLUMN = ("z", "xh")
T = 256
D = 768
GROUPS = 3
GW = 256
BF = jnp.bfloat16
F32 = jnp.float32
VMEM_LIMIT = 40 * 1024 * 1024


def nn(a, b):
    return lax.dot_general(a, b, (((1,), (0,)), ((), ())), preferred_element_type=F32)


def nt(a, b):
    return lax.dot_general(a, b, (((1,), (1,)), ((), ())), preferred_element_type=F32)


def eye(n):
    rows = lax.broadcasted_iota(jnp.int32, (n, n), 0)
    cols = lax.broadcasted_iota(jnp.int32, (n, n), 1)
    return jnp.where(rows == cols, 1.0, 0.0).astype(BF)


def layer_norm(x_ref, gain_ref, bias_ref):
    values = x_ref[...].astype(F32)
    centered = values - jnp.mean(values, axis=-1, keepdims=True)
    rstd = lax.rsqrt(jnp.mean(centered * centered, axis=-1, keepdims=True) + EPS)
    xhat = centered * rstd
    normed = (xhat * gain_ref[...] + bias_ref[...]).astype(BF)
    return normed, xhat, rstd


def row_order(core):
    p = lax.broadcasted_iota(jnp.int32, (D, 1), 0)
    second = jnp.where(p >= 384, 1, 0)
    q = p - 384 * second
    owner = (q * 171) >> 13
    b = q - 48 * owner
    z = (b * 43) >> 8
    j = b - 6 * z
    y, xl = owner >> 1, owner & 1
    to_core = jnp.where(second == 1, core, 1 - core)
    feature = ((y * 8 + z) * 2 + xl) * 12 + to_core * 6 + j
    cols = lax.broadcasted_iota(jnp.int32, (D, D), 1)
    return jnp.where(cols == feature, 1.0, 0.0).astype(BF)


def own_kernel(core_ref, x_ref, cot_ref, gain_ref, bias_ref, w_ref, wo_ref,
               qkv_ref, dmix_ref, npt_ref, xhat_ref, rstd_ref, mt_ref):
    normed, xhat, rstd = layer_norm(x_ref, gain_ref, bias_ref)
    qkv_ref[...] = nn(normed, w_ref[...]).astype(BF)
    xhat_ref[...] = xhat
    rstd_ref[...] = jnp.broadcast_to(rstd, (T, 128))
    dmix_ref[...] = nt(cot_ref[...], wo_ref[...]).astype(BF)
    mt = row_order(core_ref[0])
    mt_ref[...] = mt
    npt_ref[...] = nt(mt, normed).astype(BF)


def prev_kernel(x_ref, gain_ref, bias_ref, wk_ref, wv_ref, mt_ref, kv_ref, npt_ref, xhat_ref):
    normed, xhat, _ = layer_norm(x_ref, gain_ref, bias_ref)
    kv_ref[:, :D] = nn(normed, wk_ref[...]).astype(BF)
    kv_ref[:, D:] = nn(normed, wv_ref[...]).astype(BF)
    xhat_ref[...] = xhat
    npt_ref[...] = nt(mt_ref[...], normed).astype(BF)


def put_blocks(out_ref, rows):
    for i in range(8):
        for h in range(2):
            out_ref[2 * i + h, 0:48, :] = rows[48 * i : 48 * i + 48, 384 * h : 384 * h + 384]


def group_kernel(first, has_ref, q_ref, k_ref, v_ref, km_ref, vm_ref, dm_ref, npt_ref, nptm_ref,
                 wq_ref, wk_ref, wv_ref, *rest):
    if first:
        send_ref, keep_ref, mixt_ref, dn_ref, dnm_ref = rest
    else:
        dn_in, dnm_in, send_ref, keep_ref, mixt_ref, dn_ref, dnm_ref = rest
    has = has_ref[0] > 0
    lanes = lax.broadcasted_iota(jnp.int32, (T, 128), 1)
    low = lanes < 64
    causal = lax.broadcasted_iota(jnp.int32, (T, T), 0) <= lax.broadcasted_iota(jnp.int32, (T, T), 1)
    unit = eye(128)
    unit2 = eye(T)
    zero = jnp.zeros((), BF)
    dqs, dks, dvs = [], [], []
    for pair in range(2):
        cols = slice(128 * pair, 128 * pair + 128)
        q2 = (q_ref[:, cols].astype(F32) * 0.125).astype(BF)
        k2 = jnp.concatenate([k_ref[:, cols], km_ref[:, cols]], axis=0)
        v2 = jnp.concatenate([v_ref[:, cols], vm_ref[:, cols]], axis=0)
        dm2 = dm_ref[:, cols]
        kt2 = nt(unit, k2).astype(BF)
        vt2 = nt(unit, v2).astype(BF)
        ds_parts, p_parts, q_parts, dm_parts, dqt_parts = [], [], [], [], []
        for half in range(2):
            pick = low if half == 0 else jnp.logical_not(low)
            qa = jnp.where(pick, q2, zero)
            dma = jnp.where(pick, dm2, zero)
            st = nt(k2, qa)
            st_own = jnp.where(causal, st[:T], -1e30)
            st_mem = jnp.where(has, st[T:], -1e30)
            st = jnp.concatenate([st_own, st_mem], axis=0)
            top = jnp.max(st, axis=0, keepdims=True)
            e = jnp.exp(st - top)
            p = e * (1.0 / jnp.sum(e, axis=0, keepdims=True))
            pb = p.astype(BF)
            rows = slice(64 * half, 64 * half + 64)
            mixt_ref[128 * pair + 64 * half : 128 * pair + 64 * half + 64, :] = nn(vt2[rows], pb).astype(BF)
            dp = nt(v2, dma)
            ds = (p * (dp - jnp.sum(dp * p, axis=0, keepdims=True))).astype(BF)
            dqt_parts.append((nn(kt2[rows], ds) * 0.125).astype(BF))
            ds_parts.append(ds)
            p_parts.append(pb)
            q_parts.append(qa)
            dm_parts.append(dma)
        dks.append(nn(jnp.concatenate(ds_parts, axis=1), jnp.concatenate(q_parts, axis=0)).astype(BF))
        dvs.append(nn(jnp.concatenate(p_parts, axis=1), jnp.concatenate(dm_parts, axis=0)).astype(BF))
        dqs.append(nt(unit2, jnp.concatenate(dqt_parts, axis=0)).astype(BF))
    dq = jnp.concatenate(dqs, axis=1)
    dk = jnp.concatenate(dks, axis=1)
    dv = jnp.concatenate(dvs, axis=1)
    npt = npt_ref[...]
    npt_all = jnp.concatenate([npt, nptm_ref[...]], axis=1)
    for which, out_ref in ((0, send_ref), (1, keep_ref)):
        rows = slice(384 * which, 384 * which + 384)
        put_blocks(
            out_ref,
            jnp.concatenate(
                [nn(npt[rows], dq).astype(BF), nn(npt_all[rows], dk).astype(BF), nn(npt_all[rows], dv).astype(BF)],
                axis=1,
            ),
        )
    own = nt(dq, wq_ref[...]) + nt(dk[:T], wk_ref[...]) + nt(dv[:T], wv_ref[...])
    mem = nt(dk[T:], wk_ref[...]) + nt(dv[T:], wv_ref[...])
    if first:
        dn_ref[...] = own
        dnm_ref[...] = mem
    else:
        dn_ref[...] = dn_in[...] + own
        dnm_ref[...] = dnm_in[...] + mem


def out_kernel(m0_ref, m1_ref, m2_ref, mt_ref, cot_ref, dn_ref, dnm_ref, xhat_ref, xhatm_ref,
               send_ref, keep_ref, vec_ref, mixt_ref):
    mixt = jnp.concatenate([m0_ref[...], m1_ref[...], m2_ref[...]], axis=0)
    mixt_ref[...] = mixt
    rows = nn(nn(mt_ref[...], mixt).astype(BF), cot_ref[...]).astype(BF)
    put_blocks(send_ref, rows[:384])
    put_blocks(keep_ref, rows[384:])
    dn, dnm = dn_ref[...], dnm_ref[...]
    vec_ref[0:1, :] = jnp.sum(dn * xhat_ref[...] + dnm * xhatm_ref[...], axis=0, keepdims=True)
    vec_ref[1:2, :] = jnp.sum(dn + dnm, axis=0, keepdims=True)


def token_kernel(x_ref, cot_ref, mixt_ref, wo_ref, dn_ref, xhat_ref, rstd_ref, gain_ref, out_ref, dx_ref):
    mixed = nt(eye(T), mixt_ref[...]).astype(BF)
    out_ref[...] = (x_ref[...].astype(F32) + nn(mixed, wo_ref[...])).astype(BF)
    d_hat = dn_ref[...] * gain_ref[...]
    xhat = xhat_ref[...]
    row = rstd_ref[:, 0:1] * (
        d_hat
        - jnp.mean(d_hat, axis=-1, keepdims=True)
        - xhat * jnp.mean(d_hat * xhat, axis=-1, keepdims=True)
    )
    dx_ref[...] = (cot_ref[...].astype(F32) + row).astype(BF)


def split(value):
    high = value.astype(BF)
    return high, (value - high.astype(F32)).astype(BF)


def last_pair_kernel(keep2_ref, recv2_ref, keep3_ref, recv3_ref, vec_ref, vecr_ref, out_ref):
    add = lambda a, b: (a[...].astype(F32) + b[...].astype(F32)).astype(BF)
    out_ref[:, 0:48, 0:384] = add(keep2_ref, recv2_ref)
    out_ref[:, 0:48, 384:768] = add(keep3_ref, recv3_ref)
    total = vec_ref[...] + vecr_ref[...]
    high, low = split(total)
    rows = jnp.concatenate([high, low, jnp.zeros((4, D), BF)], axis=0)
    for i in range(16):
        out_ref[i, 48:56, :] = rows


def plane_sum_kernel(a_ref, b_ref, c_ref, out_ref):
    def total(ref, rows, cols):
        acc = ref[0, rows, cols].astype(F32)
        for i in range(1, 16):
            acc = acc + ref[i, rows, cols].astype(F32)
        return acc

    grads = slice(0, 48)
    parts = [total(a_ref, grads, slice(None)), total(b_ref, grads, slice(None)), total(c_ref, grads, slice(None))]
    sums = jnp.concatenate(parts, axis=1)
    rows = total(c_ref, slice(48, 56), slice(None))
    gain, bias = rows[0:1] + rows[2:3], rows[1:2] + rows[3:4]
    vec = jnp.concatenate([gain, bias], axis=1)
    high, low = split(vec)
    tail = jnp.concatenate([high.astype(F32), low.astype(F32)], axis=0)
    for z in range(8):
        block = jnp.concatenate([sums[6 * z : 6 * z + 6], tail], axis=0).astype(BF)
        out_ref[2 * z] = block
        out_ref[2 * z + 1] = block


def finish_kernel(factor, in_ref, qkv_ref, wout_ref, gain_ref, bias_ref):
    def total(h):
        acc = in_ref[h].astype(F32)
        for z in range(1, 8):
            acc = acc + in_ref[2 * z + h].astype(F32)
        return acc * factor

    halves = [total(0), total(1)]
    for g in range(GROUPS + 1):
        cols = slice(384 * g, 384 * g + 384)
        full = jnp.concatenate([halves[0][0:6, cols], halves[1][0:6, cols]], axis=1)
        if g < GROUPS:
            for i in range(3):
                at = D * i + GW * g
                qkv_ref[:, at : at + GW] = full[:, GW * i : GW * i + GW]
        else:
            wout_ref[...] = full
    vec = halves[0][6:7] + halves[0][7:8]
    gain_ref[...] = vec[:, :D]
    bias_ref[...] = vec[:, D:]


def call(kernel, name, out_shape, args, in_specs=None):
    vm = pl.BlockSpec(memory_space=pltpu.VMEM)
    if in_specs is None:
        in_specs = [vm] * len(args)
    specs = [vm if s is None else s for s in in_specs]
    many = isinstance(out_shape, (tuple, list))
    return pl.pallas_call(
        kernel,
        name=name,
        grid=(1,),
        in_specs=[whole(a) if s is vm else s for a, s in zip(args, specs)],
        out_specs=[whole(o) for o in out_shape] if many else whole(out_shape),
        out_shape=out_shape,
        compiler_params=pltpu.CompilerParams(vmem_limit_bytes=VMEM_LIMIT),
    )(*args)


def whole(a):
    return pl.BlockSpec(a.shape, lambda i, n=len(a.shape): (0,) * n)


SCALAR = pl.BlockSpec(memory_space=pltpu.SMEM)


def block(shape, *index):
    return pl.BlockSpec(shape, lambda i: index)


def sds(*shape, dtype=BF):
    return jax.ShapeDtypeStruct(shape, dtype)


def own_part(core, x, cot, gain, bias, w, wo):
    return call(
        own_kernel, "own_part",
        [sds(T, 3 * D), sds(T, D), sds(D, T), sds(T, D, dtype=F32), sds(T, 128, dtype=F32), sds(D, D)],
        [core, x, cot, gain, bias, w, wo], [SCALAR] + [None] * 6,
    )


def prev_part(xp, gain, bias, w, mt):
    return call(
        prev_kernel, "prev_part",
        [sds(T, 2 * D), sds(D, T), sds(T, D, dtype=F32)],
        [xp, gain, bias, w, w, mt], [None] * 3 + [block((D, D), 0, 1), block((D, D), 0, 2), None],
    )


def group_part(g, has, qkv, kvm, dmix, npt, nptm, w, sums):
    first = g == 0
    tok = lambda at: block((T, GW), 0, at)
    wt = lambda at: block((D, GW), 0, at)
    args = [has, qkv, qkv, qkv, kvm, kvm, dmix, npt, nptm, w, w, w]
    specs = [SCALAR, tok(g), tok(3 + g), tok(6 + g), tok(g), tok(3 + g), tok(g), None, None, wt(g), wt(3 + g), wt(6 + g)]
    if not first:
        args += list(sums)
        specs += [None, None]
    return call(
        functools.partial(group_kernel, first), "head_group",
        [sds(16, 48, 384), sds(16, 48, 384), sds(GW, T), sds(T, D, dtype=F32), sds(T, D, dtype=F32)],
        args, specs,
    )


def on_device(layer_input, cotangent, gain, bias, w, wo):
    x, cot = layer_input[0], cotangent[0]
    gain, bias = gain.reshape(1, D), bias.reshape(1, D)
    seq = lax.axis_size(SEQ)
    xp = lax.ppermute(x, SEQ, [(i, i + 1) for i in range(seq - 1)])
    core = lax.axis_index("c").astype(jnp.int32).reshape(1)
    has = (lax.axis_index(SEQ) > 0).astype(jnp.int32).reshape(1)
    qkv, dmix, npt, xhat, rstd, mt = own_part(core, x, cot, gain, bias, w, wo)
    kvm, nptm, xhatm = prev_part(xp, gain, bias, w, mt)

    def swap(block):
        return lax.ppermute(block, "c", [(0, 1), (1, 0)])

    def spread(block):
        return lax.all_to_all(block, PLANE, 0, 0, tiled=True)

    mixes, sums, spreads = [], None, []
    for g in range(GROUPS):
        send, keep, mixt, dn, dnm = group_part(g, has, qkv, kvm, dmix, npt, nptm, w, sums)
        sums = (dn, dnm)
        mixes.append(mixt)
        if g < GROUPS - 1:
            spreads.append(spread((keep.astype(F32) + swap(send).astype(F32)).astype(BF)))
        else:
            last = (keep, swap(send))
    send, keep, vec, mixt = call(
        out_kernel, "output_weight_part",
        [sds(16, 48, 384), sds(16, 48, 384), sds(2, D, dtype=F32), sds(D, T)],
        [*mixes, mt, cot, dn, dnm, xhat, xhatm],
    )
    both = call(last_pair_kernel, "pair_sum", sds(16, 56, 768), [*last, keep, swap(send), vec, swap(vec)])
    both = spread(both)
    out, dx = call(
        token_kernel, "token_outputs", [sds(T, D), sds(T, D)],
        [x, cot, mixt, wo, dn, xhat, rstd, gain],
    )
    mine = call(plane_sum_kernel, "plane_sum", sds(16, 8, 1536), [*spreads, both])
    mine = lax.all_to_all(mine, COLUMN, 0, 0, tiled=True)
    factor = 1.0 / float(seq * lax.axis_size("xh") * T) ** 0.5
    grad_qkv, grad_out, grad_gain, grad_bias = call(
        functools.partial(finish_kernel, factor), "finish",
        [sds(6, 3 * D, dtype=F32), sds(6, D, dtype=F32), sds(1, D, dtype=F32), sds(1, D, dtype=F32)],
        [mine],
    )
    return out[None], dx[None], grad_qkv, grad_out, grad_gain.reshape(D), grad_bias.reshape(D)


def solution(mesh):
    torus = Mesh(mesh.devices.reshape(4, 8, 2, 2, 2), ("y", "z", "xl", "c", "xh"))
    return jax.shard_map(
        on_device,
        mesh=torus,
        in_specs=(P("xh", SEQ, None), P("xh", SEQ, None), P(), P(), P(), P()),
        out_specs=(P("xh", SEQ, None), P("xh", SEQ, None), P(SEQ, None), P(SEQ, None), P(), P()),
        check_vma=False,
    )
```

time: 257 us -> 134 us (0.52)
  matrix products: 81.4 us -> 0 us
  blocking collectives: 98.7 us -> 23.1 us
  Pallas kernels: 0 us -> 30.7 us
  other arithmetic: 21.6 us -> 4.36 us
  waiting for transfers between devices: 4.55 us -> 16.1 us
  starting transfers between devices: 18.3 us -> 28.2 us
    psum x5 -> x0, blocking collectives: 88.7 us -> none  [one_axis_at_a_time(): shard = lax.psum(shard, axis)]
    dot_general x14 -> x0, matrix products: 74.7 us -> none  [the longest x1 25.5 us: attend_back(): jnp.einsum('hqk,khe->qhe', d_scores_b, keys, preferred_element_type=jnp.f...]
    pallas_call x0 -> x10, Pallas kernels: none -> 30.7 us  [call(): pl.pallas_call(kernel, name=name, grid=(1,), in_specs=[whole(a) if s is v...]
    unnamed x56 -> x102, local copies, waits for them, and re-layouts: 1.83 us -> 27.7 us
    all_to_all x1, blocking collectives: 10.1 us -> 23.1 us  [spread(): return lax.all_to_all(block, PLANE, 0, 0, tiled=True)]
    concatenate x4 -> x0, local copies, waits for them, and re-layouts: 11.8 us -> none  [the longest x2 8.11 us: on_device(): jnp.concatenate([acc_qkv[:, :feature_width], acc_qkv[:, feature_width:] +...]
    reduce_sum x7 -> x0, other arithmetic: 10.8 us -> none  [the longest x1 5.53 us: sent_and_summed(): return jnp.sum(pieces.astype(jnp.float32), axis=0)]
    all_to_all x2 -> x3, waiting for transfers between devices: 4.55 us -> 15 us  [the longest x1 10.1 us: on_device(): mine = lax.all_to_all(mine, COLUMN, 0, 0, tiled=True)]
  transfers between devices with their start and end apart: 3 -> 9, of which waited for: 1 -> 3; matrix products, arithmetic and copies ran while one was open for 7% -> 3% of each run, Pallas kernels for 0% -> 14%
where the time goes in v1:
time: 134 us; the launch traced here: 133 us
  Pallas kernels  30.7 us (23%)
  local copies, waits for them, and re-layouts  29.1 us (22%)
  starting transfers between devices  28.2 us (21%)
  blocking collectives  23.1 us (17%)
  waiting for transfers between devices  16.1 us (12%)
  other arithmetic  4.36 us (3%)
    pallas_call x10, Pallas kernels, call(): pl.pallas_call(kernel, name=name, grid=(1,), in_specs=[whole(a) if s is v...  30.7 us
    unnamed x102, local copies, waits for them, and re-layouts  27.7 us
    all_to_all x1, blocking collectives, spread(): return lax.all_to_all(block, PLANE, 0, 0, tiled=True)  23.1 us
    all_to_all x2, starting transfers between devices, spread(): return lax.all_to_all(block, PLANE, 0, 0, tiled=True)  14.8 us
    all_to_all x1, waiting for transfers between devices, on_device(): mine = lax.all_to_all(mine, COLUMN, 0, 0, tiled=True)  10.1 us
    all_to_all x1, starting transfers between devices, on_device(): mine = lax.all_to_all(mine, COLUMN, 0, 0, tiled=True)  8.97 us
    all_to_all x2, waiting for transfers between devices, spread(): return lax.all_to_all(block, PLANE, 0, 0, tiled=True)  4.84 us
    convert_element_type x2, other arithmetic, on_device(): (keep.astype(F32) + swap(send).astype(F32)).astype(BF)  3.15 us
  transfers between devices with their start and end apart: 9, of which 3 were waited for; matrix products, arithmetic and copies ran while one was open for 3% of the time, Pallas kernels for 14%

profile of v1, /device:TPU:2, one launch (start us, length us, event | category | flops | bytes accessed | tf_op | source)
XLA Modules:
  0.0 132.6 jit_solution(13681859413851619641)
XLA Ops:
  0.6 1.9 %collective-permute-start = (bf16[256,768]{1,0:T(8,128)(2,1)}, bf16[256,768]{1,0:T(8,128)(2,1)}, u32[]{:S(2)}, u32[]{:S(2)}) collective-permute-start(bf16[256,768]{1,0:T(8,128)(2,1)} %bitcast.9), channel_id=1, source_target_pairs={{0,2},{2,4},{4,6},{6,8},{8,10},{10,12},{12,14},{14,16},{16,18},{18... | collective-permute-start | bytes 1179656 | tf_op jit(solution)/shard_map/ppermute | solution.py:312
  4.0 2.0 %copy-done = bf16[768,2304]{1,0:T(8,128)(2,1)S(1)} copy-done((bf16[768,2304]{1,0:T(8,128)(2,1)S(1)}, bf16[768,2304]{1,0:T(8,128)(2,1)}, u32[]{:S(2)}) %copy-start) | copy-done | bytes 3538968
  6.0 1.3 copy-done.8
  9.2 2.2 %own_part.1 = (bf16[256,2304]{1,0:T(8,128)(2,1)S(1)}, bf16[256,768]{1,0:T(8,128)(2,1)S(1)}, bf16[768,256]{1,0:T(8,128)(2,1)S(1)}, f32[256,768]{1,0:T(8,128)S(1)}...) custom-call(s32[1]{0:T(128)} %bitcast.3.core_ref, bf16[256,768]{1,0:T(8,128)(2,1)S(1)} %bitcast.10, ...), custom_call_target="tpu_custom_call" | custom-call | tf_op jit(solution)/shard_map/own_part/pallas_call | solution.py:250
  12.4 2.7 %prev_part.1 = (bf16[256,1536]{1,0:T(8,128)(2,1)S(1)}, bf16[768,256]{1,0:T(8,128)(2,1)S(1)}, f32[256,768]{1,0:T(8,128)S(1)}) custom-call(bf16[256,768]{1,0:T(8,128)(2,1)} %collective-permute-done.x_ref, f32[1,768]{1,0:T(1,128)S(1)} %reshape.35.gain_ref, f32[1,768]{1,0:T(1,128)S(1)} %reshape.36.bias_ref, bf16[768,2304]{1,0:T(8,128)(2,1)S(1)} %copy-done.1, ...), custom_call_target="tpu_custom_call" | custom-call | tf_op jit(solution)/shard_map/prev_part/pallas_call | solution.py:250
  15.9 5.6 %head_group.3 = (bf16[16,48,384]{2,1,0:T(8,128)(2,1)S(1)}, bf16[16,48,384]{2,1,0:T(8,128)(2,1)S(1)}, bf16[256,256]{1,0:T(8,128)(2,1)S(1)}, f32[256,768]{1,0:T(8,128)S(1)}, f32[256,768]{1,0:T(8,128)S(1)}) custom-call(s32[1]{0:T(128)} %bitcast.2.has_ref, bf16[256,2304]{1,0:T(8,128)(2,1)S(1)} %get-tuple-element.40.q_ref.k_ref.v_ref, ...), custom_call_target="tpu_custom_call" | custom-call | tf_op jit(solution)/shard_map/head_group/pallas_call | solution.py:250
  22.2 2.0 %collective-permute-start.1 = (bf16[16,48,384]{2,1,0:T(8,128)(2,1)S(1)}, bf16[16,48,384]{2,1,0:T(8,128)(2,1)S(1)}, u32[]{:S(2)}, u32[]{:S(2)}) collective-permute-start(bf16[16,48,384]{2,1,0:T(8,128)(2,1)S(1)} %get-tuple-element.62), channel_id=1, source_target_pairs={{0,2},{2,0},{1,3},{3,1},{4,6},{6,4},{5,7},{7,5},{8,10},{10,8},{9,1... | collective-permute-start | bytes 1769480 | tf_op jit(solution)/shard_map/ppermute | solution.py:319
  24.2 6.4 %head_group.4 = (bf16[16,48,384]{2,1,0:T(8,128)(2,1)}, bf16[16,48,384]{2,1,0:T(8,128)(2,1)S(1)}, bf16[256,256]{1,0:T(8,128)(2,1)S(1)}, f32[256,768]{1,0:T(8,128)S(1)}, f32[256,768]{1,0:T(8,128)S(1)}) custom-call(s32[1]{0:T(128)} %bitcast.2.has_ref, bf16[256,2304]{1,0:T(8,128)(2,1)S(1)} %get-tuple-element.40.q_ref.k_ref.v_ref, ...), custom_call_target="tpu_custom_call" | custom-call | tf_op jit(solution)/shard_map/head_group/pallas_call | solution.py:250
  34.9 7.5 %all-to-all-start = ((bf16[16,48,384]{2,1,0:T(8,128)(2,1)}), bf16[16,48,384]{2,1,0:T(8,128)(2,1)}, u32[]{:S(2)}, u32[]{:S(2)}) async-start(bf16[16,48,384]{2,1,0:T(8,128)(2,1)} %add_convert_fusion.1), calls=%async_computation | async-start | bytes 1179648 | tf_op jit(solution)/shard_map/all_to_all | solution.py:322
  42.4 1.3 copy-done.3
  43.7 1.1 copy-done.5
  47.8 1.1 copy-done.32
  50.1 6.3 %head_group.5 = (bf16[16,48,384]{2,1,0:T(8,128)(2,1)}, bf16[16,48,384]{2,1,0:T(8,128)(2,1)S(1)}, bf16[256,256]{1,0:T(8,128)(2,1)S(1)}, f32[256,768]{1,0:T(8,128)S(1)}, f32[256,768]{1,0:T(8,128)S(1)}) custom-call(s32[1]{0:T(128)} %bitcast.2.has_ref, bf16[256,2304]{1,0:T(8,128)(2,1)S(1)} %copy-done.3, bf16[256,2304]{1,0:T(8,128)(2,1)S(1)} %copy-done.3, ...), custom_call_target="tpu_custom_call" | custom-call | tf_op jit(solution)/shard_map/head_group/pallas_call | solution.py:250
  56.5 2.3 %output_weight_part.1 = (bf16[16,48,384]{2,1,0:T(8,128)(2,1)}, bf16[16,48,384]{2,1,0:T(8,128)(2,1)S(1)}, f32[2,768]{1,0:T(2,128)S(1)}, bf16[768,256]{1,0:T(8,128)(2,1)S(1)}) custom-call(bf16[256,256]{1,0:T(8,128)(2,1)S(1)} %copy-done.48, bf16[256,256]{1,0:T(8,128)(2,1)S(1)} %copy-done.50, bf16[256,256]{1,0:T(8,128)(2,1)S(1)} %get-tuple-element.52.m2_ref, ...), custom_call_target="tpu_custom_call" | custom-call | tf_op jit(solution)/shard_map/output_weight_part/pallas_call | solution.py:250
  60.0 2.1 %add_convert_fusion = bf16[16,48,384]{2,1,0:T(8,128)(2,1)} fusion(bf16[16,48,384]{2,1,0:T(8,128)(2,1)} %collective-permute-done.2, bf16[16,48,384]{2,1,0:T(8,128)(2,1)S(1)} %copy-done.36), kind=kLoop, calls=%fused_computation | loop fusion | flops 1179648 | bytes 1769472 | tf_op jit(solution)/shard_map/convert_element_type | solution.py:330
  62.2 7.2 %all-to-all-start.1 = ((bf16[16,48,384]{2,1,0:T(8,128)(2,1)}), bf16[16,48,384]{2,1,0:T(8,128)(2,1)S(1)}, u32[]{:S(2)}, u32[]{:S(2)}) async-start(bf16[16,48,384]{2,1,0:T(8,128)(2,1)} %add_convert_fusion), calls=%async_computation.1 | async-start | bytes 1179648 | tf_op jit(solution)/shard_map/all_to_all | solution.py:322
  69.4 1.2 collective-permute-done.5.vecr_ref
  74.7 4.8 %all-to-all-done.1.b_ref = bf16[16,48,384]{2,1,0:T(8,128)(2,1)S(1)} async-done(((bf16[16,48,384]{2,1,0:T(8,128)(2,1)}), bf16[16,48,384]{2,1,0:T(8,128)(2,1)S(1)}, u32[]{:S(2)}, u32[]{:S(2)}) %all-to-all-start.1) | async-done | bytes 589856 | tf_op jit(solution)/shard_map/all_to_all | solution.py:322
  80.3 23.1 %all_to_all.20.c_ref = bf16[16,56,768]{2,1,0:T(8,128)(2,1)S(1)} all-to-all(bf16[16,56,768]{2,1,0:T(8,128)(2,1)S(1)} %pair_sum.1), channel_id=1, replica_groups=mesh['y'=4,'z'=8,'xl'=2,'c'=2,'xh'=2] {'y','xl','xh'}, dimensions={0} | all-to-all | bytes 2752512 | tf_op jit(solution)/shard_map/all_to_all | solution.py:322
  104.5 1.6 %plane_sum.1 = bf16[16,8,1536]{2,1,0:T(8,128)(2,1)S(1)} custom-call(bf16[16,48,384]{2,1,0:T(8,128)(2,1)} %all-to-all-done.a_ref, bf16[16,48,384]{2,1,0:T(8,128)(2,1)S(1)} %copy-done.25, bf16[16,56,768]{2,1,0:T(8,128)(2,1)S(1)} %all_to_all.20.c_ref), custom_call_target="tpu_custom_call" | custom-call | tf_op jit(solution)/shard_map/plane_sum/pallas_call | solution.py:250
  106.9 9.0 %all-to-all-start.3 = ((bf16[16,8,1536]{2,1,0:T(8,128)(2,1)}), bf16[16,8,1536]{2,1,0:T(8,128)(2,1)}, u32[]{:S(2)}, u32[]{:S(2)}) async-start(bf16[16,8,1536]{2,1,0:T(8,128)(2,1)} %copy-done.28), calls=%async_computation.3 | async-start | bytes 786432 | tf_op jit(solution)/shard_map/all_to_all | solution.py:345
  117.8 1.7 %token_outputs.1 = (bf16[256,768]{1,0:T(8,128)(2,1)}, bf16[256,768]{1,0:T(8,128)(2,1)}) custom-call(bf16[256,768]{1,0:T(8,128)(2,1)S(1)} %bitcast.11, bf16[256,768]{1,0:T(8,128)(2,1)S(1)} %bitcast.8, bf16[768,256]{1,0:T(8,128)(2,1)S(1)} %copy-done.44, bf16[768,768]{1,0:T(8,128)(2,1)S(1)} %copy-done.9, f32[256,768]{1,0:T(8,128)S(1)} %copy-done.23, ...), custom_call_target="tpu_custom_call" | custom-call | tf_op jit(solution)/shard_map/token_outputs/pallas_call | solution.py:250
  119.5 10.1 %all-to-all-done.3.in_ref = bf16[16,8,1536]{2,1,0:T(8,128)(2,1)} async-done(((bf16[16,8,1536]{2,1,0:T(8,128)(2,1)}), bf16[16,8,1536]{2,1,0:T(8,128)(2,1)}, u32[]{:S(2)}, u32[]{:S(2)}) %all-to-all-start.3) | async-done | bytes 393248 | tf_op jit(solution)/shard_map/all_to_all | solution.py:345
  129.7 1.7 %finish.1 = (f32[6,2304]{1,0:T(8,128)}, f32[6,768]{1,0:T(8,128)}, f32[1,768]{1,0:T(1,128)S(1)}, f32[1,768]{1,0:T(1,128)S(1)}) custom-call(bf16[16,8,1536]{2,1,0:T(8,128)(2,1)} %all-to-all-done.3.in_ref), custom_call_target="tpu_custom_call" | custom-call | tf_op jit(solution)/shard_map/finish/pallas_call | solution.py:250
  (113 shorter events, 25.4 us)
Async XLA Ops:
  0.6 11.7 %collective-permute-start = (bf16[256,768]{1,0:T(8,128)(2,1)}, bf16[256,768]{1,0:T(8,128)(2,1)}, u32[]{:S(2)}, u32[]{:S(2)}) collective-permute-start(bf16[256,768]{1,0:T(8,128)(2,1)} %bitcast.9), channel_id=1, source_target_pairs={{0,2},{2,4},{4,6},{6,8},{8,10},{10,12},{12,14},{14,16},{16,18},{18... | collective-permute-start | bytes 1179656 | tf_op jit(solution)/shard_map/ppermute | solution.py:312
  12.3 11.8 %copy-start.2 = (bf16[256,2304]{1,0:T(8,128)(2,1)}, bf16[256,2304]{1,0:T(8,128)(2,1)S(1)}, u32[]{:S(2)}) copy-start(bf16[256,2304]{1,0:T(8,128)(2,1)S(1)} %get-tuple-element.40.q_ref.k_ref.v_ref) | copy-start | bytes 3538948
  12.3 11.8 %copy-start.13 = (bf16[256,768]{1,0:T(8,128)(2,1)}, bf16[256,768]{1,0:T(8,128)(2,1)S(1)}, u32[]{:S(2)}) copy-start(bf16[256,768]{1,0:T(8,128)(2,1)S(1)} %get-tuple-element.43.dm_ref) | copy-start | bytes 1179652
  12.3 11.8 %copy-start.15 = (bf16[768,256]{1,0:T(8,128)(2,1)}, bf16[768,256]{1,0:T(8,128)(2,1)S(1)}, u32[]{:S(2)}) copy-start(bf16[768,256]{1,0:T(8,128)(2,1)S(1)} %get-tuple-element.44.npt_ref) | copy-start | bytes 1179652
  15.9 8.2 %copy-start.4 = (bf16[256,1536]{1,0:T(8,128)(2,1)}, bf16[256,1536]{1,0:T(8,128)(2,1)S(1)}, u32[]{:S(2)}) copy-start(bf16[256,1536]{1,0:T(8,128)(2,1)S(1)} %get-tuple-element.42.km_ref.vm_ref) | copy-start | bytes 2359300
  15.9 8.3 %copy-start.17 = (bf16[768,256]{1,0:T(8,128)(2,1)}, bf16[768,256]{1,0:T(8,128)(2,1)S(1)}, u32[]{:S(2)}) copy-start(bf16[768,256]{1,0:T(8,128)(2,1)S(1)} %get-tuple-element.45.nptm_ref) | copy-start | bytes 1179652
  22.2 11.7 %collective-permute-start.1 = (bf16[16,48,384]{2,1,0:T(8,128)(2,1)S(1)}, bf16[16,48,384]{2,1,0:T(8,128)(2,1)S(1)}, u32[]{:S(2)}, u32[]{:S(2)}) collective-permute-start(bf16[16,48,384]{2,1,0:T(8,128)(2,1)S(1)} %get-tuple-element.62), channel_id=1, source_target_pairs={{0,2},{2,0},{1,3},{3,1},{4,6},{6,4},{5,7},{7,5},{8,10},{10,8},{9,1... | collective-permute-start | bytes 1769480 | tf_op jit(solution)/shard_map/ppermute | solution.py:319
  33.8 26.2 %collective-permute-start.2 = (bf16[16,48,384]{2,1,0:T(8,128)(2,1)}, bf16[16,48,384]{2,1,0:T(8,128)(2,1)}, u32[]{:S(2)}, u32[]{:S(2)}) collective-permute-start(bf16[16,48,384]{2,1,0:T(8,128)(2,1)} %get-tuple-element.64), channel_id=1, source_target_pairs={{0,2},{2,0},{1,3},{3,1},{4,6},{6,4},{5,7},{7,5},{8,10},{10,8},{9,1... | collective-permute-start | bytes 1769480 | tf_op jit(solution)/shard_map/ppermute | solution.py:319
  34.9 27.3 %all-to-all-start = ((bf16[16,48,384]{2,1,0:T(8,128)(2,1)}), bf16[16,48,384]{2,1,0:T(8,128)(2,1)}, u32[]{:S(2)}, u32[]{:S(2)}) async-start(bf16[16,48,384]{2,1,0:T(8,128)(2,1)} %add_convert_fusion.1), calls=%async_computation | async-start | bytes 1179648 | tf_op jit(solution)/shard_map/all_to_all | solution.py:322
  50.1 6.4 %copy-start.20 = (f32[256,768]{1,0:T(8,128)S(1)}, f32[256,768]{1,0:T(8,128)}, u32[]{:S(2)}) copy-start(f32[256,768]{1,0:T(8,128)} %copy-done.19) | copy-start | bytes 2359300
  50.1 6.4 %copy-start.30 = (f32[256,768]{1,0:T(8,128)S(1)}, f32[256,768]{1,0:T(8,128)}, u32[]{:S(2)}) copy-start(f32[256,768]{1,0:T(8,128)} %copy-done.29) | copy-start | bytes 2359300
  50.1 6.4 %copy-start.48 = (bf16[256,256]{1,0:T(8,128)(2,1)S(1)}, bf16[256,256]{1,0:T(8,128)(2,1)}, u32[]{:S(2)}) copy-start(bf16[256,256]{1,0:T(8,128)(2,1)} %copy-done.47) | copy-start | bytes 393220
  50.1 6.4 %copy-start.50 = (bf16[256,256]{1,0:T(8,128)(2,1)S(1)}, bf16[256,256]{1,0:T(8,128)(2,1)}, u32[]{:S(2)}) copy-start(bf16[256,256]{1,0:T(8,128)(2,1)} %copy-done.49) | copy-start | bytes 393220
  59.5 11.1 %collective-permute-start.4 = (bf16[16,48,384]{2,1,0:T(8,128)(2,1)}, bf16[16,48,384]{2,1,0:T(8,128)(2,1)S(1)}, u32[]{:S(2)}, u32[]{:S(2)}) collective-permute-start(bf16[16,48,384]{2,1,0:T(8,128)(2,1)} %get-tuple-element.68), channel_id=1, source_target_pairs={{0,2},{2,0},{1,3},{3,1},{4,6},{6,4},{5,7},{7,5},{8,10},{10,8},{9,1... | collective-permute-start | bytes 1769480 | tf_op jit(solution)/shard_map/ppermute | solution.py:319
  59.5 11.9 %collective-permute-start.3 = (bf16[16,48,384]{2,1,0:T(8,128)(2,1)}, bf16[16,48,384]{2,1,0:T(8,128)(2,1)S(1)}, u32[]{:S(2)}, u32[]{:S(2)}) collective-permute-start(bf16[16,48,384]{2,1,0:T(8,128)(2,1)} %get-tuple-element.66), channel_id=1, source_target_pairs={{0,2},{2,0},{1,3},{3,1},{4,6},{6,4},{5,7},{7,5},{8,10},{10,8},{9,1... | collective-permute-start | bytes 1769480 | tf_op jit(solution)/shard_map/ppermute | solution.py:319
  60.0 12.2 %copy-start.38 = (bf16[16,48,384]{2,1,0:T(8,128)(2,1)S(1)}, bf16[16,48,384]{2,1,0:T(8,128)(2,1)}, u32[]{:S(2)}) copy-start(bf16[16,48,384]{2,1,0:T(8,128)(2,1)} %copy-done.37) | copy-start | bytes 1769476
  62.2 17.3 %all-to-all-start.1 = ((bf16[16,48,384]{2,1,0:T(8,128)(2,1)}), bf16[16,48,384]{2,1,0:T(8,128)(2,1)S(1)}, u32[]{:S(2)}, u32[]{:S(2)}) async-start(bf16[16,48,384]{2,1,0:T(8,128)(2,1)} %add_convert_fusion), calls=%async_computation.1 | async-start | bytes 1179648 | tf_op jit(solution)/shard_map/all_to_all | solution.py:322
  69.4 1.2 collective-permute-start.5
  104.5 11.4 %copy-start.9 = (bf16[768,768]{1,0:T(8,128)(2,1)S(1)}, bf16[768,768]{1,0:T(8,128)(2,1)}, u32[]{:S(2)}) copy-start(bf16[768,768]{1,0:T(8,128)(2,1)} %wo_ref.3) | copy-start | bytes 3538948
  104.5 11.4 %copy-start.12 = (bf16[1,256,768]{2,1,0:T(8,128)(2,1)S(1)}, bf16[1,256,768]{2,1,0:T(8,128)(2,1)}, u32[]{:S(2)}) copy-start(bf16[1,256,768]{2,1,0:T(8,128)(2,1)} %param.7) | copy-start | bytes 1179652
  104.5 11.4 %copy-start.21 = (f32[256,768]{1,0:T(8,128)S(1)}, f32[256,768]{1,0:T(8,128)}, u32[]{:S(2)}) copy-start(f32[256,768]{1,0:T(8,128)} %copy-done.19) | copy-start | bytes 2359300
  104.5 11.4 %copy-start.23 = (f32[256,768]{1,0:T(8,128)S(1)}, f32[256,768]{1,0:T(8,128)}, u32[]{:S(2)}) copy-start(f32[256,768]{1,0:T(8,128)} %copy-done.22) | copy-start | bytes 2359300
  104.5 11.4 %copy-start.27 = (bf16[1,256,768]{2,1,0:T(8,128)(2,1)S(1)}, bf16[1,256,768]{2,1,0:T(8,128)(2,1)}, u32[]{:S(2)}) copy-start(bf16[1,256,768]{2,1,0:T(8,128)(2,1)} %param.6) | copy-start | bytes 1179652
  106.9 22.8 %all-to-all-start.3 = ((bf16[16,8,1536]{2,1,0:T(8,128)(2,1)}), bf16[16,8,1536]{2,1,0:T(8,128)(2,1)}, u32[]{:S(2)}, u32[]{:S(2)}) async-start(bf16[16,8,1536]{2,1,0:T(8,128)(2,1)} %copy-done.28), calls=%async_computation.3 | async-start | bytes 786432 | tf_op jit(solution)/shard_map/all_to_all | solution.py:345
  (36 other events, 57.2 us)

commit v2 on v1

v2 whole, which is shorter than its diff:
```python
import functools

import jax
import jax.numpy as jnp
from jax import lax
from jax.experimental import pallas as pl
from jax.experimental.pallas import tpu as pltpu
from jax.sharding import Mesh
from jax.sharding import PartitionSpec as P

HEADS = 12
EPS = 1e-05
SEQ = ("y", "z", "xl", "c")
ROW = ("xl", "xh")
T = 256
D = 768
GROUPS = 3
GW = 256
BF = jnp.bfloat16
F32 = jnp.float32
LIMIT = 24


def nn(a, b):
    return lax.dot_general(a, b, (((1,), (0,)), ((), ())), preferred_element_type=F32)


def nt(a, b):
    return lax.dot_general(a, b, (((1,), (1,)), ((), ())), preferred_element_type=F32)


def eye(n):
    rows = lax.broadcasted_iota(jnp.int32, (n, n), 0)
    cols = lax.broadcasted_iota(jnp.int32, (n, n), 1)
    return jnp.where(rows == cols, 1.0, 0.0).astype(BF)


def layer_norm(x_ref, gain, bias):
    values = x_ref[...].astype(F32)
    centered = values - jnp.mean(values, axis=-1, keepdims=True)
    rstd = lax.rsqrt(jnp.mean(centered * centered, axis=-1, keepdims=True) + EPS)
    xhat = centered * rstd
    normed = (xhat * gain + bias).astype(BF)
    return normed, xhat, rstd


def row_order(at_ref):
    p = lax.broadcasted_iota(jnp.int32, (D, 1), 0)
    second = jnp.where(p >= 384, 1, 0)
    q = p - 384 * second
    owner = (q * 171) >> 13
    b = q - 48 * owner
    z = (b * 43) >> 8
    j = b - 6 * z
    y, xl = (owner >> 1) ^ at_ref[0], (owner & 1) ^ at_ref[1]
    to_core = jnp.where(second == 1, at_ref[2], 1 - at_ref[2])
    feature = ((y * 8 + z) * 2 + xl) * 12 + to_core * 6 + j
    cols = lax.broadcasted_iota(jnp.int32, (D, D), 1)
    return jnp.where(cols == feature, 1.0, 0.0).astype(BF)


def own_kernel(at_ref, gain_ref, bias_ref, x_hbm, cot_hbm, w_hbm, wo_hbm,
               qkv_ref, dmix_ref, npt_ref, xhat_ref, rstd_ref, mt_ref,
               x_ref, cot_ref, w_ref, wo_ref, sems):
    copies = [pltpu.make_async_copy(x_hbm, x_ref, sems.at[0])]
    for i in range(3):
        copies.append(pltpu.make_async_copy(w_hbm.at[:, pl.ds(D * i, D)], w_ref.at[i], sems.at[1 + i]))
    copies.append(pltpu.make_async_copy(cot_hbm, cot_ref, sems.at[4]))
    copies.append(pltpu.make_async_copy(wo_hbm, wo_ref, sems.at[5]))
    for copy in copies:
        copy.start()
    mt = row_order(at_ref)
    mt_ref[...] = mt
    copies[0].wait()
    normed, xhat, rstd = layer_norm(x_ref, gain_ref[...].reshape(1, D), bias_ref[...].reshape(1, D))
    xhat_ref[...] = xhat
    rstd_ref[...] = jnp.broadcast_to(rstd, (T, 128))
    npt_ref[...] = nt(mt, normed).astype(BF)
    for i in range(3):
        copies[1 + i].wait()
        qkv_ref[:, D * i : D * i + D] = nn(normed, w_ref[i]).astype(BF)
    copies[4].wait()
    copies[5].wait()
    dmix_ref[...] = nt(cot_ref[...], wo_ref[...]).astype(BF)


def head_group(g, has, qkv_ref, kvm_ref, dmix_ref):
    at = GW * g
    lanes = lax.broadcasted_iota(jnp.int32, (T, 128), 1)
    low = lanes < 64
    causal = lax.broadcasted_iota(jnp.int32, (T, T), 0) <= lax.broadcasted_iota(jnp.int32, (T, T), 1)
    unit = eye(128)
    unit2 = eye(T)
    zero = jnp.zeros((), BF)
    mixts, dqs, dks, dvs = [], [], [], []
    for pair in range(2):
        cq = slice(at + 128 * pair, at + 128 * pair + 128)
        ck = slice(D + cq.start, D + cq.stop)
        cv = slice(2 * D + cq.start, 2 * D + cq.stop)
        q2 = (qkv_ref[:, cq].astype(F32) * 0.125).astype(BF)
        k2 = jnp.concatenate([qkv_ref[:, ck], kvm_ref[:, cq]], axis=0)
        v2 = jnp.concatenate([qkv_ref[:, cv], kvm_ref[:, ck]], axis=0)
        dm2 = dmix_ref[:, cq]
        kt2 = nt(unit, k2).astype(BF)
        vt2 = nt(unit, v2).astype(BF)
        ds_parts, p_parts, q_parts, dm_parts, dqt_parts = [], [], [], [], []
        for half in range(2):
            pick = low if half == 0 else jnp.logical_not(low)
            qa = jnp.where(pick, q2, zero)
            dma = jnp.where(pick, dm2, zero)
            st = nt(k2, qa)
            st_own = jnp.where(causal, st[:T], -1e30)
            st_mem = jnp.where(has, st[T:], -1e30)
            st = jnp.concatenate([st_own, st_mem], axis=0)
            top = jnp.max(st, axis=0, keepdims=True)
            e = jnp.exp(st - top)
            p = e * (1.0 / jnp.sum(e, axis=0, keepdims=True))
            pb = p.astype(BF)
            rows = slice(64 * half, 64 * half + 64)
            mixts.append(nn(vt2[rows], pb).astype(BF))
            dp = nt(v2, dma)
            ds = (p * (dp - jnp.sum(dp * p, axis=0, keepdims=True))).astype(BF)
            dqt_parts.append((nn(kt2[rows], ds) * 0.125).astype(BF))
            ds_parts.append(ds)
            p_parts.append(pb)
            q_parts.append(qa)
            dm_parts.append(dma)
        dks.append(nn(jnp.concatenate(ds_parts, axis=1), jnp.concatenate(q_parts, axis=0)).astype(BF))
        dvs.append(nn(jnp.concatenate(p_parts, axis=1), jnp.concatenate(dm_parts, axis=0)).astype(BF))
        dqs.append(nt(unit2, jnp.concatenate(dqt_parts, axis=0)).astype(BF))
    dq = jnp.concatenate(dqs, axis=1)
    dk = jnp.concatenate(dks, axis=1)
    dv = jnp.concatenate(dvs, axis=1)
    return jnp.concatenate(mixts, axis=0), dq, dk, dv


def put_rows(send_ref, keep_ref, slot, xh, lhs, rhs):
    first, second = rhs[:, :384], rhs[:, 384:]
    mine = xh == 0
    for r in range(2):
        part = jnp.where(mine, first, second) if r == 0 else jnp.where(mine, second, first)
        at = 768 * r + 384 * slot
        send_ref[:, at : at + 384] = nn(lhs[:384], part).astype(BF)
        keep_ref[:, at : at + 384] = nn(lhs[384:], part).astype(BF)


def group_outputs(g, slot, at_ref, npt_all, w_ref, grads, send_ref, keep_ref):
    dq, dk, dv = grads
    rhs = jnp.concatenate([jnp.concatenate([dq, jnp.zeros((T, GW), BF)], axis=0), dk, dv], axis=1)
    put_rows(send_ref, keep_ref, slot, at_ref[3], npt_all, rhs)
    wq, wk, wv = (w_ref[:, D * i + GW * g : D * i + GW * g + GW] for i in range(3))
    own = nt(dq, wq) + nt(dk[:T], wk) + nt(dv[:T], wv)
    mem = nt(dk[T:], wk) + nt(dv[T:], wv)
    return own, mem


def first_kernel(at_ref, gain_ref, bias_ref, xp_ref, w_ref, mt_ref, qkv_ref, dmix_ref, npt_ref,
                 send_ref, keep_ref, mixt_ref, dn_ref, dnm_ref, kvm_ref, npt_all_ref, xhatm_ref):
    normed, xhat, _ = layer_norm(xp_ref, gain_ref[...].reshape(1, D), bias_ref[...].reshape(1, D))
    kvm_ref[...] = nn(normed, w_ref[:, D:]).astype(BF)
    xhatm_ref[...] = xhat
    npt_all_ref[:, :T] = npt_ref[...]
    npt_all_ref[:, T:] = nt(mt_ref[...], normed).astype(BF)
    has = at_ref[4] > 0
    npt_all = npt_all_ref[...]
    for g in range(2):
        mixt, *grads = head_group(g, has, qkv_ref, kvm_ref, dmix_ref)
        mixt_ref[GW * g : GW * g + GW, :] = mixt
        own, mem = group_outputs(g, g, at_ref, npt_all, w_ref, grads, send_ref, keep_ref)
        if g == 0:
            dn_ref[...] = own
            dnm_ref[...] = mem
        else:
            dn_ref[...] += own
            dnm_ref[...] += mem


def second_kernel(at_ref, w_ref, mt_ref, cot_ref, qkv_ref, dmix_ref, mixt_in, dn_in, dnm_in, kvm_ref, npt_all_ref,
                  xhat_ref, xhatm_ref, send_ref, keep_ref, vec_ref, mixt_ref, dn_ref):
    mixt, *grads = head_group(2, at_ref[4] > 0, qkv_ref, kvm_ref, dmix_ref)
    mixt_ref[: 2 * GW, :] = mixt_in[...]
    mixt_ref[2 * GW :, :] = mixt
    own, mem = group_outputs(2, 0, at_ref, npt_all_ref[...], w_ref, grads, send_ref, keep_ref)
    lhs = nn(mt_ref[...], mixt_ref[...]).astype(BF)
    put_rows(send_ref, keep_ref, 1, at_ref[3], lhs, cot_ref[...])
    dn, dnm = dn_in[...] + own, dnm_in[...] + mem
    dn_ref[...] = dn
    vec_ref[0:1, :] = jnp.sum(dn * xhat_ref[...] + dnm * xhatm_ref[...], axis=0, keepdims=True)
    vec_ref[1:2, :] = jnp.sum(dn + dnm, axis=0, keepdims=True)


def token_kernel(gain_ref, x_ref, cot_ref, mixt_ref, wo_ref, dn_ref, xhat_ref, rstd_ref, out_ref, dx_ref):
    mixed = nt(eye(T), mixt_ref[...]).astype(BF)
    out_ref[...] = (x_ref[...].astype(F32) + nn(mixed, wo_ref[...])).astype(BF)
    d_hat = dn_ref[...] * gain_ref[...].reshape(1, D)
    xhat = xhat_ref[...]
    row = rstd_ref[:, 0:1] * (
        d_hat
        - jnp.mean(d_hat, axis=-1, keepdims=True)
        - xhat * jnp.mean(d_hat * xhat, axis=-1, keepdims=True)
    )
    dx_ref[...] = (cot_ref[...].astype(F32) + row).astype(BF)


def split_rows(value):
    high = value.astype(BF)
    low = (value - high.astype(F32)).astype(BF)
    return jnp.concatenate([high, low, jnp.zeros((4, value.shape[1]), BF)], axis=0)


def join_rows(rows):
    return rows[0:2].astype(F32) + rows[2:4].astype(F32)


def tree(a, b, c, d):
    return (a.astype(F32) + b.astype(F32)) + (c.astype(F32) + d.astype(F32))


def pair_a_kernel(keep_ref, recv_ref, *outs):
    for k in range(4):
        rows = slice(96 * k, 96 * k + 96)
        outs[k][...] = (keep_ref[rows, :].astype(F32) + recv_ref[rows, :].astype(F32)).astype(BF)


def pair_b_kernel(keep_ref, recv_ref, vec_ref, vecr_ref, *outs):
    vec = split_rows(vec_ref[...] + vecr_ref[...])
    for k in range(4):
        cols = slice(768 * (k & 1), 768 * (k & 1) + 768)
        for y in range(4):
            rows = slice(96 * y + 48 * (k >> 1), 96 * y + 48 * (k >> 1) + 48)
            outs[k][48 * y : 48 * y + 48, :] = (
                keep_ref[rows, cols].astype(F32) + recv_ref[rows, cols].astype(F32)
            ).astype(BF)
        outs[k][192:200, :] = vec


def mid_a_kernel(a, b, c, d, *outs):
    for k in range(4):
        rows = slice(48 * (k >> 1), 48 * (k >> 1) + 48)
        cols = slice(768 * (k & 1), 768 * (k & 1) + 768)
        outs[k][...] = tree(a[rows, cols], b[rows, cols], c[rows, cols], d[rows, cols]).astype(BF)


def mid_b_kernel(a, b, c, d, *outs):
    vec = split_rows((join_rows(a[192:200]) + join_rows(b[192:200])) + (join_rows(c[192:200]) + join_rows(d[192:200])))
    for k in range(4):
        rows = slice(48 * k, 48 * k + 48)
        outs[k][0:48, :] = tree(a[rows], b[rows], c[rows], d[rows]).astype(BF)
        outs[k][48:56, :] = vec


def plane_kernel(a0, a1, a2, a3, b0, b1, b2, b3, out_ref):
    at = slice(48, 56)
    vec = (join_rows(b0[at]) + join_rows(b1[at])) + (join_rows(b2[at]) + join_rows(b3[at]))
    vec = jnp.concatenate([vec[0:1], vec[1:2]], axis=1)
    high = vec.astype(BF).astype(F32)
    tail = jnp.concatenate([high, vec - high], axis=0)
    g = slice(0, 48)
    sums = jnp.concatenate([tree(a0[...], a1[...], a2[...], a3[...]), tree(b0[g], b1[g], b2[g], b3[g])], axis=1)
    for z in range(8):
        out_ref[z] = jnp.concatenate([sums[6 * z : 6 * z + 6], tail], axis=0).astype(BF)


def column_kernel(factor, in_ref, rows_ref, gain_ref, bias_ref):
    acc = in_ref[0].astype(F32)
    for z in range(1, 8):
        acc = acc + in_ref[z].astype(F32)
    rows_ref[...] = acc.astype(BF)
    vec = (acc[6:7] + acc[7:8]) * factor
    gain_ref[...] = vec[:, :D].reshape(D)
    bias_ref[...] = vec[:, D:].reshape(D)


def finish_kernel(factor, at_ref, mine_ref, other_ref, qkv_ref, wout_ref):
    mine, other = mine_ref[...].astype(F32) * factor, other_ref[...].astype(F32) * factor
    first = at_ref[3] == 0
    halves = [jnp.where(first, mine, other), jnp.where(first, other, mine)]
    for g in range(GROUPS + 1):
        cols = slice(384 * g, 384 * g + 384)
        full = jnp.concatenate([halves[0][0:6, cols], halves[1][0:6, cols]], axis=1)
        if g < GROUPS:
            for i in range(3):
                at = D * i + GW * g
                qkv_ref[:, at : at + GW] = full[:, GW * i : GW * i + GW]
        else:
            wout_ref[...] = full


VM = pl.BlockSpec(memory_space=pltpu.VMEM)
SM = pl.BlockSpec(memory_space=pltpu.SMEM)
ANY = pl.BlockSpec(memory_space=pl.ANY)


def call(kernel, name, out_shape, args, scalars=0, anys=(), scratch=(), limit=16):
    specs = [SM if i < scalars else ANY if i in anys else VM for i in range(len(args))]
    return pl.pallas_call(
        kernel,
        name=name,
        in_specs=specs,
        out_specs=[VM] * len(out_shape),
        out_shape=out_shape,
        scratch_shapes=scratch,
        compiler_params=pltpu.CompilerParams(vmem_limit_bytes=limit * 1024 * 1024),
    )(*args)


def sds(*shape, dtype=BF):
    return jax.ShapeDtypeStruct(shape, dtype)


def on_device(layer_input, cotangent, gain, bias, w, wo):
    x, cot = layer_input[0], cotangent[0]
    seq = lax.axis_size(SEQ)
    xp = lax.ppermute(x, SEQ, [(i, i + 1) for i in range(seq - 1)])
    place = [lax.axis_index(n) for n in ("y", "xl", "c", "xh")] + [lax.axis_index(SEQ) > 0]
    at = jnp.stack([v.astype(jnp.int32) for v in place])
    row, mat, tokens = sds(T, D, dtype=F32), sds(D, D), sds(T, D)
    qkv, dmix, npt, xhat, rstd, mt = call(
        own_kernel, "own_part",
        [sds(T, 3 * D), tokens, sds(D, T), row, sds(T, 128, dtype=F32), mat],
        [at, gain, bias, x, cot, w, wo], 1, (3, 4, 5, 6),
        [pltpu.VMEM((T, D), BF), pltpu.VMEM((T, D), BF), pltpu.VMEM((3, D, D), BF), pltpu.VMEM((D, D), BF),
         pltpu.SemaphoreType.DMA((6,))],
    )
    wide = sds(384, 1536)
    send_a, keep_a, mixt, dn, dnm, kvm, npt_all, xhatm = call(
        first_kernel, "memory_and_heads",
        [wide, wide, sds(2 * GW, T), row, row, sds(T, 2 * D), sds(D, 2 * T), row],
        [at, gain, bias, xp, w, mt, qkv, dmix, npt], 1, limit=LIMIT,
    )
    send_b, keep_b, vec, mixt, dn = call(
        second_kernel, "heads_and_output_weight",
        [wide, wide, sds(2, D, dtype=F32), sds(D, T), row],
        [at, w, mt, cot, qkv, dmix, mixt, dn, dnm, kvm, npt_all, xhat, xhatm], 1, limit=LIMIT,
    )

    def swap(block):
        return lax.ppermute(block, "c", [(0, 1), (1, 0)])

    def exchange(parts, axes):
        n = lax.axis_size(axes)
        return [parts[0]] + [lax.ppermute(parts[k], axes, [(i, i ^ k) for i in range(n)]) for k in (1, 3, 2)]

    def ordered(parts):
        own, one, three, two = parts
        return [own, one, two, three]

    parts_a = call(pair_a_kernel, "pair_sum_a", [sds(96, 1536)] * 4, [keep_a, swap(send_a)])
    parts_b = call(pair_b_kernel, "pair_sum_b", [sds(200, 768)] * 4, [keep_b, swap(send_b), vec, swap(vec)])
    parts_a = ordered(exchange(parts_a, "y"))
    parts_b = ordered(exchange(parts_b, ROW))
    out, dx = call(
        token_kernel, "token_outputs", [tokens, tokens],
        [gain, x, cot, mixt, wo, dn, xhat, rstd],
    )
    parts_a = call(mid_a_kernel, "middle_sum_a", [sds(48, 768)] * 4, parts_a)
    parts_b = call(mid_b_kernel, "middle_sum_b", [sds(56, 768)] * 4, parts_b)
    parts_a = ordered(exchange(parts_a, ROW))
    parts_b = ordered(exchange(parts_b, "y"))
    (mine,) = call(plane_kernel, "plane_sum", [sds(8, 8, 1536)], [*parts_a, *parts_b])
    mine = lax.all_to_all(mine, "z", 0, 0, tiled=True)
    factor = 1.0 / float(seq * lax.axis_size("xh") * T) ** 0.5
    mine, grad_gain, grad_bias = call(
        functools.partial(column_kernel, factor), "column_sum",
        [sds(8, 1536), sds(D, dtype=F32), sds(D, dtype=F32)], [mine],
    )
    other = lax.ppermute(mine, "xh", [(0, 1), (1, 0)])
    grad_qkv, grad_out = call(
        functools.partial(finish_kernel, factor), "finish",
        [sds(6, 3 * D, dtype=F32), sds(6, D, dtype=F32)], [at, mine, other], 1,
    )
    return out[None], dx[None], grad_qkv, grad_out, grad_gain, grad_bias


def solution(mesh):
    torus = Mesh(mesh.devices.reshape(4, 8, 2, 2, 2), ("y", "z", "xl", "c", "xh"))
    return jax.shard_map(
        on_device,
        mesh=torus,
        in_specs=(P("xh", SEQ, None), P("xh", SEQ, None), P(), P(), P(), P()),
        out_specs=(P("xh", SEQ, None), P("xh", SEQ, None), P(SEQ, None), P(SEQ, None), P(), P()),
        check_vma=False,
    )
```

time: 134 us -> 99.5 us (0.74)
  local copies, waits for them, and re-layouts: 29.1 us -> 6.75 us
  blocking collectives: 23.1 us -> 17.3 us
  other arithmetic: 4.36 us -> 0 us
  starting transfers between devices: 28.2 us -> 26.3 us
    all_to_all x3 -> x0, starting transfers between devices: 23.7 us -> none  [the longest x2 14.8 us: spread(): return lax.all_to_all(block, PLANE, 0, 0, tiled=True)]
    ppermute x0 -> x13, starting transfers between devices: none -> 22.2 us  [the longest x12 19.5 us: exchange(): lax.ppermute(parts[k], axes, [(i, i ^ k) for i in range(n)])]
    unnamed x102 -> x24, local copies, waits for them, and re-layouts: 27.7 us -> 6.66 us
    all_to_all x3 -> x0, waiting for transfers between devices: 15 us -> none  [the longest x1 10.1 us: on_device(): mine = lax.all_to_all(mine, COLUMN, 0, 0, tiled=True)]
    ppermute x0 -> x13, waiting for transfers between devices: none -> 14.7 us  [the longest x12 13.9 us: exchange(): lax.ppermute(parts[k], axes, [(i, i ^ k) for i in range(n)])]
    all_to_all x1, blocking collectives: 23.1 us -> 17.3 us  [on_device(): mine = lax.all_to_all(mine, 'z', 0, 0, tiled=True)]
    convert_element_type x2 -> x0, other arithmetic: 3.15 us -> none  [on_device(): (keep.astype(F32) + swap(send).astype(F32)).astype(BF)]
    reshape x2 -> x0, local copies, waits for them, and re-layouts: 1.38 us -> none  [on_device(): gain, bias = (gain.reshape(1, D), bias.reshape(1, D))]
  transfers between devices with their start and end apart: 9 -> 17, of which waited for: 3 -> 8; matrix products, arithmetic and copies ran while one was open for 3% -> 0% of each run, Pallas kernels for 14% -> 16%
where the time goes in v2:
time: 99.5 us; the launch traced here: 97.5 us
  Pallas kernels  30.6 us (31%)
  starting transfers between devices  26.3 us (26%)
  blocking collectives  17.3 us (17%)
  waiting for transfers between devices  15.8 us (16%)
  local copies, waits for them, and re-layouts  6.75 us (7%)
    pallas_call x11, Pallas kernels, call(): pl.pallas_call(kernel, name=name, in_specs=specs, out_specs=[VM] * len(ou...  30.6 us
    ppermute x12, starting transfers between devices, exchange(): lax.ppermute(parts[k], axes, [(i, i ^ k) for i in range(n)])  19.5 us
    all_to_all x1, blocking collectives, on_device(): mine = lax.all_to_all(mine, 'z', 0, 0, tiled=True)  17.3 us
    ppermute x12, waiting for transfers between devices, exchange(): lax.ppermute(parts[k], axes, [(i, i ^ k) for i in range(n)])  13.9 us
    unnamed x24, local copies, waits for them, and re-layouts  6.66 us
    ppermute x1, starting transfers between devices, on_device(): other = lax.ppermute(mine, 'xh', [(0, 1), (1, 0)])  2.73 us
    ppermute x3, starting transfers between devices, swap(): return lax.ppermute(block, 'c', [(0, 1), (1, 0)])  2.2 us
  transfers between devices with their start and end apart: 17, of which 8 were waited for; matrix products, arithmetic and copies ran while one was open for 0% of the time, Pallas kernels for 16%

profile of v2, /device:TPU:2, one launch (start us, length us, event | category | flops | bytes accessed | tf_op | source)
XLA Modules:
  0.0 97.5 jit_solution(12170033328184030746)
XLA Ops:
  0.6 1.9 %collective-permute-start = (bf16[256,768]{1,0:T(8,128)(2,1)}, bf16[256,768]{1,0:T(8,128)(2,1)S(1)}, u32[]{:S(2)}, u32[]{:S(2)}) collective-permute-start(bf16[256,768]{1,0:T(8,128)(2,1)} %bitcast.12), channel_id=1, source_target_pairs={{0,2},{2,4},{4,6},{6,8},{8,10},{10,12},{12,14},{14,16},{16,18},{18... | collective-permute-start | bytes 1179656 | tf_op jit(solution)/shard_map/ppermute | solution.py:314
  2.7 2.0 %copy-done = bf16[768,2304]{1,0:T(8,128)(2,1)S(1)} copy-done((bf16[768,2304]{1,0:T(8,128)(2,1)S(1)}, bf16[768,2304]{1,0:T(8,128)(2,1)}, u32[]{:S(2)}) %copy-start) | copy-done | bytes 3538968
  4.7 1.3 %copy-done.2 = bf16[768,768]{1,0:T(8,128)(2,1)S(1)} copy-done((bf16[768,768]{1,0:T(8,128)(2,1)S(1)}, bf16[768,768]{1,0:T(8,128)(2,1)}, u32[]{:S(2)}) %copy-start.2) | copy-done | bytes 1179672
  5.9 1.0 %copy-done.4 = bf16[1,256,768]{2,1,0:T(8,128)(2,1)S(1)} copy-done((bf16[1,256,768]{2,1,0:T(8,128)(2,1)S(1)}, bf16[1,256,768]{2,1,0:T(8,128)(2,1)}, u32[]{:S(2)}) %copy-start.4) | copy-done | bytes 393240
  9.3 5.6 %own_part.1 = (bf16[256,2304]{1,0:T(8,128)(2,1)S(1)}, bf16[256,768]{1,0:T(8,128)(2,1)S(1)}, bf16[768,256]{1,0:T(8,128)(2,1)S(1)}, f32[256,768]{1,0:T(8,128)S(1)}...) custom-call(s32[5]{0:T(128)S(1)} %stack.27.at_ref, f32[768]{0:T(1024)S(1)} %copy-done.8, f32[768]{0:T(1024)S(1)} %copy-done.10, ...), custom_call_target="tpu_custom_call" | custom-call | tf_op jit(solution)/shard_map/own_part/pallas_call | solution.py:296
  14.9 12.9 %memory_and_heads.1 = (bf16[384,1536]{1,0:T(8,128)(2,1)S(1)}, bf16[384,1536]{1,0:T(8,128)(2,1)S(1)}, bf16[512,256]{1,0:T(8,128)(2,1)S(1)}, f32[256,768]{1,0:T(8,...) custom-call(s32[5]{0:T(128)S(1)} %stack.27.at_ref, ...), custom_call_target="tpu_custom_call" | custom-call | tf_op jit(solution)/shard_map/memory_and_heads/pallas_call | solution.py:296
  27.8 2.1 %collective-permute-start.1 = (bf16[384,1536]{1,0:T(8,128)(2,1)S(1)}, bf16[384,1536]{1,0:T(8,128)(2,1)S(1)}, u32[]{:S(2)}, u32[]{:S(2)}) collective-permute-start(bf16[384,1536]{1,0:T(8,128)(2,1)S(1)} %get-tuple-element.65), channel_id=1, source_target_pairs={{0,2},{2,0},{1,3},{3,1},{4,6},{6,4},{5,7},{7,5},{8,10},{10,8},{9,1... | collective-permute-start | bytes 3538952 | tf_op jit(solution)/shard_map/ppermute | solution.py:338
  29.9 7.5 %heads_and_output_weight.1 = (bf16[384,1536]{1,0:T(8,128)(2,1)S(1)}, bf16[384,1536]{1,0:T(8,128)(2,1)S(1)}, f32[2,768]{1,0:T(2,128)S(1)}, bf16[768,256]{1,0:T(8,128)(2,1)S(1)}, f32[256,768]{1,0:T(8,128)S(1)}) custom-call(s32[5]{0:T(128)S(1)} %stack.27.at_ref, bf16[768,2304]{1,0:T(8,128)(2,1)S(1)} %copy-done.1, ...), custom_call_target="tpu_custom_call" | custom-call | tf_op jit(solution)/shard_map/heads_and_output_weight/pallas_call | solution.py:296
  37.8 1.7 %collective-permute-start.2 = (bf16[96,1536]{1,0:T(8,128)(2,1)S(1)}, bf16[96,1536]{1,0:T(8,128)(2,1)S(1)}, u32[]{:S(2)}, u32[]{:S(2)}) collective-permute-start(bf16[96,1536]{1,0:T(8,128)(2,1)S(1)} %get-tuple-element.67), channel_id=1, source_target_pairs={{0,64},{64,0},{128,192},{192,128},{1,65},{65,1},{129,193},{193,129... | collective-permute-start | bytes 884744 | tf_op jit(solution)/shard_map/ppermute | solution.py:342
  39.5 2.9 %collective-permute-start.3 = (bf16[96,1536]{1,0:T(8,128)(2,1)S(1)}, bf16[96,1536]{1,0:T(8,128)(2,1)S(1)}, u32[]{:S(2)}, u32[]{:S(2)}) collective-permute-start(bf16[96,1536]{1,0:T(8,128)(2,1)S(1)} %get-tuple-element.68), channel_id=1, source_target_pairs={{0,128},{64,192},{128,0},{192,64},{1,129},{65,193},{129,1},{193,65... | collective-permute-start | bytes 884744 | tf_op jit(solution)/shard_map/ppermute | solution.py:342
  42.6 1.2 %collective-permute-done.9.vecr_ref = f32[2,768]{1,0:T(2,128)S(1)} collective-permute-done((f32[2,768]{1,0:T(2,128)S(1)}, f32[2,768]{1,0:T(2,128)S(1)}, u32[]{:S(2)}, u32[]{:S(2)}) %collective-permute-start.9) | collective-permute-done | bytes 6176 | tf_op jit(solution)/shard_map/ppermute | solution.py:338
  44.1 2.5 %collective-permute-start.10 = (bf16[200,768]{1,0:T(8,128)(2,1)S(1)}, bf16[200,768]{1,0:T(8,128)(2,1)S(1)}, u32[]{:S(2)}, u32[]{:S(2)}) collective-permute-start(bf16[200,768]{1,0:T(8,128)(2,1)S(1)} %get-tuple-element.78), channel_id=1, source_target_pairs={{0,1},{1,0},{4,5},{5,4},{2,3},{3,2},{6,7},{7,6},{8,9},{9,8},{12,13... | collective-permute-start | bytes 921608 | tf_op jit(solution)/shard_map/ppermute | solution.py:342
  48.5 7.7 %collective-permute-done.3.c = bf16[96,1536]{1,0:T(8,128)(2,1)S(1)} collective-permute-done((bf16[96,1536]{1,0:T(8,128)(2,1)S(1)}, bf16[96,1536]{1,0:T(8,128)(2,1)S(1)}, u32[]{:S(2)}, u32[]{:S(2)}) %collective-permute-start.3) | collective-permute-done | bytes 294944 | tf_op jit(solution)/shard_map/ppermute | solution.py:342
  56.2 2.6 %collective-permute-done.4.d = bf16[96,1536]{1,0:T(8,128)(2,1)S(1)} collective-permute-done((bf16[96,1536]{1,0:T(8,128)(2,1)S(1)}, bf16[96,1536]{1,0:T(8,128)(2,1)S(1)}, u32[]{:S(2)}, u32[]{:S(2)}) %collective-permute-start.4) | collective-permute-done | bytes 294944 | tf_op jit(solution)/shard_map/ppermute | solution.py:342
  58.9 2.7 %collective-permute-start.5 = (bf16[48,768]{1,0:T(8,128)(2,1)S(1)}, bf16[48,768]{1,0:T(8,128)(2,1)S(1)}, u32[]{:S(2)}, u32[]{:S(2)}) collective-permute-start(bf16[48,768]{1,0:T(8,128)(2,1)S(1)} %get-tuple-element.71), channel_id=1, source_target_pairs={{0,1},{1,0},{4,5},{5,4},{2,3},{3,2},{6,7},{7,6},{8,9},{9,8},{12,13... | collective-permute-start | bytes 221192 | tf_op jit(solution)/shard_map/ppermute | solution.py:342
  62.8 4.3 %collective-permute-start.14 = (bf16[56,768]{1,0:T(8,128)(2,1)S(1)}, bf16[56,768]{1,0:T(8,128)(2,1)S(1)}, u32[]{:S(2)}, u32[]{:S(2)}) collective-permute-start(bf16[56,768]{1,0:T(8,128)(2,1)S(1)} %get-tuple-element.83), channel_id=1, source_target_pairs={{0,128},{64,192},{128,0},{192,64},{1,129},{65,193},{129,1},{193,65... | collective-permute-start | bytes 258056 | tf_op jit(solution)/shard_map/ppermute | solution.py:342
  67.1 1.0 %collective-permute-start.6 = (bf16[48,768]{1,0:T(8,128)(2,1)S(1)}, bf16[48,768]{1,0:T(8,128)(2,1)S(1)}, u32[]{:S(2)}, u32[]{:S(2)}) collective-permute-start(bf16[48,768]{1,0:T(8,128)(2,1)S(1)} %get-tuple-element.72), channel_id=1, source_target_pairs={{0,4},{1,5},{4,0},{5,1},{2,6},{3,7},{6,2},{7,3},{8,12},{9,13},{12,... | collective-permute-start | bytes 221192 | tf_op jit(solution)/shard_map/ppermute | solution.py:342
  68.1 2.0 %collective-permute-start.7 = (bf16[48,768]{1,0:T(8,128)(2,1)S(1)}, bf16[48,768]{1,0:T(8,128)(2,1)S(1)}, u32[]{:S(2)}, u32[]{:S(2)}) collective-permute-start(bf16[48,768]{1,0:T(8,128)(2,1)S(1)} %get-tuple-element.73), channel_id=1, source_target_pairs={{0,5},{1,4},{4,1},{5,0},{2,7},{3,6},{6,3},{7,2},{8,13},{9,12},{12,... | collective-permute-start | bytes 221192 | tf_op jit(solution)/shard_map/ppermute | solution.py:342
  70.1 1.4 %collective-permute-done.6.a2 = bf16[48,768]{1,0:T(8,128)(2,1)S(1)} collective-permute-done((bf16[48,768]{1,0:T(8,128)(2,1)S(1)}, bf16[48,768]{1,0:T(8,128)(2,1)S(1)}, u32[]{:S(2)}, u32[]{:S(2)}) %collective-permute-start.6) | collective-permute-done | bytes 73760 | tf_op jit(solution)/shard_map/ppermute | solution.py:342
  71.4 1.0 %collective-permute-done.7.a3 = bf16[48,768]{1,0:T(8,128)(2,1)S(1)} collective-permute-done((bf16[48,768]{1,0:T(8,128)(2,1)S(1)}, bf16[48,768]{1,0:T(8,128)(2,1)S(1)}, u32[]{:S(2)}, u32[]{:S(2)}) %collective-permute-start.7) | collective-permute-done | bytes 73760 | tf_op jit(solution)/shard_map/ppermute | solution.py:342
  73.1 17.3 %all_to_all.5.in_ref = bf16[8,8,1536]{2,1,0:T(8,128)(2,1)S(1)} all-to-all(bf16[8,8,1536]{2,1,0:T(8,128)(2,1)S(1)} %plane_sum.1), channel_id=1, replica_groups=mesh['y'=4,'z'=8,'xl'=2,'c'=2,'xh'=2] {'z'}, dimensions={0} | all-to-all | bytes 393216 | tf_op jit(solution)/shard_map/all_to_all | solution.py:361
  91.0 2.7 %collective-permute-start.16 = (bf16[8,1536]{1,0:T(8,128)(2,1)S(1)}, bf16[8,1536]{1,0:T(8,128)(2,1)S(1)}, u32[]{:S(2)}, u32[]{:S(2)}) collective-permute-start(bf16[8,1536]{1,0:T(8,128)(2,1)S(1)} %get-tuple-element.85.mine_ref), channel_id=1, source_target_pairs={{0,1},{1,0},{2,3},{3,2},{4,5},{5,4},{6,7},{7,6},{8,9},{9,8},{10,11... | collective-permute-start | bytes 73736 | tf_op jit(solution)/shard_map/ppermute | solution.py:367
  93.7 1.8 %token_outputs.1 = (bf16[256,768]{1,0:T(8,128)(2,1)}, bf16[256,768]{1,0:T(8,128)(2,1)}) custom-call(f32[768]{0:T(1024)S(1)} %copy-done.9, bf16[256,768]{1,0:T(8,128)(2,1)S(1)} %bitcast.14, bf16[256,768]{1,0:T(8,128)(2,1)S(1)} %bitcast.11, bf16[768,256]{1,0:T(8,128)(2,1)S(1)} %get-tuple-element.59.mixt_ref, bf16[768,768]{1,0:T(8,128)(2,1)S(1)} %copy-done.3, ...), custom_call_target="tpu_custom_call" | custom-call | tf_op jit(solution)/shard_map/token_outputs/pallas_call | solution.py:296
  96.3 1.2 %finish.1 = (f32[6,2304]{1,0:T(8,128)}, f32[6,768]{1,0:T(8,128)}) custom-call(s32[5]{0:T(128)S(1)} %stack.27.at_ref, bf16[8,1536]{1,0:T(8,128)(2,1)S(1)} %get-tuple-element.85.mine_ref, bf16[8,1536]{1,0:T(8,128)(2,1)S(1)} %collective-permute-done.16.other_ref), custom_call_target="tpu_custom_call" | custom-call | tf_op jit(solution)/shard_map/finish/pallas_call | solution.py:296
  (47 shorter events, 8.7 us)
Async XLA Ops:
  0.6 14.2 %collective-permute-start = (bf16[256,768]{1,0:T(8,128)(2,1)}, bf16[256,768]{1,0:T(8,128)(2,1)S(1)}, u32[]{:S(2)}, u32[]{:S(2)}) collective-permute-start(bf16[256,768]{1,0:T(8,128)(2,1)} %bitcast.12), channel_id=1, source_target_pairs={{0,2},{2,4},{4,6},{6,8},{8,10},{10,12},{12,14},{14,16},{16,18},{18... | collective-permute-start | bytes 1179656 | tf_op jit(solution)/shard_map/ppermute | solution.py:314
  2.7 2.0 %copy-start = (bf16[768,2304]{1,0:T(8,128)(2,1)S(1)}, bf16[768,2304]{1,0:T(8,128)(2,1)}, u32[]{:S(2)}) copy-start(bf16[768,2304]{1,0:T(8,128)(2,1)} %w_ref.3) | copy-start | bytes 10616836
  9.3 5.6 %copy-start.1 = (bf16[768,2304]{1,0:T(8,128)(2,1)S(1)}, bf16[768,2304]{1,0:T(8,128)(2,1)}, u32[]{:S(2)}) copy-start(bf16[768,2304]{1,0:T(8,128)(2,1)} %w_ref.3) | copy-start | bytes 10616836
  9.3 5.6 %copy-start.9 = (f32[768]{0:T(1024)S(1)}, f32[768]{0:T(1024)}, u32[]{:S(2)}) copy-start(f32[768]{0:T(1024)} %gain_ref.5) | copy-start | bytes 9220
  9.3 5.6 %copy-start.11 = (f32[768]{0:T(1024)S(1)}, f32[768]{0:T(1024)}, u32[]{:S(2)}) copy-start(f32[768]{0:T(1024)} %bias_ref.3) | copy-start | bytes 9220
  14.9 15.0 %copy-start.5 = (bf16[1,256,768]{2,1,0:T(8,128)(2,1)S(1)}, bf16[1,256,768]{2,1,0:T(8,128)(2,1)}, u32[]{:S(2)}) copy-start(bf16[1,256,768]{2,1,0:T(8,128)(2,1)} %param.7) | copy-start | bytes 1179652
  27.8 9.7 %collective-permute-start.1 = (bf16[384,1536]{1,0:T(8,128)(2,1)S(1)}, bf16[384,1536]{1,0:T(8,128)(2,1)S(1)}, u32[]{:S(2)}, u32[]{:S(2)}) collective-permute-start(bf16[384,1536]{1,0:T(8,128)(2,1)S(1)} %get-tuple-element.65), channel_id=1, source_target_pairs={{0,2},{2,0},{1,3},{3,1},{4,6},{6,4},{5,7},{7,5},{8,10},{10,8},{9,1... | collective-permute-start | bytes 3538952 | tf_op jit(solution)/shard_map/ppermute | solution.py:338
  37.5 6.4 %collective-permute-start.8 = (bf16[384,1536]{1,0:T(8,128)(2,1)S(1)}, bf16[384,1536]{1,0:T(8,128)(2,1)S(1)}, u32[]{:S(2)}, u32[]{:S(2)}) collective-permute-start(bf16[384,1536]{1,0:T(8,128)(2,1)S(1)} %get-tuple-element.75), channel_id=1, source_target_pairs={{0,2},{2,0},{1,3},{3,1},{4,6},{6,4},{5,7},{7,5},{8,10},{10,8},{9,1... | collective-permute-start | bytes 3538952 | tf_op jit(solution)/shard_map/ppermute | solution.py:338
  37.8 9.9 %collective-permute-start.2 = (bf16[96,1536]{1,0:T(8,128)(2,1)S(1)}, bf16[96,1536]{1,0:T(8,128)(2,1)S(1)}, u32[]{:S(2)}, u32[]{:S(2)}) collective-permute-start(bf16[96,1536]{1,0:T(8,128)(2,1)S(1)} %get-tuple-element.67), channel_id=1, source_target_pairs={{0,64},{64,0},{128,192},{192,128},{1,65},{65,1},{129,193},{193,129... | collective-permute-start | bytes 884744 | tf_op jit(solution)/shard_map/ppermute | solution.py:342
  39.5 16.7 %collective-permute-start.3 = (bf16[96,1536]{1,0:T(8,128)(2,1)S(1)}, bf16[96,1536]{1,0:T(8,128)(2,1)S(1)}, u32[]{:S(2)}, u32[]{:S(2)}) collective-permute-start(bf16[96,1536]{1,0:T(8,128)(2,1)S(1)} %get-tuple-element.68), channel_id=1, source_target_pairs={{0,128},{64,192},{128,0},{192,64},{1,129},{65,193},{129,1},{193,65... | collective-permute-start | bytes 884744 | tf_op jit(solution)/shard_map/ppermute | solution.py:342
  42.4 16.4 %collective-permute-start.4 = (bf16[96,1536]{1,0:T(8,128)(2,1)S(1)}, bf16[96,1536]{1,0:T(8,128)(2,1)S(1)}, u32[]{:S(2)}, u32[]{:S(2)}) collective-permute-start(bf16[96,1536]{1,0:T(8,128)(2,1)S(1)} %get-tuple-element.69), channel_id=1, source_target_pairs={{0,192},{64,128},{128,64},{192,0},{1,193},{65,129},{129,65},{193,1... | collective-permute-start | bytes 884744 | tf_op jit(solution)/shard_map/ppermute | solution.py:342
  42.6 1.2 %collective-permute-start.9 = (f32[2,768]{1,0:T(2,128)S(1)}, f32[2,768]{1,0:T(2,128)S(1)}, u32[]{:S(2)}, u32[]{:S(2)}) collective-permute-start(f32[2,768]{1,0:T(2,128)S(1)} %get-tuple-element.76.vec_ref), channel_id=1, source_target_pairs={{0,2},{2,0},{1,3},{3,1},{4,6},{6,4},{5,7},{7,5},{8,10},{10,8},{9,1... | collective-permute-start | bytes 18440 | tf_op jit(solution)/shard_map/ppermute | solution.py:338
  44.1 17.6 %collective-permute-start.10 = (bf16[200,768]{1,0:T(8,128)(2,1)S(1)}, bf16[200,768]{1,0:T(8,128)(2,1)S(1)}, u32[]{:S(2)}, u32[]{:S(2)}) collective-permute-start(bf16[200,768]{1,0:T(8,128)(2,1)S(1)} %get-tuple-element.78), channel_id=1, source_target_pairs={{0,1},{1,0},{4,5},{5,4},{2,3},{3,2},{6,7},{7,6},{8,9},{9,8},{12,13... | collective-permute-start | bytes 921608 | tf_op jit(solution)/shard_map/ppermute | solution.py:342
  46.6 15.1 %collective-permute-start.11 = (bf16[200,768]{1,0:T(8,128)(2,1)S(1)}, bf16[200,768]{1,0:T(8,128)(2,1)S(1)}, u32[]{:S(2)}, u32[]{:S(2)}) collective-permute-start(bf16[200,768]{1,0:T(8,128)(2,1)S(1)} %get-tuple-element.79), channel_id=1, source_target_pairs={{0,4},{1,5},{4,0},{5,1},{2,6},{3,7},{6,2},{7,3},{8,12},{9,13},{12,... | collective-permute-start | bytes 921608 | tf_op jit(solution)/shard_map/ppermute | solution.py:342
  47.7 13.9 %collective-permute-start.12 = (bf16[200,768]{1,0:T(8,128)(2,1)S(1)}, bf16[200,768]{1,0:T(8,128)(2,1)S(1)}, u32[]{:S(2)}, u32[]{:S(2)}) collective-permute-start(bf16[200,768]{1,0:T(8,128)(2,1)S(1)} %get-tuple-element.80), channel_id=1, source_target_pairs={{0,5},{1,4},{4,1},{5,0},{2,7},{3,6},{6,3},{7,2},{8,13},{9,12},{12,... | collective-permute-start | bytes 921608 | tf_op jit(solution)/shard_map/ppermute | solution.py:342
  58.9 9.2 %collective-permute-start.5 = (bf16[48,768]{1,0:T(8,128)(2,1)S(1)}, bf16[48,768]{1,0:T(8,128)(2,1)S(1)}, u32[]{:S(2)}, u32[]{:S(2)}) collective-permute-start(bf16[48,768]{1,0:T(8,128)(2,1)S(1)} %get-tuple-element.71), channel_id=1, source_target_pairs={{0,1},{1,0},{4,5},{5,4},{2,3},{3,2},{6,7},{7,6},{8,9},{9,8},{12,13... | collective-permute-start | bytes 221192 | tf_op jit(solution)/shard_map/ppermute | solution.py:342
  61.7 32.1 %copy-start.3 = (bf16[768,768]{1,0:T(8,128)(2,1)S(1)}, bf16[768,768]{1,0:T(8,128)(2,1)}, u32[]{:S(2)}) copy-start(bf16[768,768]{1,0:T(8,128)(2,1)} %wo_ref.1) | copy-start | bytes 3538948
  61.7 32.1 %copy-start.7 = (bf16[1,256,768]{2,1,0:T(8,128)(2,1)S(1)}, bf16[1,256,768]{2,1,0:T(8,128)(2,1)}, u32[]{:S(2)}) copy-start(bf16[1,256,768]{2,1,0:T(8,128)(2,1)} %param.6) | copy-start | bytes 1179652
  61.9 10.6 %collective-permute-start.13 = (bf16[56,768]{1,0:T(8,128)(2,1)S(1)}, bf16[56,768]{1,0:T(8,128)(2,1)S(1)}, u32[]{:S(2)}, u32[]{:S(2)}) collective-permute-start(bf16[56,768]{1,0:T(8,128)(2,1)S(1)} %get-tuple-element.82), channel_id=1, source_target_pairs={{0,64},{64,0},{128,192},{192,128},{1,65},{65,1},{129,193},{193,129... | collective-permute-start | bytes 258056 | tf_op jit(solution)/shard_map/ppermute | solution.py:342
  62.8 9.6 %collective-permute-start.14 = (bf16[56,768]{1,0:T(8,128)(2,1)S(1)}, bf16[56,768]{1,0:T(8,128)(2,1)S(1)}, u32[]{:S(2)}, u32[]{:S(2)}) collective-permute-start(bf16[56,768]{1,0:T(8,128)(2,1)S(1)} %get-tuple-element.83), channel_id=1, source_target_pairs={{0,128},{64,192},{128,0},{192,64},{1,129},{65,193},{129,1},{193,65... | collective-permute-start | bytes 258056 | tf_op jit(solution)/shard_map/ppermute | solution.py:342
  67.1 5.9 %collective-permute-start.15 = (bf16[56,768]{1,0:T(8,128)(2,1)S(1)}, bf16[56,768]{1,0:T(8,128)(2,1)S(1)}, u32[]{:S(2)}, u32[]{:S(2)}) collective-permute-start(bf16[56,768]{1,0:T(8,128)(2,1)S(1)} %get-tuple-element.84), channel_id=1, source_target_pairs={{0,192},{64,128},{128,64},{192,0},{1,193},{65,129},{129,65},{193,1... | collective-permute-start | bytes 258056 | tf_op jit(solution)/shard_map/ppermute | solution.py:342
  67.1 4.4 %collective-permute-start.6 = (bf16[48,768]{1,0:T(8,128)(2,1)S(1)}, bf16[48,768]{1,0:T(8,128)(2,1)S(1)}, u32[]{:S(2)}, u32[]{:S(2)}) collective-permute-start(bf16[48,768]{1,0:T(8,128)(2,1)S(1)} %get-tuple-element.72), channel_id=1, source_target_pairs={{0,4},{1,5},{4,0},{5,1},{2,6},{3,7},{6,2},{7,3},{8,12},{9,13},{12,... | collective-permute-start | bytes 221192 | tf_op jit(solution)/shard_map/ppermute | solution.py:342
  68.1 4.4 %collective-permute-start.7 = (bf16[48,768]{1,0:T(8,128)(2,1)S(1)}, bf16[48,768]{1,0:T(8,128)(2,1)S(1)}, u32[]{:S(2)}, u32[]{:S(2)}) collective-permute-start(bf16[48,768]{1,0:T(8,128)(2,1)S(1)} %get-tuple-element.73), channel_id=1, source_target_pairs={{0,5},{1,4},{4,1},{5,0},{2,7},{3,6},{6,3},{7,2},{8,13},{9,12},{12,... | collective-permute-start | bytes 221192 | tf_op jit(solution)/shard_map/ppermute | solution.py:342
  91.0 5.3 %collective-permute-start.16 = (bf16[8,1536]{1,0:T(8,128)(2,1)S(1)}, bf16[8,1536]{1,0:T(8,128)(2,1)S(1)}, u32[]{:S(2)}, u32[]{:S(2)}) collective-permute-start(bf16[8,1536]{1,0:T(8,128)(2,1)S(1)} %get-tuple-element.85.mine_ref), channel_id=1, source_target_pairs={{0,1},{1,0},{2,3},{3,2},{4,5},{5,4},{6,7},{7,6},{8,9},{9,8},{10,11... | collective-permute-start | bytes 73736 | tf_op jit(solution)/shard_map/ppermute | solution.py:367
  (5 other events, 4.6 us)

commit v3 on v2

--- a/solution.py
+++ b/solution.py
@@ -59,29 +59,34 @@
     return jnp.where(cols == feature, 1.0, 0.0).astype(BF)
 
 
-def own_kernel(at_ref, gain_ref, bias_ref, x_hbm, cot_hbm, w_hbm, wo_hbm,
+def own_kernel(at_ref, gain_hbm, bias_hbm, x_hbm, cot_hbm, w_hbm, wo_hbm,
                qkv_ref, dmix_ref, npt_ref, xhat_ref, rstd_ref, mt_ref,
-               x_ref, cot_ref, w_ref, wo_ref, sems):
-    copies = [pltpu.make_async_copy(x_hbm, x_ref, sems.at[0])]
+               gain_ref, bias_ref, x_ref, cot_ref, w_ref, wo_ref, sems):
+    copies = [
+        pltpu.make_async_copy(x_hbm, x_ref, sems.at[0]),
+        pltpu.make_async_copy(gain_hbm, gain_ref, sems.at[1]),
+        pltpu.make_async_copy(bias_hbm, bias_ref, sems.at[2]),
+        pltpu.make_async_copy(cot_hbm, cot_ref, sems.at[3]),
+        pltpu.make_async_copy(wo_hbm, wo_ref, sems.at[4]),
+    ]
     for i in range(3):
-        copies.append(pltpu.make_async_copy(w_hbm.at[:, pl.ds(D * i, D)], w_ref.at[i], sems.at[1 + i]))
-    copies.append(pltpu.make_async_copy(cot_hbm, cot_ref, sems.at[4]))
-    copies.append(pltpu.make_async_copy(wo_hbm, wo_ref, sems.at[5]))
+        copies.append(pltpu.make_async_copy(w_hbm.at[:, pl.ds(D * i, D)], w_ref.at[i], sems.at[5 + i]))
     for copy in copies:
         copy.start()
     mt = row_order(at_ref)
     mt_ref[...] = mt
-    copies[0].wait()
+    for copy in copies[:3]:
+        copy.wait()
     normed, xhat, rstd = layer_norm(x_ref, gain_ref[...].reshape(1, D), bias_ref[...].reshape(1, D))
     xhat_ref[...] = xhat
     rstd_ref[...] = jnp.broadcast_to(rstd, (T, 128))
     npt_ref[...] = nt(mt, normed).astype(BF)
+    copies[3].wait()
+    copies[4].wait()
+    dmix_ref[...] = nt(cot_ref[...], wo_ref[...]).astype(BF)
     for i in range(3):
-        copies[1 + i].wait()
+        copies[5 + i].wait()
         qkv_ref[:, D * i : D * i + D] = nn(normed, w_ref[i]).astype(BF)
-    copies[4].wait()
-    copies[5].wait()
-    dmix_ref[...] = nt(cot_ref[...], wo_ref[...]).astype(BF)
 
 
 def head_group(g, has, qkv_ref, kvm_ref, dmix_ref):
@@ -288,11 +293,12 @@
 
 VM = pl.BlockSpec(memory_space=pltpu.VMEM)
 SM = pl.BlockSpec(memory_space=pltpu.SMEM)
-ANY = pl.BlockSpec(memory_space=pl.ANY)
+HBM = pl.BlockSpec(memory_space=pltpu.MemorySpace.HBM)
 
 
 def call(kernel, name, out_shape, args, scalars=0, anys=(), scratch=(), limit=16):
-    specs = [SM if i < scalars else ANY if i in anys else VM for i in range(len(args))]
+    specs = [SM if i < scalars else HBM if i in anys else VM for i in range(len(args))]
+    args = [pltpu.with_memory_space_constraint(a, pltpu.MemorySpace.HBM) if i in anys else a for i, a in enumerate(args)]
     return pl.pallas_call(
         kernel,
         name=name,
@@ -315,12 +321,13 @@
     place = [lax.axis_index(n) for n in ("y", "xl", "c", "xh")] + [lax.axis_index(SEQ) > 0]
     at = jnp.stack([v.astype(jnp.int32) for v in place])
     row, mat, tokens = sds(T, D, dtype=F32), sds(D, D), sds(T, D)
+    one = pltpu.VMEM((D,), F32)
     qkv, dmix, npt, xhat, rstd, mt = call(
         own_kernel, "own_part",
         [sds(T, 3 * D), tokens, sds(D, T), row, sds(T, 128, dtype=F32), mat],
-        [at, gain, bias, x, cot, w, wo], 1, (3, 4, 5, 6),
-        [pltpu.VMEM((T, D), BF), pltpu.VMEM((T, D), BF), pltpu.VMEM((3, D, D), BF), pltpu.VMEM((D, D), BF),
-         pltpu.SemaphoreType.DMA((6,))],
+        [at, gain, bias, x, cot, w, wo], 1, (1, 2, 3, 4, 5, 6),
+        [one, one, pltpu.VMEM((T, D), BF), pltpu.VMEM((T, D), BF), pltpu.VMEM((3, D, D), BF), pltpu.VMEM((D, D), BF),
+         pltpu.SemaphoreType.DMA((8,))],
     )
     wide = sds(384, 1536)
     send_a, keep_a, mixt, dn, dnm, kvm, npt_all, xhatm = call(

time: 99.5 us -> 95.6 us (0.961)
  local copies, waits for them, and re-layouts: 6.75 us -> 0.11 us
  starting transfers between devices: 26.3 us -> 28.7 us
  waiting for transfers between devices: 15.8 us -> 18.2 us
  blocking collectives: 17.3 us -> 15.8 us
    unnamed x24 -> x12, local copies, waits for them, and re-layouts: 6.66 us -> 0.02 us
    ppermute x12, starting transfers between devices: 19.5 us -> 23.3 us  [exchange(): lax.ppermute(parts[k], axes, [(i, i ^ k) for i in range(n)])]
    ppermute x1, waiting for transfers between devices: 0.01 us -> 1.95 us  [on_device(): xp = lax.ppermute(x, SEQ, [(i, i + 1) for i in range(seq - 1)])]
    ppermute x3, starting transfers between devices: 2.2 us -> 0.69 us  [swap(): return lax.ppermute(block, 'c', [(0, 1), (1, 0)])]
    all_to_all x1, blocking collectives: 17.3 us -> 15.8 us  [on_device(): mine = lax.all_to_all(mine, 'z', 0, 0, tiled=True)]
  transfers between devices with their start and end apart: 17 -> 17, of which waited for: 8 -> 9; matrix products, arithmetic and copies ran while one was open for 0% -> 0% of each run, Pallas kernels for 16% -> 17%
where the time goes in v3:
time: 95.6 us; the launch traced here: 93.9 us
  Pallas kernels  30.4 us (32%)
  starting transfers between devices  28.7 us (30%)
  waiting for transfers between devices  18.2 us (19%)
  blocking collectives  15.8 us (17%)
    pallas_call x11, Pallas kernels, call(): pl.pallas_call(kernel, name=name, in_specs=specs, out_specs=[VM] * len(ou...  30.4 us
    ppermute x12, starting transfers between devices, exchange(): lax.ppermute(parts[k], axes, [(i, i ^ k) for i in range(n)])  23.3 us
    all_to_all x1, blocking collectives, on_device(): mine = lax.all_to_all(mine, 'z', 0, 0, tiled=True)  15.8 us
    ppermute x12, waiting for transfers between devices, exchange(): lax.ppermute(parts[k], axes, [(i, i ^ k) for i in range(n)])  14.3 us
    ppermute x1, starting transfers between devices, on_device(): other = lax.ppermute(mine, 'xh', [(0, 1), (1, 0)])  2.73 us
    ppermute x1, waiting for transfers between devices, on_device(): xp = lax.ppermute(x, SEQ, [(i, i + 1) for i in range(seq - 1)])  1.95 us
    ppermute x1, starting transfers between devices, on_device(): xp = lax.ppermute(x, SEQ, [(i, i + 1) for i in range(seq - 1)])  1.92 us
  transfers between devices with their start and end apart: 17, of which 9 were waited for; matrix products, arithmetic and copies ran while one was open for 0% of the time, Pallas kernels for 17%

profile of v3, /device:TPU:2, one launch (start us, length us, event | category | flops | bytes accessed | tf_op | source)
XLA Modules:
  0.0 93.9 jit_solution(17801331156050124185)
XLA Ops:
  0.6 1.9 %collective-permute-start = (bf16[256,768]{1,0:T(8,128)(2,1)}, bf16[256,768]{1,0:T(8,128)(2,1)S(1)}, u32[]{:S(2)}, u32[]{:S(2)}) collective-permute-start(bf16[256,768]{1,0:T(8,128)(2,1)} %bitcast.12), channel_id=1, source_target_pairs={{0,2},{2,4},{4,6},{6,8},{8,10},{10,12},{12,14},{14,16},{16,18},{18... | collective-permute-start | bytes 1179656 | tf_op jit(solution)/shard_map/ppermute | solution.py:320
  2.7 5.3 %own_part.1 = (bf16[256,2304]{1,0:T(8,128)(2,1)S(1)}, bf16[256,768]{1,0:T(8,128)(2,1)S(1)}, bf16[768,256]{1,0:T(8,128)(2,1)S(1)}, f32[256,768]{1,0:T(8,128)S(1)}...) custom-call(s32[5]{0:T(128)S(1)} %stack.27.at_ref, f32[768]{0:T(1024)} %gain_ref.3, f32[768]{0:T(1024)} %bias_ref.1, ...), custom_call_target="tpu_custom_call" | custom-call | tf_op jit(solution)/shard_map/own_part/pallas_call | solution.py:302
  8.0 1.9 %collective-permute-done.xp_ref = bf16[256,768]{1,0:T(8,128)(2,1)S(1)} collective-permute-done((bf16[256,768]{1,0:T(8,128)(2,1)}, bf16[256,768]{1,0:T(8,128)(2,1)S(1)}, u32[]{:S(2)}, u32[]{:S(2)}) %collective-permute-start) | collective-permute-done | bytes 393248 | tf_op jit(solution)/shard_map/ppermute | solution.py:320
  10.0 12.9 %memory_and_heads.1 = (bf16[384,1536]{1,0:T(8,128)(2,1)S(1)}, bf16[384,1536]{1,0:T(8,128)(2,1)S(1)}, bf16[512,256]{1,0:T(8,128)(2,1)S(1)}, f32[256,768]{1,0:T(8,...) custom-call(s32[5]{0:T(128)S(1)} %stack.27.at_ref, ...), custom_call_target="tpu_custom_call" | custom-call | tf_op jit(solution)/shard_map/memory_and_heads/pallas_call | solution.py:302
  23.0 7.6 %heads_and_output_weight.1 = (bf16[384,1536]{1,0:T(8,128)(2,1)S(1)}, bf16[384,1536]{1,0:T(8,128)(2,1)S(1)}, f32[2,768]{1,0:T(2,128)S(1)}, bf16[768,256]{1,0:T(8,128)(2,1)S(1)}, f32[256,768]{1,0:T(8,128)S(1)}) custom-call(s32[5]{0:T(128)S(1)} %stack.27.at_ref, bf16[768,2304]{1,0:T(8,128)(2,1)S(1)} %copy-done, bf16[768,768]{1,0:T(8,128)(2,1)S(1)} %get-tuple-element.48.mt_ref, ...), custom_call_target="tpu_custom_call" | custom-call | tf_op jit(solution)/shard_map/heads_and_output_weight/pallas_call | solution.py:302
  31.4 1.7 %collective-permute-start.2 = (bf16[96,1536]{1,0:T(8,128)(2,1)S(1)}, bf16[96,1536]{1,0:T(8,128)(2,1)S(1)}, u32[]{:S(2)}, u32[]{:S(2)}) collective-permute-start(bf16[96,1536]{1,0:T(8,128)(2,1)S(1)} %get-tuple-element.67), channel_id=1, source_target_pairs={{0,64},{64,0},{128,192},{192,128},{1,65},{65,1},{129,193},{193,129... | collective-permute-start | bytes 884744 | tf_op jit(solution)/shard_map/ppermute | solution.py:349
  33.1 2.9 %collective-permute-start.3 = (bf16[96,1536]{1,0:T(8,128)(2,1)S(1)}, bf16[96,1536]{1,0:T(8,128)(2,1)S(1)}, u32[]{:S(2)}, u32[]{:S(2)}) collective-permute-start(bf16[96,1536]{1,0:T(8,128)(2,1)S(1)} %get-tuple-element.68), channel_id=1, source_target_pairs={{0,128},{64,192},{128,0},{192,64},{1,129},{65,193},{129,1},{193,65... | collective-permute-start | bytes 884744 | tf_op jit(solution)/shard_map/ppermute | solution.py:349
  36.2 1.2 %collective-permute-done.9.vecr_ref = f32[2,768]{1,0:T(2,128)S(1)} collective-permute-done((f32[2,768]{1,0:T(2,128)S(1)}, f32[2,768]{1,0:T(2,128)S(1)}, u32[]{:S(2)}, u32[]{:S(2)}) %collective-permute-start.9) | collective-permute-done | bytes 6176 | tf_op jit(solution)/shard_map/ppermute | solution.py:345
  37.6 2.2 %collective-permute-start.10 = (bf16[200,768]{1,0:T(8,128)(2,1)S(1)}, bf16[200,768]{1,0:T(8,128)(2,1)S(1)}, u32[]{:S(2)}, u32[]{:S(2)}) collective-permute-start(bf16[200,768]{1,0:T(8,128)(2,1)S(1)} %get-tuple-element.78), channel_id=1, source_target_pairs={{0,1},{1,0},{4,5},{5,4},{2,3},{3,2},{6,7},{7,6},{8,9},{9,8},{12,13... | collective-permute-start | bytes 921608 | tf_op jit(solution)/shard_map/ppermute | solution.py:349
  39.9 5.6 %collective-permute-start.11 = (bf16[200,768]{1,0:T(8,128)(2,1)S(1)}, bf16[200,768]{1,0:T(8,128)(2,1)S(1)}, u32[]{:S(2)}, u32[]{:S(2)}) collective-permute-start(bf16[200,768]{1,0:T(8,128)(2,1)S(1)} %get-tuple-element.79), channel_id=1, source_target_pairs={{0,4},{1,5},{4,0},{5,1},{2,6},{3,7},{6,2},{7,3},{8,12},{9,13},{12,... | collective-permute-start | bytes 921608 | tf_op jit(solution)/shard_map/ppermute | solution.py:349
  45.4 1.0 %collective-permute-start.12 = (bf16[200,768]{1,0:T(8,128)(2,1)S(1)}, bf16[200,768]{1,0:T(8,128)(2,1)S(1)}, u32[]{:S(2)}, u32[]{:S(2)}) collective-permute-start(bf16[200,768]{1,0:T(8,128)(2,1)S(1)} %get-tuple-element.80), channel_id=1, source_target_pairs={{0,5},{1,4},{4,1},{5,0},{2,7},{3,6},{6,3},{7,2},{8,13},{9,12},{12,... | collective-permute-start | bytes 921608 | tf_op jit(solution)/shard_map/ppermute | solution.py:349
  46.4 2.9 %collective-permute-done.3.c = bf16[96,1536]{1,0:T(8,128)(2,1)S(1)} collective-permute-done((bf16[96,1536]{1,0:T(8,128)(2,1)S(1)}, bf16[96,1536]{1,0:T(8,128)(2,1)S(1)}, u32[]{:S(2)}, u32[]{:S(2)}) %collective-permute-start.3) | collective-permute-done | bytes 294944 | tf_op jit(solution)/shard_map/ppermute | solution.py:349
  49.4 2.6 %collective-permute-done.4.d = bf16[96,1536]{1,0:T(8,128)(2,1)S(1)} collective-permute-done((bf16[96,1536]{1,0:T(8,128)(2,1)S(1)}, bf16[96,1536]{1,0:T(8,128)(2,1)S(1)}, u32[]{:S(2)}, u32[]{:S(2)}) %collective-permute-start.4) | collective-permute-done | bytes 294944 | tf_op jit(solution)/shard_map/ppermute | solution.py:349
  52.1 2.7 %collective-permute-start.5 = (bf16[48,768]{1,0:T(8,128)(2,1)S(1)}, bf16[48,768]{1,0:T(8,128)(2,1)S(1)}, u32[]{:S(2)}, u32[]{:S(2)}) collective-permute-start(bf16[48,768]{1,0:T(8,128)(2,1)S(1)} %get-tuple-element.71), channel_id=1, source_target_pairs={{0,1},{1,0},{4,5},{5,4},{2,3},{3,2},{6,7},{7,6},{8,9},{9,8},{12,13... | collective-permute-start | bytes 221192 | tf_op jit(solution)/shard_map/ppermute | solution.py:349
  54.8 4.6 %collective-permute-done.11.c = bf16[200,768]{1,0:T(8,128)(2,1)S(1)} collective-permute-done((bf16[200,768]{1,0:T(8,128)(2,1)S(1)}, bf16[200,768]{1,0:T(8,128)(2,1)S(1)}, u32[]{:S(2)}, u32[]{:S(2)}) %collective-permute-start.11) | collective-permute-done | bytes 307232 | tf_op jit(solution)/shard_map/ppermute | solution.py:349
  59.6 1.1 %collective-permute-start.13 = (bf16[56,768]{1,0:T(8,128)(2,1)S(1)}, bf16[56,768]{1,0:T(8,128)(2,1)S(1)}, u32[]{:S(2)}, u32[]{:S(2)}) collective-permute-start(bf16[56,768]{1,0:T(8,128)(2,1)S(1)} %get-tuple-element.82), channel_id=1, source_target_pairs={{0,64},{64,0},{128,192},{192,128},{1,65},{65,1},{129,193},{193,129... | collective-permute-start | bytes 258056 | tf_op jit(solution)/shard_map/ppermute | solution.py:349
  60.7 4.4 %collective-permute-start.14 = (bf16[56,768]{1,0:T(8,128)(2,1)S(1)}, bf16[56,768]{1,0:T(8,128)(2,1)S(1)}, u32[]{:S(2)}, u32[]{:S(2)}) collective-permute-start(bf16[56,768]{1,0:T(8,128)(2,1)S(1)} %get-tuple-element.83), channel_id=1, source_target_pairs={{0,128},{64,192},{128,0},{192,64},{1,129},{65,193},{129,1},{193,65... | collective-permute-start | bytes 258056 | tf_op jit(solution)/shard_map/ppermute | solution.py:349
  65.8 0.7 collective-permute-start.7
  66.6 2.9 %collective-permute-done.6.a2 = bf16[48,768]{1,0:T(8,128)(2,1)S(1)} collective-permute-done((bf16[48,768]{1,0:T(8,128)(2,1)S(1)}, bf16[48,768]{1,0:T(8,128)(2,1)S(1)}, u32[]{:S(2)}, u32[]{:S(2)}) %collective-permute-start.6) | collective-permute-done | bytes 73760 | tf_op jit(solution)/shard_map/ppermute | solution.py:349
  71.0 15.8 %all_to_all.5.in_ref = bf16[8,8,1536]{2,1,0:T(8,128)(2,1)S(1)} all-to-all(bf16[8,8,1536]{2,1,0:T(8,128)(2,1)S(1)} %plane_sum.1), channel_id=1, replica_groups=mesh['y'=4,'z'=8,'xl'=2,'c'=2,'xh'=2] {'z'}, dimensions={0} | all-to-all | bytes 393216 | tf_op jit(solution)/shard_map/all_to_all | solution.py:368
  87.3 2.7 %collective-permute-start.16 = (bf16[8,1536]{1,0:T(8,128)(2,1)S(1)}, bf16[8,1536]{1,0:T(8,128)(2,1)S(1)}, u32[]{:S(2)}, u32[]{:S(2)}) collective-permute-start(bf16[8,1536]{1,0:T(8,128)(2,1)S(1)} %get-tuple-element.85.mine_ref), channel_id=1, source_target_pairs={{0,1},{1,0},{2,3},{3,2},{4,5},{5,4},{6,7},{7,6},{8,9},{9,8},{10,11... | collective-permute-start | bytes 73736 | tf_op jit(solution)/shard_map/ppermute | solution.py:374
  90.1 1.8 %token_outputs.1 = (bf16[256,768]{1,0:T(8,128)(2,1)}, bf16[256,768]{1,0:T(8,128)(2,1)}) custom-call(f32[768]{0:T(1024)S(1)} %copy-done.4, bf16[256,768]{1,0:T(8,128)(2,1)S(1)} %bitcast.14, bf16[256,768]{1,0:T(8,128)(2,1)S(1)} %bitcast.11, bf16[768,256]{1,0:T(8,128)(2,1)S(1)} %get-tuple-element.59.mixt_ref, bf16[768,768]{1,0:T(8,128)(2,1)S(1)} %copy-done.1, ...), custom_call_target="tpu_custom_call" | custom-call | tf_op jit(solution)/shard_map/token_outputs/pallas_call | solution.py:302
  91.9 0.8 collective-permute-done.16.other_ref
  92.7 1.2 %finish.1 = (f32[6,2304]{1,0:T(8,128)}, f32[6,768]{1,0:T(8,128)}) custom-call(s32[5]{0:T(128)S(1)} %stack.27.at_ref, bf16[8,1536]{1,0:T(8,128)(2,1)S(1)} %get-tuple-element.85.mine_ref, bf16[8,1536]{1,0:T(8,128)(2,1)S(1)} %collective-permute-done.16.other_ref), custom_call_target="tpu_custom_call" | custom-call | tf_op jit(solution)/shard_map/finish/pallas_call | solution.py:302
  (35 shorter events, 4.7 us)
Async XLA Ops:
  0.6 9.3 %collective-permute-start = (bf16[256,768]{1,0:T(8,128)(2,1)}, bf16[256,768]{1,0:T(8,128)(2,1)S(1)}, u32[]{:S(2)}, u32[]{:S(2)}) collective-permute-start(bf16[256,768]{1,0:T(8,128)(2,1)} %bitcast.12), channel_id=1, source_target_pairs={{0,2},{2,4},{4,6},{6,8},{8,10},{10,12},{12,14},{14,16},{16,18},{18... | collective-permute-start | bytes 1179656 | tf_op jit(solution)/shard_map/ppermute | solution.py:320
  2.7 7.3 %copy-start = (bf16[768,2304]{1,0:T(8,128)(2,1)S(1)}, bf16[768,2304]{1,0:T(8,128)(2,1)}, u32[]{:S(2)}) copy-start(bf16[768,2304]{1,0:T(8,128)(2,1)} %w_ref.3) | copy-start | bytes 10616836
  2.7 7.3 %copy-start.4 = (f32[768]{0:T(1024)S(1)}, f32[768]{0:T(1024)}, u32[]{:S(2)}) copy-start(f32[768]{0:T(1024)} %gain_ref.3) | copy-start | bytes 9220
  2.7 7.3 %copy-start.5 = (f32[768]{0:T(1024)S(1)}, f32[768]{0:T(1024)}, u32[]{:S(2)}) copy-start(f32[768]{0:T(1024)} %bias_ref.1) | copy-start | bytes 9220
  9.9 13.1 %copy-start.2 = (bf16[1,256,768]{2,1,0:T(8,128)(2,1)S(1)}, bf16[1,256,768]{2,1,0:T(8,128)(2,1)}, u32[]{:S(2)}) copy-start(bf16[1,256,768]{2,1,0:T(8,128)(2,1)} %param.7) | copy-start | bytes 1179652
  22.9 8.3 %collective-permute-start.1 = (bf16[384,1536]{1,0:T(8,128)(2,1)S(1)}, bf16[384,1536]{1,0:T(8,128)(2,1)S(1)}, u32[]{:S(2)}, u32[]{:S(2)}) collective-permute-start(bf16[384,1536]{1,0:T(8,128)(2,1)S(1)} %get-tuple-element.65), channel_id=1, source_target_pairs={{0,2},{2,0},{1,3},{3,1},{4,6},{6,4},{5,7},{7,5},{8,10},{10,8},{9,1... | collective-permute-start | bytes 3538952 | tf_op jit(solution)/shard_map/ppermute | solution.py:345
  30.6 6.8 %collective-permute-start.8 = (bf16[384,1536]{1,0:T(8,128)(2,1)S(1)}, bf16[384,1536]{1,0:T(8,128)(2,1)S(1)}, u32[]{:S(2)}, u32[]{:S(2)}) collective-permute-start(bf16[384,1536]{1,0:T(8,128)(2,1)S(1)} %get-tuple-element.75), channel_id=1, source_target_pairs={{0,2},{2,0},{1,3},{3,1},{4,6},{6,4},{5,7},{7,5},{8,10},{10,8},{9,1... | collective-permute-start | bytes 3538952 | tf_op jit(solution)/shard_map/ppermute | solution.py:345
  31.4 14.0 %collective-permute-start.2 = (bf16[96,1536]{1,0:T(8,128)(2,1)S(1)}, bf16[96,1536]{1,0:T(8,128)(2,1)S(1)}, u32[]{:S(2)}, u32[]{:S(2)}) collective-permute-start(bf16[96,1536]{1,0:T(8,128)(2,1)S(1)} %get-tuple-element.67), channel_id=1, source_target_pairs={{0,64},{64,0},{128,192},{192,128},{1,65},{65,1},{129,193},{193,129... | collective-permute-start | bytes 884744 | tf_op jit(solution)/shard_map/ppermute | solution.py:349
  33.1 16.3 %collective-permute-start.3 = (bf16[96,1536]{1,0:T(8,128)(2,1)S(1)}, bf16[96,1536]{1,0:T(8,128)(2,1)S(1)}, u32[]{:S(2)}, u32[]{:S(2)}) collective-permute-start(bf16[96,1536]{1,0:T(8,128)(2,1)S(1)} %get-tuple-element.68), channel_id=1, source_target_pairs={{0,128},{64,192},{128,0},{192,64},{1,129},{65,193},{129,1},{193,65... | collective-permute-start | bytes 884744 | tf_op jit(solution)/shard_map/ppermute | solution.py:349
  36.0 16.0 %collective-permute-start.4 = (bf16[96,1536]{1,0:T(8,128)(2,1)S(1)}, bf16[96,1536]{1,0:T(8,128)(2,1)S(1)}, u32[]{:S(2)}, u32[]{:S(2)}) collective-permute-start(bf16[96,1536]{1,0:T(8,128)(2,1)S(1)} %get-tuple-element.69), channel_id=1, source_target_pairs={{0,192},{64,128},{128,64},{192,0},{1,193},{65,129},{129,65},{193,1... | collective-permute-start | bytes 884744 | tf_op jit(solution)/shard_map/ppermute | solution.py:349
  36.2 1.2 %collective-permute-start.9 = (f32[2,768]{1,0:T(2,128)S(1)}, f32[2,768]{1,0:T(2,128)S(1)}, u32[]{:S(2)}, u32[]{:S(2)}) collective-permute-start(f32[2,768]{1,0:T(2,128)S(1)} %get-tuple-element.76.vec_ref), channel_id=1, source_target_pairs={{0,2},{2,0},{1,3},{3,1},{4,6},{6,4},{5,7},{7,5},{8,10},{10,8},{9,1... | collective-permute-start | bytes 18440 | tf_op jit(solution)/shard_map/ppermute | solution.py:345
  37.6 17.2 %collective-permute-start.10 = (bf16[200,768]{1,0:T(8,128)(2,1)S(1)}, bf16[200,768]{1,0:T(8,128)(2,1)S(1)}, u32[]{:S(2)}, u32[]{:S(2)}) collective-permute-start(bf16[200,768]{1,0:T(8,128)(2,1)S(1)} %get-tuple-element.78), channel_id=1, source_target_pairs={{0,1},{1,0},{4,5},{5,4},{2,3},{3,2},{6,7},{7,6},{8,9},{9,8},{12,13... | collective-permute-start | bytes 921608 | tf_op jit(solution)/shard_map/ppermute | solution.py:349
  39.9 19.5 %collective-permute-start.11 = (bf16[200,768]{1,0:T(8,128)(2,1)S(1)}, bf16[200,768]{1,0:T(8,128)(2,1)S(1)}, u32[]{:S(2)}, u32[]{:S(2)}) collective-permute-start(bf16[200,768]{1,0:T(8,128)(2,1)S(1)} %get-tuple-element.79), channel_id=1, source_target_pairs={{0,4},{1,5},{4,0},{5,1},{2,6},{3,7},{6,2},{7,3},{8,12},{9,13},{12,... | collective-permute-start | bytes 921608 | tf_op jit(solution)/shard_map/ppermute | solution.py:349
  45.4 13.9 %collective-permute-start.12 = (bf16[200,768]{1,0:T(8,128)(2,1)S(1)}, bf16[200,768]{1,0:T(8,128)(2,1)S(1)}, u32[]{:S(2)}, u32[]{:S(2)}) collective-permute-start(bf16[200,768]{1,0:T(8,128)(2,1)S(1)} %get-tuple-element.80), channel_id=1, source_target_pairs={{0,5},{1,4},{4,1},{5,0},{2,7},{3,6},{6,3},{7,2},{8,13},{9,12},{12,... | collective-permute-start | bytes 921608 | tf_op jit(solution)/shard_map/ppermute | solution.py:349
  52.1 13.8 %collective-permute-start.5 = (bf16[48,768]{1,0:T(8,128)(2,1)S(1)}, bf16[48,768]{1,0:T(8,128)(2,1)S(1)}, u32[]{:S(2)}, u32[]{:S(2)}) collective-permute-start(bf16[48,768]{1,0:T(8,128)(2,1)S(1)} %get-tuple-element.71), channel_id=1, source_target_pairs={{0,1},{1,0},{4,5},{5,4},{2,3},{3,2},{6,7},{7,6},{8,9},{9,8},{12,13... | collective-permute-start | bytes 221192 | tf_op jit(solution)/shard_map/ppermute | solution.py:349
  59.4 30.7 %copy-start.1 = (bf16[768,768]{1,0:T(8,128)(2,1)S(1)}, bf16[768,768]{1,0:T(8,128)(2,1)}, u32[]{:S(2)}) copy-start(bf16[768,768]{1,0:T(8,128)(2,1)} %wo_ref.1) | copy-start | bytes 3538948
  59.4 30.7 %copy-start.3 = (bf16[1,256,768]{2,1,0:T(8,128)(2,1)S(1)}, bf16[1,256,768]{2,1,0:T(8,128)(2,1)}, u32[]{:S(2)}) copy-start(bf16[1,256,768]{2,1,0:T(8,128)(2,1)} %param.6) | copy-start | bytes 1179652
  59.6 10.6 %collective-permute-start.13 = (bf16[56,768]{1,0:T(8,128)(2,1)S(1)}, bf16[56,768]{1,0:T(8,128)(2,1)S(1)}, u32[]{:S(2)}, u32[]{:S(2)}) collective-permute-start(bf16[56,768]{1,0:T(8,128)(2,1)S(1)} %get-tuple-element.82), channel_id=1, source_target_pairs={{0,64},{64,0},{128,192},{192,128},{1,65},{65,1},{129,193},{193,129... | collective-permute-start | bytes 258056 | tf_op jit(solution)/shard_map/ppermute | solution.py:349
  60.7 9.5 %collective-permute-start.14 = (bf16[56,768]{1,0:T(8,128)(2,1)S(1)}, bf16[56,768]{1,0:T(8,128)(2,1)S(1)}, u32[]{:S(2)}, u32[]{:S(2)}) collective-permute-start(bf16[56,768]{1,0:T(8,128)(2,1)S(1)} %get-tuple-element.83), channel_id=1, source_target_pairs={{0,128},{64,192},{128,0},{192,64},{1,129},{65,193},{129,1},{193,65... | collective-permute-start | bytes 258056 | tf_op jit(solution)/shard_map/ppermute | solution.py:349
  65.1 5.7 %collective-permute-start.15 = (bf16[56,768]{1,0:T(8,128)(2,1)S(1)}, bf16[56,768]{1,0:T(8,128)(2,1)S(1)}, u32[]{:S(2)}, u32[]{:S(2)}) collective-permute-start(bf16[56,768]{1,0:T(8,128)(2,1)S(1)} %get-tuple-element.84), channel_id=1, source_target_pairs={{0,192},{64,128},{128,64},{192,0},{1,193},{65,129},{129,65},{193,1... | collective-permute-start | bytes 258056 | tf_op jit(solution)/shard_map/ppermute | solution.py:349
  65.1 4.4 %collective-permute-start.6 = (bf16[48,768]{1,0:T(8,128)(2,1)S(1)}, bf16[48,768]{1,0:T(8,128)(2,1)S(1)}, u32[]{:S(2)}, u32[]{:S(2)}) collective-permute-start(bf16[48,768]{1,0:T(8,128)(2,1)S(1)} %get-tuple-element.72), channel_id=1, source_target_pairs={{0,4},{1,5},{4,0},{5,1},{2,6},{3,7},{6,2},{7,3},{8,12},{9,13},{12,... | collective-permute-start | bytes 221192 | tf_op jit(solution)/shard_map/ppermute | solution.py:349
  65.8 4.4 %collective-permute-start.7 = (bf16[48,768]{1,0:T(8,128)(2,1)S(1)}, bf16[48,768]{1,0:T(8,128)(2,1)S(1)}, u32[]{:S(2)}, u32[]{:S(2)}) collective-permute-start(bf16[48,768]{1,0:T(8,128)(2,1)S(1)} %get-tuple-element.73), channel_id=1, source_target_pairs={{0,5},{1,4},{4,1},{5,0},{2,7},{3,6},{6,3},{7,2},{8,13},{9,12},{12,... | collective-permute-start | bytes 221192 | tf_op jit(solution)/shard_map/ppermute | solution.py:349
  87.3 5.3 %collective-permute-start.16 = (bf16[8,1536]{1,0:T(8,128)(2,1)S(1)}, bf16[8,1536]{1,0:T(8,128)(2,1)S(1)}, u32[]{:S(2)}, u32[]{:S(2)}) collective-permute-start(bf16[8,1536]{1,0:T(8,128)(2,1)S(1)} %get-tuple-element.85.mine_ref), channel_id=1, source_target_pairs={{0,1},{1,0},{2,3},{3,2},{4,5},{5,4},{6,7},{7,6},{8,9},{9,8},{10,11... | collective-permute-start | bytes 73736 | tf_op jit(solution)/shard_map/ppermute | solution.py:374

commit v4 on v3

v4 whole, which is shorter than its diff:
```python
import functools

import jax
import jax.numpy as jnp
from jax import lax
from jax.experimental import pallas as pl
from jax.experimental.pallas import tpu as pltpu
from jax.sharding import Mesh
from jax.sharding import PartitionSpec as P

HEADS = 12
EPS = 1e-05
SEQ = ("y", "z", "xl", "c")
PLANE = ("y", "xl", "xh")
T = 256
D = 768
GROUPS = 3
GW = 256
BF = jnp.bfloat16
F32 = jnp.float32
LIMIT = 32


def nn(a, b):
    return lax.dot_general(a, b, (((1,), (0,)), ((), ())), preferred_element_type=F32)


def nt(a, b):
    return lax.dot_general(a, b, (((1,), (1,)), ((), ())), preferred_element_type=F32)


def eye(n):
    rows = lax.broadcasted_iota(jnp.int32, (n, n), 0)
    cols = lax.broadcasted_iota(jnp.int32, (n, n), 1)
    return jnp.where(rows == cols, 1.0, 0.0).astype(BF)


def layer_norm(x_ref, gain, bias):
    values = x_ref[...].astype(F32)
    centered = values - jnp.mean(values, axis=-1, keepdims=True)
    rstd = lax.rsqrt(jnp.mean(centered * centered, axis=-1, keepdims=True) + EPS)
    xhat = centered * rstd
    normed = (xhat * gain + bias).astype(BF)
    return normed, xhat, rstd


def row_order(at_ref):
    p = lax.broadcasted_iota(jnp.int32, (D, 1), 0)
    second = jnp.where(p >= 384, 1, 0)
    q = p - 384 * second
    owner = (q * 171) >> 13
    b = q - 48 * owner
    z = (b * 43) >> 8
    j = b - 6 * z
    y, xl = owner >> 1, owner & 1
    to_core = jnp.where(second == 1, at_ref[0], 1 - at_ref[0])
    feature = ((y * 8 + z) * 2 + xl) * 12 + to_core * 6 + j
    cols = lax.broadcasted_iota(jnp.int32, (D, D), 1)
    return jnp.where(cols == feature, 1.0, 0.0).astype(BF)


def own_kernel(at_ref, gain_hbm, bias_hbm, x_hbm, cot_hbm, w_hbm, wo_hbm,
               qkv_ref, dmix_ref, npt_ref, mt_ref, xhat_hbm, rstd_hbm,
               gain_ref, bias_ref, x_ref, cot_ref, w_ref, wo_ref, xhat_ref, rstd_ref, sems):
    copies = [
        pltpu.make_async_copy(x_hbm, x_ref, sems.at[0]),
        pltpu.make_async_copy(gain_hbm, gain_ref, sems.at[1]),
        pltpu.make_async_copy(bias_hbm, bias_ref, sems.at[2]),
        pltpu.make_async_copy(cot_hbm, cot_ref, sems.at[3]),
        pltpu.make_async_copy(wo_hbm, wo_ref, sems.at[4]),
    ]
    for i in range(3):
        copies.append(pltpu.make_async_copy(w_hbm.at[:, pl.ds(D * i, D)], w_ref.at[i], sems.at[5 + i]))
    for copy in copies:
        copy.start()
    mt = row_order(at_ref)
    mt_ref[...] = mt
    for copy in copies[:3]:
        copy.wait()
    normed, xhat, rstd = layer_norm(x_ref, gain_ref[...].reshape(1, D), bias_ref[...].reshape(1, D))
    xhat_ref[...] = xhat
    rstd_ref[...] = jnp.broadcast_to(rstd, (T, 128))
    stores = [
        pltpu.make_async_copy(xhat_ref, xhat_hbm, sems.at[8]),
        pltpu.make_async_copy(rstd_ref, rstd_hbm, sems.at[9]),
    ]
    for copy in stores:
        copy.start()
    npt_ref[...] = nt(mt, normed).astype(BF)
    copies[3].wait()
    copies[4].wait()
    dmix_ref[...] = nt(cot_ref[...], wo_ref[...]).astype(BF)
    for i in range(3):
        copies[5 + i].wait()
        qkv_ref[:, D * i : D * i + D] = nn(normed, w_ref[i]).astype(BF)
    for copy in stores:
        copy.wait()


def qkv_slices(qkv_ref, kvm_ref, dmix_ref, g):
    tiles = []
    for pair in range(2):
        at = GW * g + 128 * pair
        q, k, v = (slice(D * i + at, D * i + at + 128) for i in range(3))
        tiles.append((qkv_ref[:, q], qkv_ref[:, k], qkv_ref[:, v], kvm_ref[:, q], kvm_ref[:, k], dmix_ref[:, q]))
    return tiles


def head_group(tiles, has):
    lanes = lax.broadcasted_iota(jnp.int32, (T, 128), 1)
    low = lanes < 64
    causal = lax.broadcasted_iota(jnp.int32, (T, T), 0) <= lax.broadcasted_iota(jnp.int32, (T, T), 1)
    unit = eye(128)
    unit2 = eye(T)
    zero = jnp.zeros((), BF)
    mixts, dqs, dks, dvs = [], [], [], []
    for q2, k2, v2, km2, vm2, dm2 in tiles:
        q2 = (q2.astype(F32) * 0.125).astype(BF)
        k2 = jnp.concatenate([k2, km2], axis=0)
        v2 = jnp.concatenate([v2, vm2], axis=0)
        kt2 = nt(unit, k2).astype(BF)
        vt2 = nt(unit, v2).astype(BF)
        ds_parts, p_parts, q_parts, dm_parts, dqt_parts = [], [], [], [], []
        for half in range(2):
            pick = low if half == 0 else jnp.logical_not(low)
            qa = jnp.where(pick, q2, zero)
            dma = jnp.where(pick, dm2, zero)
            st = nt(k2, qa)
            st_own = jnp.where(causal, st[:T], -1e30)
            st_mem = jnp.where(has, st[T:], -1e30)
            st = jnp.concatenate([st_own, st_mem], axis=0)
            top = jnp.max(st, axis=0, keepdims=True)
            e = jnp.exp(st - top)
            p = e * (1.0 / jnp.sum(e, axis=0, keepdims=True))
            pb = p.astype(BF)
            rows = slice(64 * half, 64 * half + 64)
            mixts.append(nn(vt2[rows], pb).astype(BF))
            dp = nt(v2, dma)
            ds = (p * (dp - jnp.sum(dp * p, axis=0, keepdims=True))).astype(BF)
            dqt_parts.append((nn(kt2[rows], ds) * 0.125).astype(BF))
            ds_parts.append(ds)
            p_parts.append(pb)
            q_parts.append(qa)
            dm_parts.append(dma)
        dks.append(nn(jnp.concatenate(ds_parts, axis=1), jnp.concatenate(q_parts, axis=0)).astype(BF))
        dvs.append(nn(jnp.concatenate(p_parts, axis=1), jnp.concatenate(dm_parts, axis=0)).astype(BF))
        dqs.append(nt(unit2, jnp.concatenate(dqt_parts, axis=0)).astype(BF))
    dq = jnp.concatenate(dqs, axis=1)
    dk = jnp.concatenate(dks, axis=1)
    dv = jnp.concatenate(dvs, axis=1)
    return jnp.concatenate(mixts, axis=0), dq, dk, dv


def put_rows(send_ref, keep_ref, slot, lhs, rhs):
    for h in range(2):
        part = rhs[:, 384 * h : 384 * h + 384]
        for k, out_ref in enumerate((send_ref, keep_ref)):
            rows = nn(lhs[384 * k : 384 * k + 384], part).astype(BF)
            for i in range(8):
                out_ref[2 * i + h, :, 384 * slot : 384 * slot + 384] = rows[48 * i : 48 * i + 48]


def put_group(slot, npt_all, grads, send_ref, keep_ref):
    dq, dk, dv = grads
    rhs = jnp.concatenate([jnp.concatenate([dq, jnp.zeros((T, GW), BF)], axis=0), dk, dv], axis=1)
    put_rows(send_ref, keep_ref, slot, npt_all, rhs)


def d_normed(wq, wk, wv, dq, dk, dv):
    own = nt(dq, wq) + nt(dk[:T], wk) + nt(dv[:T], wv)
    mem = nt(dk[T:], wk) + nt(dv[T:], wv)
    return own, mem


def first_kernel(at_ref, gain_ref, bias_ref, xp_ref, w_ref, mt_ref, qkv_ref, dmix_ref, npt_ref,
                 send_ref, keep_ref, dq_ref, dkv_ref, mixt_hbm, kvm_hbm, npt_hbm, xhatm_hbm,
                 mixt_ref, kvm_ref, npt_all_ref, xhatm_ref, sems):
    normed, xhat, _ = layer_norm(xp_ref, gain_ref[...].reshape(1, D), bias_ref[...].reshape(1, D))
    kvm_ref[...] = nn(normed, w_ref[:, D:]).astype(BF)
    xhatm_ref[...] = xhat
    npt_all_ref[:, :T] = npt_ref[...]
    npt_all_ref[:, T:] = nt(mt_ref[...], normed).astype(BF)
    copies = [
        pltpu.make_async_copy(kvm_ref, kvm_hbm, sems.at[0]),
        pltpu.make_async_copy(npt_all_ref, npt_hbm, sems.at[1]),
        pltpu.make_async_copy(xhatm_ref, xhatm_hbm, sems.at[2]),
    ]
    for copy in copies:
        copy.start()
    has = at_ref[2] > 0
    npt_all = npt_all_ref[...]
    for g in range(2):
        mixt, dq, dk, dv = head_group(qkv_slices(qkv_ref, kvm_ref, dmix_ref, g), has)
        mixt_ref[GW * g : GW * g + GW, :] = mixt
        if g == 1:
            copies.append(pltpu.make_async_copy(mixt_ref, mixt_hbm, sems.at[3]))
            copies[3].start()
        dq_ref[:, GW * g : GW * g + GW] = dq
        dkv_ref[:, GW * g : GW * g + GW] = dk
        dkv_ref[:, GW * (g + 2) : GW * (g + 2) + GW] = dv
        put_group(g, npt_all, (dq, dk, dv), send_ref, keep_ref)
    for copy in copies:
        copy.wait()


def d_normed_kernel(w_ref, dq_ref, dkv_ref, dn_hbm, dnm_hbm, dn_ref, dnm_ref, sems):
    own, mem = None, None
    for g in range(2):
        cols, vcols = slice(GW * g, GW * g + GW), slice(GW * (g + 2), GW * (g + 2) + GW)
        wq, wk, wv = (w_ref[:, D * i + GW * g : D * i + GW * g + GW] for i in range(3))
        a, b = d_normed(wq, wk, wv, dq_ref[:, cols], dkv_ref[:, cols], dkv_ref[:, vcols])
        own, mem = (a, b) if own is None else (own + a, mem + b)
    dn_ref[...] = own
    dnm_ref[...] = mem
    copies = [pltpu.make_async_copy(dn_ref, dn_hbm, sems.at[0]), pltpu.make_async_copy(dnm_ref, dnm_hbm, sems.at[1])]
    for copy in copies:
        copy.start()
    for copy in copies:
        copy.wait()


def second_kernel(at_ref, qkv_hbm, kvm_hbm, dmix_hbm, npt_hbm, mt_hbm, mixt_hbm, cot_hbm, w_hbm, dn_hbm, dnm_hbm,
                  xhat_hbm, xhatm_hbm, send_ref, keep_ref, vec_ref, mixt_ref, dn_ref,
                  q_ref, k_ref, v_ref, km_ref, vm_ref, dm_ref, npt_ref, mt_ref, cot_ref, wq_ref, wk_ref, wv_ref,
                  dnin_ref, dnmin_ref, xhat_ref, xhatm_ref, sems):
    last = 2 * GW
    col = lambda ref, i: ref.at[:, pl.ds(D * i + last, GW)]
    pairs = [
        (col(qkv_hbm, 0), q_ref), (col(qkv_hbm, 1), k_ref), (col(qkv_hbm, 2), v_ref),
        (col(kvm_hbm, 0), km_ref), (col(kvm_hbm, 1), vm_ref), (col(dmix_hbm, 0), dm_ref),
        (npt_hbm, npt_ref), (mt_hbm, mt_ref), (mixt_hbm, mixt_ref.at[pl.ds(0, last), :]), (cot_hbm, cot_ref),
        (col(w_hbm, 0), wq_ref), (col(w_hbm, 1), wk_ref), (col(w_hbm, 2), wv_ref),
        (dn_hbm, dnin_ref), (dnm_hbm, dnmin_ref), (xhat_hbm, xhat_ref), (xhatm_hbm, xhatm_ref),
    ]
    copies = [pltpu.make_async_copy(src, dst, sems.at[i]) for i, (src, dst) in enumerate(pairs)]
    for copy in copies:
        copy.start()
    for copy in copies[:6]:
        copy.wait()
    tiles = [tuple(ref[:, 128 * i : 128 * i + 128] for ref in (q_ref, k_ref, v_ref, km_ref, vm_ref, dm_ref)) for i in range(2)]
    mixt, *grads = head_group(tiles, at_ref[2] > 0)
    mixt_ref[last:, :] = mixt
    copies[6].wait()
    put_group(0, npt_ref[...], grads, send_ref, keep_ref)
    for copy in copies[7:10]:
        copy.wait()
    lhs = nn(mt_ref[...], mixt_ref[...]).astype(BF)
    put_rows(send_ref, keep_ref, 1, lhs, cot_ref[...])
    for copy in copies[10:]:
        copy.wait()
    own, mem = d_normed(wq_ref[...], wk_ref[...], wv_ref[...], *grads)
    dn, dnm = dnin_ref[...] + own, dnmin_ref[...] + mem
    dn_ref[...] = dn
    vec_ref[0:1, :] = jnp.sum(dn * xhat_ref[...] + dnm * xhatm_ref[...], axis=0, keepdims=True)
    vec_ref[1:2, :] = jnp.sum(dn + dnm, axis=0, keepdims=True)


def token_kernel(gain_ref, x_ref, cot_ref, mixt_ref, wo_ref, dn_ref, xhat_ref, rstd_ref, out_ref, dx_ref):
    mixed = nt(eye(T), mixt_ref[...]).astype(BF)
    out_ref[...] = (x_ref[...].astype(F32) + nn(mixed, wo_ref[...])).astype(BF)
    d_hat = dn_ref[...] * gain_ref[...].reshape(1, D)
    xhat = xhat_ref[...]
    row = rstd_ref[:, 0:1] * (
        d_hat
        - jnp.mean(d_hat, axis=-1, keepdims=True)
        - xhat * jnp.mean(d_hat * xhat, axis=-1, keepdims=True)
    )
    dx_ref[...] = (cot_ref[...].astype(F32) + row).astype(BF)


def split_rows(value):
    high = value.astype(BF)
    low = (value - high.astype(F32)).astype(BF)
    return jnp.concatenate([high, low, jnp.zeros((4, value.shape[1]), BF)], axis=0)


def join_rows(rows):
    return rows[0:2].astype(F32) + rows[2:4].astype(F32)


def pair_a_kernel(keep_ref, recv_ref, out_ref):
    out_ref[...] = (keep_ref[...].astype(F32) + recv_ref[...].astype(F32)).astype(BF)


def pair_b_kernel(keep_ref, recv_ref, vec_ref, vecr_ref, out_ref):
    vec = split_rows(vec_ref[...] + vecr_ref[...])
    out_ref[:, 0:48, :] = (keep_ref[...].astype(F32) + recv_ref[...].astype(F32)).astype(BF)
    for i in range(16):
        out_ref[i, 48:56, :] = vec


def plane_kernel(a_hbm, b_ref, out_ref, a_ref, sem):
    load = pltpu.make_async_copy(a_hbm, a_ref, sem)
    load.start()
    vec = join_rows(b_ref[0, 48:56, :])
    for i in range(1, 16):
        vec = vec + join_rows(b_ref[i, 48:56, :])
    vec = jnp.concatenate([vec[0:1], vec[1:2]], axis=1)
    high = vec.astype(BF).astype(F32)
    tail = jnp.concatenate([high, vec - high], axis=0)
    acc = b_ref[0, 0:48, :].astype(F32)
    for i in range(1, 16):
        acc = acc + b_ref[i, 0:48, :].astype(F32)
    load.wait()
    for k, half in enumerate((a_ref[0].astype(F32), acc)):
        cols = slice(768 * k, 768 * k + 768)
        for z in range(8):
            out_ref[z, :, cols] = jnp.concatenate([half[6 * z : 6 * z + 6], tail[:, cols]], axis=0).astype(BF)


def column_kernel(factor, in_ref, rows_ref, gain_ref, bias_ref):
    acc = in_ref[0].astype(F32)
    for z in range(1, 8):
        acc = acc + in_ref[z].astype(F32)
    rows_ref[...] = acc.astype(BF)
    vec = (acc[6:7] + acc[7:8]) * factor
    gain_ref[...] = vec[:, :D].reshape(D)
    bias_ref[...] = vec[:, D:].reshape(D)


def finish_kernel(factor, at_ref, mine_ref, other_ref, qkv_ref, wout_ref):
    mine, other = mine_ref[...].astype(F32) * factor, other_ref[...].astype(F32) * factor
    first = at_ref[1] == 0
    halves = [jnp.where(first, mine, other), jnp.where(first, other, mine)]
    for g in range(GROUPS + 1):
        cols = slice(384 * g, 384 * g + 384)
        full = jnp.concatenate([halves[0][0:6, cols], halves[1][0:6, cols]], axis=1)
        if g < GROUPS:
            for i in range(3):
                at = D * i + GW * g
                qkv_ref[:, at : at + GW] = full[:, GW * i : GW * i + GW]
        else:
            wout_ref[...] = full


VM = pl.BlockSpec(memory_space=pltpu.VMEM)
SM = pl.BlockSpec(memory_space=pltpu.SMEM)
HBM = pl.BlockSpec(memory_space=pltpu.MemorySpace.HBM)


def call(kernel, name, out_shape, args, scalars=0, hbm=(), hbm_outs=(), scratch=(), limit=16):
    args = [pltpu.with_memory_space_constraint(a, pltpu.MemorySpace.HBM) if i in hbm else a for i, a in enumerate(args)]
    return pl.pallas_call(
        kernel,
        name=name,
        in_specs=[SM if i < scalars else HBM if i in hbm else VM for i in range(len(args))],
        out_specs=[HBM if i in hbm_outs else VM for i in range(len(out_shape))],
        out_shape=[pltpu.MemorySpace.HBM(o.shape, o.dtype) if i in hbm_outs else o for i, o in enumerate(out_shape)],
        scratch_shapes=scratch,
        compiler_params=pltpu.CompilerParams(vmem_limit_bytes=limit * 1024 * 1024),
    )(*args)


def vmem(*shape, dtype=BF):
    return pltpu.VMEM(shape, dtype)


def dmas(n):
    return pltpu.SemaphoreType.DMA((n,))


def sds(*shape, dtype=BF):
    return jax.ShapeDtypeStruct(shape, dtype)


def on_device(layer_input, cotangent, gain, bias, w, wo):
    x, cot = layer_input[0], cotangent[0]
    seq = lax.axis_size(SEQ)
    xp = lax.ppermute(x, SEQ, [(i, i + 1) for i in range(seq - 1)])
    place = [lax.axis_index("c"), lax.axis_index("xh"), lax.axis_index(SEQ) > 0]
    at = jnp.stack([v.astype(jnp.int32) for v in place])
    row, mat, tokens = sds(T, D, dtype=F32), sds(D, D), sds(T, D)
    one, tile, mat_v, row_v = vmem(D, dtype=F32), vmem(T, GW), vmem(D, D), vmem(T, D, dtype=F32)
    qkv, dmix, npt, mt, xhat, rstd = call(
        own_kernel, "own_part",
        [sds(T, 3 * D), tokens, sds(D, T), mat, row, sds(T, 128, dtype=F32)],
        [at, gain, bias, x, cot, w, wo], 1, range(1, 7), (4, 5),
        [one, one, vmem(T, D), vmem(T, D), vmem(3, D, D), mat_v, row_v, vmem(T, 128, dtype=F32), dmas(10)],
    )
    wide = sds(16, 48, 768)
    send_a, keep_a, dq, dkv, mixt, kvm, npt_all, xhatm = call(
        first_kernel, "memory_and_heads",
        [wide, wide, sds(T, 2 * GW), sds(2 * T, 4 * GW), sds(2 * GW, T), sds(T, 2 * D), sds(D, 2 * T), row],
        [at, gain, bias, xp, w, mt, qkv, dmix, npt], 1, hbm_outs=range(4, 8),
        scratch=[vmem(2 * GW, T), vmem(T, 2 * D), vmem(D, 2 * T), row_v, dmas(4)], limit=LIMIT,
    )

    def swap(block):
        return lax.ppermute(block, "c", [(0, 1), (1, 0)])

    def spread(block):
        return lax.all_to_all(block, PLANE, 0, 0, tiled=True)

    dn, dnm = call(
        d_normed_kernel, "d_normed", [row, row], [w, dq, dkv], hbm_outs=(0, 1), scratch=[row_v, row_v, dmas(2)],
    )
    (parts_a,) = call(pair_a_kernel, "pair_sum_a", [wide], [keep_a, swap(send_a)])
    parts_a, kvm, dn, dnm = lax.optimization_barrier((parts_a, kvm, dn, dnm))
    parts_a = lax.psum_scatter(parts_a, "y", scatter_dimension=0, tiled=True)
    parts_a = lax.psum_scatter(parts_a, ("xl", "xh"), scatter_dimension=0, tiled=True)
    send_b, keep_b, vec, mixt, dn = call(
        second_kernel, "heads_and_output_weight",
        [wide, wide, sds(2, D, dtype=F32), sds(D, T), row],
        [at, qkv, kvm, dmix, npt_all, mt, mixt, cot, w, dn, dnm, xhat, xhatm], 1, range(1, 13),
        scratch=[tile] * 6 + [vmem(D, 2 * T), mat_v, vmem(T, D)] + [vmem(D, GW)] * 3 + [row_v] * 4 + [dmas(17)], limit=LIMIT,
    )
    (parts_b,) = call(pair_b_kernel, "pair_sum_b", [sds(16, 56, 768)], [keep_b, swap(send_b), vec, swap(vec)])
    out, dx = call(
        token_kernel, "token_outputs", [tokens, tokens],
        [gain, x, cot, mixt, wo, dn, xhat, rstd],
    )
    parts_b, out, dx = lax.optimization_barrier((parts_b, out, dx))
    parts_b = spread(parts_b)
    (mine,) = call(plane_kernel, "plane_sum", [sds(8, 8, 1536)], [parts_a, parts_b], hbm=(0,), scratch=[vmem(1, 48, 768), pltpu.SemaphoreType.DMA])
    mine = lax.all_to_all(mine, "z", 0, 0, tiled=True)
    factor = 1.0 / float(seq * lax.axis_size("xh") * T) ** 0.5
    mine, grad_gain, grad_bias = call(
        functools.partial(column_kernel, factor), "column_sum",
        [sds(8, 1536), sds(D, dtype=F32), sds(D, dtype=F32)], [mine],
    )
    other = lax.ppermute(mine, "xh", [(0, 1), (1, 0)])
    grad_qkv, grad_out = call(
        functools.partial(finish_kernel, factor), "finish",
        [sds(6, 3 * D, dtype=F32), sds(6, D, dtype=F32)], [at, mine, other], 1,
    )
    return out[None], dx[None], grad_qkv, grad_out, grad_gain, grad_bias


def solution(mesh):
    torus = Mesh(mesh.devices.reshape(4, 8, 2, 2, 2), ("y", "z", "xl", "c", "xh"))
    return jax.shard_map(
        on_device,
        mesh=torus,
        in_specs=(P("xh", SEQ, None), P("xh", SEQ, None), P(), P(), P(), P()),
        out_specs=(P("xh", SEQ, None), P("xh", SEQ, None), P(SEQ, None), P(SEQ, None), P(), P()),
        check_vma=False,
    )
```

time: 95.6 us -> 138 us (1.44)
  waiting for transfers between devices: 18.2 us -> 52.6 us
  between operations: 0.72 us -> 14.2 us
  starting transfers between devices: 28.7 us -> 15.6 us
  Pallas kernels: 30.4 us -> 37.7 us
    reduce_scatter x0 -> x2, waiting for transfers between devices: none -> 45.5 us  [the longest x1 25.9 us: on_device(): lax.psum_scatter(parts_a, ('xl', 'xh'), scatter_dimension=0, tiled=True)]
    ppermute x12 -> x0, starting transfers between devices: 23.3 us -> none  [exchange(): lax.ppermute(parts[k], axes, [(i, i ^ k) for i in range(n)])]
    ppermute x12 -> x0, waiting for transfers between devices: 14.3 us -> none  [exchange(): lax.ppermute(parts[k], axes, [(i, i ^ k) for i in range(n)])]
    all_to_all x0 -> x1, starting transfers between devices: none -> 11.7 us  [spread(): return lax.all_to_all(block, PLANE, 0, 0, tiled=True)]
    pallas_call x11 -> x10, Pallas kernels: 30.4 us -> 37.7 us  [call(): pl.pallas_call(kernel, name=name, in_specs=[SM if i < scalars else HBM if...]
    ppermute x1, waiting for transfers between devices: 0.8 us -> 4.55 us  [on_device(): other = lax.ppermute(mine, 'xh', [(0, 1), (1, 0)])]
    ppermute x1, starting transfers between devices: 2.73 us -> 0.78 us  [on_device(): other = lax.ppermute(mine, 'xh', [(0, 1), (1, 0)])]
  transfers between devices with their start and end apart: 17 -> 8, of which waited for: 9 -> 5; matrix products, arithmetic and copies ran while one was open for 0% -> 0% of each run, Pallas kernels for 17% -> 15%
where the time goes in v4:
time: 138 us; the launch traced here: 137 us
  waiting for transfers between devices  52.6 us (38%)
  Pallas kernels  37.7 us (27%)
  blocking collectives  16.6 us (12%)
  starting transfers between devices  15.6 us (11%)
  between operations  14.2 us (10%)
    pallas_call x10, Pallas kernels, call(): pl.pallas_call(kernel, name=name, in_specs=[SM if i < scalars else HBM if...  37.7 us
    reduce_scatter x1, waiting for transfers between devices, on_device(): lax.psum_scatter(parts_a, ('xl', 'xh'), scatter_dimension=0, tiled=True)  25.9 us
    reduce_scatter x1, waiting for transfers between devices, on_device(): parts_a = lax.psum_scatter(parts_a, 'y', scatter_dimension=0, tiled=True)  19.6 us
    all_to_all x1, blocking collectives, on_device(): mine = lax.all_to_all(mine, 'z', 0, 0, tiled=True)  16.6 us
    all_to_all x1, starting transfers between devices, spread(): return lax.all_to_all(block, PLANE, 0, 0, tiled=True)  11.7 us
    ppermute x1, waiting for transfers between devices, on_device(): other = lax.ppermute(mine, 'xh', [(0, 1), (1, 0)])  4.55 us
  transfers between devices with their start and end apart: 8, of which 5 were waited for; matrix products, arithmetic and copies ran while one was open for 0% of the time, Pallas kernels for 15%

profile of v4, /device:TPU:2, one launch (start us, length us, event | category | flops | bytes accessed | tf_op | source)
XLA Modules:
  0.0 136.9 jit_solution(9542113584943175623)
XLA Ops:
  7.2 1.9 %collective-permute-start = (bf16[256,768]{1,0:T(8,128)(2,1)}, bf16[256,768]{1,0:T(8,128)(2,1)}, u32[]{:S(2)}, u32[]{:S(2)}) collective-permute-start(bf16[256,768]{1,0:T(8,128)(2,1)} %bitcast.10), channel_id=1, source_target_pairs={{0,2},{2,4},{4,6},{6,8},{8,10},{10,12},{12,14},{14,16},{16,18},{18... | collective-permute-start | bytes 1179656 | tf_op jit(solution)/shard_map/ppermute | solution.py:369
  9.2 0.1 pad_add_fusion.at_ref
  9.2 5.3 %own_part.1 = (bf16[256,2304]{1,0:T(8,128)(2,1)S(1)}, bf16[256,768]{1,0:T(8,128)(2,1)S(1)}, bf16[768,256]{1,0:T(8,128)(2,1)S(1)}, bf16[768,768]{1,0:T(8,128)(2,1...) custom-call(s32[3]{0:T(128)S(1)} %pad_add_fusion.at_ref, f32[768]{0:T(1024)} %gain_ref.3, f32[768]{0:T(1024)} %bias_ref.1, ...), custom_call_target="tpu_custom_call" | custom-call | tf_op jit(solution)/shard_map/own_part/pallas_call | solution.py:343
  14.6 2.0 %collective-permute-done.xp_ref = bf16[256,768]{1,0:T(8,128)(2,1)} collective-permute-done((bf16[256,768]{1,0:T(8,128)(2,1)}, bf16[256,768]{1,0:T(8,128)(2,1)}, u32[]{:S(2)}, u32[]{:S(2)}) %collective-permute-start) | collective-permute-done | bytes 393248 | tf_op jit(solution)/shard_map/ppermute | solution.py:369
  16.6 12.8 %memory_and_heads.1 = (bf16[16,48,768]{2,1,0:T(8,128)(2,1)S(1)}, bf16[16,48,768]{2,1,0:T(8,128)(2,1)S(1)}, bf16[256,512]{1,0:T(8,128)(2,1)S(1)}, bf16[512,1024]{...) custom-call(s32[3]{0:T(128)S(1)} %pad_add_fusion.at_ref, ...), custom_call_target="tpu_custom_call" | custom-call | tf_op jit(solution)/shard_map/memory_and_heads/pallas_call | solution.py:343
  29.4 0.6 collective-permute-start.1
  30.0 2.5 %d_normed.1 = (f32[256,768]{1,0:T(8,128)}, f32[256,768]{1,0:T(8,128)}) custom-call(bf16[768,2304]{1,0:T(8,128)(2,1)S(1)} %copy-done, bf16[256,512]{1,0:T(8,128)(2,1)S(1)} %get-tuple-element.48.dq_ref, bf16[512,1024]{1,0:T(8,128)(2,1)S(1)} %get-tuple-element.49.dkv_ref), custom_call_target="tpu_custom_call" | custom-call | tf_op jit(solution)/shard_map/d_normed/pallas_call | solution.py:343
  32.5 0.0 collective-permute-done.1.recv_ref
  32.5 1.3 pair_sum_a.1
  34.0 9.9 %heads_and_output_weight.1 = (bf16[16,48,768]{2,1,0:T(8,128)(2,1)S(1)}, bf16[16,48,768]{2,1,0:T(8,128)(2,1)S(1)}, f32[2,768]{1,0:T(2,128)S(1)}, bf16[768,256]{1,0:T(8,128)(2,1)S(1)}, f32[256,768]{1,0:T(8,128)S(1)}) custom-call(s32[3]{0:T(128)S(1)} %pad_add_fusion.at_ref, bf16[256,2304]{1,0:T(8,128)(2,1)} %copy-done.1, ...), custom_call_target="tpu_custom_call" | custom-call | tf_op jit(solution)/shard_map/heads_and_output_weight/pallas_call | solution.py:343
  43.8 0.4 collective-permute-start.2
  44.2 0.2 collective-permute-start.3
  44.5 1.8 %token_outputs.1 = (bf16[256,768]{1,0:T(8,128)(2,1)}, bf16[256,768]{1,0:T(8,128)(2,1)}) custom-call(f32[768]{0:T(1024)S(1)} %copy-done.9, bf16[256,768]{1,0:T(8,128)(2,1)S(1)} %bitcast.12, bf16[256,768]{1,0:T(8,128)(2,1)S(1)} %bitcast.9, bf16[768,256]{1,0:T(8,128)(2,1)S(1)} %get-tuple-element.62.mixt_ref, bf16[768,768]{1,0:T(8,128)(2,1)S(1)} %copy-done.3, ...), custom_call_target="tpu_custom_call" | custom-call | tf_op jit(solution)/shard_map/token_outputs/pallas_call | solution.py:343
  46.3 0.5 collective-permute-done.3.vecr_ref
  46.8 1.4 %pair_sum_b.1 = bf16[16,56,768]{2,1,0:T(8,128)(2,1)} custom-call(bf16[16,48,768]{2,1,0:T(8,128)(2,1)S(1)} %get-tuple-element.59.keep_ref, bf16[16,48,768]{2,1,0:T(8,128)(2,1)S(1)} %collective-permute-done.2.recv_ref, f32[2,768]{1,0:T(2,128)S(1)} %get-tuple-element.61.vec_ref, f32[2,768]{1,0:T(2,128)S(1)} %collective-permute-done.3.vecr_ref), custom_call_target="tpu_custom_call" | custom-call | tf_op jit(solution)/shard_map/pair_sum_b/pallas_call | solution.py:343
  48.2 11.7 %all-to-all-start = ((bf16[16,56,768]{2,1,0:T(8,128)(2,1)}), bf16[16,56,768]{2,1,0:T(8,128)(2,1)S(1)}, u32[]{:S(2)}, u32[]{:S(2)}) async-start(bf16[16,56,768]{2,1,0:T(8,128)(2,1)} %pair_sum_b.1), calls=%async_computation.2 | async-start | bytes 2752512 | tf_op jit(solution)/shard_map/all_to_all | solution.py:392
  59.9 19.6 %reduce-scatter.3.cloned.1.call-done = bf16[4,48,768]{2,1,0:T(8,128)(2,1)} async-done(((bf16[16,48,768]{2,1,0:T(8,128)(2,1)}), bf16[4,48,768]{2,1,0:T(8,128)(2,1)}) %reduce-scatter.3.cloned.1.call-update) | async-done | bytes 294928 | tf_op jit(solution)/shard_map/reduce_scatter | solution.py:399
  79.5 25.9 %reduce-scatter.5.cloned.1.call-done.a_hbm = bf16[1,48,768]{2,1,0:T(8,128)(2,1)} async-done(((bf16[4,48,768]{2,1,0:T(8,128)(2,1)}), bf16[1,48,768]{2,1,0:T(8,128)(2,1)}) %reduce-scatter.5.cloned.1.call-update) | async-done | bytes 73744 | tf_op jit(solution)/shard_map/reduce_scatter | solution.py:400
  105.4 0.9 plane_sum.1
  106.3 16.6 %all_to_all.10.in_ref = bf16[8,8,1536]{2,1,0:T(8,128)(2,1)S(1)} all-to-all(bf16[8,8,1536]{2,1,0:T(8,128)(2,1)S(1)} %plane_sum.1), channel_id=1, replica_groups=mesh['y'=4,'z'=8,'xl'=2,'c'=2,'xh'=2] {'z'}, dimensions={0} | all-to-all | bytes 393216 | tf_op jit(solution)/shard_map/all_to_all | solution.py:415
  122.9 0.6 column_sum.1
  123.5 0.8 collective-permute-start.4
  124.3 4.6 %collective-permute-done.4.other_ref = bf16[8,1536]{1,0:T(8,128)(2,1)S(1)} collective-permute-done((bf16[8,1536]{1,0:T(8,128)(2,1)S(1)}, bf16[8,1536]{1,0:T(8,128)(2,1)S(1)}, u32[]{:S(2)}, u32[]{:S(2)}) %collective-permute-start.4) | collective-permute-done | bytes 24608 | tf_op jit(solution)/shard_map/ppermute | solution.py:421
  128.9 1.2 finish.1
  (28 shorter events, 0.2 us)
Async XLA Ops:
  7.2 72.3 %reduce-scatter.3.cloned.1.call-start = ((), (), s32[]{:S(2)}) async-start(), calls=%async_computation.4 | async-start | bytes 1474560 | tf_op jit(solution)/shard_map/reduce_scatter | solution.py:399
  7.2 9.4 %collective-permute-start = (bf16[256,768]{1,0:T(8,128)(2,1)}, bf16[256,768]{1,0:T(8,128)(2,1)}, u32[]{:S(2)}, u32[]{:S(2)}) collective-permute-start(bf16[256,768]{1,0:T(8,128)(2,1)} %bitcast.10), channel_id=1, source_target_pairs={{0,2},{2,4},{4,6},{6,8},{8,10},{10,12},{12,14},{14,16},{16,18},{18... | collective-permute-start | bytes 1179656 | tf_op jit(solution)/shard_map/ppermute | solution.py:369
  9.2 7.4 %copy-start = (bf16[768,2304]{1,0:T(8,128)(2,1)S(1)}, bf16[768,2304]{1,0:T(8,128)(2,1)}, u32[]{:S(2)}) copy-start(bf16[768,2304]{1,0:T(8,128)(2,1)} %w_hbm.3) | copy-start | bytes 10616836
  9.2 7.4 %copy-start.9 = (f32[768]{0:T(1024)S(1)}, f32[768]{0:T(1024)}, u32[]{:S(2)}) copy-start(f32[768]{0:T(1024)} %gain_ref.3) | copy-start | bytes 9220
  9.2 7.4 %copy-start.10 = (f32[768]{0:T(1024)S(1)}, f32[768]{0:T(1024)}, u32[]{:S(2)}) copy-start(f32[768]{0:T(1024)} %bias_ref.1) | copy-start | bytes 9220
  14.6 14.8 %copy-start.1 = (bf16[256,2304]{1,0:T(8,128)(2,1)}, bf16[256,2304]{1,0:T(8,128)(2,1)S(1)}, u32[]{:S(2)}) copy-start(bf16[256,2304]{1,0:T(8,128)(2,1)S(1)} %get-tuple-element.41.qkv_ref.qkv_hbm) | copy-start | bytes 3538948
  14.6 14.8 %copy-start.2 = (bf16[768,768]{1,0:T(8,128)(2,1)}, bf16[768,768]{1,0:T(8,128)(2,1)S(1)}, u32[]{:S(2)}) copy-start(bf16[768,768]{1,0:T(8,128)(2,1)S(1)} %get-tuple-element.42.mt_ref.mt_hbm) | copy-start | bytes 3538948
  14.6 14.8 %copy-start.6 = (bf16[256,768]{1,0:T(8,128)(2,1)}, bf16[256,768]{1,0:T(8,128)(2,1)S(1)}, u32[]{:S(2)}) copy-start(bf16[256,768]{1,0:T(8,128)(2,1)S(1)} %get-tuple-element.43.dmix_ref.dmix_hbm) | copy-start | bytes 1179652
  29.4 3.1 %collective-permute-start.1 = (bf16[16,48,768]{2,1,0:T(8,128)(2,1)S(1)}, bf16[16,48,768]{2,1,0:T(8,128)(2,1)S(1)}, u32[]{:S(2)}, u32[]{:S(2)}) collective-permute-start(bf16[16,48,768]{2,1,0:T(8,128)(2,1)S(1)} %get-tuple-element.46), channel_id=1, source_target_pairs={{0,2},{2,0},{1,3},{3,1},{4,6},{6,4},{5,7},{7,5},{8,10},{10,8},{9,1... | collective-permute-start | bytes 3538952 | tf_op jit(solution)/shard_map/ppermute | solution.py:389
  33.9 10.5 %copy-start.3 = (bf16[768,768]{1,0:T(8,128)(2,1)S(1)}, bf16[768,768]{1,0:T(8,128)(2,1)}, u32[]{:S(2)}) copy-start(bf16[768,768]{1,0:T(8,128)(2,1)} %wo_ref.1) | copy-start | bytes 3538948
  33.9 10.5 %copy-start.4 = (bf16[1,256,768]{2,1,0:T(8,128)(2,1)S(1)}, bf16[1,256,768]{2,1,0:T(8,128)(2,1)}, u32[]{:S(2)}) copy-start(bf16[1,256,768]{2,1,0:T(8,128)(2,1)} %param.7) | copy-start | bytes 1179652
  33.9 10.5 %copy-start.5 = (f32[256,768]{1,0:T(8,128)S(1)}, f32[256,768]{1,0:T(8,128)}, u32[]{:S(2)}) copy-start(f32[256,768]{1,0:T(8,128)} %get-tuple-element.57.xhat_hbm.xhat_ref) | copy-start | bytes 2359300
  33.9 10.5 %copy-start.7 = (bf16[1,256,768]{2,1,0:T(8,128)(2,1)S(1)}, bf16[1,256,768]{2,1,0:T(8,128)(2,1)}, u32[]{:S(2)}) copy-start(bf16[1,256,768]{2,1,0:T(8,128)(2,1)} %param.6) | copy-start | bytes 1179652
  33.9 10.5 %copy-start.8 = (f32[256,128]{1,0:T(8,128)S(1)}, f32[256,128]{1,0:T(8,128)}, u32[]{:S(2)}) copy-start(f32[256,128]{1,0:T(8,128)} %get-tuple-element.64.rstd_ref) | copy-start | bytes 393220
  43.8 2.9 %collective-permute-start.2 = (bf16[16,48,768]{2,1,0:T(8,128)(2,1)S(1)}, bf16[16,48,768]{2,1,0:T(8,128)(2,1)S(1)}, u32[]{:S(2)}, u32[]{:S(2)}) collective-permute-start(bf16[16,48,768]{2,1,0:T(8,128)(2,1)S(1)} %get-tuple-element.60), channel_id=1, source_target_pairs={{0,2},{2,0},{1,3},{3,1},{4,6},{6,4},{5,7},{7,5},{8,10},{10,8},{9,1... | collective-permute-start | bytes 3538952 | tf_op jit(solution)/shard_map/ppermute | solution.py:389
  44.2 2.5 %collective-permute-start.3 = (f32[2,768]{1,0:T(2,128)S(1)}, f32[2,768]{1,0:T(2,128)S(1)}, u32[]{:S(2)}, u32[]{:S(2)}) collective-permute-start(f32[2,768]{1,0:T(2,128)S(1)} %get-tuple-element.61.vec_ref), channel_id=1, source_target_pairs={{0,2},{2,0},{1,3},{3,1},{4,6},{6,4},{5,7},{7,5},{8,10},{10,8},{9,1... | collective-permute-start | bytes 18440 | tf_op jit(solution)/shard_map/ppermute | solution.py:389
  48.2 31.3 %all-to-all-start = ((bf16[16,56,768]{2,1,0:T(8,128)(2,1)}), bf16[16,56,768]{2,1,0:T(8,128)(2,1)S(1)}, u32[]{:S(2)}, u32[]{:S(2)}) async-start(bf16[16,56,768]{2,1,0:T(8,128)(2,1)} %pair_sum_b.1), calls=%async_computation.2 | async-start | bytes 2752512 | tf_op jit(solution)/shard_map/all_to_all | solution.py:392
  59.8 45.6 %reduce-scatter.5.cloned.1.call-start = ((), (), s32[]{:S(2)}) async-start(), calls=%async_computation.5 | async-start | bytes 368640 | tf_op jit(solution)/shard_map/reduce_scatter | solution.py:400
  123.5 5.3 %collective-permute-start.4 = (bf16[8,1536]{1,0:T(8,128)(2,1)S(1)}, bf16[8,1536]{1,0:T(8,128)(2,1)S(1)}, u32[]{:S(2)}, u32[]{:S(2)}) collective-permute-start(bf16[8,1536]{1,0:T(8,128)(2,1)S(1)} %get-tuple-element.71.mine_ref), channel_id=1, source_target_pairs={{0,1},{1,0},{2,3},{3,2},{4,5},{5,4},{6,7},{7,6},{8,9},{9,8},{10,11... | collective-permute-start | bytes 73736 | tf_op jit(solution)/shard_map/ppermute | solution.py:421
Sparse Core Ops, SparseCore 0:
  34.0 45.4 reduce-scatter.2
  82.0 23.3 reduce-scatter.4

commit v5 on v3

--- a/solution.py
+++ b/solution.py
@@ -29,10 +29,8 @@
     return lax.dot_general(a, b, (((1,), (1,)), ((), ())), preferred_element_type=F32)
 
 
-def eye(n):
-    rows = lax.broadcasted_iota(jnp.int32, (n, n), 0)
-    cols = lax.broadcasted_iota(jnp.int32, (n, n), 1)
-    return jnp.where(rows == cols, 1.0, 0.0).astype(BF)
+def tn(a, b):
+    return lax.dot_general(a, b, (((0,), (0,)), ((), ())), preferred_element_type=F32)
 
 
 def layer_norm(x_ref, gain, bias):
@@ -60,8 +58,8 @@
 
 
 def own_kernel(at_ref, gain_hbm, bias_hbm, x_hbm, cot_hbm, w_hbm, wo_hbm,
-               qkv_ref, dmix_ref, npt_ref, xhat_ref, rstd_ref, mt_ref,
-               gain_ref, bias_ref, x_ref, cot_ref, w_ref, wo_ref, sems):
+               qkv_ref, dmix_ref, npt_ref, xhat_ref, rstd_ref, mt_ref, gain_ref, bias_ref, cot_ref, w_ref,
+               x_ref, wo_ref, sems):
     copies = [
         pltpu.make_async_copy(x_hbm, x_ref, sems.at[0]),
         pltpu.make_async_copy(gain_hbm, gain_ref, sems.at[1]),
@@ -94,10 +92,9 @@
     lanes = lax.broadcasted_iota(jnp.int32, (T, 128), 1)
     low = lanes < 64
     causal = lax.broadcasted_iota(jnp.int32, (T, T), 0) <= lax.broadcasted_iota(jnp.int32, (T, T), 1)
-    unit = eye(128)
-    unit2 = eye(T)
+    low_keys = lax.broadcasted_iota(jnp.int32, (2 * T, 128), 1) < 64
     zero = jnp.zeros((), BF)
-    mixts, dqs, dks, dvs = [], [], [], []
+    mixes, dqs, dks, dvs = [], [], [], []
     for pair in range(2):
         cq = slice(at + 128 * pair, at + 128 * pair + 128)
         ck = slice(D + cq.start, D + cq.stop)
@@ -106,9 +103,9 @@
         k2 = jnp.concatenate([qkv_ref[:, ck], kvm_ref[:, cq]], axis=0)
         v2 = jnp.concatenate([qkv_ref[:, cv], kvm_ref[:, ck]], axis=0)
         dm2 = dmix_ref[:, cq]
-        kt2 = nt(unit, k2).astype(BF)
-        vt2 = nt(unit, v2).astype(BF)
-        ds_parts, p_parts, q_parts, dm_parts, dqt_parts = [], [], [], [], []
+        k_parts = [jnp.where(low_keys, k2, zero), jnp.where(low_keys, zero, k2)]
+        v_parts = [jnp.where(low_keys, v2, zero), jnp.where(low_keys, zero, v2)]
+        ds_parts, p_parts, q_parts, dm_parts = [], [], [], []
         for half in range(2):
             pick = low if half == 0 else jnp.logical_not(low)
             qa = jnp.where(pick, q2, zero)
@@ -121,22 +118,20 @@
             e = jnp.exp(st - top)
             p = e * (1.0 / jnp.sum(e, axis=0, keepdims=True))
             pb = p.astype(BF)
-            rows = slice(64 * half, 64 * half + 64)
-            mixts.append(nn(vt2[rows], pb).astype(BF))
             dp = nt(v2, dma)
             ds = (p * (dp - jnp.sum(dp * p, axis=0, keepdims=True))).astype(BF)
-            dqt_parts.append((nn(kt2[rows], ds) * 0.125).astype(BF))
             ds_parts.append(ds)
             p_parts.append(pb)
             q_parts.append(qa)
             dm_parts.append(dma)
         dks.append(nn(jnp.concatenate(ds_parts, axis=1), jnp.concatenate(q_parts, axis=0)).astype(BF))
         dvs.append(nn(jnp.concatenate(p_parts, axis=1), jnp.concatenate(dm_parts, axis=0)).astype(BF))
-        dqs.append(nt(unit2, jnp.concatenate(dqt_parts, axis=0)).astype(BF))
+        mixes.append(tn(jnp.concatenate(p_parts, axis=0), jnp.concatenate(v_parts, axis=0)).astype(BF))
+        dqs.append((tn(jnp.concatenate(ds_parts, axis=0), jnp.concatenate(k_parts, axis=0)) * 0.125).astype(BF))
     dq = jnp.concatenate(dqs, axis=1)
     dk = jnp.concatenate(dks, axis=1)
     dv = jnp.concatenate(dvs, axis=1)
-    return jnp.concatenate(mixts, axis=0), dq, dk, dv
+    return jnp.concatenate(mixes, axis=1), dq, dk, dv
 
 
 def put_rows(send_ref, keep_ref, slot, xh, lhs, rhs):
@@ -153,24 +148,25 @@
     dq, dk, dv = grads
     rhs = jnp.concatenate([jnp.concatenate([dq, jnp.zeros((T, GW), BF)], axis=0), dk, dv], axis=1)
     put_rows(send_ref, keep_ref, slot, at_ref[3], npt_all, rhs)
-    wq, wk, wv = (w_ref[:, D * i + GW * g : D * i + GW * g + GW] for i in range(3))
+    wq, wk, wv = (w_ref[i, :, GW * g : GW * g + GW] for i in range(3))
     own = nt(dq, wq) + nt(dk[:T], wk) + nt(dv[:T], wv)
     mem = nt(dk[T:], wk) + nt(dv[T:], wv)
     return own, mem
 
 
 def first_kernel(at_ref, gain_ref, bias_ref, xp_ref, w_ref, mt_ref, qkv_ref, dmix_ref, npt_ref,
-                 send_ref, keep_ref, mixt_ref, dn_ref, dnm_ref, kvm_ref, npt_all_ref, xhatm_ref):
+                 send_ref, keep_ref, mixed_ref, dn_ref, dnm_ref, kvm_ref, npt_all_ref, xhatm_ref):
     normed, xhat, _ = layer_norm(xp_ref, gain_ref[...].reshape(1, D), bias_ref[...].reshape(1, D))
-    kvm_ref[...] = nn(normed, w_ref[:, D:]).astype(BF)
+    for i in range(2):
+        kvm_ref[:, D * i : D * i + D] = nn(normed, w_ref[1 + i]).astype(BF)
     xhatm_ref[...] = xhat
     npt_all_ref[:, :T] = npt_ref[...]
     npt_all_ref[:, T:] = nt(mt_ref[...], normed).astype(BF)
     has = at_ref[4] > 0
     npt_all = npt_all_ref[...]
     for g in range(2):
-        mixt, *grads = head_group(g, has, qkv_ref, kvm_ref, dmix_ref)
-        mixt_ref[GW * g : GW * g + GW, :] = mixt
+        mixed, *grads = head_group(g, has, qkv_ref, kvm_ref, dmix_ref)
+        mixed_ref[:, GW * g : GW * g + GW] = mixed
         own, mem = group_outputs(g, g, at_ref, npt_all, w_ref, grads, send_ref, keep_ref)
         if g == 0:
             dn_ref[...] = own
@@ -180,13 +176,13 @@
             dnm_ref[...] += mem
 
 
-def second_kernel(at_ref, w_ref, mt_ref, cot_ref, qkv_ref, dmix_ref, mixt_in, dn_in, dnm_in, kvm_ref, npt_all_ref,
-                  xhat_ref, xhatm_ref, send_ref, keep_ref, vec_ref, mixt_ref, dn_ref):
-    mixt, *grads = head_group(2, at_ref[4] > 0, qkv_ref, kvm_ref, dmix_ref)
-    mixt_ref[: 2 * GW, :] = mixt_in[...]
-    mixt_ref[2 * GW :, :] = mixt
+def second_kernel(at_ref, w_ref, mt_ref, cot_ref, qkv_ref, dmix_ref, mixed_in, dn_in, dnm_in, kvm_ref, npt_all_ref,
+                  xhat_ref, xhatm_ref, send_ref, keep_ref, vec_ref, mixed_ref, dn_ref):
+    mixed, *grads = head_group(2, at_ref[4] > 0, qkv_ref, kvm_ref, dmix_ref)
+    mixed_ref[:, : 2 * GW] = mixed_in[...]
+    mixed_ref[:, 2 * GW :] = mixed
     own, mem = group_outputs(2, 0, at_ref, npt_all_ref[...], w_ref, grads, send_ref, keep_ref)
-    lhs = nn(mt_ref[...], mixt_ref[...]).astype(BF)
+    lhs = nt(mt_ref[...], mixed_ref[...]).astype(BF)
     put_rows(send_ref, keep_ref, 1, at_ref[3], lhs, cot_ref[...])
     dn, dnm = dn_in[...] + own, dnm_in[...] + mem
     dn_ref[...] = dn
@@ -194,9 +190,8 @@
     vec_ref[1:2, :] = jnp.sum(dn + dnm, axis=0, keepdims=True)
 
 
-def token_kernel(gain_ref, x_ref, cot_ref, mixt_ref, wo_ref, dn_ref, xhat_ref, rstd_ref, out_ref, dx_ref):
-    mixed = nt(eye(T), mixt_ref[...]).astype(BF)
-    out_ref[...] = (x_ref[...].astype(F32) + nn(mixed, wo_ref[...])).astype(BF)
+def token_kernel(gain_ref, x_ref, cot_ref, mixed_ref, wo_ref, dn_ref, xhat_ref, rstd_ref, out_ref, dx_ref):
+    out_ref[...] = (x_ref[...].astype(F32) + nn(mixed_ref[...], wo_ref[...])).astype(BF)
     d_hat = dn_ref[...] * gain_ref[...].reshape(1, D)
     xhat = xhat_ref[...]
     row = rstd_ref[:, 0:1] * (
@@ -321,24 +316,23 @@
     place = [lax.axis_index(n) for n in ("y", "xl", "c", "xh")] + [lax.axis_index(SEQ) > 0]
     at = jnp.stack([v.astype(jnp.int32) for v in place])
     row, mat, tokens = sds(T, D, dtype=F32), sds(D, D), sds(T, D)
-    one = pltpu.VMEM((D,), F32)
-    qkv, dmix, npt, xhat, rstd, mt = call(
+    one = sds(D, dtype=F32)
+    qkv, dmix, npt, xhat, rstd, mt, gain_v, bias_v, cot_v, w = call(
         own_kernel, "own_part",
-        [sds(T, 3 * D), tokens, sds(D, T), row, sds(T, 128, dtype=F32), mat],
+        [sds(T, 3 * D), tokens, sds(D, T), row, sds(T, 128, dtype=F32), mat, one, one, tokens, sds(3, D, D)],
         [at, gain, bias, x, cot, w, wo], 1, (1, 2, 3, 4, 5, 6),
-        [one, one, pltpu.VMEM((T, D), BF), pltpu.VMEM((T, D), BF), pltpu.VMEM((3, D, D), BF), pltpu.VMEM((D, D), BF),
-         pltpu.SemaphoreType.DMA((8,))],
+        [pltpu.VMEM((T, D), BF), pltpu.VMEM((D, D), BF), pltpu.SemaphoreType.DMA((8,))],
     )
     wide = sds(384, 1536)
-    send_a, keep_a, mixt, dn, dnm, kvm, npt_all, xhatm = call(
+    send_a, keep_a, mixed, dn, dnm, kvm, npt_all, xhatm = call(
         first_kernel, "memory_and_heads",
-        [wide, wide, sds(2 * GW, T), row, row, sds(T, 2 * D), sds(D, 2 * T), row],
-        [at, gain, bias, xp, w, mt, qkv, dmix, npt], 1, limit=LIMIT,
-    )
-    send_b, keep_b, vec, mixt, dn = call(
+        [wide, wide, sds(T, 2 * GW), row, row, sds(T, 2 * D), sds(D, 2 * T), row],
+        [at, gain_v, bias_v, xp, w, mt, qkv, dmix, npt], 1, limit=LIMIT,
+    )
+    send_b, keep_b, vec, mixed, dn = call(
         second_kernel, "heads_and_output_weight",
-        [wide, wide, sds(2, D, dtype=F32), sds(D, T), row],
-        [at, w, mt, cot, qkv, dmix, mixt, dn, dnm, kvm, npt_all, xhat, xhatm], 1, limit=LIMIT,
+        [wide, wide, sds(2, D, dtype=F32), tokens, row],
+        [at, w, mt, cot_v, qkv, dmix, mixed, dn, dnm, kvm, npt_all, xhat, xhatm], 1, limit=LIMIT,
     )
 
     def swap(block):
@@ -358,7 +352,7 @@
     parts_b = ordered(exchange(parts_b, ROW))
     out, dx = call(
         token_kernel, "token_outputs", [tokens, tokens],
-        [gain, x, cot, mixt, wo, dn, xhat, rstd],
+        [gain, x, cot, mixed, wo, dn, xhat, rstd],
     )
     parts_a = call(mid_a_kernel, "middle_sum_a", [sds(48, 768)] * 4, parts_a)
     parts_b = call(mid_b_kernel, "middle_sum_b", [sds(56, 768)] * 4, parts_b)

time: 95.6 us -> 90.4 us (0.946)
  Pallas kernels: 30.4 us -> 24.6 us
  waiting for transfers between devices: 18.2 us -> 19.3 us
    pallas_call x11, Pallas kernels: 30.4 us -> 24.6 us  [call(): pl.pallas_call(kernel, name=name, in_specs=specs, out_specs=[VM] * len(ou...]
  transfers between devices with their start and end apart: 17 -> 17, of which waited for: 9 -> 9; matrix products, arithmetic and copies ran while one was open for 0% -> 0% of each run, Pallas kernels for 17% -> 15%
where the time goes in v5:
time: 90.4 us; the launch traced here: 88.7 us
  starting transfers between devices  28.2 us (31%)
  Pallas kernels  24.6 us (27%)
  waiting for transfers between devices  19.3 us (21%)
  blocking collectives  15.8 us (17%)
    pallas_call x11, Pallas kernels, call(): pl.pallas_call(kernel, name=name, in_specs=specs, out_specs=[VM] * len(ou...  24.6 us
    ppermute x12, starting transfers between devices, exchange(): lax.ppermute(parts[k], axes, [(i, i ^ k) for i in range(n)])  22.7 us
    all_to_all x1, blocking collectives, on_device(): mine = lax.all_to_all(mine, 'z', 0, 0, tiled=True)  15.8 us
    ppermute x12, waiting for transfers between devices, exchange(): lax.ppermute(parts[k], axes, [(i, i ^ k) for i in range(n)])  14.9 us
    ppermute x1, starting transfers between devices, on_device(): other = lax.ppermute(mine, 'xh', [(0, 1), (1, 0)])  2.72 us
    ppermute x1, waiting for transfers between devices, on_device(): xp = lax.ppermute(x, SEQ, [(i, i + 1) for i in range(seq - 1)])  2.21 us
    ppermute x1, starting transfers between devices, on_device(): xp = lax.ppermute(x, SEQ, [(i, i + 1) for i in range(seq - 1)])  1.92 us
  transfers between devices with their start and end apart: 17, of which 9 were waited for; matrix products, arithmetic and copies ran while one was open for 0% of the time, Pallas kernels for 15%

profile of v5, /device:TPU:2, one launch (start us, length us, event | category | flops | bytes accessed | tf_op | source)
XLA Modules:
  0.0 88.7 jit_solution(12541955303502334494)
XLA Ops:
  0.6 1.9 %collective-permute-start = (bf16[256,768]{1,0:T(8,128)(2,1)}, bf16[256,768]{1,0:T(8,128)(2,1)S(1)}, u32[]{:S(2)}, u32[]{:S(2)}) collective-permute-start(bf16[256,768]{1,0:T(8,128)(2,1)} %bitcast.9), channel_id=1, source_target_pairs={{0,2},{2,4},{4,6},{6,8},{8,10},{10,12},{12,14},{14,16},{16,18},{18... | collective-permute-start | bytes 1179656 | tf_op jit(solution)/shard_map/ppermute | solution.py:315
  2.7 5.1 %own_part.1 = (bf16[256,2304]{1,0:T(8,128)(2,1)S(1)}, bf16[256,768]{1,0:T(8,128)(2,1)S(1)}, bf16[768,256]{1,0:T(8,128)(2,1)S(1)}, f32[256,768]{1,0:T(8,128)S(1)}...) custom-call(s32[5]{0:T(128)S(1)} %stack.27.at_ref, ...), custom_call_target="tpu_custom_call" | custom-call | tf_op jit(solution)/shard_map/own_part/pallas_call | solution.py:297
  7.7 2.2 %collective-permute-done.xp_ref = bf16[256,768]{1,0:T(8,128)(2,1)S(1)} collective-permute-done((bf16[256,768]{1,0:T(8,128)(2,1)}, bf16[256,768]{1,0:T(8,128)(2,1)S(1)}, u32[]{:S(2)}, u32[]{:S(2)}) %collective-permute-start) | collective-permute-done | bytes 393248 | tf_op jit(solution)/shard_map/ppermute | solution.py:315
  9.9 9.4 %memory_and_heads.1 = (bf16[384,1536]{1,0:T(8,128)(2,1)S(1)}, bf16[384,1536]{1,0:T(8,128)(2,1)S(1)}, bf16[256,512]{1,0:T(8,128)(2,1)S(1)}, f32[256,768]{1,0:T(8,...) custom-call(s32[5]{0:T(128)S(1)} %stack.27.at_ref, ...), custom_call_target="tpu_custom_call" | custom-call | tf_op jit(solution)/shard_map/memory_and_heads/pallas_call | solution.py:297
  19.6 5.7 %heads_and_output_weight.1 = (bf16[384,1536]{1,0:T(8,128)(2,1)S(1)}, bf16[384,1536]{1,0:T(8,128)(2,1)S(1)}, f32[2,768]{1,0:T(2,128)S(1)}, bf16[256,768]{1,0:T(8,128)(2,1)S(1)}, f32[256,768]{1,0:T(8,128)S(1)}) custom-call(s32[5]{0:T(128)S(1)} %stack.27.at_ref, bf16[3,768,768]{2,1,0:T(8,128)(2,1)S(1)} %get-tuple-element.52.w_ref, ...), custom_call_target="tpu_custom_call" | custom-call | tf_op jit(solution)/shard_map/heads_and_output_weight/pallas_call | solution.py:297
  26.2 1.7 %collective-permute-start.2 = (bf16[96,1536]{1,0:T(8,128)(2,1)S(1)}, bf16[96,1536]{1,0:T(8,128)(2,1)S(1)}, u32[]{:S(2)}, u32[]{:S(2)}) collective-permute-start(bf16[96,1536]{1,0:T(8,128)(2,1)S(1)} %get-tuple-element.75), channel_id=1, source_target_pairs={{0,64},{64,0},{128,192},{192,128},{1,65},{65,1},{129,193},{193,129... | collective-permute-start | bytes 884744 | tf_op jit(solution)/shard_map/ppermute | solution.py:343
  27.9 2.9 %collective-permute-start.3 = (bf16[96,1536]{1,0:T(8,128)(2,1)S(1)}, bf16[96,1536]{1,0:T(8,128)(2,1)S(1)}, u32[]{:S(2)}, u32[]{:S(2)}) collective-permute-start(bf16[96,1536]{1,0:T(8,128)(2,1)S(1)} %get-tuple-element.76), channel_id=1, source_target_pairs={{0,128},{64,192},{128,0},{192,64},{1,129},{65,193},{129,1},{193,65... | collective-permute-start | bytes 884744 | tf_op jit(solution)/shard_map/ppermute | solution.py:343
  31.0 1.2 %collective-permute-done.9.vecr_ref = f32[2,768]{1,0:T(2,128)S(1)} collective-permute-done((f32[2,768]{1,0:T(2,128)S(1)}, f32[2,768]{1,0:T(2,128)S(1)}, u32[]{:S(2)}, u32[]{:S(2)}) %collective-permute-start.9) | collective-permute-done | bytes 6176 | tf_op jit(solution)/shard_map/ppermute | solution.py:339
  32.4 2.2 %collective-permute-start.10 = (bf16[200,768]{1,0:T(8,128)(2,1)S(1)}, bf16[200,768]{1,0:T(8,128)(2,1)S(1)}, u32[]{:S(2)}, u32[]{:S(2)}) collective-permute-start(bf16[200,768]{1,0:T(8,128)(2,1)S(1)} %get-tuple-element.86), channel_id=1, source_target_pairs={{0,1},{1,0},{4,5},{5,4},{2,3},{3,2},{6,7},{7,6},{8,9},{9,8},{12,13... | collective-permute-start | bytes 921608 | tf_op jit(solution)/shard_map/ppermute | solution.py:343
  34.6 5.6 %collective-permute-start.11 = (bf16[200,768]{1,0:T(8,128)(2,1)S(1)}, bf16[200,768]{1,0:T(8,128)(2,1)S(1)}, u32[]{:S(2)}, u32[]{:S(2)}) collective-permute-start(bf16[200,768]{1,0:T(8,128)(2,1)S(1)} %get-tuple-element.87), channel_id=1, source_target_pairs={{0,4},{1,5},{4,0},{5,1},{2,6},{3,7},{6,2},{7,3},{8,12},{9,13},{12,... | collective-permute-start | bytes 921608 | tf_op jit(solution)/shard_map/ppermute | solution.py:343
  40.2 1.0 %collective-permute-start.12 = (bf16[200,768]{1,0:T(8,128)(2,1)S(1)}, bf16[200,768]{1,0:T(8,128)(2,1)S(1)}, u32[]{:S(2)}, u32[]{:S(2)}) collective-permute-start(bf16[200,768]{1,0:T(8,128)(2,1)S(1)} %get-tuple-element.88), channel_id=1, source_target_pairs={{0,5},{1,4},{4,1},{5,0},{2,7},{3,6},{6,3},{7,2},{8,13},{9,12},{12,... | collective-permute-start | bytes 921608 | tf_op jit(solution)/shard_map/ppermute | solution.py:343
  41.2 2.9 %collective-permute-done.3.c = bf16[96,1536]{1,0:T(8,128)(2,1)S(1)} collective-permute-done((bf16[96,1536]{1,0:T(8,128)(2,1)S(1)}, bf16[96,1536]{1,0:T(8,128)(2,1)S(1)}, u32[]{:S(2)}, u32[]{:S(2)}) %collective-permute-start.3) | collective-permute-done | bytes 294944 | tf_op jit(solution)/shard_map/ppermute | solution.py:343
  44.1 2.6 %collective-permute-done.4.d = bf16[96,1536]{1,0:T(8,128)(2,1)S(1)} collective-permute-done((bf16[96,1536]{1,0:T(8,128)(2,1)S(1)}, bf16[96,1536]{1,0:T(8,128)(2,1)S(1)}, u32[]{:S(2)}, u32[]{:S(2)}) %collective-permute-start.4) | collective-permute-done | bytes 294944 | tf_op jit(solution)/shard_map/ppermute | solution.py:343
  46.8 2.3 %collective-permute-start.5 = (bf16[48,768]{1,0:T(8,128)(2,1)S(1)}, bf16[48,768]{1,0:T(8,128)(2,1)S(1)}, u32[]{:S(2)}, u32[]{:S(2)}) collective-permute-start(bf16[48,768]{1,0:T(8,128)(2,1)S(1)} %get-tuple-element.79), channel_id=1, source_target_pairs={{0,1},{1,0},{4,5},{5,4},{2,3},{3,2},{6,7},{7,6},{8,9},{9,8},{12,13... | collective-permute-start | bytes 221192 | tf_op jit(solution)/shard_map/ppermute | solution.py:343
  49.1 5.3 %collective-permute-done.11.c = bf16[200,768]{1,0:T(8,128)(2,1)S(1)} collective-permute-done((bf16[200,768]{1,0:T(8,128)(2,1)S(1)}, bf16[200,768]{1,0:T(8,128)(2,1)S(1)}, u32[]{:S(2)}, u32[]{:S(2)}) %collective-permute-start.11) | collective-permute-done | bytes 307232 | tf_op jit(solution)/shard_map/ppermute | solution.py:343
  54.6 1.0 %collective-permute-start.13 = (bf16[56,768]{1,0:T(8,128)(2,1)S(1)}, bf16[56,768]{1,0:T(8,128)(2,1)S(1)}, u32[]{:S(2)}, u32[]{:S(2)}) collective-permute-start(bf16[56,768]{1,0:T(8,128)(2,1)S(1)} %get-tuple-element.90), channel_id=1, source_target_pairs={{0,64},{64,0},{128,192},{192,128},{1,65},{65,1},{129,193},{193,129... | collective-permute-start | bytes 258056 | tf_op jit(solution)/shard_map/ppermute | solution.py:343
  55.5 4.4 %collective-permute-start.14 = (bf16[56,768]{1,0:T(8,128)(2,1)S(1)}, bf16[56,768]{1,0:T(8,128)(2,1)S(1)}, u32[]{:S(2)}, u32[]{:S(2)}) collective-permute-start(bf16[56,768]{1,0:T(8,128)(2,1)S(1)} %get-tuple-element.91), channel_id=1, source_target_pairs={{0,128},{64,192},{128,0},{192,64},{1,129},{65,193},{129,1},{193,65... | collective-permute-start | bytes 258056 | tf_op jit(solution)/shard_map/ppermute | solution.py:343
  60.6 0.8 collective-permute-start.7
  61.4 2.9 %collective-permute-done.6.a2 = bf16[48,768]{1,0:T(8,128)(2,1)S(1)} collective-permute-done((bf16[48,768]{1,0:T(8,128)(2,1)S(1)}, bf16[48,768]{1,0:T(8,128)(2,1)S(1)}, u32[]{:S(2)}, u32[]{:S(2)}) %collective-permute-start.6) | collective-permute-done | bytes 73760 | tf_op jit(solution)/shard_map/ppermute | solution.py:343
  65.8 15.8 %all_to_all.5.in_ref = bf16[8,8,1536]{2,1,0:T(8,128)(2,1)S(1)} all-to-all(bf16[8,8,1536]{2,1,0:T(8,128)(2,1)S(1)} %plane_sum.1), channel_id=1, replica_groups=mesh['y'=4,'z'=8,'xl'=2,'c'=2,'xh'=2] {'z'}, dimensions={0} | all-to-all | bytes 393216 | tf_op jit(solution)/shard_map/all_to_all | solution.py:362
  82.2 2.7 %collective-permute-start.16 = (bf16[8,1536]{1,0:T(8,128)(2,1)S(1)}, bf16[8,1536]{1,0:T(8,128)(2,1)S(1)}, u32[]{:S(2)}, u32[]{:S(2)}) collective-permute-start(bf16[8,1536]{1,0:T(8,128)(2,1)S(1)} %get-tuple-element.93.mine_ref), channel_id=1, source_target_pairs={{0,1},{1,0},{2,3},{3,2},{4,5},{5,4},{6,7},{7,6},{8,9},{9,8},{10,11... | collective-permute-start | bytes 73736 | tf_op jit(solution)/shard_map/ppermute | solution.py:368
  84.9 1.6 %token_outputs.1 = (bf16[256,768]{1,0:T(8,128)(2,1)}, bf16[256,768]{1,0:T(8,128)(2,1)}) custom-call(f32[768]{0:T(1024)S(1)} %copy-done.3, bf16[256,768]{1,0:T(8,128)(2,1)S(1)} %bitcast.11, bf16[256,768]{1,0:T(8,128)(2,1)S(1)} %bitcast.13, bf16[256,768]{1,0:T(8,128)(2,1)S(1)} %get-tuple-element.67.mixed_ref, bf16[768,768]{1,0:T(8,128)(2,1)S(1)} %copy-done, ...), custom_call_target="tpu_custom_call" | custom-call | tf_op jit(solution)/shard_map/token_outputs/pallas_call | solution.py:297
  86.5 1.0 %collective-permute-done.16.other_ref = bf16[8,1536]{1,0:T(8,128)(2,1)S(1)} collective-permute-done((bf16[8,1536]{1,0:T(8,128)(2,1)S(1)}, bf16[8,1536]{1,0:T(8,128)(2,1)S(1)}, u32[]{:S(2)}, u32[]{:S(2)}) %collective-permute-start.16) | collective-permute-done | bytes 24608 | tf_op jit(solution)/shard_map/ppermute | solution.py:368
  87.5 1.2 %finish.1 = (f32[6,2304]{1,0:T(8,128)}, f32[6,768]{1,0:T(8,128)}) custom-call(s32[5]{0:T(128)S(1)} %stack.27.at_ref, bf16[8,1536]{1,0:T(8,128)(2,1)S(1)} %get-tuple-element.93.mine_ref, bf16[8,1536]{1,0:T(8,128)(2,1)S(1)} %collective-permute-done.16.other_ref), custom_call_target="tpu_custom_call" | custom-call | tf_op jit(solution)/shard_map/finish/pallas_call | solution.py:297
  (31 shorter events, 4.8 us)
Async XLA Ops:
  0.6 9.3 %collective-permute-start = (bf16[256,768]{1,0:T(8,128)(2,1)}, bf16[256,768]{1,0:T(8,128)(2,1)S(1)}, u32[]{:S(2)}, u32[]{:S(2)}) collective-permute-start(bf16[256,768]{1,0:T(8,128)(2,1)} %bitcast.9), channel_id=1, source_target_pairs={{0,2},{2,4},{4,6},{6,8},{8,10},{10,12},{12,14},{14,16},{16,18},{18... | collective-permute-start | bytes 1179656 | tf_op jit(solution)/shard_map/ppermute | solution.py:315
  19.3 6.6 %collective-permute-start.1 = (bf16[384,1536]{1,0:T(8,128)(2,1)S(1)}, bf16[384,1536]{1,0:T(8,128)(2,1)S(1)}, u32[]{:S(2)}, u32[]{:S(2)}) collective-permute-start(bf16[384,1536]{1,0:T(8,128)(2,1)S(1)} %get-tuple-element.73), channel_id=1, source_target_pairs={{0,2},{2,0},{1,3},{3,1},{4,6},{6,4},{5,7},{7,5},{8,10},{10,8},{9,1... | collective-permute-start | bytes 3538952 | tf_op jit(solution)/shard_map/ppermute | solution.py:339
  25.3 6.8 %collective-permute-start.8 = (bf16[384,1536]{1,0:T(8,128)(2,1)S(1)}, bf16[384,1536]{1,0:T(8,128)(2,1)S(1)}, u32[]{:S(2)}, u32[]{:S(2)}) collective-permute-start(bf16[384,1536]{1,0:T(8,128)(2,1)S(1)} %get-tuple-element.83), channel_id=1, source_target_pairs={{0,2},{2,0},{1,3},{3,1},{4,6},{6,4},{5,7},{7,5},{8,10},{10,8},{9,1... | collective-permute-start | bytes 3538952 | tf_op jit(solution)/shard_map/ppermute | solution.py:339
  26.2 14.1 %collective-permute-start.2 = (bf16[96,1536]{1,0:T(8,128)(2,1)S(1)}, bf16[96,1536]{1,0:T(8,128)(2,1)S(1)}, u32[]{:S(2)}, u32[]{:S(2)}) collective-permute-start(bf16[96,1536]{1,0:T(8,128)(2,1)S(1)} %get-tuple-element.75), channel_id=1, source_target_pairs={{0,64},{64,0},{128,192},{192,128},{1,65},{65,1},{129,193},{193,129... | collective-permute-start | bytes 884744 | tf_op jit(solution)/shard_map/ppermute | solution.py:343
  27.9 16.2 %collective-permute-start.3 = (bf16[96,1536]{1,0:T(8,128)(2,1)S(1)}, bf16[96,1536]{1,0:T(8,128)(2,1)S(1)}, u32[]{:S(2)}, u32[]{:S(2)}) collective-permute-start(bf16[96,1536]{1,0:T(8,128)(2,1)S(1)} %get-tuple-element.76), channel_id=1, source_target_pairs={{0,128},{64,192},{128,0},{192,64},{1,129},{65,193},{129,1},{193,65... | collective-permute-start | bytes 884744 | tf_op jit(solution)/shard_map/ppermute | solution.py:343
  30.8 15.9 %collective-permute-start.4 = (bf16[96,1536]{1,0:T(8,128)(2,1)S(1)}, bf16[96,1536]{1,0:T(8,128)(2,1)S(1)}, u32[]{:S(2)}, u32[]{:S(2)}) collective-permute-start(bf16[96,1536]{1,0:T(8,128)(2,1)S(1)} %get-tuple-element.77), channel_id=1, source_target_pairs={{0,192},{64,128},{128,64},{192,0},{1,193},{65,129},{129,65},{193,1... | collective-permute-start | bytes 884744 | tf_op jit(solution)/shard_map/ppermute | solution.py:343
  31.0 1.2 %collective-permute-start.9 = (f32[2,768]{1,0:T(2,128)S(1)}, f32[2,768]{1,0:T(2,128)S(1)}, u32[]{:S(2)}, u32[]{:S(2)}) collective-permute-start(f32[2,768]{1,0:T(2,128)S(1)} %get-tuple-element.84.vec_ref), channel_id=1, source_target_pairs={{0,2},{2,0},{1,3},{3,1},{4,6},{6,4},{5,7},{7,5},{8,10},{10,8},{9,1... | collective-permute-start | bytes 18440 | tf_op jit(solution)/shard_map/ppermute | solution.py:339
  32.4 16.7 %collective-permute-start.10 = (bf16[200,768]{1,0:T(8,128)(2,1)S(1)}, bf16[200,768]{1,0:T(8,128)(2,1)S(1)}, u32[]{:S(2)}, u32[]{:S(2)}) collective-permute-start(bf16[200,768]{1,0:T(8,128)(2,1)S(1)} %get-tuple-element.86), channel_id=1, source_target_pairs={{0,1},{1,0},{4,5},{5,4},{2,3},{3,2},{6,7},{7,6},{8,9},{9,8},{12,13... | collective-permute-start | bytes 921608 | tf_op jit(solution)/shard_map/ppermute | solution.py:343
  34.6 19.7 %collective-permute-start.11 = (bf16[200,768]{1,0:T(8,128)(2,1)S(1)}, bf16[200,768]{1,0:T(8,128)(2,1)S(1)}, u32[]{:S(2)}, u32[]{:S(2)}) collective-permute-start(bf16[200,768]{1,0:T(8,128)(2,1)S(1)} %get-tuple-element.87), channel_id=1, source_target_pairs={{0,4},{1,5},{4,0},{5,1},{2,6},{3,7},{6,2},{7,3},{8,12},{9,13},{12,... | collective-permute-start | bytes 921608 | tf_op jit(solution)/shard_map/ppermute | solution.py:343
  40.2 14.1 %collective-permute-start.12 = (bf16[200,768]{1,0:T(8,128)(2,1)S(1)}, bf16[200,768]{1,0:T(8,128)(2,1)S(1)}, u32[]{:S(2)}, u32[]{:S(2)}) collective-permute-start(bf16[200,768]{1,0:T(8,128)(2,1)S(1)} %get-tuple-element.88), channel_id=1, source_target_pairs={{0,5},{1,4},{4,1},{5,0},{2,7},{3,6},{6,3},{7,2},{8,13},{9,12},{12,... | collective-permute-start | bytes 921608 | tf_op jit(solution)/shard_map/ppermute | solution.py:343
  46.8 13.8 %collective-permute-start.5 = (bf16[48,768]{1,0:T(8,128)(2,1)S(1)}, bf16[48,768]{1,0:T(8,128)(2,1)S(1)}, u32[]{:S(2)}, u32[]{:S(2)}) collective-permute-start(bf16[48,768]{1,0:T(8,128)(2,1)S(1)} %get-tuple-element.79), channel_id=1, source_target_pairs={{0,1},{1,0},{4,5},{5,4},{2,3},{3,2},{6,7},{7,6},{8,9},{9,8},{12,13... | collective-permute-start | bytes 221192 | tf_op jit(solution)/shard_map/ppermute | solution.py:343
  54.4 30.5 %copy-start = (bf16[768,768]{1,0:T(8,128)(2,1)S(1)}, bf16[768,768]{1,0:T(8,128)(2,1)}, u32[]{:S(2)}) copy-start(bf16[768,768]{1,0:T(8,128)(2,1)} %wo_ref.1) | copy-start | bytes 3538948
  54.4 30.5 %copy-start.1 = (bf16[1,256,768]{2,1,0:T(8,128)(2,1)S(1)}, bf16[1,256,768]{2,1,0:T(8,128)(2,1)}, u32[]{:S(2)}) copy-start(bf16[1,256,768]{2,1,0:T(8,128)(2,1)} %param.6) | copy-start | bytes 1179652
  54.4 30.5 %copy-start.2 = (bf16[1,256,768]{2,1,0:T(8,128)(2,1)S(1)}, bf16[1,256,768]{2,1,0:T(8,128)(2,1)}, u32[]{:S(2)}) copy-start(bf16[1,256,768]{2,1,0:T(8,128)(2,1)} %param.7) | copy-start | bytes 1179652
  54.4 30.5 %copy-start.3 = (f32[768]{0:T(1024)S(1)}, f32[768]{0:T(1024)}, u32[]{:S(2)}) copy-start(f32[768]{0:T(1024)} %gain_ref.1) | copy-start | bytes 9220
  54.6 10.4 %collective-permute-start.13 = (bf16[56,768]{1,0:T(8,128)(2,1)S(1)}, bf16[56,768]{1,0:T(8,128)(2,1)S(1)}, u32[]{:S(2)}, u32[]{:S(2)}) collective-permute-start(bf16[56,768]{1,0:T(8,128)(2,1)S(1)} %get-tuple-element.90), channel_id=1, source_target_pairs={{0,64},{64,0},{128,192},{192,128},{1,65},{65,1},{129,193},{193,129... | collective-permute-start | bytes 258056 | tf_op jit(solution)/shard_map/ppermute | solution.py:343
  55.5 9.5 %collective-permute-start.14 = (bf16[56,768]{1,0:T(8,128)(2,1)S(1)}, bf16[56,768]{1,0:T(8,128)(2,1)S(1)}, u32[]{:S(2)}, u32[]{:S(2)}) collective-permute-start(bf16[56,768]{1,0:T(8,128)(2,1)S(1)} %get-tuple-element.91), channel_id=1, source_target_pairs={{0,128},{64,192},{128,0},{192,64},{1,129},{65,193},{129,1},{193,65... | collective-permute-start | bytes 258056 | tf_op jit(solution)/shard_map/ppermute | solution.py:343
  59.9 5.7 %collective-permute-start.15 = (bf16[56,768]{1,0:T(8,128)(2,1)S(1)}, bf16[56,768]{1,0:T(8,128)(2,1)S(1)}, u32[]{:S(2)}, u32[]{:S(2)}) collective-permute-start(bf16[56,768]{1,0:T(8,128)(2,1)S(1)} %get-tuple-element.92), channel_id=1, source_target_pairs={{0,192},{64,128},{128,64},{192,0},{1,193},{65,129},{129,65},{193,1... | collective-permute-start | bytes 258056 | tf_op jit(solution)/shard_map/ppermute | solution.py:343
  60.0 4.4 %collective-permute-start.6 = (bf16[48,768]{1,0:T(8,128)(2,1)S(1)}, bf16[48,768]{1,0:T(8,128)(2,1)S(1)}, u32[]{:S(2)}, u32[]{:S(2)}) collective-permute-start(bf16[48,768]{1,0:T(8,128)(2,1)S(1)} %get-tuple-element.80), channel_id=1, source_target_pairs={{0,4},{1,5},{4,0},{5,1},{2,6},{3,7},{6,2},{7,3},{8,12},{9,13},{12,... | collective-permute-start | bytes 221192 | tf_op jit(solution)/shard_map/ppermute | solution.py:343
  60.6 4.4 %collective-permute-start.7 = (bf16[48,768]{1,0:T(8,128)(2,1)S(1)}, bf16[48,768]{1,0:T(8,128)(2,1)S(1)}, u32[]{:S(2)}, u32[]{:S(2)}) collective-permute-start(bf16[48,768]{1,0:T(8,128)(2,1)S(1)} %get-tuple-element.81), channel_id=1, source_target_pairs={{0,5},{1,4},{4,1},{5,0},{2,7},{3,6},{6,3},{7,2},{8,13},{9,12},{12,... | collective-permute-start | bytes 221192 | tf_op jit(solution)/shard_map/ppermute | solution.py:343
  82.2 5.3 %collective-permute-start.16 = (bf16[8,1536]{1,0:T(8,128)(2,1)S(1)}, bf16[8,1536]{1,0:T(8,128)(2,1)S(1)}, u32[]{:S(2)}, u32[]{:S(2)}) collective-permute-start(bf16[8,1536]{1,0:T(8,128)(2,1)S(1)} %get-tuple-element.93.mine_ref), channel_id=1, source_target_pairs={{0,1},{1,0},{2,3},{3,2},{4,5},{5,4},{6,7},{7,6},{8,9},{9,8},{10,11... | collective-permute-start | bytes 73736 | tf_op jit(solution)/shard_map/ppermute | solution.py:368

commit v6 on v5

--- a/solution.py
+++ b/solution.py
@@ -212,40 +212,88 @@
     return rows[0:2].astype(F32) + rows[2:4].astype(F32)
 
 
+def fold_rows(value):
+    high = value.astype(BF)
+    low = (value - high.astype(F32)).astype(BF)
+    return jnp.concatenate([high[:, :384], high[:, 384:], low[:, :384], low[:, 384:]], axis=0)
+
+
+def unfold_rows(rows):
+    rows = rows.astype(F32)
+    return jnp.concatenate([rows[0:2] + rows[4:6], rows[2:4] + rows[6:8]], axis=1)
+
+
 def tree(a, b, c, d):
     return (a.astype(F32) + b.astype(F32)) + (c.astype(F32) + d.astype(F32))
 
 
+RING_Y = (1, 3, 2)
+RING_X = (2, 3, 1)
+
+
+def halving_order(ring):
+    one, two, far = ring
+    return [((one, far), (0, two)), ((two, far), (0, one))]
+
+
 def pair_a_kernel(keep_ref, recv_ref, *outs):
-    for k in range(4):
-        rows = slice(96 * k, 96 * k + 96)
-        outs[k][...] = (keep_ref[rows, :].astype(F32) + recv_ref[rows, :].astype(F32)).astype(BF)
+    for part, groups in enumerate(halving_order(RING_Y)):
+        cols = slice(768 * part, 768 * part + 768)
+        for kept, places in enumerate(groups):
+            for i, k in enumerate(places):
+                rows = slice(96 * k, 96 * k + 96)
+                outs[2 * part + kept][96 * i : 96 * i + 96, :] = (
+                    keep_ref[rows, cols].astype(F32) + recv_ref[rows, cols].astype(F32)
+                ).astype(BF)
 
 
 def pair_b_kernel(keep_ref, recv_ref, vec_ref, vecr_ref, *outs):
-    vec = split_rows(vec_ref[...] + vecr_ref[...])
-    for k in range(4):
-        cols = slice(768 * (k & 1), 768 * (k & 1) + 768)
-        for y in range(4):
-            rows = slice(96 * y + 48 * (k >> 1), 96 * y + 48 * (k >> 1) + 48)
-            outs[k][48 * y : 48 * y + 48, :] = (
-                keep_ref[rows, cols].astype(F32) + recv_ref[rows, cols].astype(F32)
-            ).astype(BF)
-        outs[k][192:200, :] = vec
-
-
-def mid_a_kernel(a, b, c, d, *outs):
+    for part, groups in enumerate(halving_order(RING_X)):
+        for kept, places in enumerate(groups):
+            out = outs[2 * part + kept]
+            for i, k in enumerate(places):
+                at = 768 * (k & 1) + 384 * part
+                for y in range(4):
+                    rows = slice(96 * y + 48 * (k >> 1), 96 * y + 48 * (k >> 1) + 48)
+                    out[192 * i + 48 * y : 192 * i + 48 * y + 48, :] = (
+                        keep_ref[rows, at : at + 384].astype(F32) + recv_ref[rows, at : at + 384].astype(F32)
+                    ).astype(BF)
+    vec = fold_rows(vec_ref[...] + vecr_ref[...])
+    outs[0][384:392, :] = vec
+    outs[1][384:392, :] = vec
+
+
+def step_a_kernel(recv0_ref, keep0_ref, recv1_ref, keep1_ref, send0_ref, send1_ref, own_ref):
+    for part, (recv, keep, send) in enumerate(((recv0_ref, keep0_ref, send0_ref), (recv1_ref, keep1_ref, send1_ref))):
+        add = lambda rows: keep[rows, :].astype(F32) + recv[rows, :].astype(F32)
+        own_ref[:, 768 * part : 768 * part + 768] = add(slice(0, 96))
+        send[...] = add(slice(96, 192)).astype(BF)
+
+
+def step_b_kernel(recv0_ref, keep0_ref, recv1_ref, keep1_ref, send0_ref, send1_ref, own_ref, vec_ref):
+    for part, (recv, keep, send) in enumerate(((recv0_ref, keep0_ref, send0_ref), (recv1_ref, keep1_ref, send1_ref))):
+        add = lambda rows: keep[rows, :].astype(F32) + recv[rows, :].astype(F32)
+        own_ref[:, 384 * part : 384 * part + 384] = add(slice(0, 192))
+        send[0:192, :] = add(slice(192, 384)).astype(BF)
+    vec = unfold_rows(keep0_ref[384:392, :]) + unfold_rows(recv0_ref[384:392, :])
+    rows = fold_rows(vec)
+    vec_ref[...] = unfold_rows(rows)
+    send0_ref[192:200, :] = rows
+
+
+def mid_a_kernel(own_ref, recv0_ref, recv1_ref, *outs):
     for k in range(4):
         rows = slice(48 * (k >> 1), 48 * (k >> 1) + 48)
-        cols = slice(768 * (k & 1), 768 * (k & 1) + 768)
-        outs[k][...] = tree(a[rows, cols], b[rows, cols], c[rows, cols], d[rows, cols]).astype(BF)
-
-
-def mid_b_kernel(a, b, c, d, *outs):
-    vec = split_rows((join_rows(a[192:200]) + join_rows(b[192:200])) + (join_rows(c[192:200]) + join_rows(d[192:200])))
+        recv = recv1_ref if k & 1 else recv0_ref
+        outs[k][...] = (own_ref[rows, 768 * (k & 1) : 768 * (k & 1) + 768] + recv[rows, :].astype(F32)).astype(BF)
+
+
+def mid_b_kernel(own_ref, vec_ref, recv0_ref, recv1_ref, *outs):
+    vec = split_rows(vec_ref[...] + unfold_rows(recv0_ref[192:200, :]))
     for k in range(4):
         rows = slice(48 * k, 48 * k + 48)
-        outs[k][0:48, :] = tree(a[rows], b[rows], c[rows], d[rows]).astype(BF)
+        outs[k][0:48, 0:384] = (own_ref[rows, 0:384] + recv0_ref[rows, :].astype(F32)).astype(BF)
+        outs[k][0:48, 384:768] = (own_ref[rows, 384:768] + recv1_ref[rows, :].astype(F32)).astype(BF)
         outs[k][48:56, :] = vec
 
 
@@ -338,26 +386,39 @@
     def swap(block):
         return lax.ppermute(block, "c", [(0, 1), (1, 0)])
 
+    def permute(block, axes, k):
+        n = lax.axis_size(axes)
+        return lax.ppermute(block, axes, [(i, i ^ k) for i in range(n)])
+
     def exchange(parts, axes):
-        n = lax.axis_size(axes)
-        return [parts[0]] + [lax.ppermute(parts[k], axes, [(i, i ^ k) for i in range(n)]) for k in (1, 3, 2)]
-
-    def ordered(parts):
-        own, one, three, two = parts
-        return [own, one, two, three]
-
-    parts_a = call(pair_a_kernel, "pair_sum_a", [sds(96, 1536)] * 4, [keep_a, swap(send_a)])
-    parts_b = call(pair_b_kernel, "pair_sum_b", [sds(200, 768)] * 4, [keep_b, swap(send_b), vec, swap(vec)])
-    parts_a = ordered(exchange(parts_a, "y"))
-    parts_b = ordered(exchange(parts_b, ROW))
+        return [parts[0]] + [permute(parts[k], axes, k) for k in (1, 2, 3)]
+
+    half = sds(192, 768)
+    send0_a, keep0_a, send1_a, keep1_a = call(pair_a_kernel, "pair_sum_a", [half] * 4, [keep_a, swap(send_a)])
+    send0_b, keep0_b, send1_b, keep1_b = call(
+        pair_b_kernel, "pair_sum_b", [sds(392, 384), sds(392, 384), sds(384, 384), sds(384, 384)],
+        [keep_b, swap(send_b), vec, swap(vec)],
+    )
+    got_a = [permute(send0_a, "y", RING_Y[0]), permute(send1_a, "y", RING_Y[1])]
+    got_b = [permute(send0_b, ROW, RING_X[0]), permute(send1_b, ROW, RING_X[1])]
     out, dx = call(
         token_kernel, "token_outputs", [tokens, tokens],
         [gain, x, cot, mixed, wo, dn, xhat, rstd],
     )
-    parts_a = call(mid_a_kernel, "middle_sum_a", [sds(48, 768)] * 4, parts_a)
-    parts_b = call(mid_b_kernel, "middle_sum_b", [sds(56, 768)] * 4, parts_b)
-    parts_a = ordered(exchange(parts_a, ROW))
-    parts_b = ordered(exchange(parts_b, "y"))
+    send0_a, send1_a, own_a = call(
+        step_a_kernel, "step_sum_a", [sds(96, 768), sds(96, 768), sds(96, 1536, dtype=F32)],
+        [got_a[0], keep0_a, got_a[1], keep1_a],
+    )
+    got_a = [permute(send0_a, "y", RING_Y[1]), permute(send1_a, "y", RING_Y[0])]
+    send0_b, send1_b, own_b, vec = call(
+        step_b_kernel, "step_sum_b", [sds(200, 384), sds(192, 384), sds(192, 768, dtype=F32), sds(2, D, dtype=F32)],
+        [got_b[0], keep0_b, got_b[1], keep1_b],
+    )
+    got_b = [permute(send0_b, ROW, RING_X[1]), permute(send1_b, ROW, RING_X[0])]
+    parts_a = call(mid_a_kernel, "middle_sum_a", [sds(48, 768)] * 4, [own_a, *got_a])
+    parts_b = call(mid_b_kernel, "middle_sum_b", [sds(56, 768)] * 4, [own_b, vec, *got_b])
+    parts_a = exchange(parts_a, ROW)
+    parts_b = exchange(parts_b, "y")
     (mine,) = call(plane_kernel, "plane_sum", [sds(8, 8, 1536)], [*parts_a, *parts_b])
     mine = lax.all_to_all(mine, "z", 0, 0, tiled=True)
     factor = 1.0 / float(seq * lax.axis_size("xh") * T) ** 0.5

time: 90.4 us -> 88.3 us (0.977); the launches traced: 88.7 us -> 88.2 us
  waiting for transfers between devices: 19.3 us -> 17.3 us
  starting transfers between devices: 28.2 us -> 29.2 us
    ppermute x12 -> x14, waiting for transfers between devices: 14.9 us -> 12.2 us  [permute(): return lax.ppermute(block, axes, [(i, i ^ k) for i in range(n)])]
    ppermute x12 -> x14, starting transfers between devices: 22.7 us -> 24.5 us  [permute(): return lax.ppermute(block, axes, [(i, i ^ k) for i in range(n)])]
    pallas_call x11 -> x13, Pallas kernels: 24.6 us -> 24.7 us  [call(): pl.pallas_call(kernel, name=name, in_specs=specs, out_specs=[VM] * len(ou...]
  transfers between devices with their start and end apart: 17 -> 19, of which waited for: 9 -> 8; matrix products, arithmetic and copies ran while one was open for 0% -> 0% of each run, Pallas kernels for 15% -> 15%
where the time goes in v6:
time: 88.3 us; the launch traced here: 88.2 us
  starting transfers between devices  29.2 us (33%)
  Pallas kernels  24.7 us (28%)
  waiting for transfers between devices  17.3 us (20%)
  blocking collectives  16.1 us (18%)
    pallas_call x13, Pallas kernels, call(): pl.pallas_call(kernel, name=name, in_specs=specs, out_specs=[VM] * len(ou...  24.7 us
    ppermute x14, starting transfers between devices, permute(): return lax.ppermute(block, axes, [(i, i ^ k) for i in range(n)])  24.5 us
    all_to_all x1, blocking collectives, on_device(): mine = lax.all_to_all(mine, 'z', 0, 0, tiled=True)  16.1 us
    ppermute x14, waiting for transfers between devices, permute(): return lax.ppermute(block, axes, [(i, i ^ k) for i in range(n)])  12.2 us
    ppermute x1, waiting for transfers between devices, on_device(): xp = lax.ppermute(x, SEQ, [(i, i + 1) for i in range(seq - 1)])  2.21 us
    ppermute x1, starting transfers between devices, on_device(): other = lax.ppermute(mine, 'xh', [(0, 1), (1, 0)])  1.97 us
    ppermute x1, starting transfers between devices, on_device(): xp = lax.ppermute(x, SEQ, [(i, i + 1) for i in range(seq - 1)])  1.92 us
    ppermute x1, waiting for transfers between devices, on_device(): other = lax.ppermute(mine, 'xh', [(0, 1), (1, 0)])  1.77 us
  transfers between devices with their start and end apart: 19, of which 8 were waited for; matrix products, arithmetic and copies ran while one was open for 0% of the time, Pallas kernels for 15%

profile of v6, /device:TPU:2, one launch (start us, length us, event | category | flops | bytes accessed | tf_op | source)
XLA Modules:
  0.0 88.2 jit_solution(9930864087426504745)
XLA Ops:
  0.6 1.9 %collective-permute-start = (bf16[256,768]{1,0:T(8,128)(2,1)}, bf16[256,768]{1,0:T(8,128)(2,1)S(1)}, u32[]{:S(2)}, u32[]{:S(2)}) collective-permute-start(bf16[256,768]{1,0:T(8,128)(2,1)} %bitcast.9), channel_id=1, source_target_pairs={{0,2},{2,4},{4,6},{6,8},{8,10},{10,12},{12,14},{14,16},{16,18},{18... | collective-permute-start | bytes 1179656 | tf_op jit(solution)/shard_map/ppermute | solution.py:363
  2.7 5.1 %own_part.1 = (bf16[256,2304]{1,0:T(8,128)(2,1)S(1)}, bf16[256,768]{1,0:T(8,128)(2,1)S(1)}, bf16[768,256]{1,0:T(8,128)(2,1)S(1)}, f32[256,768]{1,0:T(8,128)S(1)}...) custom-call(s32[5]{0:T(128)S(1)} %stack.27.at_ref, ...), custom_call_target="tpu_custom_call" | custom-call | tf_op jit(solution)/shard_map/own_part/pallas_call | solution.py:345
  7.7 2.2 %collective-permute-done.xp_ref = bf16[256,768]{1,0:T(8,128)(2,1)S(1)} collective-permute-done((bf16[256,768]{1,0:T(8,128)(2,1)}, bf16[256,768]{1,0:T(8,128)(2,1)S(1)}, u32[]{:S(2)}, u32[]{:S(2)}) %collective-permute-start) | collective-permute-done | bytes 393248 | tf_op jit(solution)/shard_map/ppermute | solution.py:363
  9.9 9.4 %memory_and_heads.1 = (bf16[384,1536]{1,0:T(8,128)(2,1)S(1)}, bf16[384,1536]{1,0:T(8,128)(2,1)S(1)}, bf16[256,512]{1,0:T(8,128)(2,1)S(1)}, f32[256,768]{1,0:T(8,...) custom-call(s32[5]{0:T(128)S(1)} %stack.27.at_ref, ...), custom_call_target="tpu_custom_call" | custom-call | tf_op jit(solution)/shard_map/memory_and_heads/pallas_call | solution.py:345
  19.6 5.7 %heads_and_output_weight.1 = (bf16[384,1536]{1,0:T(8,128)(2,1)S(1)}, bf16[384,1536]{1,0:T(8,128)(2,1)S(1)}, f32[2,768]{1,0:T(2,128)S(1)}, bf16[256,768]{1,0:T(8,128)(2,1)S(1)}, f32[256,768]{1,0:T(8,128)S(1)}) custom-call(s32[5]{0:T(128)S(1)} %stack.27.at_ref, bf16[3,768,768]{2,1,0:T(8,128)(2,1)S(1)} %get-tuple-element.59.w_ref, ...), custom_call_target="tpu_custom_call" | custom-call | tf_op jit(solution)/shard_map/heads_and_output_weight/pallas_call | solution.py:345
  26.2 1.7 %collective-permute-start.2 = (bf16[192,768]{1,0:T(8,128)(2,1)S(1)}, bf16[192,768]{1,0:T(8,128)(2,1)S(1)}, u32[]{:S(2)}, u32[]{:S(2)}) collective-permute-start(bf16[192,768]{1,0:T(8,128)(2,1)S(1)} %get-tuple-element.81), channel_id=1, source_target_pairs={{0,64},{64,0},{128,192},{192,128},{1,65},{65,1},{129,193},{193,129... | collective-permute-start | bytes 884744 | tf_op jit(solution)/shard_map/ppermute | solution.py:391
  27.9 2.2 %collective-permute-start.3 = (bf16[192,768]{1,0:T(8,128)(2,1)S(1)}, bf16[192,768]{1,0:T(8,128)(2,1)S(1)}, u32[]{:S(2)}, u32[]{:S(2)}) collective-permute-start(bf16[192,768]{1,0:T(8,128)(2,1)S(1)} %get-tuple-element.83), channel_id=1, source_target_pairs={{0,192},{64,128},{128,64},{192,0},{1,193},{65,129},{129,65},{193,1... | collective-permute-start | bytes 884744 | tf_op jit(solution)/shard_map/ppermute | solution.py:391
  31.5 5.0 %collective-permute-start.11 = (bf16[392,384]{1,0:T(8,128)(2,1)S(1)}, bf16[392,384]{1,0:T(8,128)(2,1)S(1)}, u32[]{:S(2)}, u32[]{:S(2)}) collective-permute-start(bf16[392,384]{1,0:T(8,128)(2,1)S(1)} %get-tuple-element.95), channel_id=1, source_target_pairs={{0,4},{1,5},{4,0},{5,1},{2,6},{3,7},{6,2},{7,3},{8,12},{9,13},{12,... | collective-permute-start | bytes 903176 | tf_op jit(solution)/shard_map/ppermute | solution.py:391
  37.9 2.3 %collective-permute-start.4 = (bf16[96,768]{1,0:T(8,128)(2,1)S(1)}, bf16[96,768]{1,0:T(8,128)(2,1)S(1)}, u32[]{:S(2)}, u32[]{:S(2)}) collective-permute-start(bf16[96,768]{1,0:T(8,128)(2,1)S(1)} %get-tuple-element.86), channel_id=1, source_target_pairs={{0,192},{64,128},{128,64},{192,0},{1,193},{65,129},{129,65},{193,1... | collective-permute-start | bytes 442376 | tf_op jit(solution)/shard_map/ppermute | solution.py:391
  40.1 5.2 %collective-permute-done.12.recv1_ref = bf16[384,384]{1,0:T(8,128)(2,1)S(1)} collective-permute-done((bf16[384,384]{1,0:T(8,128)(2,1)S(1)}, bf16[384,384]{1,0:T(8,128)(2,1)S(1)}, u32[]{:S(2)}, u32[]{:S(2)}) %collective-permute-start.12) | collective-permute-done | bytes 294944 | tf_op jit(solution)/shard_map/ppermute | solution.py:391
  46.7 3.4 %collective-permute-start.14 = (bf16[192,384]{1,0:T(8,128)(2,1)S(1)}, bf16[192,384]{1,0:T(8,128)(2,1)S(1)}, u32[]{:S(2)}, u32[]{:S(2)}) collective-permute-start(bf16[192,384]{1,0:T(8,128)(2,1)S(1)} %get-tuple-element.102), channel_id=1, source_target_pairs={{0,4},{1,5},{4,0},{5,1},{2,6},{3,7},{6,2},{7,3},{8,12},{9,13},{12,... | collective-permute-start | bytes 442376 | tf_op jit(solution)/shard_map/ppermute | solution.py:391
  50.3 3.5 %collective-permute-done.14.recv1_ref = bf16[192,384]{1,0:T(8,128)(2,1)S(1)} collective-permute-done((bf16[192,384]{1,0:T(8,128)(2,1)S(1)}, bf16[192,384]{1,0:T(8,128)(2,1)S(1)}, u32[]{:S(2)}, u32[]{:S(2)}) %collective-permute-start.14) | collective-permute-done | bytes 147488 | tf_op jit(solution)/shard_map/ppermute | solution.py:391
  53.9 1.3 %collective-permute-start.15 = (bf16[56,768]{1,0:T(8,128)(2,1)S(1)}, bf16[56,768]{1,0:T(8,128)(2,1)S(1)}, u32[]{:S(2)}, u32[]{:S(2)}) collective-permute-start(bf16[56,768]{1,0:T(8,128)(2,1)S(1)} %get-tuple-element.104), channel_id=1, source_target_pairs={{0,64},{64,0},{128,192},{192,128},{1,65},{65,1},{129,193},{193,129... | collective-permute-start | bytes 258056 | tf_op jit(solution)/shard_map/ppermute | solution.py:391
  55.1 1.7 %collective-permute-start.16 = (bf16[56,768]{1,0:T(8,128)(2,1)S(1)}, bf16[56,768]{1,0:T(8,128)(2,1)S(1)}, u32[]{:S(2)}, u32[]{:S(2)}) collective-permute-start(bf16[56,768]{1,0:T(8,128)(2,1)S(1)} %get-tuple-element.105), channel_id=1, source_target_pairs={{0,128},{64,192},{128,0},{192,64},{1,129},{65,193},{129,1},{193,65... | collective-permute-start | bytes 258056 | tf_op jit(solution)/shard_map/ppermute | solution.py:391
  56.8 2.0 %collective-permute-start.17 = (bf16[56,768]{1,0:T(8,128)(2,1)S(1)}, bf16[56,768]{1,0:T(8,128)(2,1)S(1)}, u32[]{:S(2)}, u32[]{:S(2)}) collective-permute-start(bf16[56,768]{1,0:T(8,128)(2,1)S(1)} %get-tuple-element.106), channel_id=1, source_target_pairs={{0,192},{64,128},{128,64},{192,0},{1,193},{65,129},{129,65},{193,1... | collective-permute-start | bytes 258056 | tf_op jit(solution)/shard_map/ppermute | solution.py:391
  58.9 1.6 %collective-permute-start.7 = (bf16[48,768]{1,0:T(8,128)(2,1)S(1)}, bf16[48,768]{1,0:T(8,128)(2,1)S(1)}, u32[]{:S(2)}, u32[]{:S(2)}) collective-permute-start(bf16[48,768]{1,0:T(8,128)(2,1)S(1)} %get-tuple-element.90), channel_id=1, source_target_pairs={{0,4},{1,5},{4,0},{5,1},{2,6},{3,7},{6,2},{7,3},{8,12},{9,13},{12,... | collective-permute-start | bytes 221192 | tf_op jit(solution)/shard_map/ppermute | solution.py:391
  60.5 1.3 %collective-permute-start.8 = (bf16[48,768]{1,0:T(8,128)(2,1)S(1)}, bf16[48,768]{1,0:T(8,128)(2,1)S(1)}, u32[]{:S(2)}, u32[]{:S(2)}) collective-permute-start(bf16[48,768]{1,0:T(8,128)(2,1)S(1)} %get-tuple-element.91), channel_id=1, source_target_pairs={{0,5},{1,4},{4,1},{5,0},{2,7},{3,6},{6,3},{7,2},{8,13},{9,12},{12,... | collective-permute-start | bytes 221192 | tf_op jit(solution)/shard_map/ppermute | solution.py:391
  61.8 1.4 %collective-permute-done.7.a2 = bf16[48,768]{1,0:T(8,128)(2,1)S(1)} collective-permute-done((bf16[48,768]{1,0:T(8,128)(2,1)S(1)}, bf16[48,768]{1,0:T(8,128)(2,1)S(1)}, u32[]{:S(2)}, u32[]{:S(2)}) %collective-permute-start.7) | collective-permute-done | bytes 73760 | tf_op jit(solution)/shard_map/ppermute | solution.py:391
  63.2 1.6 %collective-permute-done.8.a3 = bf16[48,768]{1,0:T(8,128)(2,1)S(1)} collective-permute-done((bf16[48,768]{1,0:T(8,128)(2,1)S(1)}, bf16[48,768]{1,0:T(8,128)(2,1)S(1)}, u32[]{:S(2)}, u32[]{:S(2)}) %collective-permute-start.8) | collective-permute-done | bytes 73760 | tf_op jit(solution)/shard_map/ppermute | solution.py:391
  65.0 16.1 %all_to_all.5.in_ref = bf16[8,8,1536]{2,1,0:T(8,128)(2,1)S(1)} all-to-all(bf16[8,8,1536]{2,1,0:T(8,128)(2,1)S(1)} %plane_sum.1), channel_id=1, replica_groups=mesh['y'=4,'z'=8,'xl'=2,'c'=2,'xh'=2] {'z'}, dimensions={0} | all-to-all | bytes 393216 | tf_op jit(solution)/shard_map/all_to_all | solution.py:423
  81.7 2.0 %collective-permute-start.18 = (bf16[8,1536]{1,0:T(8,128)(2,1)S(1)}, bf16[8,1536]{1,0:T(8,128)(2,1)S(1)}, u32[]{:S(2)}, u32[]{:S(2)}) collective-permute-start(bf16[8,1536]{1,0:T(8,128)(2,1)S(1)} %get-tuple-element.107.mine_ref), channel_id=1, source_target_pairs={{0,1},{1,0},{2,3},{3,2},{4,5},{5,4},{6,7},{7,6},{8,9},{9,8},{10,11... | collective-permute-start | bytes 73736 | tf_op jit(solution)/shard_map/ppermute | solution.py:429
  83.6 1.6 %token_outputs.1 = (bf16[256,768]{1,0:T(8,128)(2,1)}, bf16[256,768]{1,0:T(8,128)(2,1)}) custom-call(f32[768]{0:T(1024)S(1)} %copy-done.3, bf16[256,768]{1,0:T(8,128)(2,1)S(1)} %bitcast.11, bf16[256,768]{1,0:T(8,128)(2,1)S(1)} %bitcast.13, bf16[256,768]{1,0:T(8,128)(2,1)S(1)} %get-tuple-element.74.mixed_ref, bf16[768,768]{1,0:T(8,128)(2,1)S(1)} %copy-done, ...), custom_call_target="tpu_custom_call" | custom-call | tf_op jit(solution)/shard_map/token_outputs/pallas_call | solution.py:345
  85.2 1.8 %collective-permute-done.18.other_ref = bf16[8,1536]{1,0:T(8,128)(2,1)S(1)} collective-permute-done((bf16[8,1536]{1,0:T(8,128)(2,1)S(1)}, bf16[8,1536]{1,0:T(8,128)(2,1)S(1)}, u32[]{:S(2)}, u32[]{:S(2)}) %collective-permute-start.18) | collective-permute-done | bytes 24608 | tf_op jit(solution)/shard_map/ppermute | solution.py:429
  87.0 1.2 %finish.1 = (f32[6,2304]{1,0:T(8,128)}, f32[6,768]{1,0:T(8,128)}) custom-call(s32[5]{0:T(128)S(1)} %stack.27.at_ref, bf16[8,1536]{1,0:T(8,128)(2,1)S(1)} %get-tuple-element.107.mine_ref, bf16[8,1536]{1,0:T(8,128)(2,1)S(1)} %collective-permute-done.18.other_ref), custom_call_target="tpu_custom_call" | custom-call | tf_op jit(solution)/shard_map/finish/pallas_call | solution.py:345
  (37 shorter events, 6.4 us)
Async XLA Ops:
  0.6 9.3 %collective-permute-start = (bf16[256,768]{1,0:T(8,128)(2,1)}, bf16[256,768]{1,0:T(8,128)(2,1)S(1)}, u32[]{:S(2)}, u32[]{:S(2)}) collective-permute-start(bf16[256,768]{1,0:T(8,128)(2,1)} %bitcast.9), channel_id=1, source_target_pairs={{0,2},{2,4},{4,6},{6,8},{8,10},{10,12},{12,14},{14,16},{16,18},{18... | collective-permute-start | bytes 1179656 | tf_op jit(solution)/shard_map/ppermute | solution.py:363
  19.3 6.6 %collective-permute-start.1 = (bf16[384,1536]{1,0:T(8,128)(2,1)S(1)}, bf16[384,1536]{1,0:T(8,128)(2,1)S(1)}, u32[]{:S(2)}, u32[]{:S(2)}) collective-permute-start(bf16[384,1536]{1,0:T(8,128)(2,1)S(1)} %get-tuple-element.80), channel_id=1, source_target_pairs={{0,2},{2,0},{1,3},{3,1},{4,6},{6,4},{5,7},{7,5},{8,10},{10,8},{9,1... | collective-permute-start | bytes 3538952 | tf_op jit(solution)/shard_map/ppermute | solution.py:387
  25.3 5.9 %collective-permute-start.9 = (bf16[384,1536]{1,0:T(8,128)(2,1)S(1)}, bf16[384,1536]{1,0:T(8,128)(2,1)S(1)}, u32[]{:S(2)}, u32[]{:S(2)}) collective-permute-start(bf16[384,1536]{1,0:T(8,128)(2,1)S(1)} %get-tuple-element.93), channel_id=1, source_target_pairs={{0,2},{2,0},{1,3},{3,1},{4,6},{6,4},{5,7},{7,5},{8,10},{10,8},{9,1... | collective-permute-start | bytes 3538952 | tf_op jit(solution)/shard_map/ppermute | solution.py:387
  26.2 11.1 %collective-permute-start.2 = (bf16[192,768]{1,0:T(8,128)(2,1)S(1)}, bf16[192,768]{1,0:T(8,128)(2,1)S(1)}, u32[]{:S(2)}, u32[]{:S(2)}) collective-permute-start(bf16[192,768]{1,0:T(8,128)(2,1)S(1)} %get-tuple-element.81), channel_id=1, source_target_pairs={{0,64},{64,0},{128,192},{192,128},{1,65},{65,1},{129,193},{193,129... | collective-permute-start | bytes 884744 | tf_op jit(solution)/shard_map/ppermute | solution.py:391
  27.9 9.9 %collective-permute-start.3 = (bf16[192,768]{1,0:T(8,128)(2,1)S(1)}, bf16[192,768]{1,0:T(8,128)(2,1)S(1)}, u32[]{:S(2)}, u32[]{:S(2)}) collective-permute-start(bf16[192,768]{1,0:T(8,128)(2,1)S(1)} %get-tuple-element.83), channel_id=1, source_target_pairs={{0,192},{64,128},{128,64},{192,0},{1,193},{65,129},{129,65},{193,1... | collective-permute-start | bytes 884744 | tf_op jit(solution)/shard_map/ppermute | solution.py:391
  30.0 1.2 %collective-permute-start.10 = (f32[2,768]{1,0:T(2,128)S(1)}, f32[2,768]{1,0:T(2,128)S(1)}, u32[]{:S(2)}, u32[]{:S(2)}) collective-permute-start(f32[2,768]{1,0:T(2,128)S(1)} %get-tuple-element.94.vec_ref), channel_id=1, source_target_pairs={{0,2},{2,0},{1,3},{3,1},{4,6},{6,4},{5,7},{7,5},{8,10},{10,8},{9,1... | collective-permute-start | bytes 18440 | tf_op jit(solution)/shard_map/ppermute | solution.py:387
  31.5 13.8 %collective-permute-start.11 = (bf16[392,384]{1,0:T(8,128)(2,1)S(1)}, bf16[392,384]{1,0:T(8,128)(2,1)S(1)}, u32[]{:S(2)}, u32[]{:S(2)}) collective-permute-start(bf16[392,384]{1,0:T(8,128)(2,1)S(1)} %get-tuple-element.95), channel_id=1, source_target_pairs={{0,4},{1,5},{4,0},{5,1},{2,6},{3,7},{6,2},{7,3},{8,12},{9,13},{12,... | collective-permute-start | bytes 903176 | tf_op jit(solution)/shard_map/ppermute | solution.py:391
  36.5 8.8 %collective-permute-start.12 = (bf16[384,384]{1,0:T(8,128)(2,1)S(1)}, bf16[384,384]{1,0:T(8,128)(2,1)S(1)}, u32[]{:S(2)}, u32[]{:S(2)}) collective-permute-start(bf16[384,384]{1,0:T(8,128)(2,1)S(1)} %get-tuple-element.97), channel_id=1, source_target_pairs={{0,5},{1,4},{4,1},{5,0},{2,7},{3,6},{6,3},{7,2},{8,13},{9,12},{12,... | collective-permute-start | bytes 884744 | tf_op jit(solution)/shard_map/ppermute | solution.py:391
  37.9 12.2 %collective-permute-start.4 = (bf16[96,768]{1,0:T(8,128)(2,1)S(1)}, bf16[96,768]{1,0:T(8,128)(2,1)S(1)}, u32[]{:S(2)}, u32[]{:S(2)}) collective-permute-start(bf16[96,768]{1,0:T(8,128)(2,1)S(1)} %get-tuple-element.86), channel_id=1, source_target_pairs={{0,192},{64,128},{128,64},{192,0},{1,193},{65,129},{129,65},{193,1... | collective-permute-start | bytes 442376 | tf_op jit(solution)/shard_map/ppermute | solution.py:391
  40.1 10.0 %collective-permute-start.5 = (bf16[96,768]{1,0:T(8,128)(2,1)S(1)}, bf16[96,768]{1,0:T(8,128)(2,1)S(1)}, u32[]{:S(2)}, u32[]{:S(2)}) collective-permute-start(bf16[96,768]{1,0:T(8,128)(2,1)S(1)} %get-tuple-element.87), channel_id=1, source_target_pairs={{0,64},{64,0},{128,192},{192,128},{1,65},{65,1},{129,193},{193,129... | collective-permute-start | bytes 442376 | tf_op jit(solution)/shard_map/ppermute | solution.py:391
  45.5 8.3 %collective-permute-start.13 = (bf16[200,384]{1,0:T(8,128)(2,1)S(1)}, bf16[200,384]{1,0:T(8,128)(2,1)S(1)}, u32[]{:S(2)}, u32[]{:S(2)}) collective-permute-start(bf16[200,384]{1,0:T(8,128)(2,1)S(1)} %get-tuple-element.101), channel_id=1, source_target_pairs={{0,5},{1,4},{4,1},{5,0},{2,7},{3,6},{6,3},{7,2},{8,13},{9,12},{12,... | collective-permute-start | bytes 460808 | tf_op jit(solution)/shard_map/ppermute | solution.py:391
  46.7 7.1 %collective-permute-start.14 = (bf16[192,384]{1,0:T(8,128)(2,1)S(1)}, bf16[192,384]{1,0:T(8,128)(2,1)S(1)}, u32[]{:S(2)}, u32[]{:S(2)}) collective-permute-start(bf16[192,384]{1,0:T(8,128)(2,1)S(1)} %get-tuple-element.102), channel_id=1, source_target_pairs={{0,4},{1,5},{4,0},{5,1},{2,6},{3,7},{6,2},{7,3},{8,12},{9,13},{12,... | collective-permute-start | bytes 442376 | tf_op jit(solution)/shard_map/ppermute | solution.py:391
  50.2 33.5 %copy-start = (bf16[768,768]{1,0:T(8,128)(2,1)S(1)}, bf16[768,768]{1,0:T(8,128)(2,1)}, u32[]{:S(2)}) copy-start(bf16[768,768]{1,0:T(8,128)(2,1)} %wo_ref.1) | copy-start | bytes 3538948
  50.2 33.5 %copy-start.1 = (bf16[1,256,768]{2,1,0:T(8,128)(2,1)S(1)}, bf16[1,256,768]{2,1,0:T(8,128)(2,1)}, u32[]{:S(2)}) copy-start(bf16[1,256,768]{2,1,0:T(8,128)(2,1)} %param.6) | copy-start | bytes 1179652
  50.2 33.5 %copy-start.2 = (bf16[1,256,768]{2,1,0:T(8,128)(2,1)S(1)}, bf16[1,256,768]{2,1,0:T(8,128)(2,1)}, u32[]{:S(2)}) copy-start(bf16[1,256,768]{2,1,0:T(8,128)(2,1)} %param.7) | copy-start | bytes 1179652
  50.2 33.4 %copy-start.3 = (f32[768]{0:T(1024)S(1)}, f32[768]{0:T(1024)}, u32[]{:S(2)}) copy-start(f32[768]{0:T(1024)} %gain_ref.1) | copy-start | bytes 9220
  50.2 10.3 %collective-permute-start.6 = (bf16[48,768]{1,0:T(8,128)(2,1)S(1)}, bf16[48,768]{1,0:T(8,128)(2,1)S(1)}, u32[]{:S(2)}, u32[]{:S(2)}) collective-permute-start(bf16[48,768]{1,0:T(8,128)(2,1)S(1)} %get-tuple-element.89), channel_id=1, source_target_pairs={{0,1},{1,0},{4,5},{5,4},{2,3},{3,2},{6,7},{7,6},{8,9},{9,8},{12,13... | collective-permute-start | bytes 221192 | tf_op jit(solution)/shard_map/ppermute | solution.py:391
  53.9 11.0 %collective-permute-start.15 = (bf16[56,768]{1,0:T(8,128)(2,1)S(1)}, bf16[56,768]{1,0:T(8,128)(2,1)S(1)}, u32[]{:S(2)}, u32[]{:S(2)}) collective-permute-start(bf16[56,768]{1,0:T(8,128)(2,1)S(1)} %get-tuple-element.104), channel_id=1, source_target_pairs={{0,64},{64,0},{128,192},{192,128},{1,65},{65,1},{129,193},{193,129... | collective-permute-start | bytes 258056 | tf_op jit(solution)/shard_map/ppermute | solution.py:391
  55.1 9.7 %collective-permute-start.16 = (bf16[56,768]{1,0:T(8,128)(2,1)S(1)}, bf16[56,768]{1,0:T(8,128)(2,1)S(1)}, u32[]{:S(2)}, u32[]{:S(2)}) collective-permute-start(bf16[56,768]{1,0:T(8,128)(2,1)S(1)} %get-tuple-element.105), channel_id=1, source_target_pairs={{0,128},{64,192},{128,0},{192,64},{1,129},{65,193},{129,1},{193,65... | collective-permute-start | bytes 258056 | tf_op jit(solution)/shard_map/ppermute | solution.py:391
  56.8 8.0 %collective-permute-start.17 = (bf16[56,768]{1,0:T(8,128)(2,1)S(1)}, bf16[56,768]{1,0:T(8,128)(2,1)S(1)}, u32[]{:S(2)}, u32[]{:S(2)}) collective-permute-start(bf16[56,768]{1,0:T(8,128)(2,1)S(1)} %get-tuple-element.106), channel_id=1, source_target_pairs={{0,192},{64,128},{128,64},{192,0},{1,193},{65,129},{129,65},{193,1... | collective-permute-start | bytes 258056 | tf_op jit(solution)/shard_map/ppermute | solution.py:391
  58.9 4.4 %collective-permute-start.7 = (bf16[48,768]{1,0:T(8,128)(2,1)S(1)}, bf16[48,768]{1,0:T(8,128)(2,1)S(1)}, u32[]{:S(2)}, u32[]{:S(2)}) collective-permute-start(bf16[48,768]{1,0:T(8,128)(2,1)S(1)} %get-tuple-element.90), channel_id=1, source_target_pairs={{0,4},{1,5},{4,0},{5,1},{2,6},{3,7},{6,2},{7,3},{8,12},{9,13},{12,... | collective-permute-start | bytes 221192 | tf_op jit(solution)/shard_map/ppermute | solution.py:391
  60.5 4.4 %collective-permute-start.8 = (bf16[48,768]{1,0:T(8,128)(2,1)S(1)}, bf16[48,768]{1,0:T(8,128)(2,1)S(1)}, u32[]{:S(2)}, u32[]{:S(2)}) collective-permute-start(bf16[48,768]{1,0:T(8,128)(2,1)S(1)} %get-tuple-element.91), channel_id=1, source_target_pairs={{0,5},{1,4},{4,1},{5,0},{2,7},{3,6},{6,3},{7,2},{8,13},{9,12},{12,... | collective-permute-start | bytes 221192 | tf_op jit(solution)/shard_map/ppermute | solution.py:391
  81.7 5.3 %collective-permute-start.18 = (bf16[8,1536]{1,0:T(8,128)(2,1)S(1)}, bf16[8,1536]{1,0:T(8,128)(2,1)S(1)}, u32[]{:S(2)}, u32[]{:S(2)}) collective-permute-start(bf16[8,1536]{1,0:T(8,128)(2,1)S(1)} %get-tuple-element.107.mine_ref), channel_id=1, source_target_pairs={{0,1},{1,0},{2,3},{3,2},{4,5},{5,4},{6,7},{7,6},{8,9},{9,8},{10,11... | collective-permute-start | bytes 73736 | tf_op jit(solution)/shard_map/ppermute | solution.py:429

commit v7 on v6

--- a/solution.py
+++ b/solution.py
@@ -137,11 +137,12 @@
 def put_rows(send_ref, keep_ref, slot, xh, lhs, rhs):
     first, second = rhs[:, :384], rhs[:, 384:]
     mine = xh == 0
-    for r in range(2):
-        part = jnp.where(mine, first, second) if r == 0 else jnp.where(mine, second, first)
-        at = 768 * r + 384 * slot
-        send_ref[:, at : at + 384] = nn(lhs[:384], part).astype(BF)
-        keep_ref[:, at : at + 384] = nn(lhs[384:], part).astype(BF)
+    rhs = jnp.concatenate([jnp.where(mine, first, second), jnp.where(mine, second, first)], axis=1)
+    for out_ref, rows in ((send_ref, lhs[:384]), (keep_ref, lhs[384:])):
+        sums = nn(rows, rhs).astype(BF)
+        for r in range(2):
+            at = 768 * r + 384 * slot
+            out_ref[0:384, at : at + 384] = sums[:, 384 * r : 384 * r + 384]
 
 
 def group_outputs(g, slot, at_ref, npt_all, w_ref, grads, send_ref, keep_ref):
@@ -177,7 +178,7 @@
 
 
 def second_kernel(at_ref, w_ref, mt_ref, cot_ref, qkv_ref, dmix_ref, mixed_in, dn_in, dnm_in, kvm_ref, npt_all_ref,
-                  xhat_ref, xhatm_ref, send_ref, keep_ref, vec_ref, mixed_ref, dn_ref):
+                  xhat_ref, xhatm_ref, send_ref, keep_ref, mixed_ref, dn_ref):
     mixed, *grads = head_group(2, at_ref[4] > 0, qkv_ref, kvm_ref, dmix_ref)
     mixed_ref[:, : 2 * GW] = mixed_in[...]
     mixed_ref[:, 2 * GW :] = mixed
@@ -186,8 +187,13 @@
     put_rows(send_ref, keep_ref, 1, at_ref[3], lhs, cot_ref[...])
     dn, dnm = dn_in[...] + own, dnm_in[...] + mem
     dn_ref[...] = dn
-    vec_ref[0:1, :] = jnp.sum(dn * xhat_ref[...] + dnm * xhatm_ref[...], axis=0, keepdims=True)
-    vec_ref[1:2, :] = jnp.sum(dn + dnm, axis=0, keepdims=True)
+    vec = jnp.concatenate(
+        [jnp.sum(dn * xhat_ref[...] + dnm * xhatm_ref[...], axis=0, keepdims=True), jnp.sum(dn + dnm, axis=0, keepdims=True)],
+        axis=0,
+    )
+    rows = split_rows(vec)
+    for out_ref in (send_ref, keep_ref):
+        out_ref[384:392, 0:D] = rows
 
 
 def token_kernel(gain_ref, x_ref, cot_ref, mixed_ref, wo_ref, dn_ref, xhat_ref, rstd_ref, out_ref, dx_ref):
@@ -247,7 +253,7 @@
                 ).astype(BF)
 
 
-def pair_b_kernel(keep_ref, recv_ref, vec_ref, vecr_ref, *outs):
+def pair_b_kernel(keep_ref, recv_ref, *outs):
     for part, groups in enumerate(halving_order(RING_X)):
         for kept, places in enumerate(groups):
             out = outs[2 * part + kept]
@@ -258,7 +264,7 @@
                     out[192 * i + 48 * y : 192 * i + 48 * y + 48, :] = (
                         keep_ref[rows, at : at + 384].astype(F32) + recv_ref[rows, at : at + 384].astype(F32)
                     ).astype(BF)
-    vec = fold_rows(vec_ref[...] + vecr_ref[...])
+    vec = fold_rows(join_rows(keep_ref[384:392, 0:D]) + join_rows(recv_ref[384:392, 0:D]))
     outs[0][384:392, :] = vec
     outs[1][384:392, :] = vec
 
@@ -377,9 +383,9 @@
         [wide, wide, sds(T, 2 * GW), row, row, sds(T, 2 * D), sds(D, 2 * T), row],
         [at, gain_v, bias_v, xp, w, mt, qkv, dmix, npt], 1, limit=LIMIT,
     )
-    send_b, keep_b, vec, mixed, dn = call(
+    send_b, keep_b, mixed, dn = call(
         second_kernel, "heads_and_output_weight",
-        [wide, wide, sds(2, D, dtype=F32), tokens, row],
+        [sds(392, 1536), sds(392, 1536), tokens, row],
         [at, w, mt, cot_v, qkv, dmix, mixed, dn, dnm, kvm, npt_all, xhat, xhatm], 1, limit=LIMIT,
     )
 
@@ -397,7 +403,7 @@
     send0_a, keep0_a, send1_a, keep1_a = call(pair_a_kernel, "pair_sum_a", [half] * 4, [keep_a, swap(send_a)])
     send0_b, keep0_b, send1_b, keep1_b = call(
         pair_b_kernel, "pair_sum_b", [sds(392, 384), sds(392, 384), sds(384, 384), sds(384, 384)],
-        [keep_b, swap(send_b), vec, swap(vec)],
+        [keep_b, swap(send_b)],
     )
     got_a = [permute(send0_a, "y", RING_Y[0]), permute(send1_a, "y", RING_Y[1])]
     got_b = [permute(send0_b, ROW, RING_X[0]), permute(send1_b, ROW, RING_X[1])]

time: 88.3 us -> 86.2 us (0.976)
  waiting for transfers between devices: 17.3 us -> 14.6 us
    ppermute x14, waiting for transfers between devices: 12.2 us -> 10.7 us  [permute(): return lax.ppermute(block, axes, [(i, i ^ k) for i in range(n)])]
    ppermute x3 -> x2, waiting for transfers between devices: 1.17 us -> 0.01 us  [swap(): return lax.ppermute(block, 'c', [(0, 1), (1, 0)])]
  transfers between devices with their start and end apart: 19 -> 18, of which waited for: 8 -> 7; matrix products, arithmetic and copies ran while one was open for 0% -> 0% of each run, Pallas kernels for 15% -> 15%
where the time goes in v7:
time: 86.2 us; the launch traced here: 85.3 us
  starting transfers between devices  29.7 us (34%)
  Pallas kernels  24 us (28%)
  blocking collectives  16.1 us (19%)
  waiting for transfers between devices  14.6 us (17%)
    ppermute x14, starting transfers between devices, permute(): return lax.ppermute(block, axes, [(i, i ^ k) for i in range(n)])  24.8 us
    pallas_call x13, Pallas kernels, call(): pl.pallas_call(kernel, name=name, in_specs=specs, out_specs=[VM] * len(ou...  24 us
    all_to_all x1, blocking collectives, on_device(): mine = lax.all_to_all(mine, 'z', 0, 0, tiled=True)  16.1 us
    ppermute x14, waiting for transfers between devices, permute(): return lax.ppermute(block, axes, [(i, i ^ k) for i in range(n)])  10.7 us
    ppermute x1, waiting for transfers between devices, on_device(): xp = lax.ppermute(x, SEQ, [(i, i + 1) for i in range(seq - 1)])  2.21 us
    ppermute x1, starting transfers between devices, on_device(): other = lax.ppermute(mine, 'xh', [(0, 1), (1, 0)])  2.11 us
    ppermute x1, starting transfers between devices, on_device(): xp = lax.ppermute(x, SEQ, [(i, i + 1) for i in range(seq - 1)])  1.92 us
  transfers between devices with their start and end apart: 18, of which 7 were waited for; matrix products, arithmetic and copies ran while one was open for 0% of the time, Pallas kernels for 15%

profile of v7, /device:TPU:2, one launch (start us, length us, event | category | flops | bytes accessed | tf_op | source)
XLA Modules:
  0.0 85.3 jit_solution(12082119561607206556)
XLA Ops:
  0.6 1.9 %collective-permute-start = (bf16[256,768]{1,0:T(8,128)(2,1)}, bf16[256,768]{1,0:T(8,128)(2,1)S(1)}, u32[]{:S(2)}, u32[]{:S(2)}) collective-permute-start(bf16[256,768]{1,0:T(8,128)(2,1)} %bitcast.9), channel_id=1, source_target_pairs={{0,2},{2,4},{4,6},{6,8},{8,10},{10,12},{12,14},{14,16},{16,18},{18... | collective-permute-start | bytes 1179656 | tf_op jit(solution)/shard_map/ppermute | solution.py:369
  2.7 5.1 %own_part.1 = (bf16[256,2304]{1,0:T(8,128)(2,1)S(1)}, bf16[256,768]{1,0:T(8,128)(2,1)S(1)}, bf16[768,256]{1,0:T(8,128)(2,1)S(1)}, f32[256,768]{1,0:T(8,128)S(1)}...) custom-call(s32[5]{0:T(128)S(1)} %stack.27.at_ref, ...), custom_call_target="tpu_custom_call" | custom-call | tf_op jit(solution)/shard_map/own_part/pallas_call | solution.py:351
  7.7 2.2 %collective-permute-done.xp_ref = bf16[256,768]{1,0:T(8,128)(2,1)S(1)} collective-permute-done((bf16[256,768]{1,0:T(8,128)(2,1)}, bf16[256,768]{1,0:T(8,128)(2,1)S(1)}, u32[]{:S(2)}, u32[]{:S(2)}) %collective-permute-start) | collective-permute-done | bytes 393248 | tf_op jit(solution)/shard_map/ppermute | solution.py:369
  9.9 9.0 %memory_and_heads.1 = (bf16[384,1536]{1,0:T(8,128)(2,1)S(1)}, bf16[384,1536]{1,0:T(8,128)(2,1)S(1)}, bf16[256,512]{1,0:T(8,128)(2,1)S(1)}, f32[256,768]{1,0:T(8,...) custom-call(s32[5]{0:T(128)S(1)} %stack.27.at_ref, ...), custom_call_target="tpu_custom_call" | custom-call | tf_op jit(solution)/shard_map/memory_and_heads/pallas_call | solution.py:351
  19.2 5.4 %heads_and_output_weight.1 = (bf16[392,1536]{1,0:T(8,128)(2,1)S(1)}, bf16[392,1536]{1,0:T(8,128)(2,1)S(1)}, bf16[256,768]{1,0:T(8,128)(2,1)S(1)}, f32[256,768]{1,0:T(8,128)S(1)}) custom-call(s32[5]{0:T(128)S(1)} %stack.27.at_ref, bf16[3,768,768]{2,1,0:T(8,128)(2,1)S(1)} %get-tuple-element.58.w_ref, bf16[768,768]{1,0:T(8,128)(2,1)S(1)} %get-tuple-element.59.mt_ref, ...), custom_call_target="tpu_custom_call" | custom-call | tf_op jit(solution)/shard_map/heads_and_output_weight/pallas_call | solution.py:351
  25.5 1.7 %collective-permute-start.2 = (bf16[192,768]{1,0:T(8,128)(2,1)S(1)}, bf16[192,768]{1,0:T(8,128)(2,1)S(1)}, u32[]{:S(2)}, u32[]{:S(2)}) collective-permute-start(bf16[192,768]{1,0:T(8,128)(2,1)S(1)} %get-tuple-element.80), channel_id=1, source_target_pairs={{0,64},{64,0},{128,192},{192,128},{1,65},{65,1},{129,193},{193,129... | collective-permute-start | bytes 884744 | tf_op jit(solution)/shard_map/ppermute | solution.py:397
  27.2 2.2 %collective-permute-start.3 = (bf16[192,768]{1,0:T(8,128)(2,1)S(1)}, bf16[192,768]{1,0:T(8,128)(2,1)S(1)}, u32[]{:S(2)}, u32[]{:S(2)}) collective-permute-start(bf16[192,768]{1,0:T(8,128)(2,1)S(1)} %get-tuple-element.82), channel_id=1, source_target_pairs={{0,192},{64,128},{128,64},{192,0},{1,193},{65,129},{129,65},{193,1... | collective-permute-start | bytes 884744 | tf_op jit(solution)/shard_map/ppermute | solution.py:397
  29.7 5.0 %collective-permute-start.10 = (bf16[392,384]{1,0:T(8,128)(2,1)S(1)}, bf16[392,384]{1,0:T(8,128)(2,1)S(1)}, u32[]{:S(2)}, u32[]{:S(2)}) collective-permute-start(bf16[392,384]{1,0:T(8,128)(2,1)S(1)} %get-tuple-element.93), channel_id=1, source_target_pairs={{0,4},{1,5},{4,0},{5,1},{2,6},{3,7},{6,2},{7,3},{8,12},{9,13},{12,... | collective-permute-start | bytes 903176 | tf_op jit(solution)/shard_map/ppermute | solution.py:397
  35.5 1.6 %collective-permute-done.3.recv1_ref = bf16[192,768]{1,0:T(8,128)(2,1)S(1)} collective-permute-done((bf16[192,768]{1,0:T(8,128)(2,1)S(1)}, bf16[192,768]{1,0:T(8,128)(2,1)S(1)}, u32[]{:S(2)}, u32[]{:S(2)}) %collective-permute-start.3) | collective-permute-done | bytes 294944 | tf_op jit(solution)/shard_map/ppermute | solution.py:397
  37.2 2.3 %collective-permute-start.4 = (bf16[96,768]{1,0:T(8,128)(2,1)S(1)}, bf16[96,768]{1,0:T(8,128)(2,1)S(1)}, u32[]{:S(2)}, u32[]{:S(2)}) collective-permute-start(bf16[96,768]{1,0:T(8,128)(2,1)S(1)} %get-tuple-element.85), channel_id=1, source_target_pairs={{0,192},{64,128},{128,64},{192,0},{1,193},{65,129},{129,65},{193,1... | collective-permute-start | bytes 442376 | tf_op jit(solution)/shard_map/ppermute | solution.py:397
  39.5 3.3 %collective-permute-done.11.recv1_ref = bf16[384,384]{1,0:T(8,128)(2,1)S(1)} collective-permute-done((bf16[384,384]{1,0:T(8,128)(2,1)S(1)}, bf16[384,384]{1,0:T(8,128)(2,1)S(1)}, u32[]{:S(2)}, u32[]{:S(2)}) %collective-permute-start.11) | collective-permute-done | bytes 294944 | tf_op jit(solution)/shard_map/ppermute | solution.py:397
  42.9 2.3 %collective-permute-start.12 = (bf16[200,384]{1,0:T(8,128)(2,1)S(1)}, bf16[200,384]{1,0:T(8,128)(2,1)S(1)}, u32[]{:S(2)}, u32[]{:S(2)}) collective-permute-start(bf16[200,384]{1,0:T(8,128)(2,1)S(1)} %get-tuple-element.99), channel_id=1, source_target_pairs={{0,5},{1,4},{4,1},{5,0},{2,7},{3,6},{6,3},{7,2},{8,13},{9,12},{12,... | collective-permute-start | bytes 460808 | tf_op jit(solution)/shard_map/ppermute | solution.py:397
  45.3 2.3 %collective-permute-start.13 = (bf16[192,384]{1,0:T(8,128)(2,1)S(1)}, bf16[192,384]{1,0:T(8,128)(2,1)S(1)}, u32[]{:S(2)}, u32[]{:S(2)}) collective-permute-start(bf16[192,384]{1,0:T(8,128)(2,1)S(1)} %get-tuple-element.100), channel_id=1, source_target_pairs={{0,4},{1,5},{4,0},{5,1},{2,6},{3,7},{6,2},{7,3},{8,12},{9,13},{12,... | collective-permute-start | bytes 442376 | tf_op jit(solution)/shard_map/ppermute | solution.py:397
  47.8 2.9 %collective-permute-done.13.recv1_ref = bf16[192,384]{1,0:T(8,128)(2,1)S(1)} collective-permute-done((bf16[192,384]{1,0:T(8,128)(2,1)S(1)}, bf16[192,384]{1,0:T(8,128)(2,1)S(1)}, u32[]{:S(2)}, u32[]{:S(2)}) %collective-permute-start.13) | collective-permute-done | bytes 147488 | tf_op jit(solution)/shard_map/ppermute | solution.py:397
  50.8 2.7 %collective-permute-start.14 = (bf16[56,768]{1,0:T(8,128)(2,1)S(1)}, bf16[56,768]{1,0:T(8,128)(2,1)S(1)}, u32[]{:S(2)}, u32[]{:S(2)}) collective-permute-start(bf16[56,768]{1,0:T(8,128)(2,1)S(1)} %get-tuple-element.102), channel_id=1, source_target_pairs={{0,64},{64,0},{128,192},{192,128},{1,65},{65,1},{129,193},{193,129... | collective-permute-start | bytes 258056 | tf_op jit(solution)/shard_map/ppermute | solution.py:397
  53.4 2.3 %collective-permute-start.15 = (bf16[56,768]{1,0:T(8,128)(2,1)S(1)}, bf16[56,768]{1,0:T(8,128)(2,1)S(1)}, u32[]{:S(2)}, u32[]{:S(2)}) collective-permute-start(bf16[56,768]{1,0:T(8,128)(2,1)S(1)} %get-tuple-element.103), channel_id=1, source_target_pairs={{0,128},{64,192},{128,0},{192,64},{1,129},{65,193},{129,1},{193,65... | collective-permute-start | bytes 258056 | tf_op jit(solution)/shard_map/ppermute | solution.py:397
  56.2 1.4 %collective-permute-start.7 = (bf16[48,768]{1,0:T(8,128)(2,1)S(1)}, bf16[48,768]{1,0:T(8,128)(2,1)S(1)}, u32[]{:S(2)}, u32[]{:S(2)}) collective-permute-start(bf16[48,768]{1,0:T(8,128)(2,1)S(1)} %get-tuple-element.89), channel_id=1, source_target_pairs={{0,4},{1,5},{4,0},{5,1},{2,6},{3,7},{6,2},{7,3},{8,12},{9,13},{12,... | collective-permute-start | bytes 221192 | tf_op jit(solution)/shard_map/ppermute | solution.py:397
  57.6 1.5 %collective-permute-start.8 = (bf16[48,768]{1,0:T(8,128)(2,1)S(1)}, bf16[48,768]{1,0:T(8,128)(2,1)S(1)}, u32[]{:S(2)}, u32[]{:S(2)}) collective-permute-start(bf16[48,768]{1,0:T(8,128)(2,1)S(1)} %get-tuple-element.90), channel_id=1, source_target_pairs={{0,5},{1,4},{4,1},{5,0},{2,7},{3,6},{6,3},{7,2},{8,13},{9,12},{12,... | collective-permute-start | bytes 221192 | tf_op jit(solution)/shard_map/ppermute | solution.py:397
  59.0 1.5 %collective-permute-done.7.a2 = bf16[48,768]{1,0:T(8,128)(2,1)S(1)} collective-permute-done((bf16[48,768]{1,0:T(8,128)(2,1)S(1)}, bf16[48,768]{1,0:T(8,128)(2,1)S(1)}, u32[]{:S(2)}, u32[]{:S(2)}) %collective-permute-start.7) | collective-permute-done | bytes 73760 | tf_op jit(solution)/shard_map/ppermute | solution.py:397
  60.5 1.4 %collective-permute-done.8.a3 = bf16[48,768]{1,0:T(8,128)(2,1)S(1)} collective-permute-done((bf16[48,768]{1,0:T(8,128)(2,1)S(1)}, bf16[48,768]{1,0:T(8,128)(2,1)S(1)}, u32[]{:S(2)}, u32[]{:S(2)}) %collective-permute-start.8) | collective-permute-done | bytes 73760 | tf_op jit(solution)/shard_map/ppermute | solution.py:397
  62.1 16.1 %all_to_all.5.in_ref = bf16[8,8,1536]{2,1,0:T(8,128)(2,1)S(1)} all-to-all(bf16[8,8,1536]{2,1,0:T(8,128)(2,1)S(1)} %plane_sum.1), channel_id=1, replica_groups=mesh['y'=4,'z'=8,'xl'=2,'c'=2,'xh'=2] {'z'}, dimensions={0} | all-to-all | bytes 393216 | tf_op jit(solution)/shard_map/all_to_all | solution.py:429
  78.8 2.1 %collective-permute-start.17 = (bf16[8,1536]{1,0:T(8,128)(2,1)S(1)}, bf16[8,1536]{1,0:T(8,128)(2,1)S(1)}, u32[]{:S(2)}, u32[]{:S(2)}) collective-permute-start(bf16[8,1536]{1,0:T(8,128)(2,1)S(1)} %get-tuple-element.105.mine_ref), channel_id=1, source_target_pairs={{0,1},{1,0},{2,3},{3,2},{4,5},{5,4},{6,7},{7,6},{8,9},{9,8},{10,11... | collective-permute-start | bytes 73736 | tf_op jit(solution)/shard_map/ppermute | solution.py:435
  80.9 1.6 %token_outputs.1 = (bf16[256,768]{1,0:T(8,128)(2,1)}, bf16[256,768]{1,0:T(8,128)(2,1)}) custom-call(f32[768]{0:T(1024)S(1)} %copy-done.3, bf16[256,768]{1,0:T(8,128)(2,1)S(1)} %bitcast.11, bf16[256,768]{1,0:T(8,128)(2,1)S(1)} %bitcast.13, bf16[256,768]{1,0:T(8,128)(2,1)S(1)} %get-tuple-element.73.mixed_ref, bf16[768,768]{1,0:T(8,128)(2,1)S(1)} %copy-done, ...), custom_call_target="tpu_custom_call" | custom-call | tf_op jit(solution)/shard_map/token_outputs/pallas_call | solution.py:351
  82.4 1.7 %collective-permute-done.17.other_ref = bf16[8,1536]{1,0:T(8,128)(2,1)S(1)} collective-permute-done((bf16[8,1536]{1,0:T(8,128)(2,1)S(1)}, bf16[8,1536]{1,0:T(8,128)(2,1)S(1)}, u32[]{:S(2)}, u32[]{:S(2)}) %collective-permute-start.17) | collective-permute-done | bytes 24608 | tf_op jit(solution)/shard_map/ppermute | solution.py:435
  (35 shorter events, 5.3 us)
Async XLA Ops:
  0.6 9.3 %collective-permute-start = (bf16[256,768]{1,0:T(8,128)(2,1)}, bf16[256,768]{1,0:T(8,128)(2,1)S(1)}, u32[]{:S(2)}, u32[]{:S(2)}) collective-permute-start(bf16[256,768]{1,0:T(8,128)(2,1)} %bitcast.9), channel_id=1, source_target_pairs={{0,2},{2,4},{4,6},{6,8},{8,10},{10,12},{12,14},{14,16},{16,18},{18... | collective-permute-start | bytes 1179656 | tf_op jit(solution)/shard_map/ppermute | solution.py:369
  18.9 6.3 %collective-permute-start.1 = (bf16[384,1536]{1,0:T(8,128)(2,1)S(1)}, bf16[384,1536]{1,0:T(8,128)(2,1)S(1)}, u32[]{:S(2)}, u32[]{:S(2)}) collective-permute-start(bf16[384,1536]{1,0:T(8,128)(2,1)S(1)} %get-tuple-element.79), channel_id=1, source_target_pairs={{0,2},{2,0},{1,3},{3,1},{4,6},{6,4},{5,7},{7,5},{8,10},{10,8},{9,1... | collective-permute-start | bytes 3538952 | tf_op jit(solution)/shard_map/ppermute | solution.py:393
  24.7 4.7 %collective-permute-start.9 = (bf16[392,1536]{1,0:T(8,128)(2,1)S(1)}, bf16[392,1536]{1,0:T(8,128)(2,1)S(1)}, u32[]{:S(2)}, u32[]{:S(2)}) collective-permute-start(bf16[392,1536]{1,0:T(8,128)(2,1)S(1)} %get-tuple-element.92), channel_id=1, source_target_pairs={{0,2},{2,0},{1,3},{3,1},{4,6},{6,4},{5,7},{7,5},{8,10},{10,8},{9,1... | collective-permute-start | bytes 3612680 | tf_op jit(solution)/shard_map/ppermute | solution.py:393
  25.5 9.9 %collective-permute-start.2 = (bf16[192,768]{1,0:T(8,128)(2,1)S(1)}, bf16[192,768]{1,0:T(8,128)(2,1)S(1)}, u32[]{:S(2)}, u32[]{:S(2)}) collective-permute-start(bf16[192,768]{1,0:T(8,128)(2,1)S(1)} %get-tuple-element.80), channel_id=1, source_target_pairs={{0,64},{64,0},{128,192},{192,128},{1,65},{65,1},{129,193},{193,129... | collective-permute-start | bytes 884744 | tf_op jit(solution)/shard_map/ppermute | solution.py:397
  27.2 9.9 %collective-permute-start.3 = (bf16[192,768]{1,0:T(8,128)(2,1)S(1)}, bf16[192,768]{1,0:T(8,128)(2,1)S(1)}, u32[]{:S(2)}, u32[]{:S(2)}) collective-permute-start(bf16[192,768]{1,0:T(8,128)(2,1)S(1)} %get-tuple-element.82), channel_id=1, source_target_pairs={{0,192},{64,128},{128,64},{192,0},{1,193},{65,129},{129,65},{193,1... | collective-permute-start | bytes 884744 | tf_op jit(solution)/shard_map/ppermute | solution.py:397
  29.7 13.1 %collective-permute-start.10 = (bf16[392,384]{1,0:T(8,128)(2,1)S(1)}, bf16[392,384]{1,0:T(8,128)(2,1)S(1)}, u32[]{:S(2)}, u32[]{:S(2)}) collective-permute-start(bf16[392,384]{1,0:T(8,128)(2,1)S(1)} %get-tuple-element.93), channel_id=1, source_target_pairs={{0,4},{1,5},{4,0},{5,1},{2,6},{3,7},{6,2},{7,3},{8,12},{9,13},{12,... | collective-permute-start | bytes 903176 | tf_op jit(solution)/shard_map/ppermute | solution.py:397
  34.7 8.1 %collective-permute-start.11 = (bf16[384,384]{1,0:T(8,128)(2,1)S(1)}, bf16[384,384]{1,0:T(8,128)(2,1)S(1)}, u32[]{:S(2)}, u32[]{:S(2)}) collective-permute-start(bf16[384,384]{1,0:T(8,128)(2,1)S(1)} %get-tuple-element.95), channel_id=1, source_target_pairs={{0,5},{1,4},{4,1},{5,0},{2,7},{3,6},{6,3},{7,2},{8,13},{9,12},{12,... | collective-permute-start | bytes 884744 | tf_op jit(solution)/shard_map/ppermute | solution.py:397
  37.2 10.4 %collective-permute-start.4 = (bf16[96,768]{1,0:T(8,128)(2,1)S(1)}, bf16[96,768]{1,0:T(8,128)(2,1)S(1)}, u32[]{:S(2)}, u32[]{:S(2)}) collective-permute-start(bf16[96,768]{1,0:T(8,128)(2,1)S(1)} %get-tuple-element.85), channel_id=1, source_target_pairs={{0,192},{64,128},{128,64},{192,0},{1,193},{65,129},{129,65},{193,1... | collective-permute-start | bytes 442376 | tf_op jit(solution)/shard_map/ppermute | solution.py:397
  39.5 8.1 %collective-permute-start.5 = (bf16[96,768]{1,0:T(8,128)(2,1)S(1)}, bf16[96,768]{1,0:T(8,128)(2,1)S(1)}, u32[]{:S(2)}, u32[]{:S(2)}) collective-permute-start(bf16[96,768]{1,0:T(8,128)(2,1)S(1)} %get-tuple-element.86), channel_id=1, source_target_pairs={{0,64},{64,0},{128,192},{192,128},{1,65},{65,1},{129,193},{193,129... | collective-permute-start | bytes 442376 | tf_op jit(solution)/shard_map/ppermute | solution.py:397
  42.9 7.7 %collective-permute-start.12 = (bf16[200,384]{1,0:T(8,128)(2,1)S(1)}, bf16[200,384]{1,0:T(8,128)(2,1)S(1)}, u32[]{:S(2)}, u32[]{:S(2)}) collective-permute-start(bf16[200,384]{1,0:T(8,128)(2,1)S(1)} %get-tuple-element.99), channel_id=1, source_target_pairs={{0,5},{1,4},{4,1},{5,0},{2,7},{3,6},{6,3},{7,2},{8,13},{9,12},{12,... | collective-permute-start | bytes 460808 | tf_op jit(solution)/shard_map/ppermute | solution.py:397
  45.3 5.4 %collective-permute-start.13 = (bf16[192,384]{1,0:T(8,128)(2,1)S(1)}, bf16[192,384]{1,0:T(8,128)(2,1)S(1)}, u32[]{:S(2)}, u32[]{:S(2)}) collective-permute-start(bf16[192,384]{1,0:T(8,128)(2,1)S(1)} %get-tuple-element.100), channel_id=1, source_target_pairs={{0,4},{1,5},{4,0},{5,1},{2,6},{3,7},{6,2},{7,3},{8,12},{9,13},{12,... | collective-permute-start | bytes 442376 | tf_op jit(solution)/shard_map/ppermute | solution.py:397
  47.6 33.3 %copy-start = (bf16[768,768]{1,0:T(8,128)(2,1)S(1)}, bf16[768,768]{1,0:T(8,128)(2,1)}, u32[]{:S(2)}) copy-start(bf16[768,768]{1,0:T(8,128)(2,1)} %wo_ref.1) | copy-start | bytes 3538948
  47.6 33.2 %copy-start.1 = (bf16[1,256,768]{2,1,0:T(8,128)(2,1)S(1)}, bf16[1,256,768]{2,1,0:T(8,128)(2,1)}, u32[]{:S(2)}) copy-start(bf16[1,256,768]{2,1,0:T(8,128)(2,1)} %param.6) | copy-start | bytes 1179652
  47.6 33.2 %copy-start.2 = (bf16[1,256,768]{2,1,0:T(8,128)(2,1)S(1)}, bf16[1,256,768]{2,1,0:T(8,128)(2,1)}, u32[]{:S(2)}) copy-start(bf16[1,256,768]{2,1,0:T(8,128)(2,1)} %param.7) | copy-start | bytes 1179652
  47.7 33.2 %copy-start.3 = (f32[768]{0:T(1024)S(1)}, f32[768]{0:T(1024)}, u32[]{:S(2)}) copy-start(f32[768]{0:T(1024)} %gain_ref.1) | copy-start | bytes 9220
  47.7 9.9 %collective-permute-start.6 = (bf16[48,768]{1,0:T(8,128)(2,1)S(1)}, bf16[48,768]{1,0:T(8,128)(2,1)S(1)}, u32[]{:S(2)}, u32[]{:S(2)}) collective-permute-start(bf16[48,768]{1,0:T(8,128)(2,1)S(1)} %get-tuple-element.88), channel_id=1, source_target_pairs={{0,1},{1,0},{4,5},{5,4},{2,3},{3,2},{6,7},{7,6},{8,9},{9,8},{12,13... | collective-permute-start | bytes 221192 | tf_op jit(solution)/shard_map/ppermute | solution.py:397
  50.8 11.2 %collective-permute-start.14 = (bf16[56,768]{1,0:T(8,128)(2,1)S(1)}, bf16[56,768]{1,0:T(8,128)(2,1)S(1)}, u32[]{:S(2)}, u32[]{:S(2)}) collective-permute-start(bf16[56,768]{1,0:T(8,128)(2,1)S(1)} %get-tuple-element.102), channel_id=1, source_target_pairs={{0,64},{64,0},{128,192},{192,128},{1,65},{65,1},{129,193},{193,129... | collective-permute-start | bytes 258056 | tf_op jit(solution)/shard_map/ppermute | solution.py:397
  53.4 8.5 %collective-permute-start.15 = (bf16[56,768]{1,0:T(8,128)(2,1)S(1)}, bf16[56,768]{1,0:T(8,128)(2,1)S(1)}, u32[]{:S(2)}, u32[]{:S(2)}) collective-permute-start(bf16[56,768]{1,0:T(8,128)(2,1)S(1)} %get-tuple-element.103), channel_id=1, source_target_pairs={{0,128},{64,192},{128,0},{192,64},{1,129},{65,193},{129,1},{193,65... | collective-permute-start | bytes 258056 | tf_op jit(solution)/shard_map/ppermute | solution.py:397
  55.7 6.2 %collective-permute-start.16 = (bf16[56,768]{1,0:T(8,128)(2,1)S(1)}, bf16[56,768]{1,0:T(8,128)(2,1)S(1)}, u32[]{:S(2)}, u32[]{:S(2)}) collective-permute-start(bf16[56,768]{1,0:T(8,128)(2,1)S(1)} %get-tuple-element.104), channel_id=1, source_target_pairs={{0,192},{64,128},{128,64},{192,0},{1,193},{65,129},{129,65},{193,1... | collective-permute-start | bytes 258056 | tf_op jit(solution)/shard_map/ppermute | solution.py:397
  56.2 4.4 %collective-permute-start.7 = (bf16[48,768]{1,0:T(8,128)(2,1)S(1)}, bf16[48,768]{1,0:T(8,128)(2,1)S(1)}, u32[]{:S(2)}, u32[]{:S(2)}) collective-permute-start(bf16[48,768]{1,0:T(8,128)(2,1)S(1)} %get-tuple-element.89), channel_id=1, source_target_pairs={{0,4},{1,5},{4,0},{5,1},{2,6},{3,7},{6,2},{7,3},{8,12},{9,13},{12,... | collective-permute-start | bytes 221192 | tf_op jit(solution)/shard_map/ppermute | solution.py:397
  57.6 4.4 %collective-permute-start.8 = (bf16[48,768]{1,0:T(8,128)(2,1)S(1)}, bf16[48,768]{1,0:T(8,128)(2,1)S(1)}, u32[]{:S(2)}, u32[]{:S(2)}) collective-permute-start(bf16[48,768]{1,0:T(8,128)(2,1)S(1)} %get-tuple-element.90), channel_id=1, source_target_pairs={{0,5},{1,4},{4,1},{5,0},{2,7},{3,6},{6,3},{7,2},{8,13},{9,12},{12,... | collective-permute-start | bytes 221192 | tf_op jit(solution)/shard_map/ppermute | solution.py:397
  78.8 5.3 %collective-permute-start.17 = (bf16[8,1536]{1,0:T(8,128)(2,1)S(1)}, bf16[8,1536]{1,0:T(8,128)(2,1)S(1)}, u32[]{:S(2)}, u32[]{:S(2)}) collective-permute-start(bf16[8,1536]{1,0:T(8,128)(2,1)S(1)} %get-tuple-element.105.mine_ref), channel_id=1, source_target_pairs={{0,1},{1,0},{2,3},{3,2},{4,5},{5,4},{6,7},{7,6},{8,9},{9,8},{10,11... | collective-permute-start | bytes 73736 | tf_op jit(solution)/shard_map/ppermute | solution.py:435

commit v8 on v7

--- a/solution.py
+++ b/solution.py
@@ -383,47 +383,53 @@
         [wide, wide, sds(T, 2 * GW), row, row, sds(T, 2 * D), sds(D, 2 * T), row],
         [at, gain_v, bias_v, xp, w, mt, qkv, dmix, npt], 1, limit=LIMIT,
     )
+    def swap(block):
+        return lax.ppermute(block, "c", [(0, 1), (1, 0)])
+
+    def permute(block, axes, k):
+        n = lax.axis_size(axes)
+        return lax.ppermute(block, axes, [(i, i ^ k) for i in range(n)])
+
+    def exchange(parts, axes):
+        return [parts[0]] + [permute(parts[k], axes, k) for k in (1, 2, 3)]
+
+    half = sds(192, 768)
+    send0_a, keep0_a, send1_a, keep1_a = call(pair_a_kernel, "pair_sum_a", [half] * 4, [keep_a, swap(send_a)])
+    got_a = [permute(send0_a, "y", RING_Y[0]), permute(send1_a, "y", RING_Y[1])]
+    keep0_a, kvm = lax.optimization_barrier((keep0_a, kvm))
     send_b, keep_b, mixed, dn = call(
         second_kernel, "heads_and_output_weight",
         [sds(392, 1536), sds(392, 1536), tokens, row],
         [at, w, mt, cot_v, qkv, dmix, mixed, dn, dnm, kvm, npt_all, xhat, xhatm], 1, limit=LIMIT,
     )
 
-    def swap(block):
-        return lax.ppermute(block, "c", [(0, 1), (1, 0)])
-
-    def permute(block, axes, k):
-        n = lax.axis_size(axes)
-        return lax.ppermute(block, axes, [(i, i ^ k) for i in range(n)])
-
-    def exchange(parts, axes):
-        return [parts[0]] + [permute(parts[k], axes, k) for k in (1, 2, 3)]
-
-    half = sds(192, 768)
-    send0_a, keep0_a, send1_a, keep1_a = call(pair_a_kernel, "pair_sum_a", [half] * 4, [keep_a, swap(send_a)])
+    send_b, *got_a = lax.optimization_barrier((send_b, *got_a))
+    recv_b = swap(send_b)
+    send0_a, send1_a, own_a = call(
+        step_a_kernel, "step_sum_a", [sds(96, 768), sds(96, 768), sds(96, 1536, dtype=F32)],
+        [got_a[0], keep0_a, got_a[1], keep1_a],
+    )
+    got_a = [permute(send0_a, "y", RING_Y[1]), permute(send1_a, "y", RING_Y[0])]
+    keep_b, own_a = lax.optimization_barrier((keep_b, own_a))
     send0_b, keep0_b, send1_b, keep1_b = call(
         pair_b_kernel, "pair_sum_b", [sds(392, 384), sds(392, 384), sds(384, 384), sds(384, 384)],
-        [keep_b, swap(send_b)],
-    )
-    got_a = [permute(send0_a, "y", RING_Y[0]), permute(send1_a, "y", RING_Y[1])]
+        [keep_b, recv_b],
+    )
     got_b = [permute(send0_b, ROW, RING_X[0]), permute(send1_b, ROW, RING_X[1])]
     out, dx = call(
         token_kernel, "token_outputs", [tokens, tokens],
         [gain, x, cot, mixed, wo, dn, xhat, rstd],
     )
-    send0_a, send1_a, own_a = call(
-        step_a_kernel, "step_sum_a", [sds(96, 768), sds(96, 768), sds(96, 1536, dtype=F32)],
-        [got_a[0], keep0_a, got_a[1], keep1_a],
-    )
-    got_a = [permute(send0_a, "y", RING_Y[1]), permute(send1_a, "y", RING_Y[0])]
+    parts_a = call(mid_a_kernel, "middle_sum_a", [sds(48, 768)] * 4, [own_a, *got_a])
+    parts_a = exchange(parts_a, ROW)
+    keep0_b, parts_a[0] = lax.optimization_barrier((keep0_b, parts_a[0]))
     send0_b, send1_b, own_b, vec = call(
         step_b_kernel, "step_sum_b", [sds(200, 384), sds(192, 384), sds(192, 768, dtype=F32), sds(2, D, dtype=F32)],
         [got_b[0], keep0_b, got_b[1], keep1_b],
     )
     got_b = [permute(send0_b, ROW, RING_X[1]), permute(send1_b, ROW, RING_X[0])]
-    parts_a = call(mid_a_kernel, "middle_sum_a", [sds(48, 768)] * 4, [own_a, *got_a])
+    own_b, *parts_a = lax.optimization_barrier((own_b, *parts_a))
     parts_b = call(mid_b_kernel, "middle_sum_b", [sds(56, 768)] * 4, [own_b, vec, *got_b])
-    parts_a = exchange(parts_a, ROW)
     parts_b = exchange(parts_b, "y")
     (mine,) = call(plane_kernel, "plane_sum", [sds(8, 8, 1536)], [*parts_a, *parts_b])
     mine = lax.all_to_all(mine, "z", 0, 0, tiled=True)

time: 86.2 us -> 95.8 us (1.11)
  waiting for transfers between devices: 14.6 us -> 24.4 us
    ppermute x2, waiting for transfers between devices: 0.01 us -> 5.58 us  [swap(): return lax.ppermute(block, 'c', [(0, 1), (1, 0)])]
    ppermute x14, waiting for transfers between devices: 10.7 us -> 15.3 us  [permute(): return lax.ppermute(block, axes, [(i, i ^ k) for i in range(n)])]
  transfers between devices with their start and end apart: 18 -> 18, of which waited for: 7 -> 12; matrix products, arithmetic and copies ran while one was open for 0% -> 0% of each run, Pallas kernels for 15% -> 13%
where the time goes in v8:
time: 95.8 us; the launch traced here: 95.3 us
  starting transfers between devices  29.9 us (31%)
  waiting for transfers between devices  24.4 us (25%)
  Pallas kernels  24 us (25%)
  blocking collectives  16.1 us (17%)
    ppermute x14, starting transfers between devices, permute(): return lax.ppermute(block, axes, [(i, i ^ k) for i in range(n)])  25.4 us
    pallas_call x13, Pallas kernels, call(): pl.pallas_call(kernel, name=name, in_specs=specs, out_specs=[VM] * len(ou...  24 us
    all_to_all x1, blocking collectives, on_device(): mine = lax.all_to_all(mine, 'z', 0, 0, tiled=True)  16.1 us
    ppermute x14, waiting for transfers between devices, permute(): return lax.ppermute(block, axes, [(i, i ^ k) for i in range(n)])  15.3 us
    ppermute x2, waiting for transfers between devices, swap(): return lax.ppermute(block, 'c', [(0, 1), (1, 0)])  5.58 us
    ppermute x1, starting transfers between devices, on_device(): other = lax.ppermute(mine, 'xh', [(0, 1), (1, 0)])  2.47 us
    ppermute x1, waiting for transfers between devices, on_device(): xp = lax.ppermute(x, SEQ, [(i, i + 1) for i in range(seq - 1)])  2.21 us
    ppermute x1, starting transfers between devices, on_device(): xp = lax.ppermute(x, SEQ, [(i, i + 1) for i in range(seq - 1)])  1.92 us
  transfers between devices with their start and end apart: 18, of which 12 were waited for; matrix products, arithmetic and copies ran while one was open for 0% of the time, Pallas kernels for 13%

profile of v8, /device:TPU:2, one launch (start us, length us, event | category | flops | bytes accessed | tf_op | source)
XLA Modules:
  0.0 95.3 jit_solution(6480253748205857429)
XLA Ops:
  0.6 1.9 %collective-permute-start = (bf16[256,768]{1,0:T(8,128)(2,1)}, bf16[256,768]{1,0:T(8,128)(2,1)S(1)}, u32[]{:S(2)}, u32[]{:S(2)}) collective-permute-start(bf16[256,768]{1,0:T(8,128)(2,1)} %bitcast.9), channel_id=1, source_target_pairs={{0,2},{2,4},{4,6},{6,8},{8,10},{10,12},{12,14},{14,16},{16,18},{18... | collective-permute-start | bytes 1179656 | tf_op jit(solution)/shard_map/ppermute | solution.py:369
  2.7 5.1 %own_part.1 = (bf16[256,2304]{1,0:T(8,128)(2,1)S(1)}, bf16[256,768]{1,0:T(8,128)(2,1)S(1)}, bf16[768,256]{1,0:T(8,128)(2,1)S(1)}, f32[256,768]{1,0:T(8,128)S(1)}...) custom-call(s32[5]{0:T(128)S(1)} %stack.27.at_ref, ...), custom_call_target="tpu_custom_call" | custom-call | tf_op jit(solution)/shard_map/own_part/pallas_call | solution.py:351
  7.7 2.2 %collective-permute-done.xp_ref = bf16[256,768]{1,0:T(8,128)(2,1)S(1)} collective-permute-done((bf16[256,768]{1,0:T(8,128)(2,1)}, bf16[256,768]{1,0:T(8,128)(2,1)S(1)}, u32[]{:S(2)}, u32[]{:S(2)}) %collective-permute-start) | collective-permute-done | bytes 393248 | tf_op jit(solution)/shard_map/ppermute | solution.py:369
  9.9 9.0 %memory_and_heads.1 = (bf16[384,1536]{1,0:T(8,128)(2,1)S(1)}, bf16[384,1536]{1,0:T(8,128)(2,1)S(1)}, bf16[256,512]{1,0:T(8,128)(2,1)S(1)}, f32[256,768]{1,0:T(8,...) custom-call(s32[5]{0:T(128)S(1)} %stack.27.at_ref, ...), custom_call_target="tpu_custom_call" | custom-call | tf_op jit(solution)/shard_map/memory_and_heads/pallas_call | solution.py:351
  19.0 2.8 %collective-permute-done.1.recv_ref = bf16[384,1536]{1,0:T(8,128)(2,1)S(1)} collective-permute-done((bf16[384,1536]{1,0:T(8,128)(2,1)S(1)}, bf16[384,1536]{1,0:T(8,128)(2,1)S(1)}, u32[]{:S(2)}, u32[]{:S(2)}) %collective-permute-start.1) | collective-permute-done | bytes 1179680 | tf_op jit(solution)/shard_map/ppermute | solution.py:387
  22.2 1.9 %collective-permute-start.2 = (bf16[192,768]{1,0:T(8,128)(2,1)S(1)}, bf16[192,768]{1,0:T(8,128)(2,1)S(1)}, u32[]{:S(2)}, u32[]{:S(2)}) collective-permute-start(bf16[192,768]{1,0:T(8,128)(2,1)S(1)} %get-tuple-element.98), channel_id=1, source_target_pairs={{0,64},{64,0},{128,192},{192,128},{1,65},{65,1},{129,193},{193,129... | collective-permute-start | bytes 884744 | tf_op jit(solution)/shard_map/ppermute | solution.py:391
  24.0 2.2 %collective-permute-start.3 = (bf16[192,768]{1,0:T(8,128)(2,1)S(1)}, bf16[192,768]{1,0:T(8,128)(2,1)S(1)}, u32[]{:S(2)}, u32[]{:S(2)}) collective-permute-start(bf16[192,768]{1,0:T(8,128)(2,1)S(1)} %get-tuple-element.99), channel_id=1, source_target_pairs={{0,192},{64,128},{128,64},{192,0},{1,193},{65,129},{129,65},{193,1... | collective-permute-start | bytes 884744 | tf_op jit(solution)/shard_map/ppermute | solution.py:391
  26.2 5.4 %heads_and_output_weight.1 = (bf16[392,1536]{1,0:T(8,128)(2,1)S(1)}, bf16[392,1536]{1,0:T(8,128)(2,1)S(1)}, bf16[256,768]{1,0:T(8,128)(2,1)S(1)}, f32[256,768]{1,0:T(8,128)S(1)}) custom-call(s32[5]{0:T(128)S(1)} %stack.27.at_ref, bf16[3,768,768]{2,1,0:T(8,128)(2,1)S(1)} %get-tuple-element.72.w_ref, bf16[768,768]{1,0:T(8,128)(2,1)S(1)} %get-tuple-element.73.mt_ref, ...), custom_call_target="tpu_custom_call" | custom-call | tf_op jit(solution)/shard_map/heads_and_output_weight/pallas_call | solution.py:351
  31.7 2.4 %collective-permute-done.3.recv1_ref = bf16[192,768]{1,0:T(8,128)(2,1)S(1)} collective-permute-done((bf16[192,768]{1,0:T(8,128)(2,1)S(1)}, bf16[192,768]{1,0:T(8,128)(2,1)S(1)}, u32[]{:S(2)}, u32[]{:S(2)}) %collective-permute-start.3) | collective-permute-done | bytes 294944 | tf_op jit(solution)/shard_map/ppermute | solution.py:391
  34.2 2.7 %collective-permute-done.4.recv_ref = bf16[392,1536]{1,0:T(8,128)(2,1)S(1)} collective-permute-done((bf16[392,1536]{1,0:T(8,128)(2,1)S(1)}, bf16[392,1536]{1,0:T(8,128)(2,1)S(1)}, u32[]{:S(2)}, u32[]{:S(2)}) %collective-permute-start.4) | collective-permute-done | bytes 1204256 | tf_op jit(solution)/shard_map/ppermute | solution.py:387
  37.2 5.0 %collective-permute-start.5 = (bf16[392,384]{1,0:T(8,128)(2,1)S(1)}, bf16[392,384]{1,0:T(8,128)(2,1)S(1)}, u32[]{:S(2)}, u32[]{:S(2)}) collective-permute-start(bf16[392,384]{1,0:T(8,128)(2,1)S(1)} %get-tuple-element.107), channel_id=1, source_target_pairs={{0,4},{1,5},{4,0},{5,1},{2,6},{3,7},{6,2},{7,3},{8,12},{9,13},{12,... | collective-permute-start | bytes 903176 | tf_op jit(solution)/shard_map/ppermute | solution.py:391
  43.0 2.2 %collective-permute-start.6 = (bf16[96,768]{1,0:T(8,128)(2,1)S(1)}, bf16[96,768]{1,0:T(8,128)(2,1)S(1)}, u32[]{:S(2)}, u32[]{:S(2)}) collective-permute-start(bf16[96,768]{1,0:T(8,128)(2,1)S(1)} %get-tuple-element.110), channel_id=1, source_target_pairs={{0,192},{64,128},{128,64},{192,0},{1,193},{65,129},{129,65},{193,1... | collective-permute-start | bytes 442376 | tf_op jit(solution)/shard_map/ppermute | solution.py:391
  45.2 4.6 %collective-permute-done.6.recv0_ref = bf16[96,768]{1,0:T(8,128)(2,1)S(1)} collective-permute-done((bf16[96,768]{1,0:T(8,128)(2,1)S(1)}, bf16[96,768]{1,0:T(8,128)(2,1)S(1)}, u32[]{:S(2)}, u32[]{:S(2)}) %collective-permute-start.6) | collective-permute-done | bytes 147488 | tf_op jit(solution)/shard_map/ppermute | solution.py:391
  52.4 3.4 %collective-permute-start.13 = (bf16[192,384]{1,0:T(8,128)(2,1)S(1)}, bf16[192,384]{1,0:T(8,128)(2,1)S(1)}, u32[]{:S(2)}, u32[]{:S(2)}) collective-permute-start(bf16[192,384]{1,0:T(8,128)(2,1)S(1)} %get-tuple-element.128), channel_id=1, source_target_pairs={{0,4},{1,5},{4,0},{5,1},{2,6},{3,7},{6,2},{7,3},{8,12},{9,13},{12,... | collective-permute-start | bytes 442376 | tf_op jit(solution)/shard_map/ppermute | solution.py:391
  55.8 2.1 %collective-permute-start.10 = (bf16[48,768]{1,0:T(8,128)(2,1)S(1)}, bf16[48,768]{1,0:T(8,128)(2,1)S(1)}, u32[]{:S(2)}, u32[]{:S(2)}) collective-permute-start(bf16[48,768]{1,0:T(8,128)(2,1)S(1)} %get-tuple-element.119), channel_id=1, source_target_pairs={{0,4},{1,5},{4,0},{5,1},{2,6},{3,7},{6,2},{7,3},{8,12},{9,13},{12,... | collective-permute-start | bytes 221192 | tf_op jit(solution)/shard_map/ppermute | solution.py:391
  57.9 2.0 %collective-permute-start.11 = (bf16[48,768]{1,0:T(8,128)(2,1)S(1)}, bf16[48,768]{1,0:T(8,128)(2,1)S(1)}, u32[]{:S(2)}, u32[]{:S(2)}) collective-permute-start(bf16[48,768]{1,0:T(8,128)(2,1)S(1)} %get-tuple-element.120), channel_id=1, source_target_pairs={{0,5},{1,4},{4,1},{5,0},{2,7},{3,6},{6,3},{7,2},{8,13},{9,12},{12,... | collective-permute-start | bytes 221192 | tf_op jit(solution)/shard_map/ppermute | solution.py:391
  59.9 1.8 %collective-permute-done.9.a1 = bf16[48,768]{1,0:T(8,128)(2,1)S(1)} collective-permute-done((bf16[48,768]{1,0:T(8,128)(2,1)S(1)}, bf16[48,768]{1,0:T(8,128)(2,1)S(1)}, u32[]{:S(2)}, u32[]{:S(2)}) %collective-permute-start.9) | collective-permute-done | bytes 73760 | tf_op jit(solution)/shard_map/ppermute | solution.py:391
  62.8 3.4 %collective-permute-start.15 = (bf16[56,768]{1,0:T(8,128)(2,1)S(1)}, bf16[56,768]{1,0:T(8,128)(2,1)S(1)}, u32[]{:S(2)}, u32[]{:S(2)}) collective-permute-start(bf16[56,768]{1,0:T(8,128)(2,1)S(1)} %get-tuple-element.131), channel_id=1, source_target_pairs={{0,128},{64,192},{128,0},{192,64},{1,129},{65,193},{129,1},{193,65... | collective-permute-start | bytes 258056 | tf_op jit(solution)/shard_map/ppermute | solution.py:391
  67.3 2.3 %collective-permute-done.15.b2 = bf16[56,768]{1,0:T(8,128)(2,1)S(1)} collective-permute-done((bf16[56,768]{1,0:T(8,128)(2,1)S(1)}, bf16[56,768]{1,0:T(8,128)(2,1)S(1)}, u32[]{:S(2)}, u32[]{:S(2)}) %collective-permute-start.15) | collective-permute-done | bytes 86048 | tf_op jit(solution)/shard_map/ppermute | solution.py:391
  69.7 2.3 %collective-permute-done.16.b3 = bf16[56,768]{1,0:T(8,128)(2,1)S(1)} collective-permute-done((bf16[56,768]{1,0:T(8,128)(2,1)S(1)}, bf16[56,768]{1,0:T(8,128)(2,1)S(1)}, u32[]{:S(2)}, u32[]{:S(2)}) %collective-permute-start.16) | collective-permute-done | bytes 86048 | tf_op jit(solution)/shard_map/ppermute | solution.py:391
  72.1 16.1 %all_to_all.5.in_ref = bf16[8,8,1536]{2,1,0:T(8,128)(2,1)S(1)} all-to-all(bf16[8,8,1536]{2,1,0:T(8,128)(2,1)S(1)} %plane_sum.1), channel_id=1, replica_groups=mesh['y'=4,'z'=8,'xl'=2,'c'=2,'xh'=2] {'z'}, dimensions={0} | all-to-all | bytes 393216 | tf_op jit(solution)/shard_map/all_to_all | solution.py:435
  88.8 2.5 %collective-permute-start.17 = (bf16[8,1536]{1,0:T(8,128)(2,1)S(1)}, bf16[8,1536]{1,0:T(8,128)(2,1)S(1)}, u32[]{:S(2)}, u32[]{:S(2)}) collective-permute-start(bf16[8,1536]{1,0:T(8,128)(2,1)S(1)} %get-tuple-element.133.mine_ref), channel_id=1, source_target_pairs={{0,1},{1,0},{2,3},{3,2},{4,5},{5,4},{6,7},{7,6},{8,9},{9,8},{10,11... | collective-permute-start | bytes 73736 | tf_op jit(solution)/shard_map/ppermute | solution.py:441
  91.3 1.6 %token_outputs.1 = (bf16[256,768]{1,0:T(8,128)(2,1)}, bf16[256,768]{1,0:T(8,128)(2,1)}) custom-call(f32[768]{0:T(1024)S(1)} %copy-done.3, bf16[256,768]{1,0:T(8,128)(2,1)S(1)} %bitcast.11, bf16[256,768]{1,0:T(8,128)(2,1)S(1)} %bitcast.13, bf16[256,768]{1,0:T(8,128)(2,1)S(1)} %get-tuple-element.91.mixed_ref, bf16[768,768]{1,0:T(8,128)(2,1)S(1)} %copy-done, ...), custom_call_target="tpu_custom_call" | custom-call | tf_op jit(solution)/shard_map/token_outputs/pallas_call | solution.py:351
  92.8 1.3 %collective-permute-done.17.other_ref = bf16[8,1536]{1,0:T(8,128)(2,1)S(1)} collective-permute-done((bf16[8,1536]{1,0:T(8,128)(2,1)S(1)}, bf16[8,1536]{1,0:T(8,128)(2,1)S(1)}, u32[]{:S(2)}, u32[]{:S(2)}) %collective-permute-start.17) | collective-permute-done | bytes 24608 | tf_op jit(solution)/shard_map/ppermute | solution.py:441
  (35 shorter events, 8.4 us)
Async XLA Ops:
  0.6 9.3 %collective-permute-start = (bf16[256,768]{1,0:T(8,128)(2,1)}, bf16[256,768]{1,0:T(8,128)(2,1)S(1)}, u32[]{:S(2)}, u32[]{:S(2)}) collective-permute-start(bf16[256,768]{1,0:T(8,128)(2,1)} %bitcast.9), channel_id=1, source_target_pairs={{0,2},{2,4},{4,6},{6,8},{8,10},{10,12},{12,14},{14,16},{16,18},{18... | collective-permute-start | bytes 1179656 | tf_op jit(solution)/shard_map/ppermute | solution.py:369
  18.9 2.9 %collective-permute-start.1 = (bf16[384,1536]{1,0:T(8,128)(2,1)S(1)}, bf16[384,1536]{1,0:T(8,128)(2,1)S(1)}, u32[]{:S(2)}, u32[]{:S(2)}) collective-permute-start(bf16[384,1536]{1,0:T(8,128)(2,1)S(1)} %get-tuple-element.84), channel_id=1, source_target_pairs={{0,2},{2,0},{1,3},{3,1},{4,6},{6,4},{5,7},{7,5},{8,10},{10,8},{9,1... | collective-permute-start | bytes 3538952 | tf_op jit(solution)/shard_map/ppermute | solution.py:387
  22.2 9.5 %collective-permute-start.2 = (bf16[192,768]{1,0:T(8,128)(2,1)S(1)}, bf16[192,768]{1,0:T(8,128)(2,1)S(1)}, u32[]{:S(2)}, u32[]{:S(2)}) collective-permute-start(bf16[192,768]{1,0:T(8,128)(2,1)S(1)} %get-tuple-element.98), channel_id=1, source_target_pairs={{0,64},{64,0},{128,192},{192,128},{1,65},{65,1},{129,193},{193,129... | collective-permute-start | bytes 884744 | tf_op jit(solution)/shard_map/ppermute | solution.py:391
  24.0 10.0 %collective-permute-start.3 = (bf16[192,768]{1,0:T(8,128)(2,1)S(1)}, bf16[192,768]{1,0:T(8,128)(2,1)S(1)}, u32[]{:S(2)}, u32[]{:S(2)}) collective-permute-start(bf16[192,768]{1,0:T(8,128)(2,1)S(1)} %get-tuple-element.99), channel_id=1, source_target_pairs={{0,192},{64,128},{128,64},{192,0},{1,193},{65,129},{129,65},{193,1... | collective-permute-start | bytes 884744 | tf_op jit(solution)/shard_map/ppermute | solution.py:391
  34.0 2.9 %collective-permute-start.4 = (bf16[392,1536]{1,0:T(8,128)(2,1)S(1)}, bf16[392,1536]{1,0:T(8,128)(2,1)S(1)}, u32[]{:S(2)}, u32[]{:S(2)}) collective-permute-start(bf16[392,1536]{1,0:T(8,128)(2,1)S(1)} %get-tuple-element.106), channel_id=1, source_target_pairs={{0,2},{2,0},{1,3},{3,1},{4,6},{6,4},{5,7},{7,5},{8,10},{10,8},{9,1... | collective-permute-start | bytes 3612680 | tf_op jit(solution)/shard_map/ppermute | solution.py:387
  37.2 13.8 %collective-permute-start.5 = (bf16[392,384]{1,0:T(8,128)(2,1)S(1)}, bf16[392,384]{1,0:T(8,128)(2,1)S(1)}, u32[]{:S(2)}, u32[]{:S(2)}) collective-permute-start(bf16[392,384]{1,0:T(8,128)(2,1)S(1)} %get-tuple-element.107), channel_id=1, source_target_pairs={{0,4},{1,5},{4,0},{5,1},{2,6},{3,7},{6,2},{7,3},{8,12},{9,13},{12,... | collective-permute-start | bytes 903176 | tf_op jit(solution)/shard_map/ppermute | solution.py:391
  42.2 8.8 %collective-permute-start.8 = (bf16[384,384]{1,0:T(8,128)(2,1)S(1)}, bf16[384,384]{1,0:T(8,128)(2,1)S(1)}, u32[]{:S(2)}, u32[]{:S(2)}) collective-permute-start(bf16[384,384]{1,0:T(8,128)(2,1)S(1)} %get-tuple-element.114), channel_id=1, source_target_pairs={{0,5},{1,4},{4,1},{5,0},{2,7},{3,6},{6,3},{7,2},{8,13},{9,12},{12,... | collective-permute-start | bytes 884744 | tf_op jit(solution)/shard_map/ppermute | solution.py:391
  43.0 6.8 %collective-permute-start.6 = (bf16[96,768]{1,0:T(8,128)(2,1)S(1)}, bf16[96,768]{1,0:T(8,128)(2,1)S(1)}, u32[]{:S(2)}, u32[]{:S(2)}) collective-permute-start(bf16[96,768]{1,0:T(8,128)(2,1)S(1)} %get-tuple-element.110), channel_id=1, source_target_pairs={{0,192},{64,128},{128,64},{192,0},{1,193},{65,129},{129,65},{193,1... | collective-permute-start | bytes 442376 | tf_op jit(solution)/shard_map/ppermute | solution.py:391
  45.2 5.3 %collective-permute-start.7 = (bf16[96,768]{1,0:T(8,128)(2,1)S(1)}, bf16[96,768]{1,0:T(8,128)(2,1)S(1)}, u32[]{:S(2)}, u32[]{:S(2)}) collective-permute-start(bf16[96,768]{1,0:T(8,128)(2,1)S(1)} %get-tuple-element.111), channel_id=1, source_target_pairs={{0,64},{64,0},{128,192},{192,128},{1,65},{65,1},{129,193},{193,129... | collective-permute-start | bytes 442376 | tf_op jit(solution)/shard_map/ppermute | solution.py:391
  51.2 40.1 %copy-start = (bf16[768,768]{1,0:T(8,128)(2,1)S(1)}, bf16[768,768]{1,0:T(8,128)(2,1)}, u32[]{:S(2)}) copy-start(bf16[768,768]{1,0:T(8,128)(2,1)} %wo_ref.1) | copy-start | bytes 3538948
  51.2 40.1 %copy-start.1 = (bf16[1,256,768]{2,1,0:T(8,128)(2,1)S(1)}, bf16[1,256,768]{2,1,0:T(8,128)(2,1)}, u32[]{:S(2)}) copy-start(bf16[1,256,768]{2,1,0:T(8,128)(2,1)} %param.6) | copy-start | bytes 1179652
  51.2 40.1 %copy-start.2 = (bf16[1,256,768]{2,1,0:T(8,128)(2,1)S(1)}, bf16[1,256,768]{2,1,0:T(8,128)(2,1)}, u32[]{:S(2)}) copy-start(bf16[1,256,768]{2,1,0:T(8,128)(2,1)} %param.7) | copy-start | bytes 1179652
  51.2 40.1 %copy-start.3 = (f32[768]{0:T(1024)S(1)}, f32[768]{0:T(1024)}, u32[]{:S(2)}) copy-start(f32[768]{0:T(1024)} %gain_ref.1) | copy-start | bytes 9220
  51.2 11.2 %collective-permute-start.12 = (bf16[200,384]{1,0:T(8,128)(2,1)S(1)}, bf16[200,384]{1,0:T(8,128)(2,1)S(1)}, u32[]{:S(2)}, u32[]{:S(2)}) collective-permute-start(bf16[200,384]{1,0:T(8,128)(2,1)S(1)} %get-tuple-element.127), channel_id=1, source_target_pairs={{0,5},{1,4},{4,1},{5,0},{2,7},{3,6},{6,3},{7,2},{8,13},{9,12},{12,... | collective-permute-start | bytes 460808 | tf_op jit(solution)/shard_map/ppermute | solution.py:391
  52.4 10.1 %collective-permute-start.13 = (bf16[192,384]{1,0:T(8,128)(2,1)S(1)}, bf16[192,384]{1,0:T(8,128)(2,1)S(1)}, u32[]{:S(2)}, u32[]{:S(2)}) collective-permute-start(bf16[192,384]{1,0:T(8,128)(2,1)S(1)} %get-tuple-element.128), channel_id=1, source_target_pairs={{0,4},{1,5},{4,0},{5,1},{2,6},{3,7},{6,2},{7,3},{8,12},{9,13},{12,... | collective-permute-start | bytes 442376 | tf_op jit(solution)/shard_map/ppermute | solution.py:391
  55.8 5.9 %collective-permute-start.9 = (bf16[48,768]{1,0:T(8,128)(2,1)S(1)}, bf16[48,768]{1,0:T(8,128)(2,1)S(1)}, u32[]{:S(2)}, u32[]{:S(2)}) collective-permute-start(bf16[48,768]{1,0:T(8,128)(2,1)S(1)} %get-tuple-element.118), channel_id=1, source_target_pairs={{0,1},{1,0},{4,5},{5,4},{2,3},{3,2},{6,7},{7,6},{8,9},{9,8},{12,13... | collective-permute-start | bytes 221192 | tf_op jit(solution)/shard_map/ppermute | solution.py:391
  55.8 5.9 %collective-permute-start.10 = (bf16[48,768]{1,0:T(8,128)(2,1)S(1)}, bf16[48,768]{1,0:T(8,128)(2,1)S(1)}, u32[]{:S(2)}, u32[]{:S(2)}) collective-permute-start(bf16[48,768]{1,0:T(8,128)(2,1)S(1)} %get-tuple-element.119), channel_id=1, source_target_pairs={{0,4},{1,5},{4,0},{5,1},{2,6},{3,7},{6,2},{7,3},{8,12},{9,13},{12,... | collective-permute-start | bytes 221192 | tf_op jit(solution)/shard_map/ppermute | solution.py:391
  57.9 4.5 %collective-permute-start.11 = (bf16[48,768]{1,0:T(8,128)(2,1)S(1)}, bf16[48,768]{1,0:T(8,128)(2,1)S(1)}, u32[]{:S(2)}, u32[]{:S(2)}) collective-permute-start(bf16[48,768]{1,0:T(8,128)(2,1)S(1)} %get-tuple-element.120), channel_id=1, source_target_pairs={{0,5},{1,4},{4,1},{5,0},{2,7},{3,6},{6,3},{7,2},{8,13},{9,12},{12,... | collective-permute-start | bytes 221192 | tf_op jit(solution)/shard_map/ppermute | solution.py:391
  62.5 4.8 %collective-permute-start.14 = (bf16[56,768]{1,0:T(8,128)(2,1)S(1)}, bf16[56,768]{1,0:T(8,128)(2,1)S(1)}, u32[]{:S(2)}, u32[]{:S(2)}) collective-permute-start(bf16[56,768]{1,0:T(8,128)(2,1)S(1)} %get-tuple-element.130), channel_id=1, source_target_pairs={{0,64},{64,0},{128,192},{192,128},{1,65},{65,1},{129,193},{193,129... | collective-permute-start | bytes 258056 | tf_op jit(solution)/shard_map/ppermute | solution.py:391
  62.8 6.8 %collective-permute-start.15 = (bf16[56,768]{1,0:T(8,128)(2,1)S(1)}, bf16[56,768]{1,0:T(8,128)(2,1)S(1)}, u32[]{:S(2)}, u32[]{:S(2)}) collective-permute-start(bf16[56,768]{1,0:T(8,128)(2,1)S(1)} %get-tuple-element.131), channel_id=1, source_target_pairs={{0,128},{64,192},{128,0},{192,64},{1,129},{65,193},{129,1},{193,65... | collective-permute-start | bytes 258056 | tf_op jit(solution)/shard_map/ppermute | solution.py:391
  66.3 5.7 %collective-permute-start.16 = (bf16[56,768]{1,0:T(8,128)(2,1)S(1)}, bf16[56,768]{1,0:T(8,128)(2,1)S(1)}, u32[]{:S(2)}, u32[]{:S(2)}) collective-permute-start(bf16[56,768]{1,0:T(8,128)(2,1)S(1)} %get-tuple-element.132), channel_id=1, source_target_pairs={{0,192},{64,128},{128,64},{192,0},{1,193},{65,129},{129,65},{193,1... | collective-permute-start | bytes 258056 | tf_op jit(solution)/shard_map/ppermute | solution.py:391
  88.8 5.3 %collective-permute-start.17 = (bf16[8,1536]{1,0:T(8,128)(2,1)S(1)}, bf16[8,1536]{1,0:T(8,128)(2,1)S(1)}, u32[]{:S(2)}, u32[]{:S(2)}) collective-permute-start(bf16[8,1536]{1,0:T(8,128)(2,1)S(1)} %get-tuple-element.133.mine_ref), channel_id=1, source_target_pairs={{0,1},{1,0},{2,3},{3,2},{4,5},{5,4},{6,7},{7,6},{8,9},{9,8},{10,11... | collective-permute-start | bytes 73736 | tf_op jit(solution)/shard_map/ppermute | solution.py:441

commit v9 on v7

--- a/solution.py
+++ b/solution.py
@@ -288,10 +288,18 @@
 
 
 def mid_a_kernel(own_ref, recv0_ref, recv1_ref, *outs):
-    for k in range(4):
-        rows = slice(48 * (k >> 1), 48 * (k >> 1) + 48)
-        recv = recv1_ref if k & 1 else recv0_ref
-        outs[k][...] = (own_ref[rows, 768 * (k & 1) : 768 * (k & 1) + 768] + recv[rows, :].astype(F32)).astype(BF)
+    for out, places in zip(outs, halving_order(RING_X)[0]):
+        for i, k in enumerate(places):
+            rows = slice(48 * (k >> 1), 48 * (k >> 1) + 48)
+            recv = recv1_ref if k & 1 else recv0_ref
+            out[48 * i : 48 * i + 48, :] = (
+                own_ref[rows, 768 * (k & 1) : 768 * (k & 1) + 768] + recv[rows, :].astype(F32)
+            ).astype(BF)
+
+
+def last_a_kernel(recv_ref, keep_ref, send_ref, own_ref):
+    own_ref[...] = keep_ref[0:48, :].astype(F32) + recv_ref[0:48, :].astype(F32)
+    send_ref[...] = (keep_ref[48:96, :].astype(F32) + recv_ref[48:96, :].astype(F32)).astype(BF)
 
 
 def mid_b_kernel(own_ref, vec_ref, recv0_ref, recv1_ref, *outs):
@@ -303,14 +311,14 @@
         outs[k][48:56, :] = vec
 
 
-def plane_kernel(a0, a1, a2, a3, b0, b1, b2, b3, out_ref):
+def plane_kernel(own_a_ref, recv_a_ref, b0, b1, b2, b3, out_ref):
     at = slice(48, 56)
     vec = (join_rows(b0[at]) + join_rows(b1[at])) + (join_rows(b2[at]) + join_rows(b3[at]))
     vec = jnp.concatenate([vec[0:1], vec[1:2]], axis=1)
     high = vec.astype(BF).astype(F32)
     tail = jnp.concatenate([high, vec - high], axis=0)
     g = slice(0, 48)
-    sums = jnp.concatenate([tree(a0[...], a1[...], a2[...], a3[...]), tree(b0[g], b1[g], b2[g], b3[g])], axis=1)
+    sums = jnp.concatenate([own_a_ref[...] + recv_a_ref[...].astype(F32), tree(b0[g], b1[g], b2[g], b3[g])], axis=1)
     for z in range(8):
         out_ref[z] = jnp.concatenate([sums[6 * z : 6 * z + 6], tail], axis=0).astype(BF)
 
@@ -421,11 +429,13 @@
         [got_b[0], keep0_b, got_b[1], keep1_b],
     )
     got_b = [permute(send0_b, ROW, RING_X[1]), permute(send1_b, ROW, RING_X[0])]
-    parts_a = call(mid_a_kernel, "middle_sum_a", [sds(48, 768)] * 4, [own_a, *got_a])
+    send_a, keep_a = call(mid_a_kernel, "middle_sum_a", [sds(96, 768)] * 2, [own_a, *got_a])
+    got_a = permute(send_a, ROW, RING_X[0])
     parts_b = call(mid_b_kernel, "middle_sum_b", [sds(56, 768)] * 4, [own_b, vec, *got_b])
-    parts_a = exchange(parts_a, ROW)
+    send_a, own_a = call(last_a_kernel, "last_sum_a", [sds(48, 768), sds(48, 768, dtype=F32)], [got_a, keep_a])
+    got_a = permute(send_a, ROW, RING_X[1])
     parts_b = exchange(parts_b, "y")
-    (mine,) = call(plane_kernel, "plane_sum", [sds(8, 8, 1536)], [*parts_a, *parts_b])
+    (mine,) = call(plane_kernel, "plane_sum", [sds(8, 8, 1536)], [own_a, got_a, *parts_b])
     mine = lax.all_to_all(mine, "z", 0, 0, tiled=True)
     factor = 1.0 / float(seq * lax.axis_size("xh") * T) ** 0.5
     mine, grad_gain, grad_bias = call(

time: 86.2 us -> 86.6 us (level)
  waiting for transfers between devices: 14.6 us -> 15.6 us
    ppermute x14 -> x13, waiting for transfers between devices: 10.7 us -> 11.6 us  [permute(): return lax.ppermute(block, axes, [(i, i ^ k) for i in range(n)])]
    ppermute x14 -> x13, starting transfers between devices: 24.8 us -> 24.2 us  [permute(): return lax.ppermute(block, axes, [(i, i ^ k) for i in range(n)])]
    pallas_call x13 -> x14, Pallas kernels: 24 us -> 24 us  [call(): pl.pallas_call(kernel, name=name, in_specs=specs, out_specs=[VM] * len(ou...]
  transfers between devices with their start and end apart: 18 -> 17, of which waited for: 7 -> 7; matrix products, arithmetic and copies ran while one was open for 0% -> 0% of each run, Pallas kernels for 15% -> 15%
where the time goes in v9:
time: 86.6 us; the launch traced here: 85.1 us
  starting transfers between devices  29 us (33%)
  Pallas kernels  24 us (28%)
  blocking collectives  15.8 us (18%)
  waiting for transfers between devices  15.6 us (18%)
    ppermute x13, starting transfers between devices, permute(): return lax.ppermute(block, axes, [(i, i ^ k) for i in range(n)])  24.2 us
    pallas_call x14, Pallas kernels, call(): pl.pallas_call(kernel, name=name, in_specs=specs, out_specs=[VM] * len(ou...  24 us
    all_to_all x1, blocking collectives, on_device(): mine = lax.all_to_all(mine, 'z', 0, 0, tiled=True)  15.8 us
    ppermute x13, waiting for transfers between devices, permute(): return lax.ppermute(block, axes, [(i, i ^ k) for i in range(n)])  11.6 us
    ppermute x1, waiting for transfers between devices, on_device(): xp = lax.ppermute(x, SEQ, [(i, i + 1) for i in range(seq - 1)])  2.21 us
    ppermute x1, starting transfers between devices, on_device(): other = lax.ppermute(mine, 'xh', [(0, 1), (1, 0)])  2.03 us
    ppermute x1, starting transfers between devices, on_device(): xp = lax.ppermute(x, SEQ, [(i, i + 1) for i in range(seq - 1)])  1.92 us
    ppermute x1, waiting for transfers between devices, on_device(): other = lax.ppermute(mine, 'xh', [(0, 1), (1, 0)])  1.74 us
  transfers between devices with their start and end apart: 17, of which 7 were waited for; matrix products, arithmetic and copies ran while one was open for 0% of the time, Pallas kernels for 15%

profile of v9, /device:TPU:2, one launch (start us, length us, event | category | flops | bytes accessed | tf_op | source)
XLA Modules:
  0.0 85.1 jit_solution(9161123788576917504)
XLA Ops:
  0.6 1.9 %collective-permute-start = (bf16[256,768]{1,0:T(8,128)(2,1)}, bf16[256,768]{1,0:T(8,128)(2,1)S(1)}, u32[]{:S(2)}, u32[]{:S(2)}) collective-permute-start(bf16[256,768]{1,0:T(8,128)(2,1)} %bitcast.9), channel_id=1, source_target_pairs={{0,2},{2,4},{4,6},{6,8},{8,10},{10,12},{12,14},{14,16},{16,18},{18... | collective-permute-start | bytes 1179656 | tf_op jit(solution)/shard_map/ppermute | solution.py:377
  2.7 5.1 %own_part.1 = (bf16[256,2304]{1,0:T(8,128)(2,1)S(1)}, bf16[256,768]{1,0:T(8,128)(2,1)S(1)}, bf16[768,256]{1,0:T(8,128)(2,1)S(1)}, f32[256,768]{1,0:T(8,128)S(1)}...) custom-call(s32[5]{0:T(128)S(1)} %stack.27.at_ref, ...), custom_call_target="tpu_custom_call" | custom-call | tf_op jit(solution)/shard_map/own_part/pallas_call | solution.py:359
  7.7 2.2 %collective-permute-done.xp_ref = bf16[256,768]{1,0:T(8,128)(2,1)S(1)} collective-permute-done((bf16[256,768]{1,0:T(8,128)(2,1)}, bf16[256,768]{1,0:T(8,128)(2,1)S(1)}, u32[]{:S(2)}, u32[]{:S(2)}) %collective-permute-start) | collective-permute-done | bytes 393248 | tf_op jit(solution)/shard_map/ppermute | solution.py:377
  9.9 9.0 %memory_and_heads.1 = (bf16[384,1536]{1,0:T(8,128)(2,1)S(1)}, bf16[384,1536]{1,0:T(8,128)(2,1)S(1)}, bf16[256,512]{1,0:T(8,128)(2,1)S(1)}, f32[256,768]{1,0:T(8,...) custom-call(s32[5]{0:T(128)S(1)} %stack.27.at_ref, ...), custom_call_target="tpu_custom_call" | custom-call | tf_op jit(solution)/shard_map/memory_and_heads/pallas_call | solution.py:359
  19.2 5.4 %heads_and_output_weight.1 = (bf16[392,1536]{1,0:T(8,128)(2,1)S(1)}, bf16[392,1536]{1,0:T(8,128)(2,1)S(1)}, bf16[256,768]{1,0:T(8,128)(2,1)S(1)}, f32[256,768]{1,0:T(8,128)S(1)}) custom-call(s32[5]{0:T(128)S(1)} %stack.27.at_ref, bf16[3,768,768]{2,1,0:T(8,128)(2,1)S(1)} %get-tuple-element.58.w_ref, bf16[768,768]{1,0:T(8,128)(2,1)S(1)} %get-tuple-element.59.mt_ref, ...), custom_call_target="tpu_custom_call" | custom-call | tf_op jit(solution)/shard_map/heads_and_output_weight/pallas_call | solution.py:359
  25.5 1.7 %collective-permute-start.2 = (bf16[192,768]{1,0:T(8,128)(2,1)S(1)}, bf16[192,768]{1,0:T(8,128)(2,1)S(1)}, u32[]{:S(2)}, u32[]{:S(2)}) collective-permute-start(bf16[192,768]{1,0:T(8,128)(2,1)S(1)} %get-tuple-element.80), channel_id=1, source_target_pairs={{0,64},{64,0},{128,192},{192,128},{1,65},{65,1},{129,193},{193,129... | collective-permute-start | bytes 884744 | tf_op jit(solution)/shard_map/ppermute | solution.py:405
  27.2 2.2 %collective-permute-start.3 = (bf16[192,768]{1,0:T(8,128)(2,1)S(1)}, bf16[192,768]{1,0:T(8,128)(2,1)S(1)}, u32[]{:S(2)}, u32[]{:S(2)}) collective-permute-start(bf16[192,768]{1,0:T(8,128)(2,1)S(1)} %get-tuple-element.82), channel_id=1, source_target_pairs={{0,192},{64,128},{128,64},{192,0},{1,193},{65,129},{129,65},{193,1... | collective-permute-start | bytes 884744 | tf_op jit(solution)/shard_map/ppermute | solution.py:405
  29.7 5.0 %collective-permute-start.9 = (bf16[392,384]{1,0:T(8,128)(2,1)S(1)}, bf16[392,384]{1,0:T(8,128)(2,1)S(1)}, u32[]{:S(2)}, u32[]{:S(2)}) collective-permute-start(bf16[392,384]{1,0:T(8,128)(2,1)S(1)} %get-tuple-element.93), channel_id=1, source_target_pairs={{0,4},{1,5},{4,0},{5,1},{2,6},{3,7},{6,2},{7,3},{8,12},{9,13},{12,... | collective-permute-start | bytes 903176 | tf_op jit(solution)/shard_map/ppermute | solution.py:405
  35.5 1.6 %collective-permute-done.3.recv1_ref = bf16[192,768]{1,0:T(8,128)(2,1)S(1)} collective-permute-done((bf16[192,768]{1,0:T(8,128)(2,1)S(1)}, bf16[192,768]{1,0:T(8,128)(2,1)S(1)}, u32[]{:S(2)}, u32[]{:S(2)}) %collective-permute-start.3) | collective-permute-done | bytes 294944 | tf_op jit(solution)/shard_map/ppermute | solution.py:405
  37.2 2.3 %collective-permute-start.4 = (bf16[96,768]{1,0:T(8,128)(2,1)S(1)}, bf16[96,768]{1,0:T(8,128)(2,1)S(1)}, u32[]{:S(2)}, u32[]{:S(2)}) collective-permute-start(bf16[96,768]{1,0:T(8,128)(2,1)S(1)} %get-tuple-element.85), channel_id=1, source_target_pairs={{0,192},{64,128},{128,64},{192,0},{1,193},{65,129},{129,65},{193,1... | collective-permute-start | bytes 442376 | tf_op jit(solution)/shard_map/ppermute | solution.py:405
  39.5 3.3 %collective-permute-done.10.recv1_ref = bf16[384,384]{1,0:T(8,128)(2,1)S(1)} collective-permute-done((bf16[384,384]{1,0:T(8,128)(2,1)S(1)}, bf16[384,384]{1,0:T(8,128)(2,1)S(1)}, u32[]{:S(2)}, u32[]{:S(2)}) %collective-permute-start.10) | collective-permute-done | bytes 294944 | tf_op jit(solution)/shard_map/ppermute | solution.py:405
  42.9 2.3 %collective-permute-start.11 = (bf16[200,384]{1,0:T(8,128)(2,1)S(1)}, bf16[200,384]{1,0:T(8,128)(2,1)S(1)}, u32[]{:S(2)}, u32[]{:S(2)}) collective-permute-start(bf16[200,384]{1,0:T(8,128)(2,1)S(1)} %get-tuple-element.99), channel_id=1, source_target_pairs={{0,5},{1,4},{4,1},{5,0},{2,7},{3,6},{6,3},{7,2},{8,13},{9,12},{12,... | collective-permute-start | bytes 460808 | tf_op jit(solution)/shard_map/ppermute | solution.py:405
  45.3 2.3 %collective-permute-start.12 = (bf16[192,384]{1,0:T(8,128)(2,1)S(1)}, bf16[192,384]{1,0:T(8,128)(2,1)S(1)}, u32[]{:S(2)}, u32[]{:S(2)}) collective-permute-start(bf16[192,384]{1,0:T(8,128)(2,1)S(1)} %get-tuple-element.100), channel_id=1, source_target_pairs={{0,4},{1,5},{4,0},{5,1},{2,6},{3,7},{6,2},{7,3},{8,12},{9,13},{12,... | collective-permute-start | bytes 442376 | tf_op jit(solution)/shard_map/ppermute | solution.py:405
  47.6 2.0 %collective-permute-start.6 = (bf16[96,768]{1,0:T(8,128)(2,1)S(1)}, bf16[96,768]{1,0:T(8,128)(2,1)S(1)}, u32[]{:S(2)}, u32[]{:S(2)}) collective-permute-start(bf16[96,768]{1,0:T(8,128)(2,1)S(1)} %get-tuple-element.87), channel_id=1, source_target_pairs={{0,4},{1,5},{4,0},{5,1},{2,6},{3,7},{6,2},{7,3},{8,12},{9,13},{12,... | collective-permute-start | bytes 442376 | tf_op jit(solution)/shard_map/ppermute | solution.py:405
  49.6 1.7 %collective-permute-done.12.recv1_ref = bf16[192,384]{1,0:T(8,128)(2,1)S(1)} collective-permute-done((bf16[192,384]{1,0:T(8,128)(2,1)S(1)}, bf16[192,384]{1,0:T(8,128)(2,1)S(1)}, u32[]{:S(2)}, u32[]{:S(2)}) %collective-permute-start.12) | collective-permute-done | bytes 147488 | tf_op jit(solution)/shard_map/ppermute | solution.py:405
  51.5 1.4 %collective-permute-start.13 = (bf16[56,768]{1,0:T(8,128)(2,1)S(1)}, bf16[56,768]{1,0:T(8,128)(2,1)S(1)}, u32[]{:S(2)}, u32[]{:S(2)}) collective-permute-start(bf16[56,768]{1,0:T(8,128)(2,1)S(1)} %get-tuple-element.102), channel_id=1, source_target_pairs={{0,64},{64,0},{128,192},{192,128},{1,65},{65,1},{129,193},{193,129... | collective-permute-start | bytes 258056 | tf_op jit(solution)/shard_map/ppermute | solution.py:405
  52.9 3.6 %collective-permute-start.14 = (bf16[56,768]{1,0:T(8,128)(2,1)S(1)}, bf16[56,768]{1,0:T(8,128)(2,1)S(1)}, u32[]{:S(2)}, u32[]{:S(2)}) collective-permute-start(bf16[56,768]{1,0:T(8,128)(2,1)S(1)} %get-tuple-element.103), channel_id=1, source_target_pairs={{0,128},{64,192},{128,0},{192,64},{1,129},{65,193},{129,1},{193,65... | collective-permute-start | bytes 258056 | tf_op jit(solution)/shard_map/ppermute | solution.py:405
  57.2 2.6 %collective-permute-done.14.b2 = bf16[56,768]{1,0:T(8,128)(2,1)S(1)} collective-permute-done((bf16[56,768]{1,0:T(8,128)(2,1)S(1)}, bf16[56,768]{1,0:T(8,128)(2,1)S(1)}, u32[]{:S(2)}, u32[]{:S(2)}) %collective-permute-start.14) | collective-permute-done | bytes 86048 | tf_op jit(solution)/shard_map/ppermute | solution.py:405
  59.8 2.3 %collective-permute-done.15.b3 = bf16[56,768]{1,0:T(8,128)(2,1)S(1)} collective-permute-done((bf16[56,768]{1,0:T(8,128)(2,1)S(1)}, bf16[56,768]{1,0:T(8,128)(2,1)S(1)}, u32[]{:S(2)}, u32[]{:S(2)}) %collective-permute-start.15) | collective-permute-done | bytes 86048 | tf_op jit(solution)/shard_map/ppermute | solution.py:405
  62.2 15.8 %all_to_all.5.in_ref = bf16[8,8,1536]{2,1,0:T(8,128)(2,1)S(1)} all-to-all(bf16[8,8,1536]{2,1,0:T(8,128)(2,1)S(1)} %plane_sum.1), channel_id=1, replica_groups=mesh['y'=4,'z'=8,'xl'=2,'c'=2,'xh'=2] {'z'}, dimensions={0} | all-to-all | bytes 393216 | tf_op jit(solution)/shard_map/all_to_all | solution.py:439
  78.6 2.0 %collective-permute-start.16 = (bf16[8,1536]{1,0:T(8,128)(2,1)S(1)}, bf16[8,1536]{1,0:T(8,128)(2,1)S(1)}, u32[]{:S(2)}, u32[]{:S(2)}) collective-permute-start(bf16[8,1536]{1,0:T(8,128)(2,1)S(1)} %get-tuple-element.105.mine_ref), channel_id=1, source_target_pairs={{0,1},{1,0},{2,3},{3,2},{4,5},{5,4},{6,7},{7,6},{8,9},{9,8},{10,11... | collective-permute-start | bytes 73736 | tf_op jit(solution)/shard_map/ppermute | solution.py:445
  80.7 1.6 %token_outputs.1 = (bf16[256,768]{1,0:T(8,128)(2,1)}, bf16[256,768]{1,0:T(8,128)(2,1)}) custom-call(f32[768]{0:T(1024)S(1)} %copy-done.3, bf16[256,768]{1,0:T(8,128)(2,1)S(1)} %bitcast.11, bf16[256,768]{1,0:T(8,128)(2,1)S(1)} %bitcast.13, bf16[256,768]{1,0:T(8,128)(2,1)S(1)} %get-tuple-element.73.mixed_ref, bf16[768,768]{1,0:T(8,128)(2,1)S(1)} %copy-done, ...), custom_call_target="tpu_custom_call" | custom-call | tf_op jit(solution)/shard_map/token_outputs/pallas_call | solution.py:359
  82.2 1.7 %collective-permute-done.16.other_ref = bf16[8,1536]{1,0:T(8,128)(2,1)S(1)} collective-permute-done((bf16[8,1536]{1,0:T(8,128)(2,1)S(1)}, bf16[8,1536]{1,0:T(8,128)(2,1)S(1)}, u32[]{:S(2)}, u32[]{:S(2)}) %collective-permute-start.16) | collective-permute-done | bytes 24608 | tf_op jit(solution)/shard_map/ppermute | solution.py:445
  83.9 1.2 %finish.1 = (f32[6,2304]{1,0:T(8,128)}, f32[6,768]{1,0:T(8,128)}) custom-call(s32[5]{0:T(128)S(1)} %stack.27.at_ref, bf16[8,1536]{1,0:T(8,128)(2,1)S(1)} %get-tuple-element.105.mine_ref, bf16[8,1536]{1,0:T(8,128)(2,1)S(1)} %collective-permute-done.16.other_ref), custom_call_target="tpu_custom_call" | custom-call | tf_op jit(solution)/shard_map/finish/pallas_call | solution.py:359
  (34 shorter events, 4.2 us)
Async XLA Ops:
  0.6 9.3 %collective-permute-start = (bf16[256,768]{1,0:T(8,128)(2,1)}, bf16[256,768]{1,0:T(8,128)(2,1)S(1)}, u32[]{:S(2)}, u32[]{:S(2)}) collective-permute-start(bf16[256,768]{1,0:T(8,128)(2,1)} %bitcast.9), channel_id=1, source_target_pairs={{0,2},{2,4},{4,6},{6,8},{8,10},{10,12},{12,14},{14,16},{16,18},{18... | collective-permute-start | bytes 1179656 | tf_op jit(solution)/shard_map/ppermute | solution.py:377
  18.9 6.3 %collective-permute-start.1 = (bf16[384,1536]{1,0:T(8,128)(2,1)S(1)}, bf16[384,1536]{1,0:T(8,128)(2,1)S(1)}, u32[]{:S(2)}, u32[]{:S(2)}) collective-permute-start(bf16[384,1536]{1,0:T(8,128)(2,1)S(1)} %get-tuple-element.79), channel_id=1, source_target_pairs={{0,2},{2,0},{1,3},{3,1},{4,6},{6,4},{5,7},{7,5},{8,10},{10,8},{9,1... | collective-permute-start | bytes 3538952 | tf_op jit(solution)/shard_map/ppermute | solution.py:401
  24.7 4.7 %collective-permute-start.8 = (bf16[392,1536]{1,0:T(8,128)(2,1)S(1)}, bf16[392,1536]{1,0:T(8,128)(2,1)S(1)}, u32[]{:S(2)}, u32[]{:S(2)}) collective-permute-start(bf16[392,1536]{1,0:T(8,128)(2,1)S(1)} %get-tuple-element.92), channel_id=1, source_target_pairs={{0,2},{2,0},{1,3},{3,1},{4,6},{6,4},{5,7},{7,5},{8,10},{10,8},{9,1... | collective-permute-start | bytes 3612680 | tf_op jit(solution)/shard_map/ppermute | solution.py:401
  25.5 9.9 %collective-permute-start.2 = (bf16[192,768]{1,0:T(8,128)(2,1)S(1)}, bf16[192,768]{1,0:T(8,128)(2,1)S(1)}, u32[]{:S(2)}, u32[]{:S(2)}) collective-permute-start(bf16[192,768]{1,0:T(8,128)(2,1)S(1)} %get-tuple-element.80), channel_id=1, source_target_pairs={{0,64},{64,0},{128,192},{192,128},{1,65},{65,1},{129,193},{193,129... | collective-permute-start | bytes 884744 | tf_op jit(solution)/shard_map/ppermute | solution.py:405
  27.2 9.9 %collective-permute-start.3 = (bf16[192,768]{1,0:T(8,128)(2,1)S(1)}, bf16[192,768]{1,0:T(8,128)(2,1)S(1)}, u32[]{:S(2)}, u32[]{:S(2)}) collective-permute-start(bf16[192,768]{1,0:T(8,128)(2,1)S(1)} %get-tuple-element.82), channel_id=1, source_target_pairs={{0,192},{64,128},{128,64},{192,0},{1,193},{65,129},{129,65},{193,1... | collective-permute-start | bytes 884744 | tf_op jit(solution)/shard_map/ppermute | solution.py:405
  29.7 13.1 %collective-permute-start.9 = (bf16[392,384]{1,0:T(8,128)(2,1)S(1)}, bf16[392,384]{1,0:T(8,128)(2,1)S(1)}, u32[]{:S(2)}, u32[]{:S(2)}) collective-permute-start(bf16[392,384]{1,0:T(8,128)(2,1)S(1)} %get-tuple-element.93), channel_id=1, source_target_pairs={{0,4},{1,5},{4,0},{5,1},{2,6},{3,7},{6,2},{7,3},{8,12},{9,13},{12,... | collective-permute-start | bytes 903176 | tf_op jit(solution)/shard_map/ppermute | solution.py:405
  34.7 8.1 %collective-permute-start.10 = (bf16[384,384]{1,0:T(8,128)(2,1)S(1)}, bf16[384,384]{1,0:T(8,128)(2,1)S(1)}, u32[]{:S(2)}, u32[]{:S(2)}) collective-permute-start(bf16[384,384]{1,0:T(8,128)(2,1)S(1)} %get-tuple-element.95), channel_id=1, source_target_pairs={{0,5},{1,4},{4,1},{5,0},{2,7},{3,6},{6,3},{7,2},{8,13},{9,12},{12,... | collective-permute-start | bytes 884744 | tf_op jit(solution)/shard_map/ppermute | solution.py:405
  37.2 10.4 %collective-permute-start.4 = (bf16[96,768]{1,0:T(8,128)(2,1)S(1)}, bf16[96,768]{1,0:T(8,128)(2,1)S(1)}, u32[]{:S(2)}, u32[]{:S(2)}) collective-permute-start(bf16[96,768]{1,0:T(8,128)(2,1)S(1)} %get-tuple-element.85), channel_id=1, source_target_pairs={{0,192},{64,128},{128,64},{192,0},{1,193},{65,129},{129,65},{193,1... | collective-permute-start | bytes 442376 | tf_op jit(solution)/shard_map/ppermute | solution.py:405
  39.5 8.1 %collective-permute-start.5 = (bf16[96,768]{1,0:T(8,128)(2,1)S(1)}, bf16[96,768]{1,0:T(8,128)(2,1)S(1)}, u32[]{:S(2)}, u32[]{:S(2)}) collective-permute-start(bf16[96,768]{1,0:T(8,128)(2,1)S(1)} %get-tuple-element.86), channel_id=1, source_target_pairs={{0,64},{64,0},{128,192},{192,128},{1,65},{65,1},{129,193},{193,129... | collective-permute-start | bytes 442376 | tf_op jit(solution)/shard_map/ppermute | solution.py:405
  42.9 8.4 %collective-permute-start.11 = (bf16[200,384]{1,0:T(8,128)(2,1)S(1)}, bf16[200,384]{1,0:T(8,128)(2,1)S(1)}, u32[]{:S(2)}, u32[]{:S(2)}) collective-permute-start(bf16[200,384]{1,0:T(8,128)(2,1)S(1)} %get-tuple-element.99), channel_id=1, source_target_pairs={{0,5},{1,4},{4,1},{5,0},{2,7},{3,6},{6,3},{7,2},{8,13},{9,12},{12,... | collective-permute-start | bytes 460808 | tf_op jit(solution)/shard_map/ppermute | solution.py:405
  45.3 6.1 %collective-permute-start.12 = (bf16[192,384]{1,0:T(8,128)(2,1)S(1)}, bf16[192,384]{1,0:T(8,128)(2,1)S(1)}, u32[]{:S(2)}, u32[]{:S(2)}) collective-permute-start(bf16[192,384]{1,0:T(8,128)(2,1)S(1)} %get-tuple-element.100), channel_id=1, source_target_pairs={{0,4},{1,5},{4,0},{5,1},{2,6},{3,7},{6,2},{7,3},{8,12},{9,13},{12,... | collective-permute-start | bytes 442376 | tf_op jit(solution)/shard_map/ppermute | solution.py:405
  47.6 8.8 %collective-permute-start.6 = (bf16[96,768]{1,0:T(8,128)(2,1)S(1)}, bf16[96,768]{1,0:T(8,128)(2,1)S(1)}, u32[]{:S(2)}, u32[]{:S(2)}) collective-permute-start(bf16[96,768]{1,0:T(8,128)(2,1)S(1)} %get-tuple-element.87), channel_id=1, source_target_pairs={{0,4},{1,5},{4,0},{5,1},{2,6},{3,7},{6,2},{7,3},{8,12},{9,13},{12,... | collective-permute-start | bytes 442376 | tf_op jit(solution)/shard_map/ppermute | solution.py:405
  51.4 29.3 %copy-start = (bf16[768,768]{1,0:T(8,128)(2,1)S(1)}, bf16[768,768]{1,0:T(8,128)(2,1)}, u32[]{:S(2)}) copy-start(bf16[768,768]{1,0:T(8,128)(2,1)} %wo_ref.1) | copy-start | bytes 3538948
  51.4 29.3 %copy-start.1 = (bf16[1,256,768]{2,1,0:T(8,128)(2,1)S(1)}, bf16[1,256,768]{2,1,0:T(8,128)(2,1)}, u32[]{:S(2)}) copy-start(bf16[1,256,768]{2,1,0:T(8,128)(2,1)} %param.6) | copy-start | bytes 1179652
  51.4 29.3 %copy-start.2 = (bf16[1,256,768]{2,1,0:T(8,128)(2,1)S(1)}, bf16[1,256,768]{2,1,0:T(8,128)(2,1)}, u32[]{:S(2)}) copy-start(bf16[1,256,768]{2,1,0:T(8,128)(2,1)} %param.7) | copy-start | bytes 1179652
  51.4 29.2 %copy-start.3 = (f32[768]{0:T(1024)S(1)}, f32[768]{0:T(1024)}, u32[]{:S(2)}) copy-start(f32[768]{0:T(1024)} %gain_ref.1) | copy-start | bytes 9220
  51.5 5.7 %collective-permute-start.13 = (bf16[56,768]{1,0:T(8,128)(2,1)S(1)}, bf16[56,768]{1,0:T(8,128)(2,1)S(1)}, u32[]{:S(2)}, u32[]{:S(2)}) collective-permute-start(bf16[56,768]{1,0:T(8,128)(2,1)S(1)} %get-tuple-element.102), channel_id=1, source_target_pairs={{0,64},{64,0},{128,192},{192,128},{1,65},{65,1},{129,193},{193,129... | collective-permute-start | bytes 258056 | tf_op jit(solution)/shard_map/ppermute | solution.py:405
  52.9 6.9 %collective-permute-start.14 = (bf16[56,768]{1,0:T(8,128)(2,1)S(1)}, bf16[56,768]{1,0:T(8,128)(2,1)S(1)}, u32[]{:S(2)}, u32[]{:S(2)}) collective-permute-start(bf16[56,768]{1,0:T(8,128)(2,1)S(1)} %get-tuple-element.103), channel_id=1, source_target_pairs={{0,128},{64,192},{128,0},{192,64},{1,129},{65,193},{129,1},{193,65... | collective-permute-start | bytes 258056 | tf_op jit(solution)/shard_map/ppermute | solution.py:405
  56.4 5.7 %collective-permute-start.15 = (bf16[56,768]{1,0:T(8,128)(2,1)S(1)}, bf16[56,768]{1,0:T(8,128)(2,1)S(1)}, u32[]{:S(2)}, u32[]{:S(2)}) collective-permute-start(bf16[56,768]{1,0:T(8,128)(2,1)S(1)} %get-tuple-element.104), channel_id=1, source_target_pairs={{0,192},{64,128},{128,64},{192,0},{1,193},{65,129},{129,65},{193,1... | collective-permute-start | bytes 258056 | tf_op jit(solution)/shard_map/ppermute | solution.py:405
  56.5 5.7 %collective-permute-start.7 = (bf16[48,768]{1,0:T(8,128)(2,1)S(1)}, bf16[48,768]{1,0:T(8,128)(2,1)S(1)}, u32[]{:S(2)}, u32[]{:S(2)}) collective-permute-start(bf16[48,768]{1,0:T(8,128)(2,1)S(1)} %get-tuple-element.90), channel_id=1, source_target_pairs={{0,5},{1,4},{4,1},{5,0},{2,7},{3,6},{6,3},{7,2},{8,13},{9,12},{12,... | collective-permute-start | bytes 221192 | tf_op jit(solution)/shard_map/ppermute | solution.py:405
  78.6 5.3 %collective-permute-start.16 = (bf16[8,1536]{1,0:T(8,128)(2,1)S(1)}, bf16[8,1536]{1,0:T(8,128)(2,1)S(1)}, u32[]{:S(2)}, u32[]{:S(2)}) collective-permute-start(bf16[8,1536]{1,0:T(8,128)(2,1)S(1)} %get-tuple-element.105.mine_ref), channel_id=1, source_target_pairs={{0,1},{1,0},{2,3},{3,2},{4,5},{5,4},{6,7},{7,6},{8,9},{9,8},{10,11... | collective-permute-start | bytes 73736 | tf_op jit(solution)/shard_map/ppermute | solution.py:445

commit v10 on v9

--- a/solution.py
+++ b/solution.py
@@ -405,7 +405,8 @@
         return lax.ppermute(block, axes, [(i, i ^ k) for i in range(n)])
 
     def exchange(parts, axes):
-        return [parts[0]] + [permute(parts[k], axes, k) for k in (1, 2, 3)]
+        got = {k: permute(parts[k], axes, k) for k in (2, 1, 3)}
+        return [parts[0], got[1], got[2], got[3]]
 
     half = sds(192, 768)
     send0_a, keep0_a, send1_a, keep1_a = call(pair_a_kernel, "pair_sum_a", [half] * 4, [keep_a, swap(send_a)])

time: 86.6 us -> 86.6 us (level)
  no operation moved by 1% of the time
where the time goes in v10:
time: 86.6 us; the launch traced here: 85.1 us
  starting transfers between devices  29 us (33%)
  Pallas kernels  24 us (28%)
  blocking collectives  15.8 us (18%)
  waiting for transfers between devices  15.6 us (18%)
    ppermute x13, starting transfers between devices, permute(): return lax.ppermute(block, axes, [(i, i ^ k) for i in range(n)])  24.2 us
    pallas_call x14, Pallas kernels, call(): pl.pallas_call(kernel, name=name, in_specs=specs, out_specs=[VM] * len(ou...  24 us
    all_to_all x1, blocking collectives, on_device(): mine = lax.all_to_all(mine, 'z', 0, 0, tiled=True)  15.8 us
    ppermute x13, waiting for transfers between devices, permute(): return lax.ppermute(block, axes, [(i, i ^ k) for i in range(n)])  11.6 us
    ppermute x1, waiting for transfers between devices, on_device(): xp = lax.ppermute(x, SEQ, [(i, i + 1) for i in range(seq - 1)])  2.21 us
    ppermute x1, starting transfers between devices, on_device(): other = lax.ppermute(mine, 'xh', [(0, 1), (1, 0)])  2.03 us
    ppermute x1, starting transfers between devices, on_device(): xp = lax.ppermute(x, SEQ, [(i, i + 1) for i in range(seq - 1)])  1.92 us
    ppermute x1, waiting for transfers between devices, on_device(): other = lax.ppermute(mine, 'xh', [(0, 1), (1, 0)])  1.74 us
  transfers between devices with their start and end apart: 17, of which 7 were waited for; matrix products, arithmetic and copies ran while one was open for 0% of the time, Pallas kernels for 15%

profile of v10, /device:TPU:2, one launch (start us, length us, event | category | flops | bytes accessed | tf_op | source)
XLA Modules:
  0.0 85.1 jit_solution(9161123788576917504)
XLA Ops:
  0.6 1.9 %collective-permute-start = (bf16[256,768]{1,0:T(8,128)(2,1)}, bf16[256,768]{1,0:T(8,128)(2,1)S(1)}, u32[]{:S(2)}, u32[]{:S(2)}) collective-permute-start(bf16[256,768]{1,0:T(8,128)(2,1)} %bitcast.9), channel_id=1, source_target_pairs={{0,2},{2,4},{4,6},{6,8},{8,10},{10,12},{12,14},{14,16},{16,18},{18... | collective-permute-start | bytes 1179656 | tf_op jit(solution)/shard_map/ppermute | solution.py:377
  2.7 5.1 %own_part.1 = (bf16[256,2304]{1,0:T(8,128)(2,1)S(1)}, bf16[256,768]{1,0:T(8,128)(2,1)S(1)}, bf16[768,256]{1,0:T(8,128)(2,1)S(1)}, f32[256,768]{1,0:T(8,128)S(1)}...) custom-call(s32[5]{0:T(128)S(1)} %stack.27.at_ref, ...), custom_call_target="tpu_custom_call" | custom-call | tf_op jit(solution)/shard_map/own_part/pallas_call | solution.py:359
  7.7 2.2 %collective-permute-done.xp_ref = bf16[256,768]{1,0:T(8,128)(2,1)S(1)} collective-permute-done((bf16[256,768]{1,0:T(8,128)(2,1)}, bf16[256,768]{1,0:T(8,128)(2,1)S(1)}, u32[]{:S(2)}, u32[]{:S(2)}) %collective-permute-start) | collective-permute-done | bytes 393248 | tf_op jit(solution)/shard_map/ppermute | solution.py:377
  9.9 9.0 %memory_and_heads.1 = (bf16[384,1536]{1,0:T(8,128)(2,1)S(1)}, bf16[384,1536]{1,0:T(8,128)(2,1)S(1)}, bf16[256,512]{1,0:T(8,128)(2,1)S(1)}, f32[256,768]{1,0:T(8,...) custom-call(s32[5]{0:T(128)S(1)} %stack.27.at_ref, ...), custom_call_target="tpu_custom_call" | custom-call | tf_op jit(solution)/shard_map/memory_and_heads/pallas_call | solution.py:359
  19.2 5.4 %heads_and_output_weight.1 = (bf16[392,1536]{1,0:T(8,128)(2,1)S(1)}, bf16[392,1536]{1,0:T(8,128)(2,1)S(1)}, bf16[256,768]{1,0:T(8,128)(2,1)S(1)}, f32[256,768]{1,0:T(8,128)S(1)}) custom-call(s32[5]{0:T(128)S(1)} %stack.27.at_ref, bf16[3,768,768]{2,1,0:T(8,128)(2,1)S(1)} %get-tuple-element.58.w_ref, bf16[768,768]{1,0:T(8,128)(2,1)S(1)} %get-tuple-element.59.mt_ref, ...), custom_call_target="tpu_custom_call" | custom-call | tf_op jit(solution)/shard_map/heads_and_output_weight/pallas_call | solution.py:359
  25.5 1.7 %collective-permute-start.2 = (bf16[192,768]{1,0:T(8,128)(2,1)S(1)}, bf16[192,768]{1,0:T(8,128)(2,1)S(1)}, u32[]{:S(2)}, u32[]{:S(2)}) collective-permute-start(bf16[192,768]{1,0:T(8,128)(2,1)S(1)} %get-tuple-element.80), channel_id=1, source_target_pairs={{0,64},{64,0},{128,192},{192,128},{1,65},{65,1},{129,193},{193,129... | collective-permute-start | bytes 884744 | tf_op jit(solution)/shard_map/ppermute | solution.py:405
  27.2 2.2 %collective-permute-start.3 = (bf16[192,768]{1,0:T(8,128)(2,1)S(1)}, bf16[192,768]{1,0:T(8,128)(2,1)S(1)}, u32[]{:S(2)}, u32[]{:S(2)}) collective-permute-start(bf16[192,768]{1,0:T(8,128)(2,1)S(1)} %get-tuple-element.82), channel_id=1, source_target_pairs={{0,192},{64,128},{128,64},{192,0},{1,193},{65,129},{129,65},{193,1... | collective-permute-start | bytes 884744 | tf_op jit(solution)/shard_map/ppermute | solution.py:405
  29.7 5.0 %collective-permute-start.9 = (bf16[392,384]{1,0:T(8,128)(2,1)S(1)}, bf16[392,384]{1,0:T(8,128)(2,1)S(1)}, u32[]{:S(2)}, u32[]{:S(2)}) collective-permute-start(bf16[392,384]{1,0:T(8,128)(2,1)S(1)} %get-tuple-element.93), channel_id=1, source_target_pairs={{0,4},{1,5},{4,0},{5,1},{2,6},{3,7},{6,2},{7,3},{8,12},{9,13},{12,... | collective-permute-start | bytes 903176 | tf_op jit(solution)/shard_map/ppermute | solution.py:405
  35.5 1.6 %collective-permute-done.3.recv1_ref = bf16[192,768]{1,0:T(8,128)(2,1)S(1)} collective-permute-done((bf16[192,768]{1,0:T(8,128)(2,1)S(1)}, bf16[192,768]{1,0:T(8,128)(2,1)S(1)}, u32[]{:S(2)}, u32[]{:S(2)}) %collective-permute-start.3) | collective-permute-done | bytes 294944 | tf_op jit(solution)/shard_map/ppermute | solution.py:405
  37.2 2.3 %collective-permute-start.4 = (bf16[96,768]{1,0:T(8,128)(2,1)S(1)}, bf16[96,768]{1,0:T(8,128)(2,1)S(1)}, u32[]{:S(2)}, u32[]{:S(2)}) collective-permute-start(bf16[96,768]{1,0:T(8,128)(2,1)S(1)} %get-tuple-element.85), channel_id=1, source_target_pairs={{0,192},{64,128},{128,64},{192,0},{1,193},{65,129},{129,65},{193,1... | collective-permute-start | bytes 442376 | tf_op jit(solution)/shard_map/ppermute | solution.py:405
  39.5 3.3 %collective-permute-done.10.recv1_ref = bf16[384,384]{1,0:T(8,128)(2,1)S(1)} collective-permute-done((bf16[384,384]{1,0:T(8,128)(2,1)S(1)}, bf16[384,384]{1,0:T(8,128)(2,1)S(1)}, u32[]{:S(2)}, u32[]{:S(2)}) %collective-permute-start.10) | collective-permute-done | bytes 294944 | tf_op jit(solution)/shard_map/ppermute | solution.py:405
  42.9 2.3 %collective-permute-start.11 = (bf16[200,384]{1,0:T(8,128)(2,1)S(1)}, bf16[200,384]{1,0:T(8,128)(2,1)S(1)}, u32[]{:S(2)}, u32[]{:S(2)}) collective-permute-start(bf16[200,384]{1,0:T(8,128)(2,1)S(1)} %get-tuple-element.99), channel_id=1, source_target_pairs={{0,5},{1,4},{4,1},{5,0},{2,7},{3,6},{6,3},{7,2},{8,13},{9,12},{12,... | collective-permute-start | bytes 460808 | tf_op jit(solution)/shard_map/ppermute | solution.py:405
  45.3 2.3 %collective-permute-start.12 = (bf16[192,384]{1,0:T(8,128)(2,1)S(1)}, bf16[192,384]{1,0:T(8,128)(2,1)S(1)}, u32[]{:S(2)}, u32[]{:S(2)}) collective-permute-start(bf16[192,384]{1,0:T(8,128)(2,1)S(1)} %get-tuple-element.100), channel_id=1, source_target_pairs={{0,4},{1,5},{4,0},{5,1},{2,6},{3,7},{6,2},{7,3},{8,12},{9,13},{12,... | collective-permute-start | bytes 442376 | tf_op jit(solution)/shard_map/ppermute | solution.py:405
  47.6 2.0 %collective-permute-start.6 = (bf16[96,768]{1,0:T(8,128)(2,1)S(1)}, bf16[96,768]{1,0:T(8,128)(2,1)S(1)}, u32[]{:S(2)}, u32[]{:S(2)}) collective-permute-start(bf16[96,768]{1,0:T(8,128)(2,1)S(1)} %get-tuple-element.87), channel_id=1, source_target_pairs={{0,4},{1,5},{4,0},{5,1},{2,6},{3,7},{6,2},{7,3},{8,12},{9,13},{12,... | collective-permute-start | bytes 442376 | tf_op jit(solution)/shard_map/ppermute | solution.py:405
  49.6 1.7 %collective-permute-done.12.recv1_ref = bf16[192,384]{1,0:T(8,128)(2,1)S(1)} collective-permute-done((bf16[192,384]{1,0:T(8,128)(2,1)S(1)}, bf16[192,384]{1,0:T(8,128)(2,1)S(1)}, u32[]{:S(2)}, u32[]{:S(2)}) %collective-permute-start.12) | collective-permute-done | bytes 147488 | tf_op jit(solution)/shard_map/ppermute | solution.py:405
  51.5 1.4 %collective-permute-start.13 = (bf16[56,768]{1,0:T(8,128)(2,1)S(1)}, bf16[56,768]{1,0:T(8,128)(2,1)S(1)}, u32[]{:S(2)}, u32[]{:S(2)}) collective-permute-start(bf16[56,768]{1,0:T(8,128)(2,1)S(1)} %get-tuple-element.102), channel_id=1, source_target_pairs={{0,64},{64,0},{128,192},{192,128},{1,65},{65,1},{129,193},{193,129... | collective-permute-start | bytes 258056 | tf_op jit(solution)/shard_map/ppermute | solution.py:405
  52.9 3.6 %collective-permute-start.14 = (bf16[56,768]{1,0:T(8,128)(2,1)S(1)}, bf16[56,768]{1,0:T(8,128)(2,1)S(1)}, u32[]{:S(2)}, u32[]{:S(2)}) collective-permute-start(bf16[56,768]{1,0:T(8,128)(2,1)S(1)} %get-tuple-element.103), channel_id=1, source_target_pairs={{0,128},{64,192},{128,0},{192,64},{1,129},{65,193},{129,1},{193,65... | collective-permute-start | bytes 258056 | tf_op jit(solution)/shard_map/ppermute | solution.py:405
  57.2 2.6 %collective-permute-done.14.b2 = bf16[56,768]{1,0:T(8,128)(2,1)S(1)} collective-permute-done((bf16[56,768]{1,0:T(8,128)(2,1)S(1)}, bf16[56,768]{1,0:T(8,128)(2,1)S(1)}, u32[]{:S(2)}, u32[]{:S(2)}) %collective-permute-start.14) | collective-permute-done | bytes 86048 | tf_op jit(solution)/shard_map/ppermute | solution.py:405
  59.8 2.3 %collective-permute-done.15.b3 = bf16[56,768]{1,0:T(8,128)(2,1)S(1)} collective-permute-done((bf16[56,768]{1,0:T(8,128)(2,1)S(1)}, bf16[56,768]{1,0:T(8,128)(2,1)S(1)}, u32[]{:S(2)}, u32[]{:S(2)}) %collective-permute-start.15) | collective-permute-done | bytes 86048 | tf_op jit(solution)/shard_map/ppermute | solution.py:405
  62.2 15.8 %all_to_all.5.in_ref = bf16[8,8,1536]{2,1,0:T(8,128)(2,1)S(1)} all-to-all(bf16[8,8,1536]{2,1,0:T(8,128)(2,1)S(1)} %plane_sum.1), channel_id=1, replica_groups=mesh['y'=4,'z'=8,'xl'=2,'c'=2,'xh'=2] {'z'}, dimensions={0} | all-to-all | bytes 393216 | tf_op jit(solution)/shard_map/all_to_all | solution.py:440
  78.6 2.0 %collective-permute-start.16 = (bf16[8,1536]{1,0:T(8,128)(2,1)S(1)}, bf16[8,1536]{1,0:T(8,128)(2,1)S(1)}, u32[]{:S(2)}, u32[]{:S(2)}) collective-permute-start(bf16[8,1536]{1,0:T(8,128)(2,1)S(1)} %get-tuple-element.105.mine_ref), channel_id=1, source_target_pairs={{0,1},{1,0},{2,3},{3,2},{4,5},{5,4},{6,7},{7,6},{8,9},{9,8},{10,11... | collective-permute-start | bytes 73736 | tf_op jit(solution)/shard_map/ppermute | solution.py:446
  80.7 1.6 %token_outputs.1 = (bf16[256,768]{1,0:T(8,128)(2,1)}, bf16[256,768]{1,0:T(8,128)(2,1)}) custom-call(f32[768]{0:T(1024)S(1)} %copy-done.3, bf16[256,768]{1,0:T(8,128)(2,1)S(1)} %bitcast.11, bf16[256,768]{1,0:T(8,128)(2,1)S(1)} %bitcast.13, bf16[256,768]{1,0:T(8,128)(2,1)S(1)} %get-tuple-element.73.mixed_ref, bf16[768,768]{1,0:T(8,128)(2,1)S(1)} %copy-done, ...), custom_call_target="tpu_custom_call" | custom-call | tf_op jit(solution)/shard_map/token_outputs/pallas_call | solution.py:359
  82.2 1.7 %collective-permute-done.16.other_ref = bf16[8,1536]{1,0:T(8,128)(2,1)S(1)} collective-permute-done((bf16[8,1536]{1,0:T(8,128)(2,1)S(1)}, bf16[8,1536]{1,0:T(8,128)(2,1)S(1)}, u32[]{:S(2)}, u32[]{:S(2)}) %collective-permute-start.16) | collective-permute-done | bytes 24608 | tf_op jit(solution)/shard_map/ppermute | solution.py:446
  83.9 1.2 %finish.1 = (f32[6,2304]{1,0:T(8,128)}, f32[6,768]{1,0:T(8,128)}) custom-call(s32[5]{0:T(128)S(1)} %stack.27.at_ref, bf16[8,1536]{1,0:T(8,128)(2,1)S(1)} %get-tuple-element.105.mine_ref, bf16[8,1536]{1,0:T(8,128)(2,1)S(1)} %collective-permute-done.16.other_ref), custom_call_target="tpu_custom_call" | custom-call | tf_op jit(solution)/shard_map/finish/pallas_call | solution.py:359
  (34 shorter events, 4.2 us)
Async XLA Ops:
  0.6 9.3 %collective-permute-start = (bf16[256,768]{1,0:T(8,128)(2,1)}, bf16[256,768]{1,0:T(8,128)(2,1)S(1)}, u32[]{:S(2)}, u32[]{:S(2)}) collective-permute-start(bf16[256,768]{1,0:T(8,128)(2,1)} %bitcast.9), channel_id=1, source_target_pairs={{0,2},{2,4},{4,6},{6,8},{8,10},{10,12},{12,14},{14,16},{16,18},{18... | collective-permute-start | bytes 1179656 | tf_op jit(solution)/shard_map/ppermute | solution.py:377
  18.9 6.3 %collective-permute-start.1 = (bf16[384,1536]{1,0:T(8,128)(2,1)S(1)}, bf16[384,1536]{1,0:T(8,128)(2,1)S(1)}, u32[]{:S(2)}, u32[]{:S(2)}) collective-permute-start(bf16[384,1536]{1,0:T(8,128)(2,1)S(1)} %get-tuple-element.79), channel_id=1, source_target_pairs={{0,2},{2,0},{1,3},{3,1},{4,6},{6,4},{5,7},{7,5},{8,10},{10,8},{9,1... | collective-permute-start | bytes 3538952 | tf_op jit(solution)/shard_map/ppermute | solution.py:401
  24.7 4.7 %collective-permute-start.8 = (bf16[392,1536]{1,0:T(8,128)(2,1)S(1)}, bf16[392,1536]{1,0:T(8,128)(2,1)S(1)}, u32[]{:S(2)}, u32[]{:S(2)}) collective-permute-start(bf16[392,1536]{1,0:T(8,128)(2,1)S(1)} %get-tuple-element.92), channel_id=1, source_target_pairs={{0,2},{2,0},{1,3},{3,1},{4,6},{6,4},{5,7},{7,5},{8,10},{10,8},{9,1... | collective-permute-start | bytes 3612680 | tf_op jit(solution)/shard_map/ppermute | solution.py:401
  25.5 9.9 %collective-permute-start.2 = (bf16[192,768]{1,0:T(8,128)(2,1)S(1)}, bf16[192,768]{1,0:T(8,128)(2,1)S(1)}, u32[]{:S(2)}, u32[]{:S(2)}) collective-permute-start(bf16[192,768]{1,0:T(8,128)(2,1)S(1)} %get-tuple-element.80), channel_id=1, source_target_pairs={{0,64},{64,0},{128,192},{192,128},{1,65},{65,1},{129,193},{193,129... | collective-permute-start | bytes 884744 | tf_op jit(solution)/shard_map/ppermute | solution.py:405
  27.2 9.9 %collective-permute-start.3 = (bf16[192,768]{1,0:T(8,128)(2,1)S(1)}, bf16[192,768]{1,0:T(8,128)(2,1)S(1)}, u32[]{:S(2)}, u32[]{:S(2)}) collective-permute-start(bf16[192,768]{1,0:T(8,128)(2,1)S(1)} %get-tuple-element.82), channel_id=1, source_target_pairs={{0,192},{64,128},{128,64},{192,0},{1,193},{65,129},{129,65},{193,1... | collective-permute-start | bytes 884744 | tf_op jit(solution)/shard_map/ppermute | solution.py:405
  29.7 13.1 %collective-permute-start.9 = (bf16[392,384]{1,0:T(8,128)(2,1)S(1)}, bf16[392,384]{1,0:T(8,128)(2,1)S(1)}, u32[]{:S(2)}, u32[]{:S(2)}) collective-permute-start(bf16[392,384]{1,0:T(8,128)(2,1)S(1)} %get-tuple-element.93), channel_id=1, source_target_pairs={{0,4},{1,5},{4,0},{5,1},{2,6},{3,7},{6,2},{7,3},{8,12},{9,13},{12,... | collective-permute-start | bytes 903176 | tf_op jit(solution)/shard_map/ppermute | solution.py:405
  34.7 8.1 %collective-permute-start.10 = (bf16[384,384]{1,0:T(8,128)(2,1)S(1)}, bf16[384,384]{1,0:T(8,128)(2,1)S(1)}, u32[]{:S(2)}, u32[]{:S(2)}) collective-permute-start(bf16[384,384]{1,0:T(8,128)(2,1)S(1)} %get-tuple-element.95), channel_id=1, source_target_pairs={{0,5},{1,4},{4,1},{5,0},{2,7},{3,6},{6,3},{7,2},{8,13},{9,12},{12,... | collective-permute-start | bytes 884744 | tf_op jit(solution)/shard_map/ppermute | solution.py:405
  37.2 10.4 %collective-permute-start.4 = (bf16[96,768]{1,0:T(8,128)(2,1)S(1)}, bf16[96,768]{1,0:T(8,128)(2,1)S(1)}, u32[]{:S(2)}, u32[]{:S(2)}) collective-permute-start(bf16[96,768]{1,0:T(8,128)(2,1)S(1)} %get-tuple-element.85), channel_id=1, source_target_pairs={{0,192},{64,128},{128,64},{192,0},{1,193},{65,129},{129,65},{193,1... | collective-permute-start | bytes 442376 | tf_op jit(solution)/shard_map/ppermute | solution.py:405
  39.5 8.1 %collective-permute-start.5 = (bf16[96,768]{1,0:T(8,128)(2,1)S(1)}, bf16[96,768]{1,0:T(8,128)(2,1)S(1)}, u32[]{:S(2)}, u32[]{:S(2)}) collective-permute-start(bf16[96,768]{1,0:T(8,128)(2,1)S(1)} %get-tuple-element.86), channel_id=1, source_target_pairs={{0,64},{64,0},{128,192},{192,128},{1,65},{65,1},{129,193},{193,129... | collective-permute-start | bytes 442376 | tf_op jit(solution)/shard_map/ppermute | solution.py:405
  42.9 8.4 %collective-permute-start.11 = (bf16[200,384]{1,0:T(8,128)(2,1)S(1)}, bf16[200,384]{1,0:T(8,128)(2,1)S(1)}, u32[]{:S(2)}, u32[]{:S(2)}) collective-permute-start(bf16[200,384]{1,0:T(8,128)(2,1)S(1)} %get-tuple-element.99), channel_id=1, source_target_pairs={{0,5},{1,4},{4,1},{5,0},{2,7},{3,6},{6,3},{7,2},{8,13},{9,12},{12,... | collective-permute-start | bytes 460808 | tf_op jit(solution)/shard_map/ppermute | solution.py:405
  45.3 6.1 %collective-permute-start.12 = (bf16[192,384]{1,0:T(8,128)(2,1)S(1)}, bf16[192,384]{1,0:T(8,128)(2,1)S(1)}, u32[]{:S(2)}, u32[]{:S(2)}) collective-permute-start(bf16[192,384]{1,0:T(8,128)(2,1)S(1)} %get-tuple-element.100), channel_id=1, source_target_pairs={{0,4},{1,5},{4,0},{5,1},{2,6},{3,7},{6,2},{7,3},{8,12},{9,13},{12,... | collective-permute-start | bytes 442376 | tf_op jit(solution)/shard_map/ppermute | solution.py:405
  47.6 8.8 %collective-permute-start.6 = (bf16[96,768]{1,0:T(8,128)(2,1)S(1)}, bf16[96,768]{1,0:T(8,128)(2,1)S(1)}, u32[]{:S(2)}, u32[]{:S(2)}) collective-permute-start(bf16[96,768]{1,0:T(8,128)(2,1)S(1)} %get-tuple-element.87), channel_id=1, source_target_pairs={{0,4},{1,5},{4,0},{5,1},{2,6},{3,7},{6,2},{7,3},{8,12},{9,13},{12,... | collective-permute-start | bytes 442376 | tf_op jit(solution)/shard_map/ppermute | solution.py:405
  51.4 29.3 %copy-start = (bf16[768,768]{1,0:T(8,128)(2,1)S(1)}, bf16[768,768]{1,0:T(8,128)(2,1)}, u32[]{:S(2)}) copy-start(bf16[768,768]{1,0:T(8,128)(2,1)} %wo_ref.1) | copy-start | bytes 3538948
  51.4 29.3 %copy-start.1 = (bf16[1,256,768]{2,1,0:T(8,128)(2,1)S(1)}, bf16[1,256,768]{2,1,0:T(8,128)(2,1)}, u32[]{:S(2)}) copy-start(bf16[1,256,768]{2,1,0:T(8,128)(2,1)} %param.6) | copy-start | bytes 1179652
  51.4 29.3 %copy-start.2 = (bf16[1,256,768]{2,1,0:T(8,128)(2,1)S(1)}, bf16[1,256,768]{2,1,0:T(8,128)(2,1)}, u32[]{:S(2)}) copy-start(bf16[1,256,768]{2,1,0:T(8,128)(2,1)} %param.7) | copy-start | bytes 1179652
  51.4 29.2 %copy-start.3 = (f32[768]{0:T(1024)S(1)}, f32[768]{0:T(1024)}, u32[]{:S(2)}) copy-start(f32[768]{0:T(1024)} %gain_ref.1) | copy-start | bytes 9220
  51.5 5.7 %collective-permute-start.13 = (bf16[56,768]{1,0:T(8,128)(2,1)S(1)}, bf16[56,768]{1,0:T(8,128)(2,1)S(1)}, u32[]{:S(2)}, u32[]{:S(2)}) collective-permute-start(bf16[56,768]{1,0:T(8,128)(2,1)S(1)} %get-tuple-element.102), channel_id=1, source_target_pairs={{0,64},{64,0},{128,192},{192,128},{1,65},{65,1},{129,193},{193,129... | collective-permute-start | bytes 258056 | tf_op jit(solution)/shard_map/ppermute | solution.py:405
  52.9 6.9 %collective-permute-start.14 = (bf16[56,768]{1,0:T(8,128)(2,1)S(1)}, bf16[56,768]{1,0:T(8,128)(2,1)S(1)}, u32[]{:S(2)}, u32[]{:S(2)}) collective-permute-start(bf16[56,768]{1,0:T(8,128)(2,1)S(1)} %get-tuple-element.103), channel_id=1, source_target_pairs={{0,128},{64,192},{128,0},{192,64},{1,129},{65,193},{129,1},{193,65... | collective-permute-start | bytes 258056 | tf_op jit(solution)/shard_map/ppermute | solution.py:405
  56.4 5.7 %collective-permute-start.15 = (bf16[56,768]{1,0:T(8,128)(2,1)S(1)}, bf16[56,768]{1,0:T(8,128)(2,1)S(1)}, u32[]{:S(2)}, u32[]{:S(2)}) collective-permute-start(bf16[56,768]{1,0:T(8,128)(2,1)S(1)} %get-tuple-element.104), channel_id=1, source_target_pairs={{0,192},{64,128},{128,64},{192,0},{1,193},{65,129},{129,65},{193,1... | collective-permute-start | bytes 258056 | tf_op jit(solution)/shard_map/ppermute | solution.py:405
  56.5 5.7 %collective-permute-start.7 = (bf16[48,768]{1,0:T(8,128)(2,1)S(1)}, bf16[48,768]{1,0:T(8,128)(2,1)S(1)}, u32[]{:S(2)}, u32[]{:S(2)}) collective-permute-start(bf16[48,768]{1,0:T(8,128)(2,1)S(1)} %get-tuple-element.90), channel_id=1, source_target_pairs={{0,5},{1,4},{4,1},{5,0},{2,7},{3,6},{6,3},{7,2},{8,13},{9,12},{12,... | collective-permute-start | bytes 221192 | tf_op jit(solution)/shard_map/ppermute | solution.py:405
  78.6 5.3 %collective-permute-start.16 = (bf16[8,1536]{1,0:T(8,128)(2,1)S(1)}, bf16[8,1536]{1,0:T(8,128)(2,1)S(1)}, u32[]{:S(2)}, u32[]{:S(2)}) collective-permute-start(bf16[8,1536]{1,0:T(8,128)(2,1)S(1)} %get-tuple-element.105.mine_ref), channel_id=1, source_target_pairs={{0,1},{1,0},{2,3},{3,2},{4,5},{5,4},{6,7},{7,6},{8,9},{9,8},{10,11... | collective-permute-start | bytes 73736 | tf_op jit(solution)/shard_map/ppermute | solution.py:446
